TPU v7x, 512 devices: a whole 4x4x16 slice. The times are simulated.
512 devices in a mesh: stream: 32 (over z, core), xsec: 16 (over y, x).
Axes of the slice: x: 4, y: 4, z: 16, core: 2. Of those that a mesh axis runs over, the one named last changes fastest.
Arguments:
- right_sides: float32 [32, 2048, 2048], P('stream', None, 'xsec'), may hold values from -6 to 6
- lower_first: bfloat16 [32, 2048, 2048], P('stream', None, 'xsec'), may hold values from -0.0625 to 0.0625
- upper_first: bfloat16 [32, 2048, 2048], P('stream', None, 'xsec'), may hold values from -0.0625 to 0.0625
- lower_second: bfloat16 [32, 2048, 2048], P('stream', None, 'xsec'), may hold values from -0.0625 to 0.0625
- upper_second: bfloat16 [32, 2048, 2048], P('stream', None, 'xsec'), may hold values from -0.0625 to 0.0625
Outputs:
- reduced: float32 [32, 2048, 2048], P('stream', None, 'xsec')
All inputs are finite; a program needn't handle non-finite values.
Results may differ from a plain program's by a relative error of at most 0.0023.
Values may be sent and summed in bfloat16 or wider, within the bound.
No kernel may reach another device: no remote copies, remote signals or barrier semaphores. Data moves between devices by JAX's collectives and lax.ppermute only.
A program may use at most 128 MiB of HBM per device.

v0:
```python
import jax
import jax.numpy as jnp
from jax import lax
from jax.sharding import PartitionSpec as P


def extended(value, sides, width):
    for axis, dim in sides:
        size, length = (lax.axis_size(axis), value.shape[dim])
        up = [(i, (i + 1) % size) for i in range(size - 1)]
        down = [(j, i) for i, j in up]
        last = lax.slice_in_dim(value, length - width, length, axis=dim)
        first = lax.slice_in_dim(value, 0, width, axis=dim)
        before = lax.ppermute(last, axis, up)
        after = lax.ppermute(first, axis, down)
        value = jnp.concatenate([before, value, after], axis=dim)
    return value


def shifted(value, axis, steps):
    count = lax.axis_size(axis)
    first, last = (max(0, -steps), min(count, count - steps))
    return lax.ppermute(value, axis, [(source, source + steps) for source in range(first, last)])


def neighbours_near(outgoing):
    padded = extended(outgoing[None], (("stream", 0),), 1)
    return (padded[0], padded[2])


def neighbours_far(outgoing):
    from_below = shifted(outgoing, "stream", 2)
    from_above = shifted(outgoing, "stream", -2)
    return (from_below, from_above)


def reduce_level(current, lower_blocks, upper_blocks, neighbours):
    outgoing = current.astype(jnp.bfloat16)
    from_below, from_above = neighbours(outgoing)
    lower_piece = lax.all_gather(lower_blocks, "xsec", axis=2, tiled=True)
    upper_piece = lax.all_gather(upper_blocks, "xsec", axis=2, tiled=True)
    total = jnp.dot(lower_piece[0], from_below, preferred_element_type=jnp.float32)
    total = total + jnp.dot(upper_piece[0], from_above, preferred_element_type=jnp.float32)
    return current + total


def on_device(right_sides, lower_first, upper_first, lower_second, upper_second):
    level_one = reduce_level(right_sides[0], lower_first, upper_first, neighbours_near)
    level_two = reduce_level(level_one, lower_second, upper_second, neighbours_far)
    return level_two[None]


def solution(mesh):
    return jax.shard_map(
        on_device,
        mesh=mesh,
        in_specs=(
            P("stream", None, "xsec"),
            P("stream", None, "xsec"),
            P("stream", None, "xsec"),
            P("stream", None, "xsec"),
            P("stream", None, "xsec"),
        ),
        out_specs=P("stream", None, "xsec"),
        check_vma=False,
    )
```

profile of v0, /device:TPU:1, one launch (start us, length us, event | category | flops | bytes accessed | tf_op | source)
XLA Modules:
  0.0 410.1 jit_solution(17927725365922115572)
XLA Ops:
  6.5 0.0 copy-start
  6.5 0.0 all-gather.7.cloned.1.call-start
  6.5 0.7 all-gather.7.cloned.1.call-update
  7.3 0.0 all-gather.5.cloned.1.call-start
  7.3 0.7 all-gather.5.cloned.1.call-update
  8.0 0.0 all-gather.11.cloned.1.call-start
  8.1 0.7 all-gather.11.cloned.1.call-update
  8.7 0.0 all-gather.9.cloned.1.call-start
  8.8 0.5 all-gather.9.cloned.1.call-update
  9.3 1.3 convert_element_type.7
  10.6 8.8 %collective-permute-start.1 = (bf16[1,2048,128]{2,1,0:T(8,128)(2,1)S(1)}, bf16[1,2048,128]{2,1,0:T(8,128)(2,1)}, u32[]{:S(2)}, u32[]{:S(2)}) collective-permute-start(bf16[1,2048,128]{2,1,0:T(8,128)(2,1)S(1)} %convert_element_type.7), channel_id=1, source_target_pairs={{16,0},{32,16},{48,32},{64,48},{80,64},{96,80},{112,96},{128,112},... | collective-permute-start | bytes 1572872 | tf_op jit(solution)/shard_map/ppermute | solution.py:15
  19.4 1.9 collective-permute-start
  21.3 1.2 collective-permute-done.1
  22.5 86.0 %all-gather.7.cloned.1.call-done = bf16[1,2048,2048]{2,1,0:T(8,128)(2,1)} async-done(((bf16[1,2048,128]{2,1,0:T(8,128)(2,1)}), bf16[1,2048,2048]{2,1,0:T(8,128)(2,1)}) %all-gather.7.cloned.1.call-update) | async-done | bytes 8388624 | tf_op jit(solution)/shard_map/all_gather | solution.py:41
  108.5 5.8 %fusion.4 = f32[2048,128]{1,0:T(8,128)S(1)} fusion(bf16[1,2048,2048]{2,1,0:T(8,128)(2,1)} %all-gather.7.cloned.1.call-done, bf16[1,2048,128]{2,1,0:T(8,128)(2,1)} %collective-permute-done.1), kind=kOutput, calls=%fused_computation.4 | convolution fusion | flops 1073741824 | bytes 9961472 | tf_op jit(solution)/shard_map/dot_general | solution.py:43
  114.2 0.0 collective-permute-done
  114.3 0.0 copy-start.1
  114.3 0.8 copy-done.1
  115.1 89.6 %all-gather.5.cloned.1.call-done = bf16[1,2048,2048]{2,1,0:T(8,128)(2,1)} async-done(((bf16[1,2048,128]{2,1,0:T(8,128)(2,1)}), bf16[1,2048,2048]{2,1,0:T(8,128)(2,1)}) %all-gather.5.cloned.1.call-update) | async-done | bytes 8388624 | tf_op jit(solution)/shard_map/all_gather | solution.py:40
  204.6 0.0 copy-done
  204.6 6.6 %fusion.28 = (bf16[2048,128]{1,0:T(8,128)(2,1)}, f32[2048,128]{1,0:T(8,128)S(1)}) fusion(f32[2048,128]{1,0:T(8,128)S(1)} %fusion.4, bf16[1,2048,128]{2,1,0:T(8,128)(2,1)} %copy-done.1, bf16[1,2048,2048]{2,1,0:T(8,128)(2,1)} %all-gather.5.cloned.1.call-done, f32[1,2048,128]{2,1,0:T(8,128)S(1)} %copy-done), kind=kOutput, calls=%fused_computation.16 | convolution fusion | flops 1074528256 | bytes 12582912 | tf_op jit(solution)/shard_map/dot_general | solution.py:42
  211.3 1.3 collective-permute-start.3
  212.6 4.0 collective-permute-start.2
  216.6 84.2 %all-gather.11.cloned.1.call-done = bf16[1,2048,2048]{2,1,0:T(8,128)(2,1)} async-done(((bf16[1,2048,128]{2,1,0:T(8,128)(2,1)}), bf16[1,2048,2048]{2,1,0:T(8,128)(2,1)}) %all-gather.11.cloned.1.call-update) | async-done | bytes 8388624 | tf_op jit(solution)/shard_map/all_gather | solution.py:41
  300.8 0.0 collective-permute-done.3
  300.8 5.7 %fusion = f32[128,2048]{0,1:T(8,128)S(1)} fusion(bf16[2048,128]{1,0:T(8,128)(2,1)S(1)} %collective-permute-done.3, bf16[1,2048,2048]{2,1,0:T(8,128)(2,1)} %all-gather.11.cloned.1.call-done), kind=kOutput, calls=%fused_computation | convolution fusion | flops 1073741824 | bytes 9961472 | tf_op jit(solution)/shard_map/dot_general | solution.py:43
  306.6 90.3 %all-gather.9.cloned.1.call-done = bf16[1,2048,2048]{2,1,0:T(8,128)(2,1)} async-done(((bf16[1,2048,128]{2,1,0:T(8,128)(2,1)}), bf16[1,2048,2048]{2,1,0:T(8,128)(2,1)}) %all-gather.9.cloned.1.call-update) | async-done | bytes 8388624 | tf_op jit(solution)/shard_map/all_gather | solution.py:40
  396.9 0.0 collective-permute-done.2
  396.9 6.7 %fusion.20 = f32[1,2048,128]{2,1,0:T(8,128)} fusion(f32[2048,128]{1,0:T(8,128)S(1)} %get-tuple-element.6, f32[128,2048]{0,1:T(8,128)S(1)} %fusion, bf16[2048,128]{1,0:T(8,128)(2,1)S(1)} %collective-permute-done.2, bf16[1,2048,2048]{2,1,0:T(8,128)(2,1)} %all-gather.9.cloned.1.call-done), kind=kOutput, calls=%fused_computation.12 | convolution fusion | flops 1074266112 | bytes 12058624 | tf_op jit(solution)/shard_map/dot_general | solution.py:42
Async XLA Ops:
  6.5 198.1 %copy-start = (f32[1,2048,128]{2,1,0:T(8,128)S(1)}, f32[1,2048,128]{2,1,0:T(8,128)}, u32[]{:S(2)}) copy-start(f32[1,2048,128]{2,1,0:T(8,128)} %param.5) | copy-start | bytes 3145732
  6.5 101.9 %all-gather.7.cloned.1.call-start = ((), (), s32[]{:S(2)}) async-start(), calls=%async_computation.1 | async-start | bytes 8912896 | tf_op jit(solution)/shard_map/all_gather | solution.py:41
  7.3 197.4 %all-gather.5.cloned.1.call-start = ((), (), s32[]{:S(2)}) async-start(), calls=%async_computation | async-start | bytes 8912896 | tf_op jit(solution)/shard_map/all_gather | solution.py:40
  8.0 292.8 %all-gather.11.cloned.1.call-start = ((), (), s32[]{:S(2)}) async-start(), calls=%async_computation.3 | async-start | bytes 8912896 | tf_op jit(solution)/shard_map/all_gather | solution.py:41
  8.7 388.1 %all-gather.9.cloned.1.call-start = ((), (), s32[]{:S(2)}) async-start(), calls=%async_computation.2 | async-start | bytes 8912896 | tf_op jit(solution)/shard_map/all_gather | solution.py:40
  10.6 11.9 %collective-permute-start.1 = (bf16[1,2048,128]{2,1,0:T(8,128)(2,1)S(1)}, bf16[1,2048,128]{2,1,0:T(8,128)(2,1)}, u32[]{:S(2)}, u32[]{:S(2)}) collective-permute-start(bf16[1,2048,128]{2,1,0:T(8,128)(2,1)S(1)} %convert_element_type.7), channel_id=1, source_target_pairs={{16,0},{32,16},{48,32},{64,48},{80,64},{96,80},{112,96},{128,112},... | collective-permute-start | bytes 1572872 | tf_op jit(solution)/shard_map/ppermute | solution.py:15
  19.4 94.9 %collective-permute-start = (bf16[1,2048,128]{2,1,0:T(8,128)(2,1)S(1)}, bf16[1,2048,128]{2,1,0:T(8,128)(2,1)S(1)}, u32[]{:S(2)}, u32[]{:S(2)}) collective-permute-start(bf16[1,2048,128]{2,1,0:T(8,128)(2,1)S(1)} %convert_element_type.7), channel_id=1, source_target_pairs={{0,16},{16,32},{32,48},{48,64},{64,80},{80,96},{96,112},{112,128},... | collective-permute-start | bytes 1572872 | tf_op jit(solution)/shard_map/ppermute | solution.py:14
  114.3 0.8 copy-start.1
  211.3 89.6 %collective-permute-start.3 = (bf16[2048,128]{1,0:T(8,128)(2,1)}, bf16[2048,128]{1,0:T(8,128)(2,1)S(1)}, u32[]{:S(2)}, u32[]{:S(2)}) collective-permute-start(bf16[2048,128]{1,0:T(8,128)(2,1)} %get-tuple-element.5), channel_id=1, source_target_pairs={{32,0},{48,16},{64,32},{80,48},{96,64},{112,80},{128,96},{144,112}... | collective-permute-start | bytes 1572872 | tf_op jit(solution)/shard_map/ppermute | solution.py:23
  212.6 184.3 %collective-permute-start.2 = (bf16[2048,128]{1,0:T(8,128)(2,1)}, bf16[2048,128]{1,0:T(8,128)(2,1)S(1)}, u32[]{:S(2)}, u32[]{:S(2)}) collective-permute-start(bf16[2048,128]{1,0:T(8,128)(2,1)} %get-tuple-element.5), channel_id=1, source_target_pairs={{0,32},{16,48},{32,64},{48,80},{64,96},{80,112},{96,128},{112,144}... | collective-permute-start | bytes 1572872 | tf_op jit(solution)/shard_map/ppermute | solution.py:23
Sparse Core Ops, SparseCore 0:
  10.3 98.0 all-gather.6
  111.5 93.1 all-gather.4
  207.6 93.1 all-gather.10
  303.7 93.1 all-gather.8
where the time goes:
time: 410 us
  waiting for transfers between devices  354 us (86%)
  matrix products  24.8 us (6%)
  starting transfers between devices  16.1 us (4%)
  between operations  13.2 us (3%)
    all_gather x2, waiting for transfers between devices, reduce_level(): lower_piece = lax.all_gather(lower_blocks, 'xsec', axis=2, tiled=True)  180 us
    all_gather x2, waiting for transfers between devices, reduce_level(): upper_piece = lax.all_gather(upper_blocks, 'xsec', axis=2, tiled=True)  170 us
    dot_general x2, matrix products, reduce_level(): jnp.dot(lower_piece[0], from_below, preferred_element_type=jnp.float32)  13.3 us
    dot_general x2, matrix products, reduce_level(): jnp.dot(upper_piece[0], from_above, preferred_element_type=jnp.float32)  11.5 us
    ppermute x1, starting transfers between devices, extended(): after = lax.ppermute(first, axis, down)  8.79 us
  transfers between devices with their start and end apart: 8, of which 5 were waited for; matrix products, arithmetic and copies ran while one was open for 5% of the time, Pallas kernels for 0%

commit v1 on v0

v1 whole, which is shorter than its diff:
```python
import jax
import jax.numpy as jnp
from jax import lax
from jax.experimental import pallas as pl
from jax.experimental.pallas import tpu as pltpu
from jax.sharding import Mesh, PartitionSpec as P

Z, CORES, Y, X = 16, 2, 4, 4
PLANES = Z * CORES
M = 2048
BLK = M // Y
COL = 128
AXES = ("z", "core", "y", "x")


def device_index(plane, y, x):
    return (plane * Y + y) * X + x


def moved(value, planes, ys):
    pairs = []
    for plane in range(PLANES):
        if not 0 <= plane + planes < PLANES:
            continue
        for y in range(Y):
            for x in range(X):
                pairs.append(
                    (
                        device_index(plane, y, x),
                        device_index(plane + planes, (y + ys) % Y, x),
                    )
                )
    return lax.ppermute(value, AXES, pairs)


def first_kernel(y_ref, a_ref, *refs):
    below, above = refs[0:4], refs[4:8]
    rhs_ref, corr_ref, sent_ref, acc_ref = refs[8:]
    step = pl.program_id(0)

    @pl.when(step == 0)
    def _():
        acc_ref[...] = jnp.zeros_like(acc_ref)

    total = acc_ref[...]
    for which, parts in ((0, below), (1, above)):
        left = jnp.concatenate([a_ref[x, 0, which] for x in range(X)], axis=1)
        right = jnp.concatenate([part[...] for part in parts], axis=1)
        total = total + jnp.dot(left, right, preferred_element_type=jnp.float32)
    acc_ref[...] = total

    @pl.when(step == Y - 1)
    def _():
        for d in range(Y):
            piece = acc_ref[:, d * COL : (d + 1) * COL]
            corr_ref[d] = piece
            owner = lax.rem(y_ref[0] + d, Y)
            sent_ref[d] = (rhs_ref[owner] + piece).astype(jnp.bfloat16)


def first_level(y, blocks, below, above, rhs):
    part = pl.BlockSpec((BLK, COL), lambda k, y: (k, 0))
    whole = pl.BlockSpec((Y, BLK, COL), lambda k, y: (0, 0, 0))
    return pl.pallas_call(
        first_kernel,
        name="first_level",
        out_shape=(
            jax.ShapeDtypeStruct((Y, BLK, COL), jnp.float32),
            jax.ShapeDtypeStruct((Y, BLK, COL), jnp.bfloat16),
        ),
        grid_spec=pltpu.PrefetchScalarGridSpec(
            num_scalar_prefetch=1,
            grid=(Y,),
            in_specs=[
                pl.BlockSpec((X, 1, 2, BLK, COL), lambda k, y: (0, k, 0, 0, 0))
            ]
            + [part] * 8
            + [whole],
            out_specs=(whole, whole),
            scratch_shapes=[pltpu.VMEM((BLK, Y * COL), jnp.float32)],
        ),
        compiler_params=pltpu.CompilerParams(vmem_limit_bytes=40 << 20),
        cost_estimate=pl.CostEstimate(
            flops=4 * BLK * M * Y * COL, bytes_accessed=11 << 20, transcendentals=0
        ),
    )(y, blocks, *below, *above, rhs)


def second_kernel(
    y_ref, lo_ref, up_ref, below, above, corr_ref, rhs_ref, own_ref, *outs
):
    step = pl.program_id(0)
    total = None
    for a_ref, b_ref in ((lo_ref, below), (up_ref, above)):
        left = jnp.concatenate([a_ref[x] for x in range(X)], axis=1)
        right = jnp.concatenate([b_ref[d] for d in range(Y)], axis=1)
        term = jnp.dot(left, right, preferred_element_type=jnp.float32)
        total = term if total is None else total + term
    here = step == y_ref[0]
    for d in range(Y):
        piece = total[:, d * COL : (d + 1) * COL]
        piece = piece + jnp.where(here, corr_ref[d], 0.0)
        if d == 0:
            own_ref[...] = piece + rhs_ref[...]
        else:
            outs[d - 1][...] = piece.astype(jnp.bfloat16)


def second_level(y, lo, up, below, above, corr, rhs):
    rows = pl.BlockSpec((BLK, COL), lambda m, y: (m, 0))
    blocks = pl.BlockSpec((X, BLK, COL), lambda m, y: (0, m, 0))
    whole = pl.BlockSpec((Y, BLK, COL), lambda m, y: (0, 0, 0))
    return pl.pallas_call(
        second_kernel,
        name="second_level",
        out_shape=(jax.ShapeDtypeStruct((M, COL), jnp.float32),)
        + (jax.ShapeDtypeStruct((M, COL), jnp.bfloat16),) * 3,
        grid_spec=pltpu.PrefetchScalarGridSpec(
            num_scalar_prefetch=1,
            grid=(Y,),
            in_specs=[blocks, blocks, whole, whole, whole, rows],
            out_specs=(rows,) * 4,
        ),
        compiler_params=pltpu.CompilerParams(vmem_limit_bytes=40 << 20),
        cost_estimate=pl.CostEstimate(
            flops=4 * BLK * M * Y * COL, bytes_accessed=9 << 20, transcendentals=0
        ),
    )(y, lo, up, below, above, corr, rhs)


def on_device(right_sides, lower_first, upper_first, lower_second, upper_second):
    rhs = right_sides[0]
    y = lax.axis_index("y").astype(jnp.int32)[None]

    lo_two = lax.all_gather(lower_second[0], "x", axis=0)

    sent_one = rhs.astype(jnp.bfloat16)
    own = [sent_one] + [moved(sent_one, 0, -d) for d in range(1, Y)]

    firsts = jnp.stack(
        [lower_first[0].reshape(Y, BLK, COL), upper_first[0].reshape(Y, BLK, COL)],
        axis=1,
    )
    firsts = lax.all_to_all(firsts, "y", 0, 0, tiled=True)
    blocks = lax.all_gather(firsts, "x", axis=0)

    below = [moved(part, 1, 0) for part in own]
    above = [moved(part, -1, 0) for part in own]
    rhs_rows = lax.all_to_all(rhs.reshape(Y, BLK, COL), "y", 0, 0, tiled=True)

    upper, blocks = lax.optimization_barrier((upper_second[0], blocks))
    up_two = lax.all_gather(upper, "x", axis=0)

    corr, sent_two = first_level(y, blocks, below, above, rhs_rows)
    below_two = moved(sent_two, 2, 0)
    above_two = moved(sent_two, -2, 0)
    total, *parts = second_level(y, lo_two, up_two, below_two, above_two, corr, rhs)
    for d in range(1, Y):
        total = total + moved(parts[d - 1], 0, d).astype(jnp.float32)
    return total[None]


def solution(mesh):
    fine = Mesh(mesh.devices.reshape(Z, CORES, Y, X), AXES)
    spec = P(("z", "core"), None, ("y", "x"))
    return jax.shard_map(
        on_device,
        mesh=fine,
        in_specs=(spec,) * 5,
        out_specs=spec,
        check_vma=False,
    )
```

time: 410 us -> 220 us (0.54)
  waiting for transfers between devices: 354 us -> 111 us
  starting transfers between devices: 16.1 us -> 56.4 us
  matrix products: 24.8 us -> 0 us
  blocking collectives: 0 us -> 14.7 us
  Pallas kernels: 0 us -> 9.89 us
  local copies, waits for them, and re-layouts: 0.79 us -> 7.56 us
    all_gather x4 -> x3, waiting for transfers between devices: 350 us -> 63.3 us  [the longest x1 63.3 us: on_device(): blocks = lax.all_gather(firsts, 'x', axis=0)]
    ppermute x4 -> x16, waiting for transfers between devices: 1.18 us -> 46.7 us  [moved(): return lax.ppermute(value, AXES, pairs)]
    ppermute x4 -> x16, starting transfers between devices: 16 us -> 52.6 us  [moved(): return lax.ppermute(value, AXES, pairs)]
    dot_general x4 -> x0, matrix products: 24.8 us -> none  [the longest x2 13.3 us: reduce_level(): jnp.dot(lower_piece[0], from_below, preferred_element_type=jnp.float32)]
    all_to_all x0 -> x1, blocking collectives: none -> 14.7 us  [on_device(): firsts = lax.all_to_all(firsts, 'y', 0, 0, tiled=True)]
    pallas_call x0 -> x2, Pallas kernels: none -> 9.89 us  [the longest x1 5.57 us: first_level(): pl.pallas_call(first_kernel, name='first_level', out_shape=(jax.ShapeDtyp...]
    unnamed x4 -> x10, local copies, waits for them, and re-layouts: 0.79 us -> 7.56 us
  transfers between devices with their start and end apart: 8 -> 20, of which waited for: 5 -> 9; matrix products, arithmetic and copies ran while one was open for 5% -> 1% of each run, Pallas kernels for 0% -> 3%
where the time goes in v1:
time: 220 us; the launch traced here: 217 us
  waiting for transfers between devices  111 us (50%)
  starting transfers between devices  56.4 us (26%)
  blocking collectives  14.7 us (7%)
  between operations  13.3 us (6%)
  Pallas kernels  9.89 us (4%)
  local copies, waits for them, and re-layouts  7.56 us (3%)
  other arithmetic  4.54 us (2%)
    all_gather x1, waiting for transfers between devices, on_device(): blocks = lax.all_gather(firsts, 'x', axis=0)  63.3 us
    ppermute x16, starting transfers between devices, moved(): return lax.ppermute(value, AXES, pairs)  52.6 us
    ppermute x16, waiting for transfers between devices, moved(): return lax.ppermute(value, AXES, pairs)  46.7 us
    all_to_all x1, blocking collectives, on_device(): firsts = lax.all_to_all(firsts, 'y', 0, 0, tiled=True)  14.7 us
    unnamed x10, local copies, waits for them, and re-layouts  7.56 us
    pallas_call x1, Pallas kernels, first_level(): pl.pallas_call(first_kernel, name='first_level', out_shape=(jax.ShapeDtyp...  5.57 us
  transfers between devices with their start and end apart: 20, of which 9 were waited for; matrix products, arithmetic and copies ran while one was open for 1% of the time, Pallas kernels for 3%

profile of v1, /device:TPU:1, one launch (start us, length us, event | category | flops | bytes accessed | tf_op | source)
XLA Modules:
  0.0 217.2 jit_solution(1043543509405599994)
XLA Ops:
  7.8 14.7 %all_to_all.10 = bf16[4,2,512,128]{3,2,1,0:T(8,128)(2,1)} all-to-all(bf16[4,2,512,128]{3,2,1,0:T(8,128)(2,1)S(1)} %pad_maximum_fusion), channel_id=1, replica_groups=mesh['z'=16,'core'=2,'y'=4,'x'=4] {'y'}, dimensions={0} | all-to-all | bytes 2097152 | tf_op jit(solution)/shard_map/all_to_all | solution.py:144
  23.4 63.3 %all-gather.8.cloned.1.call-done = bf16[16,2,512,128]{3,2,1,0:T(8,128)(2,1)} async-done(((bf16[4,2,512,128]{3,2,1,0:T(8,128)(2,1)}), bf16[16,2,512,128]{3,2,1,0:T(8,128)(2,1)}) %all-gather.8.cloned.1.call-update) | async-done | bytes 4194320 | tf_op jit(solution)/shard_map/all_gather | solution.py:145
  86.7 2.1 bitcast_convert_fusion
  88.8 3.1 %collective-permute-start.5 = (bf16[2048,128]{1,0:T(8,128)(2,1)}, bf16[2048,128]{1,0:T(8,128)(2,1)}, u32[]{:S(2)}, u32[]{:S(2)}) collective-permute-start(bf16[2048,128]{1,0:T(8,128)(2,1)} %bitcast_convert_fusion), channel_id=1, source_target_pairs={{0,4},{1,5},{2,6},{3,7},{4,8},{5,9},{6,10},{7,11},{8,12},{9,13},{1... | collective-permute-start | bytes 1572872 | tf_op jit(solution)/shard_map/ppermute | solution.py:33
  91.9 3.4 %collective-permute-start.1 = (bf16[2048,128]{1,0:T(8,128)(2,1)}, bf16[2048,128]{1,0:T(8,128)(2,1)}, u32[]{:S(2)}, u32[]{:S(2)}) collective-permute-start(bf16[2048,128]{1,0:T(8,128)(2,1)} %bitcast_convert_fusion), channel_id=1, source_target_pairs={{0,12},{1,13},{2,14},{3,15},{4,0},{5,1},{6,2},{7,3},{8,4},{9,5},{1... | collective-permute-start | bytes 1572872 | tf_op jit(solution)/shard_map/ppermute | solution.py:33
  95.3 3.4 %collective-permute-start.3 = (bf16[2048,128]{1,0:T(8,128)(2,1)}, bf16[2048,128]{1,0:T(8,128)(2,1)}, u32[]{:S(2)}, u32[]{:S(2)}) collective-permute-start(bf16[2048,128]{1,0:T(8,128)(2,1)} %bitcast_convert_fusion), channel_id=1, source_target_pairs={{0,8},{1,9},{2,10},{3,11},{4,12},{5,13},{6,14},{7,15},{8,0},{9,1},... | collective-permute-start | bytes 1572872 | tf_op jit(solution)/shard_map/ppermute | solution.py:33
  98.7 4.6 %collective-permute-start = (bf16[2048,128]{1,0:T(8,128)(2,1)}, bf16[2048,128]{1,0:T(8,128)(2,1)S(1)}, u32[]{:S(2)}, u32[]{:S(2)}) collective-permute-start(bf16[2048,128]{1,0:T(8,128)(2,1)} %bitcast_convert_fusion), channel_id=1, source_target_pairs={{0,16},{1,17},{2,18},{3,19},{4,20},{5,21},{6,22},{7,23},{8,24},{9,... | collective-permute-start | bytes 1572872 | tf_op jit(solution)/shard_map/ppermute | solution.py:33
  103.3 1.9 collective-permute-start.7
  105.2 3.4 %collective-permute-start.10 = (bf16[2048,128]{1,0:T(8,128)(2,1)}, bf16[2048,128]{1,0:T(8,128)(2,1)S(1)}, u32[]{:S(2)}, u32[]{:S(2)}) collective-permute-start(bf16[2048,128]{1,0:T(8,128)(2,1)} %collective-permute-done.5), channel_id=1, source_target_pairs={{16,0},{17,1},{18,2},{19,3},{20,4},{21,5},{22,6},{23,7},{24,8},{25... | collective-permute-start | bytes 1572872 | tf_op jit(solution)/shard_map/ppermute | solution.py:33
  108.6 3.8 %all-to-all-start.1 = ((f32[4,512,128]{2,1,0:T(8,128)}), f32[4,512,128]{2,1,0:T(8,128)S(1)}, u32[]{:S(2)}, u32[]{:S(2)}) async-start(f32[4,512,128]{2,1,0:T(8,128)} %bitcast.7), calls=%async_computation.1 | async-start | bytes 2097152 | tf_op jit(solution)/shard_map/all_to_all | solution.py:149
  112.4 8.2 %collective-permute-start.6 = (bf16[2048,128]{1,0:T(8,128)(2,1)}, bf16[2048,128]{1,0:T(8,128)(2,1)S(1)}, u32[]{:S(2)}, u32[]{:S(2)}) collective-permute-start(bf16[2048,128]{1,0:T(8,128)(2,1)} %collective-permute-done.5), channel_id=1, source_target_pairs={{0,16},{1,17},{2,18},{3,19},{4,20},{5,21},{6,22},{7,23},{8,24},{9,... | collective-permute-start | bytes 1572872 | tf_op jit(solution)/shard_map/ppermute | solution.py:33
  120.6 2.3 %collective-permute-start.2 = (bf16[2048,128]{1,0:T(8,128)(2,1)}, bf16[2048,128]{1,0:T(8,128)(2,1)}, u32[]{:S(2)}, u32[]{:S(2)}) collective-permute-start(bf16[2048,128]{1,0:T(8,128)(2,1)} %collective-permute-done.1), channel_id=1, source_target_pairs={{0,16},{1,17},{2,18},{3,19},{4,20},{5,21},{6,22},{7,23},{8,24},{9,... | collective-permute-start | bytes 1572872 | tf_op jit(solution)/shard_map/ppermute | solution.py:33
  122.9 3.2 %collective-permute-start.4 = (bf16[2048,128]{1,0:T(8,128)(2,1)}, bf16[2048,128]{1,0:T(8,128)(2,1)}, u32[]{:S(2)}, u32[]{:S(2)}) collective-permute-start(bf16[2048,128]{1,0:T(8,128)(2,1)} %collective-permute-done.3), channel_id=1, source_target_pairs={{0,16},{1,17},{2,18},{3,19},{4,20},{5,21},{6,22},{7,23},{8,24},{9,... | collective-permute-start | bytes 1572872 | tf_op jit(solution)/shard_map/ppermute | solution.py:33
  126.2 1.9 collective-permute-start.8
  128.1 1.9 collective-permute-start.9
  130.0 2.6 %collective-permute-done.2.refs_1_ = bf16[2048,128]{1,0:T(8,128)(2,1)} collective-permute-done((bf16[2048,128]{1,0:T(8,128)(2,1)}, bf16[2048,128]{1,0:T(8,128)(2,1)}, u32[]{:S(2)}, u32[]{:S(2)}) %collective-permute-start.2) | collective-permute-done | bytes 524320 | tf_op jit(solution)/shard_map/ppermute | solution.py:33
  132.7 5.6 %collective-permute-done.4.refs_2_ = bf16[2048,128]{1,0:T(8,128)(2,1)} collective-permute-done((bf16[2048,128]{1,0:T(8,128)(2,1)}, bf16[2048,128]{1,0:T(8,128)(2,1)}, u32[]{:S(2)}, u32[]{:S(2)}) %collective-permute-start.4) | collective-permute-done | bytes 524320 | tf_op jit(solution)/shard_map/ppermute | solution.py:33
  138.3 4.3 %collective-permute-done.9.refs_6_ = bf16[2048,128]{1,0:T(8,128)(2,1)} collective-permute-done((bf16[2048,128]{1,0:T(8,128)(2,1)}, bf16[2048,128]{1,0:T(8,128)(2,1)}, u32[]{:S(2)}, u32[]{:S(2)}) %collective-permute-start.9) | collective-permute-done | bytes 524320 | tf_op jit(solution)/shard_map/ppermute | solution.py:33
  142.6 2.2 %copy-done = bf16[16,2,512,128]{3,2,1,0:T(8,128)(2,1)S(1)} copy-done((bf16[16,2,512,128]{3,2,1,0:T(8,128)(2,1)S(1)}, bf16[16,2,512,128]{3,2,1,0:T(8,128)(2,1)}, u32[]{:S(2)}) %copy-start) | copy-done | bytes 4194328
  144.8 5.6 %first_level.1 = (f32[4,512,128]{2,1,0:T(8,128)S(1)}, bf16[4,512,128]{2,1,0:T(8,128)(2,1)}) custom-call(s32[1]{0:T(128)} %bitcast.y_ref, bf16[4,4,2,512,128]{4,3,2,1,0:T(8,128)(2,1)S(1)} %bitcast.11, bf16[2048,128]{1,0:T(8,128)(2,1)S(1)} %collective-permute-done.refs_0_, bf16[2048,128]{1,0:T(8,128)(2,1)} %collective-permute-done.2.refs_1_, ...), custom_call_target="tpu_custom_call" | custom-call | flops 2147483648 | bytes 11534336 | tf_op jit(solution)/shard_map/first_level/pallas_call | solution.py:64
  151.3 3.2 %collective-permute-start.11 = (bf16[4,512,128]{2,1,0:T(8,128)(2,1)}, bf16[4,512,128]{2,1,0:T(8,128)(2,1)S(1)}, u32[]{:S(2)}, u32[]{:S(2)}) collective-permute-start(bf16[4,512,128]{2,1,0:T(8,128)(2,1)} %get-tuple-element.15), channel_id=1, source_target_pairs={{0,32},{1,33},{2,34},{3,35},{4,36},{5,37},{6,38},{7,39},{8,40},{9,... | collective-permute-start | bytes 1572872 | tf_op jit(solution)/shard_map/ppermute | solution.py:33
  155.9 9.8 %collective-permute-done.11.below = bf16[4,512,128]{2,1,0:T(8,128)(2,1)S(1)} collective-permute-done((bf16[4,512,128]{2,1,0:T(8,128)(2,1)}, bf16[4,512,128]{2,1,0:T(8,128)(2,1)S(1)}, u32[]{:S(2)}, u32[]{:S(2)}) %collective-permute-start.11) | collective-permute-done | bytes 524320 | tf_op jit(solution)/shard_map/ppermute | solution.py:33
  165.7 4.0 %collective-permute-done.12.above = bf16[4,512,128]{2,1,0:T(8,128)(2,1)S(1)} collective-permute-done((bf16[4,512,128]{2,1,0:T(8,128)(2,1)}, bf16[4,512,128]{2,1,0:T(8,128)(2,1)S(1)}, u32[]{:S(2)}, u32[]{:S(2)}) %collective-permute-start.12) | collective-permute-done | bytes 524320 | tf_op jit(solution)/shard_map/ppermute | solution.py:33
  169.7 1.6 copy-done.1
  171.3 1.6 copy-done.2
  174.1 4.3 %second_level.1 = (f32[2048,128]{1,0:T(8,128)S(1)}, bf16[2048,128]{1,0:T(8,128)(2,1)S(1)}, bf16[2048,128]{1,0:T(8,128)(2,1)S(1)}, bf16[2048,128]{1,0:T(8,128)(2,1)S(1)}) custom-call(s32[1]{0:T(128)} %bitcast.y_ref, bf16[4,2048,128]{2,1,0:T(8,128)(2,1)S(1)} %copy-done.1, bf16[4,2048,128]{2,1,0:T(8,128)(2,1)S(1)} %bitcast.12, ...), custom_call_target="tpu_custom_call" | custom-call | flops 2147483648 | bytes 9437184 | tf_op jit(solution)/shard_map/second_level/pallas_call | solution.py:113
  178.5 3.8 %collective-permute-start.13 = (bf16[2048,128]{1,0:T(8,128)(2,1)S(1)}, bf16[2048,128]{1,0:T(8,128)(2,1)S(1)}, u32[]{:S(2)}, u32[]{:S(2)}) collective-permute-start(bf16[2048,128]{1,0:T(8,128)(2,1)S(1)} %get-tuple-element.18), channel_id=1, source_target_pairs={{0,4},{1,5},{2,6},{3,7},{4,8},{5,9},{6,10},{7,11},{8,12},{9,13},{1... | collective-permute-start | bytes 1572872 | tf_op jit(solution)/shard_map/ppermute | solution.py:33
  182.3 5.0 %collective-permute-start.14 = (bf16[2048,128]{1,0:T(8,128)(2,1)S(1)}, bf16[2048,128]{1,0:T(8,128)(2,1)S(1)}, u32[]{:S(2)}, u32[]{:S(2)}) collective-permute-start(bf16[2048,128]{1,0:T(8,128)(2,1)S(1)} %get-tuple-element.19), channel_id=1, source_target_pairs={{0,8},{1,9},{2,10},{3,11},{4,12},{5,13},{6,14},{7,15},{8,0},{9,1},... | collective-permute-start | bytes 1572872 | tf_op jit(solution)/shard_map/ppermute | solution.py:33
  187.3 1.9 collective-permute-start.15
  189.2 6.2 %collective-permute-done.13 = bf16[2048,128]{1,0:T(8,128)(2,1)S(1)} collective-permute-done((bf16[2048,128]{1,0:T(8,128)(2,1)S(1)}, bf16[2048,128]{1,0:T(8,128)(2,1)S(1)}, u32[]{:S(2)}, u32[]{:S(2)}) %collective-permute-start.13) | collective-permute-done | bytes 524320 | tf_op jit(solution)/shard_map/ppermute | solution.py:33
  195.5 12.7 %collective-permute-done.14 = bf16[2048,128]{1,0:T(8,128)(2,1)S(1)} collective-permute-done((bf16[2048,128]{1,0:T(8,128)(2,1)S(1)}, bf16[2048,128]{1,0:T(8,128)(2,1)S(1)}, u32[]{:S(2)}, u32[]{:S(2)}) %collective-permute-start.14) | collective-permute-done | bytes 524320 | tf_op jit(solution)/shard_map/ppermute | solution.py:33
  208.2 1.4 collective-permute-done.15
  (27 shorter events, 6.8 us)
Async XLA Ops:
  6.5 80.1 %all-gather.8.cloned.1.call-start = ((), (), s32[]{:S(2)}) async-start(), calls=%async_computation.3 | async-start | bytes 5242880 | tf_op jit(solution)/shard_map/all_gather | solution.py:145
  22.6 133.3 %all-gather.6.cloned.1.call-start = ((), (), s32[]{:S(2)}) async-start(), calls=%async_computation.2 | async-start | bytes 2621440 | tf_op jit(solution)/shard_map/all_gather | solution.py:135
  23.3 146.4 %all-gather.10.cloned.1.call-start = ((), (), s32[]{:S(2)}) async-start(), calls=%async_computation.4 | async-start | bytes 2621440 | tf_op jit(solution)/shard_map/all_gather | solution.py:152
  88.8 16.5 %collective-permute-start.5 = (bf16[2048,128]{1,0:T(8,128)(2,1)}, bf16[2048,128]{1,0:T(8,128)(2,1)}, u32[]{:S(2)}, u32[]{:S(2)}) collective-permute-start(bf16[2048,128]{1,0:T(8,128)(2,1)} %bitcast_convert_fusion), channel_id=1, source_target_pairs={{0,4},{1,5},{2,6},{3,7},{4,8},{5,9},{6,10},{7,11},{8,12},{9,13},{1... | collective-permute-start | bytes 1572872 | tf_op jit(solution)/shard_map/ppermute | solution.py:33
  91.9 20.5 %collective-permute-start.1 = (bf16[2048,128]{1,0:T(8,128)(2,1)}, bf16[2048,128]{1,0:T(8,128)(2,1)}, u32[]{:S(2)}, u32[]{:S(2)}) collective-permute-start(bf16[2048,128]{1,0:T(8,128)(2,1)} %bitcast_convert_fusion), channel_id=1, source_target_pairs={{0,12},{1,13},{2,14},{3,15},{4,0},{5,1},{6,2},{7,3},{8,4},{9,5},{1... | collective-permute-start | bytes 1572872 | tf_op jit(solution)/shard_map/ppermute | solution.py:33
  95.3 25.4 %collective-permute-start.3 = (bf16[2048,128]{1,0:T(8,128)(2,1)}, bf16[2048,128]{1,0:T(8,128)(2,1)}, u32[]{:S(2)}, u32[]{:S(2)}) collective-permute-start(bf16[2048,128]{1,0:T(8,128)(2,1)} %bitcast_convert_fusion), channel_id=1, source_target_pairs={{0,8},{1,9},{2,10},{3,11},{4,12},{5,13},{6,14},{7,15},{8,0},{9,1},... | collective-permute-start | bytes 1572872 | tf_op jit(solution)/shard_map/ppermute | solution.py:33
  98.7 24.2 %collective-permute-start = (bf16[2048,128]{1,0:T(8,128)(2,1)}, bf16[2048,128]{1,0:T(8,128)(2,1)S(1)}, u32[]{:S(2)}, u32[]{:S(2)}) collective-permute-start(bf16[2048,128]{1,0:T(8,128)(2,1)} %bitcast_convert_fusion), channel_id=1, source_target_pairs={{0,16},{1,17},{2,18},{3,19},{4,20},{5,21},{6,22},{7,23},{8,24},{9,... | collective-permute-start | bytes 1572872 | tf_op jit(solution)/shard_map/ppermute | solution.py:33
  103.3 22.8 %collective-permute-start.7 = (bf16[2048,128]{1,0:T(8,128)(2,1)}, bf16[2048,128]{1,0:T(8,128)(2,1)S(1)}, u32[]{:S(2)}, u32[]{:S(2)}) collective-permute-start(bf16[2048,128]{1,0:T(8,128)(2,1)} %bitcast_convert_fusion), channel_id=1, source_target_pairs={{16,0},{17,1},{18,2},{19,3},{20,4},{21,5},{22,6},{23,7},{24,8},{25... | collective-permute-start | bytes 1572872 | tf_op jit(solution)/shard_map/ppermute | solution.py:33
  105.2 22.8 %collective-permute-start.10 = (bf16[2048,128]{1,0:T(8,128)(2,1)}, bf16[2048,128]{1,0:T(8,128)(2,1)S(1)}, u32[]{:S(2)}, u32[]{:S(2)}) collective-permute-start(bf16[2048,128]{1,0:T(8,128)(2,1)} %collective-permute-done.5), channel_id=1, source_target_pairs={{16,0},{17,1},{18,2},{19,3},{20,4},{21,5},{22,6},{23,7},{24,8},{25... | collective-permute-start | bytes 1572872 | tf_op jit(solution)/shard_map/ppermute | solution.py:33
  108.6 21.4 %all-to-all-start.1 = ((f32[4,512,128]{2,1,0:T(8,128)}), f32[4,512,128]{2,1,0:T(8,128)S(1)}, u32[]{:S(2)}, u32[]{:S(2)}) async-start(f32[4,512,128]{2,1,0:T(8,128)} %bitcast.7), calls=%async_computation.1 | async-start | bytes 2097152 | tf_op jit(solution)/shard_map/all_to_all | solution.py:149
  112.4 25.9 %collective-permute-start.6 = (bf16[2048,128]{1,0:T(8,128)(2,1)}, bf16[2048,128]{1,0:T(8,128)(2,1)S(1)}, u32[]{:S(2)}, u32[]{:S(2)}) collective-permute-start(bf16[2048,128]{1,0:T(8,128)(2,1)} %collective-permute-done.5), channel_id=1, source_target_pairs={{0,16},{1,17},{2,18},{3,19},{4,20},{5,21},{6,22},{7,23},{8,24},{9,... | collective-permute-start | bytes 1572872 | tf_op jit(solution)/shard_map/ppermute | solution.py:33
  120.6 12.0 %collective-permute-start.2 = (bf16[2048,128]{1,0:T(8,128)(2,1)}, bf16[2048,128]{1,0:T(8,128)(2,1)}, u32[]{:S(2)}, u32[]{:S(2)}) collective-permute-start(bf16[2048,128]{1,0:T(8,128)(2,1)} %collective-permute-done.1), channel_id=1, source_target_pairs={{0,16},{1,17},{2,18},{3,19},{4,20},{5,21},{6,22},{7,23},{8,24},{9,... | collective-permute-start | bytes 1572872 | tf_op jit(solution)/shard_map/ppermute | solution.py:33
  122.9 15.3 %collective-permute-start.4 = (bf16[2048,128]{1,0:T(8,128)(2,1)}, bf16[2048,128]{1,0:T(8,128)(2,1)}, u32[]{:S(2)}, u32[]{:S(2)}) collective-permute-start(bf16[2048,128]{1,0:T(8,128)(2,1)} %collective-permute-done.3), channel_id=1, source_target_pairs={{0,16},{1,17},{2,18},{3,19},{4,20},{5,21},{6,22},{7,23},{8,24},{9,... | collective-permute-start | bytes 1572872 | tf_op jit(solution)/shard_map/ppermute | solution.py:33
  126.2 12.1 %collective-permute-start.8 = (bf16[2048,128]{1,0:T(8,128)(2,1)}, bf16[2048,128]{1,0:T(8,128)(2,1)}, u32[]{:S(2)}, u32[]{:S(2)}) collective-permute-start(bf16[2048,128]{1,0:T(8,128)(2,1)} %collective-permute-done.1), channel_id=1, source_target_pairs={{16,0},{17,1},{18,2},{19,3},{20,4},{21,5},{22,6},{23,7},{24,8},{25... | collective-permute-start | bytes 1572872 | tf_op jit(solution)/shard_map/ppermute | solution.py:33
  128.1 14.5 %collective-permute-start.9 = (bf16[2048,128]{1,0:T(8,128)(2,1)}, bf16[2048,128]{1,0:T(8,128)(2,1)}, u32[]{:S(2)}, u32[]{:S(2)}) collective-permute-start(bf16[2048,128]{1,0:T(8,128)(2,1)} %collective-permute-done.3), channel_id=1, source_target_pairs={{16,0},{17,1},{18,2},{19,3},{20,4},{21,5},{22,6},{23,7},{24,8},{25... | collective-permute-start | bytes 1572872 | tf_op jit(solution)/shard_map/ppermute | solution.py:33
  142.6 2.2 %copy-start = (bf16[16,2,512,128]{3,2,1,0:T(8,128)(2,1)S(1)}, bf16[16,2,512,128]{3,2,1,0:T(8,128)(2,1)}, u32[]{:S(2)}) copy-start(bf16[16,2,512,128]{3,2,1,0:T(8,128)(2,1)} %all-gather.8.cloned.1.call-done) | copy-start | bytes 12582916
  150.4 1.0 copy-start.3
  151.3 14.4 %collective-permute-start.11 = (bf16[4,512,128]{2,1,0:T(8,128)(2,1)}, bf16[4,512,128]{2,1,0:T(8,128)(2,1)S(1)}, u32[]{:S(2)}, u32[]{:S(2)}) collective-permute-start(bf16[4,512,128]{2,1,0:T(8,128)(2,1)} %get-tuple-element.15), channel_id=1, source_target_pairs={{0,32},{1,33},{2,34},{3,35},{4,36},{5,37},{6,38},{7,39},{8,40},{9,... | collective-permute-start | bytes 1572872 | tf_op jit(solution)/shard_map/ppermute | solution.py:33
  154.5 15.2 %collective-permute-start.12 = (bf16[4,512,128]{2,1,0:T(8,128)(2,1)}, bf16[4,512,128]{2,1,0:T(8,128)(2,1)S(1)}, u32[]{:S(2)}, u32[]{:S(2)}) collective-permute-start(bf16[4,512,128]{2,1,0:T(8,128)(2,1)} %get-tuple-element.15), channel_id=1, source_target_pairs={{32,0},{33,1},{34,2},{35,3},{36,4},{37,5},{38,6},{39,7},{40,8},{41... | collective-permute-start | bytes 1572872 | tf_op jit(solution)/shard_map/ppermute | solution.py:33
  169.7 1.6 copy-start.1
  171.3 1.6 copy-start.2
  172.9 1.2 copy-start.4
  178.5 17.0 %collective-permute-start.13 = (bf16[2048,128]{1,0:T(8,128)(2,1)S(1)}, bf16[2048,128]{1,0:T(8,128)(2,1)S(1)}, u32[]{:S(2)}, u32[]{:S(2)}) collective-permute-start(bf16[2048,128]{1,0:T(8,128)(2,1)S(1)} %get-tuple-element.18), channel_id=1, source_target_pairs={{0,4},{1,5},{2,6},{3,7},{4,8},{5,9},{6,10},{7,11},{8,12},{9,13},{1... | collective-permute-start | bytes 1572872 | tf_op jit(solution)/shard_map/ppermute | solution.py:33
  182.3 25.9 %collective-permute-start.14 = (bf16[2048,128]{1,0:T(8,128)(2,1)S(1)}, bf16[2048,128]{1,0:T(8,128)(2,1)S(1)}, u32[]{:S(2)}, u32[]{:S(2)}) collective-permute-start(bf16[2048,128]{1,0:T(8,128)(2,1)S(1)} %get-tuple-element.19), channel_id=1, source_target_pairs={{0,8},{1,9},{2,10},{3,11},{4,12},{5,13},{6,14},{7,15},{8,0},{9,1},... | collective-permute-start | bytes 1572872 | tf_op jit(solution)/shard_map/ppermute | solution.py:33
  187.3 22.2 %collective-permute-start.15 = (bf16[2048,128]{1,0:T(8,128)(2,1)S(1)}, bf16[2048,128]{1,0:T(8,128)(2,1)S(1)}, u32[]{:S(2)}, u32[]{:S(2)}) collective-permute-start(bf16[2048,128]{1,0:T(8,128)(2,1)S(1)} %get-tuple-element.20), channel_id=1, source_target_pairs={{0,12},{1,13},{2,14},{3,15},{4,0},{5,1},{6,2},{7,3},{8,4},{9,5},{1... | collective-permute-start | bytes 1572872 | tf_op jit(solution)/shard_map/ppermute | solution.py:33
Sparse Core Ops, SparseCore 0:
  22.7 63.9 all-gather.7
  88.8 38.9 all-gather.5
  129.8 38.5 all-gather.9

commit v2 on v1

v2 whole, which is shorter than its diff:
```python
import jax
import jax.numpy as jnp
from jax import lax
from jax.experimental import pallas as pl
from jax.experimental.pallas import tpu as pltpu
from jax.sharding import Mesh, PartitionSpec as P

Z, CORES, Y, X = 16, 2, 4, 4
PLANES = Z * CORES
M = 2048
BLK = M // Y
COL = 128
AXES = ("z", "core", "y", "x")


def device_index(plane, y, x):
    return (plane * Y + y) * X + x


def moved(value, planes=0, ys=0, xs=0):
    pairs = []
    for plane in range(PLANES):
        if not 0 <= plane + planes < PLANES:
            continue
        for y in range(Y):
            for x in range(X):
                target = device_index(plane + planes, (y + ys) % Y, (x + xs) % X)
                pairs.append((device_index(plane, y, x), target))
    return lax.ppermute(value, AXES, pairs)


def after(value, *before):
    return lax.optimization_barrier((value,) + before)[0]


def rows_in_order(at_ref, ref, row):
    return [
        ref[row + (pl.ds(pl.multiple_of(lax.rem(at_ref[1] + e, X) * COL, COL), COL),)]
        for e in range(X)
    ]


def first_kernel(at_ref, *refs):
    lower, upper = refs[0:4], refs[4:8]
    below, above = refs[8:12], refs[12:16]
    rhs_ref, corr_ref, sent_ref, acc_ref = refs[16:]
    step = pl.program_id(0)

    @pl.when(step == 0)
    def _():
        acc_ref[...] = jnp.zeros_like(acc_ref)

    total = acc_ref[...]
    for blocks, parts in ((lower, below), (upper, above)):
        left = jnp.concatenate([block[0] for block in blocks], axis=1)
        right = [
            jnp.concatenate(rows_in_order(at_ref, part, ()), axis=0) for part in parts
        ]
        right = jnp.concatenate(right, axis=1)
        total = total + jnp.dot(left, right, preferred_element_type=jnp.float32)
    acc_ref[...] = total

    @pl.when(step == Y - 1)
    def _():
        for d in range(Y):
            piece = acc_ref[:, d * COL : (d + 1) * COL]
            corr_ref[d] = piece
            owner = lax.rem(at_ref[0] + d, Y)
            sent_ref[d] = (rhs_ref[owner] + piece).astype(jnp.bfloat16)


def first_level(at, lower, upper, below, above, rhs):
    block = pl.BlockSpec((1, BLK, COL), lambda k, at: (k, 0, 0))
    part = pl.BlockSpec((BLK, COL), lambda k, at: (k, 0))
    whole = pl.BlockSpec((Y, BLK, COL), lambda k, at: (0, 0, 0))
    return pl.pallas_call(
        first_kernel,
        name="first_level",
        out_shape=(
            jax.ShapeDtypeStruct((Y, BLK, COL), jnp.float32),
            jax.ShapeDtypeStruct((Y, BLK, COL), jnp.bfloat16),
        ),
        grid_spec=pltpu.PrefetchScalarGridSpec(
            num_scalar_prefetch=1,
            grid=(Y,),
            in_specs=[block] * 8 + [part] * 8 + [whole],
            out_specs=(whole, whole),
            scratch_shapes=[pltpu.VMEM((BLK, Y * COL), jnp.float32)],
        ),
        compiler_params=pltpu.CompilerParams(vmem_limit_bytes=20 << 20),
        cost_estimate=pl.CostEstimate(
            flops=4 * BLK * M * Y * COL, bytes_accessed=11 << 20, transcendentals=0
        ),
    )(at, *lower, *upper, *below, *above, rhs)


def second_kernel(at_ref, *refs):
    lower, upper = refs[0:4], refs[4:8]
    below, above, corr_ref, rhs_ref, own_ref, *outs = refs[8:]
    step = pl.program_id(0)
    total = None
    for blocks, b_ref in ((lower, below), (upper, above)):
        left = jnp.concatenate([block[...] for block in blocks], axis=1)
        right = [
            jnp.concatenate(rows_in_order(at_ref, b_ref, (d,)), axis=0)
            for d in range(Y)
        ]
        right = jnp.concatenate(right, axis=1)
        term = jnp.dot(left, right, preferred_element_type=jnp.float32)
        total = term if total is None else total + term
    here = step == at_ref[0]
    for d in range(Y):
        piece = total[:, d * COL : (d + 1) * COL]
        piece = piece + jnp.where(here, corr_ref[d], 0.0)
        if d == 0:
            own_ref[...] = piece + rhs_ref[...]
        else:
            outs[d - 1][...] = piece.astype(jnp.bfloat16)


def second_level(at, lower, upper, below, above, corr, rhs):
    rows = pl.BlockSpec((BLK, COL), lambda m, at: (m, 0))
    whole = pl.BlockSpec((Y, BLK, COL), lambda m, at: (0, 0, 0))
    return pl.pallas_call(
        second_kernel,
        name="second_level",
        out_shape=(jax.ShapeDtypeStruct((M, COL), jnp.float32),)
        + (jax.ShapeDtypeStruct((M, COL), jnp.bfloat16),) * 3,
        grid_spec=pltpu.PrefetchScalarGridSpec(
            num_scalar_prefetch=1,
            grid=(Y,),
            in_specs=[rows] * 8 + [whole, whole, whole, rows],
            out_specs=(rows,) * 4,
        ),
        compiler_params=pltpu.CompilerParams(vmem_limit_bytes=20 << 20),
        cost_estimate=pl.CostEstimate(
            flops=4 * BLK * M * Y * COL, bytes_accessed=9 << 20, transcendentals=0
        ),
    )(at, *lower, *upper, below, above, corr, rhs)


def on_device(right_sides, lower_first, upper_first, lower_second, upper_second):
    rhs = right_sides[0]
    at = jnp.stack([lax.axis_index("y"), lax.axis_index("x")]).astype(jnp.int32)

    def exchanged(value):
        return lax.all_to_all(value.reshape(Y, BLK, COL), "y", 0, 0, tiled=True)

    lo, up = exchanged(lower_first[0]), exchanged(upper_first[0])
    lo_two, up_two = lower_second[0], upper_second[0]
    lo_two_left, lo_two_right = moved(lo_two, xs=1), moved(lo_two, xs=-1)

    sent_one = rhs.astype(jnp.bfloat16)
    below, above = [moved(sent_one, 1)], [moved(sent_one, -1)]

    lo_left, lo_right = moved(lo, xs=1), moved(lo, xs=-1)
    up_left, up_right = moved(up, xs=1), moved(up, xs=-1)
    late = after(sent_one, up)
    for d in range(1, Y):
        part = moved(late, ys=-d)
        below.append(moved(part, 1))
        above.append(moved(part, -1))
    lo_far, up_far = moved(lo_left, xs=1), moved(up_right, xs=-1)
    rhs_rows = exchanged(after(rhs, up))

    up_two_in = after(up_two, lo_left, up_right)
    up_two_left, up_two_right = moved(up_two_in, xs=1), moved(up_two_in, xs=-1)
    lo_two_far = moved(after(lo_two_left, lo_far), xs=1)
    up_two_far = moved(up_two_right, xs=-1)

    corr, sent_two = first_level(
        at,
        (lo, lo_right, lo_far, lo_left),
        (up, up_right, up_far, up_left),
        below,
        above,
        rhs_rows,
    )
    below_two, above_two = moved(sent_two, 2), moved(sent_two, -2)
    total, *parts = second_level(
        at,
        (lo_two, lo_two_right, lo_two_far, lo_two_left),
        (up_two, up_two_right, up_two_far, up_two_left),
        below_two,
        above_two,
        corr,
        rhs,
    )
    for d in range(1, Y):
        total = total + moved(parts[d - 1], ys=d).astype(jnp.float32)
    return total[None]


def solution(mesh):
    fine = Mesh(mesh.devices.reshape(Z, CORES, Y, X), AXES)
    spec = P(("z", "core"), None, ("y", "x"))
    return jax.shard_map(
        on_device,
        mesh=fine,
        in_specs=(spec,) * 5,
        out_specs=spec,
        check_vma=False,
    )
```

time: 220 us -> 168 us (0.76)
  waiting for transfers between devices: 111 us -> 48.4 us
  starting transfers between devices: 56.4 us -> 96.5 us
  blocking collectives: 14.7 us -> 0 us
  between operations: 13.3 us -> 0.47 us
    all_gather x3 -> x0, waiting for transfers between devices: 63.3 us -> none  [the longest x1 63.3 us: on_device(): blocks = lax.all_gather(firsts, 'x', axis=0)]
    ppermute x16 -> x28, starting transfers between devices: 52.6 us -> 80.8 us  [moved(): return lax.ppermute(value, AXES, pairs)]
    all_to_all x1 -> x0, blocking collectives: 14.7 us -> none  [on_device(): firsts = lax.all_to_all(firsts, 'y', 0, 0, tiled=True)]
    all_to_all x1 -> x3, starting transfers between devices: 3.79 us -> 15.7 us  [exchanged(): return lax.all_to_all(value.reshape(Y, BLK, COL), 'y', 0, 0, tiled=True)]
    ppermute x16 -> x28, waiting for transfers between devices: 46.7 us -> 48.4 us  [moved(): return lax.ppermute(value, AXES, pairs)]
    unnamed x10 -> x24, local copies, waits for them, and re-layouts: 7.56 us -> 7.6 us
  transfers between devices with their start and end apart: 20 -> 31, of which waited for: 9 -> 11; matrix products, arithmetic and copies ran while one was open for 1% -> 1% of each run, Pallas kernels for 3% -> 3%
where the time goes in v2:
time: 168 us; the launch traced here: 166 us
  starting transfers between devices  96.5 us (57%)
  waiting for transfers between devices  48.4 us (29%)
  Pallas kernels  10.7 us (6%)
  local copies, waits for them, and re-layouts  7.6 us (5%)
  other arithmetic  2.53 us (2%)
    ppermute x28, starting transfers between devices, moved(): return lax.ppermute(value, AXES, pairs)  80.8 us
    ppermute x28, waiting for transfers between devices, moved(): return lax.ppermute(value, AXES, pairs)  48.4 us
    all_to_all x3, starting transfers between devices, exchanged(): return lax.all_to_all(value.reshape(Y, BLK, COL), 'y', 0, 0, tiled=True)  15.7 us
    unnamed x24, local copies, waits for them, and re-layouts  7.6 us
    pallas_call x1, Pallas kernels, first_level(): pl.pallas_call(first_kernel, name='first_level', out_shape=(jax.ShapeDtyp...  5.47 us
    pallas_call x1, Pallas kernels, second_level(): pl.pallas_call(second_kernel, name='second_level', out_shape=(jax.ShapeDt...  5.18 us
  transfers between devices with their start and end apart: 31, of which 11 were waited for; matrix products, arithmetic and copies ran while one was open for 1% of the time, Pallas kernels for 3%

profile of v2, /device:TPU:1, one launch (start us, length us, event | category | flops | bytes accessed | tf_op | source)
XLA Modules:
  0.0 166.1 jit_solution(3025117530057685614)
XLA Ops:
  0.0 5.0 %all-to-all-start.1 = ((bf16[4,512,128]{2,1,0:T(8,128)(2,1)}), bf16[4,512,128]{2,1,0:T(8,128)(2,1)S(1)}, u32[]{:S(2)}, u32[]{:S(2)}) async-start(bf16[4,512,128]{2,1,0:T(8,128)(2,1)} %bitcast.17), calls=%async_computation.1 | async-start | bytes 1048576 | tf_op jit(solution)/shard_map/all_to_all | solution.py:147
  6.3 4.4 %collective-permute-start.12 = (bf16[2048,128]{1,0:T(8,128)(2,1)S(1)}, bf16[2048,128]{1,0:T(8,128)(2,1)S(1)}, u32[]{:S(2)}, u32[]{:S(2)}) collective-permute-start(bf16[2048,128]{1,0:T(8,128)(2,1)S(1)} %bitcast_convert_fusion), channel_id=1, source_target_pairs={{0,16},{1,17},{2,18},{3,19},{4,20},{5,21},{6,22},{7,23},{8,24},{9,... | collective-permute-start | bytes 1572872 | tf_op jit(solution)/shard_map/ppermute | solution.py:29
  10.7 4.2 %collective-permute-start.19 = (bf16[2048,128]{1,0:T(8,128)(2,1)S(1)}, bf16[2048,128]{1,0:T(8,128)(2,1)S(1)}, u32[]{:S(2)}, u32[]{:S(2)}) collective-permute-start(bf16[2048,128]{1,0:T(8,128)(2,1)S(1)} %bitcast_convert_fusion), channel_id=1, source_target_pairs={{16,0},{17,1},{18,2},{19,3},{20,4},{21,5},{22,6},{23,7},{24,8},{25... | collective-permute-start | bytes 1572872 | tf_op jit(solution)/shard_map/ppermute | solution.py:29
  14.9 4.5 %all-to-all-start = ((bf16[4,512,128]{2,1,0:T(8,128)(2,1)}), bf16[4,512,128]{2,1,0:T(8,128)(2,1)S(1)}, u32[]{:S(2)}, u32[]{:S(2)}) async-start(bf16[4,512,128]{2,1,0:T(8,128)(2,1)} %bitcast.3), calls=%async_computation | async-start | bytes 1048576 | tf_op jit(solution)/shard_map/all_to_all | solution.py:147
  19.4 4.6 %collective-permute-start.13 = (bf16[2048,128]{1,0:T(8,128)(2,1)S(1)}, bf16[2048,128]{1,0:T(8,128)(2,1)}, u32[]{:S(2)}, u32[]{:S(2)}) collective-permute-start(bf16[2048,128]{1,0:T(8,128)(2,1)S(1)} %bitcast_convert_fusion), channel_id=1, source_target_pairs={{0,12},{1,13},{2,14},{3,15},{4,0},{5,1},{6,2},{7,3},{8,4},{9,5},{1... | collective-permute-start | bytes 1572872 | tf_op jit(solution)/shard_map/ppermute | solution.py:29
  24.0 2.5 %collective-permute-start.15 = (bf16[2048,128]{1,0:T(8,128)(2,1)S(1)}, bf16[2048,128]{1,0:T(8,128)(2,1)}, u32[]{:S(2)}, u32[]{:S(2)}) collective-permute-start(bf16[2048,128]{1,0:T(8,128)(2,1)S(1)} %bitcast_convert_fusion), channel_id=1, source_target_pairs={{0,8},{1,9},{2,10},{3,11},{4,12},{5,13},{6,14},{7,15},{8,0},{9,1},... | collective-permute-start | bytes 1572872 | tf_op jit(solution)/shard_map/ppermute | solution.py:29
  26.5 2.5 %collective-permute-start.17 = (bf16[2048,128]{1,0:T(8,128)(2,1)S(1)}, bf16[2048,128]{1,0:T(8,128)(2,1)}, u32[]{:S(2)}, u32[]{:S(2)}) collective-permute-start(bf16[2048,128]{1,0:T(8,128)(2,1)S(1)} %bitcast_convert_fusion), channel_id=1, source_target_pairs={{0,4},{1,5},{2,6},{3,7},{4,8},{5,9},{6,10},{7,11},{8,12},{9,13},{1... | collective-permute-start | bytes 1572872 | tf_op jit(solution)/shard_map/ppermute | solution.py:29
  31.2 3.1 %collective-permute-start.2 = (bf16[4,512,128]{2,1,0:T(8,128)(2,1)S(1)}, bf16[4,512,128]{2,1,0:T(8,128)(2,1)S(1)}, u32[]{:S(2)}, u32[]{:S(2)}) collective-permute-start(bf16[4,512,128]{2,1,0:T(8,128)(2,1)S(1)} %all-to-all-done.refs_0_), channel_id=1, source_target_pairs={{0,1},{1,2},{2,3},{3,0},{4,5},{5,6},{6,7},{7,4},{8,9},{9,10},{10,1... | collective-permute-start | bytes 1572872 | tf_op jit(solution)/shard_map/ppermute | solution.py:29
  34.3 2.5 %collective-permute-done.13 = bf16[2048,128]{1,0:T(8,128)(2,1)} collective-permute-done((bf16[2048,128]{1,0:T(8,128)(2,1)S(1)}, bf16[2048,128]{1,0:T(8,128)(2,1)}, u32[]{:S(2)}, u32[]{:S(2)}) %collective-permute-start.13) | collective-permute-done | bytes 524320 | tf_op jit(solution)/shard_map/ppermute | solution.py:29
  38.7 4.6 %collective-permute-start.9 = (bf16[4,512,128]{2,1,0:T(8,128)(2,1)S(1)}, bf16[4,512,128]{2,1,0:T(8,128)(2,1)S(1)}, u32[]{:S(2)}, u32[]{:S(2)}) collective-permute-start(bf16[4,512,128]{2,1,0:T(8,128)(2,1)S(1)} %all-to-all-done.refs_0_), channel_id=1, source_target_pairs={{0,3},{1,0},{2,1},{3,2},{4,7},{5,4},{6,5},{7,6},{8,11},{9,8},{10,9... | collective-permute-start | bytes 1572872 | tf_op jit(solution)/shard_map/ppermute | solution.py:29
  43.3 9.3 %collective-permute-done.17 = bf16[2048,128]{1,0:T(8,128)(2,1)} collective-permute-done((bf16[2048,128]{1,0:T(8,128)(2,1)S(1)}, bf16[2048,128]{1,0:T(8,128)(2,1)}, u32[]{:S(2)}, u32[]{:S(2)}) %collective-permute-start.17) | collective-permute-done | bytes 524320 | tf_op jit(solution)/shard_map/ppermute | solution.py:29
  56.4 3.7 %collective-permute-start.18 = (bf16[2048,128]{1,0:T(8,128)(2,1)}, bf16[2048,128]{1,0:T(8,128)(2,1)}, u32[]{:S(2)}, u32[]{:S(2)}) collective-permute-start(bf16[2048,128]{1,0:T(8,128)(2,1)} %collective-permute-done.17), channel_id=1, source_target_pairs={{0,16},{1,17},{2,18},{3,19},{4,20},{5,21},{6,22},{7,23},{8,24},{9,... | collective-permute-start | bytes 1572872 | tf_op jit(solution)/shard_map/ppermute | solution.py:29
  68.4 6.2 %all-to-all-start.2 = ((f32[4,512,128]{2,1,0:T(8,128)}), f32[4,512,128]{2,1,0:T(8,128)S(1)}, u32[]{:S(2)}, u32[]{:S(2)}) async-start(f32[4,512,128]{2,1,0:T(8,128)} %bitcast.7), calls=%async_computation.2 | async-start | bytes 2097152 | tf_op jit(solution)/shard_map/all_to_all | solution.py:147
  74.6 2.4 %collective-permute-start.10 = (bf16[4,512,128]{2,1,0:T(8,128)(2,1)}, bf16[4,512,128]{2,1,0:T(8,128)(2,1)}, u32[]{:S(2)}, u32[]{:S(2)}) collective-permute-start(bf16[4,512,128]{2,1,0:T(8,128)(2,1)} %copy-done), channel_id=1, source_target_pairs={{0,3},{1,0},{2,1},{3,2},{4,7},{5,4},{6,5},{7,6},{8,11},{9,8},{10,9... | collective-permute-start | bytes 1572872 | tf_op jit(solution)/shard_map/ppermute | solution.py:29
  77.0 2.8 %collective-permute-start.3 = (bf16[4,512,128]{2,1,0:T(8,128)(2,1)}, bf16[4,512,128]{2,1,0:T(8,128)(2,1)}, u32[]{:S(2)}, u32[]{:S(2)}) collective-permute-start(bf16[4,512,128]{2,1,0:T(8,128)(2,1)} %copy-done.2), channel_id=1, source_target_pairs={{0,1},{1,2},{2,3},{3,0},{4,5},{5,6},{6,7},{7,4},{8,9},{9,10},{10,1... | collective-permute-start | bytes 1572872 | tf_op jit(solution)/shard_map/ppermute | solution.py:29
  81.8 4.6 %collective-permute-start.6 = (bf16[2048,128]{1,0:T(8,128)(2,1)}, bf16[2048,128]{1,0:T(8,128)(2,1)}, u32[]{:S(2)}, u32[]{:S(2)}) collective-permute-start(bf16[2048,128]{1,0:T(8,128)(2,1)} %bitcast.14), channel_id=1, source_target_pairs={{0,3},{1,0},{2,1},{3,2},{4,7},{5,4},{6,5},{7,6},{8,11},{9,8},{10,9... | collective-permute-start | bytes 1572872 | tf_op jit(solution)/shard_map/ppermute | solution.py:29
  86.4 2.5 %collective-permute-start = (bf16[2048,128]{1,0:T(8,128)(2,1)}, bf16[2048,128]{1,0:T(8,128)(2,1)}, u32[]{:S(2)}, u32[]{:S(2)}) collective-permute-start(bf16[2048,128]{1,0:T(8,128)(2,1)} %bitcast.12), channel_id=1, source_target_pairs={{0,3},{1,0},{2,1},{3,2},{4,7},{5,4},{6,5},{7,6},{8,11},{9,8},{10,9... | collective-permute-start | bytes 1572872 | tf_op jit(solution)/shard_map/ppermute | solution.py:29
  99.6 5.5 %first_level.1 = (f32[4,512,128]{2,1,0:T(8,128)S(1)}, bf16[4,512,128]{2,1,0:T(8,128)(2,1)S(1)}) custom-call(s32[2]{0:T(128)S(1)} %pad_add_fusion.at_ref, bf16[4,512,128]{2,1,0:T(8,128)(2,1)S(1)} %all-to-all-done.refs_0_, bf16[4,512,128]{2,1,0:T(8,128)(2,1)S(1)} %copy-done.7, bf16[4,512,128]{2,1,0:T(8,128)(2,1)} %collective-permute-done.3.refs_2_, ...), custom_call_target="tpu_custom_call" | custom-call | flops 2147483648 | bytes 11534336 | tf_op jit(solution)/shard_map/first_level/pallas_call | solution.py:76
  105.1 4.8 %collective-permute-start.23 = (bf16[4,512,128]{2,1,0:T(8,128)(2,1)S(1)}, bf16[4,512,128]{2,1,0:T(8,128)(2,1)S(1)}, u32[]{:S(2)}, u32[]{:S(2)}) collective-permute-start(bf16[4,512,128]{2,1,0:T(8,128)(2,1)S(1)} %get-tuple-element.19), channel_id=1, source_target_pairs={{0,32},{1,33},{2,34},{3,35},{4,36},{5,37},{6,38},{7,39},{8,40},{9,... | collective-permute-start | bytes 1572872 | tf_op jit(solution)/shard_map/ppermute | solution.py:29
  111.2 2.8 %collective-permute-start.7 = (bf16[2048,128]{1,0:T(8,128)(2,1)}, bf16[2048,128]{1,0:T(8,128)(2,1)S(1)}, u32[]{:S(2)}, u32[]{:S(2)}) collective-permute-start(bf16[2048,128]{1,0:T(8,128)(2,1)} %collective-permute-done.6.refs_5_), channel_id=1, source_target_pairs={{0,3},{1,0},{2,1},{3,2},{4,7},{5,4},{6,5},{7,6},{8,11},{9,8},{10,9... | collective-permute-start | bytes 1572872 | tf_op jit(solution)/shard_map/ppermute | solution.py:29
  114.0 2.4 %collective-permute-start.4 = (bf16[2048,128]{1,0:T(8,128)(2,1)}, bf16[2048,128]{1,0:T(8,128)(2,1)S(1)}, u32[]{:S(2)}, u32[]{:S(2)}) collective-permute-start(bf16[2048,128]{1,0:T(8,128)(2,1)} %collective-permute-done.1.refs_3_), channel_id=1, source_target_pairs={{0,1},{1,2},{2,3},{3,0},{4,5},{5,6},{6,7},{7,4},{8,9},{9,10},{10,1... | collective-permute-start | bytes 1572872 | tf_op jit(solution)/shard_map/ppermute | solution.py:29
  116.5 4.2 %collective-permute-done.23.refs_8_ = bf16[4,512,128]{2,1,0:T(8,128)(2,1)S(1)} collective-permute-done((bf16[4,512,128]{2,1,0:T(8,128)(2,1)S(1)}, bf16[4,512,128]{2,1,0:T(8,128)(2,1)S(1)}, u32[]{:S(2)}, u32[]{:S(2)}) %collective-permute-start.23) | collective-permute-done | bytes 524320 | tf_op jit(solution)/shard_map/ppermute | solution.py:29
  120.7 2.7 %collective-permute-done.24.refs_9_ = bf16[4,512,128]{2,1,0:T(8,128)(2,1)S(1)} collective-permute-done((bf16[4,512,128]{2,1,0:T(8,128)(2,1)S(1)}, bf16[4,512,128]{2,1,0:T(8,128)(2,1)S(1)}, u32[]{:S(2)}, u32[]{:S(2)}) %collective-permute-start.24) | collective-permute-done | bytes 524320 | tf_op jit(solution)/shard_map/ppermute | solution.py:29
  123.4 2.7 %collective-permute-done.7.refs_6_ = bf16[2048,128]{1,0:T(8,128)(2,1)S(1)} collective-permute-done((bf16[2048,128]{1,0:T(8,128)(2,1)}, bf16[2048,128]{1,0:T(8,128)(2,1)S(1)}, u32[]{:S(2)}, u32[]{:S(2)}) %collective-permute-start.7) | collective-permute-done | bytes 524320 | tf_op jit(solution)/shard_map/ppermute | solution.py:29
  126.0 4.1 %collective-permute-done.4.refs_2_ = bf16[2048,128]{1,0:T(8,128)(2,1)S(1)} collective-permute-done((bf16[2048,128]{1,0:T(8,128)(2,1)}, bf16[2048,128]{1,0:T(8,128)(2,1)S(1)}, u32[]{:S(2)}, u32[]{:S(2)}) %collective-permute-start.4) | collective-permute-done | bytes 524320 | tf_op jit(solution)/shard_map/ppermute | solution.py:29
  130.1 5.2 %second_level.1 = (f32[2048,128]{1,0:T(8,128)S(1)}, bf16[2048,128]{1,0:T(8,128)(2,1)S(1)}, bf16[2048,128]{1,0:T(8,128)(2,1)S(1)}, bf16[2048,128]{1,0:T(8,128)(2,1)S(1)}) custom-call(s32[2]{0:T(128)S(1)} %pad_add_fusion.at_ref, bf16[2048,128]{1,0:T(8,128)(2,1)S(1)} %bitcast.13, bf16[2048,128]{1,0:T(8,128)(2,1)} %collective-permute-done.refs_1_, ...), custom_call_target="tpu_custom_call" | custom-call | flops 2147483648 | bytes 9437184 | tf_op jit(solution)/shard_map/second_level/pallas_call | solution.py:124
  135.3 3.4 %collective-permute-start.25 = (bf16[2048,128]{1,0:T(8,128)(2,1)S(1)}, bf16[2048,128]{1,0:T(8,128)(2,1)S(1)}, u32[]{:S(2)}, u32[]{:S(2)}) collective-permute-start(bf16[2048,128]{1,0:T(8,128)(2,1)S(1)} %get-tuple-element.22), channel_id=1, source_target_pairs={{0,4},{1,5},{2,6},{3,7},{4,8},{5,9},{6,10},{7,11},{8,12},{9,13},{1... | collective-permute-start | bytes 1572872 | tf_op jit(solution)/shard_map/ppermute | solution.py:29
  138.7 3.7 %collective-permute-start.26 = (bf16[2048,128]{1,0:T(8,128)(2,1)S(1)}, bf16[2048,128]{1,0:T(8,128)(2,1)S(1)}, u32[]{:S(2)}, u32[]{:S(2)}) collective-permute-start(bf16[2048,128]{1,0:T(8,128)(2,1)S(1)} %get-tuple-element.23), channel_id=1, source_target_pairs={{0,8},{1,9},{2,10},{3,11},{4,12},{5,13},{6,14},{7,15},{8,0},{9,1},... | collective-permute-start | bytes 1572872 | tf_op jit(solution)/shard_map/ppermute | solution.py:29
  142.4 3.1 %collective-permute-start.27 = (bf16[2048,128]{1,0:T(8,128)(2,1)S(1)}, bf16[2048,128]{1,0:T(8,128)(2,1)S(1)}, u32[]{:S(2)}, u32[]{:S(2)}) collective-permute-start(bf16[2048,128]{1,0:T(8,128)(2,1)S(1)} %get-tuple-element.24), channel_id=1, source_target_pairs={{0,12},{1,13},{2,14},{3,15},{4,0},{5,1},{6,2},{7,3},{8,4},{9,5},{1... | collective-permute-start | bytes 1572872 | tf_op jit(solution)/shard_map/ppermute | solution.py:29
  145.5 4.8 %collective-permute-done.25 = bf16[2048,128]{1,0:T(8,128)(2,1)S(1)} collective-permute-done((bf16[2048,128]{1,0:T(8,128)(2,1)S(1)}, bf16[2048,128]{1,0:T(8,128)(2,1)S(1)}, u32[]{:S(2)}, u32[]{:S(2)}) %collective-permute-start.25) | collective-permute-done | bytes 524320 | tf_op jit(solution)/shard_map/ppermute | solution.py:29
  150.2 11.2 %collective-permute-done.26 = bf16[2048,128]{1,0:T(8,128)(2,1)S(1)} collective-permute-done((bf16[2048,128]{1,0:T(8,128)(2,1)S(1)}, bf16[2048,128]{1,0:T(8,128)(2,1)S(1)}, u32[]{:S(2)}, u32[]{:S(2)}) %collective-permute-start.26) | collective-permute-done | bytes 524320 | tf_op jit(solution)/shard_map/ppermute | solution.py:29
  161.4 3.5 %collective-permute-done.27 = bf16[2048,128]{1,0:T(8,128)(2,1)S(1)} collective-permute-done((bf16[2048,128]{1,0:T(8,128)(2,1)S(1)}, bf16[2048,128]{1,0:T(8,128)(2,1)S(1)}, u32[]{:S(2)}, u32[]{:S(2)}) %collective-permute-start.27) | collective-permute-done | bytes 524320 | tf_op jit(solution)/shard_map/ppermute | solution.py:29
  (59 shorter events, 32.4 us)
Async XLA Ops:
  0.0 14.9 %all-to-all-start.1 = ((bf16[4,512,128]{2,1,0:T(8,128)(2,1)}), bf16[4,512,128]{2,1,0:T(8,128)(2,1)S(1)}, u32[]{:S(2)}, u32[]{:S(2)}) async-start(bf16[4,512,128]{2,1,0:T(8,128)(2,1)} %bitcast.17), calls=%async_computation.1 | async-start | bytes 1048576 | tf_op jit(solution)/shard_map/all_to_all | solution.py:147
  6.3 22.7 %collective-permute-start.12 = (bf16[2048,128]{1,0:T(8,128)(2,1)S(1)}, bf16[2048,128]{1,0:T(8,128)(2,1)S(1)}, u32[]{:S(2)}, u32[]{:S(2)}) collective-permute-start(bf16[2048,128]{1,0:T(8,128)(2,1)S(1)} %bitcast_convert_fusion), channel_id=1, source_target_pairs={{0,16},{1,17},{2,18},{3,19},{4,20},{5,21},{6,22},{7,23},{8,24},{9,... | collective-permute-start | bytes 1572872 | tf_op jit(solution)/shard_map/ppermute | solution.py:29
  10.7 20.5 %collective-permute-start.19 = (bf16[2048,128]{1,0:T(8,128)(2,1)S(1)}, bf16[2048,128]{1,0:T(8,128)(2,1)S(1)}, u32[]{:S(2)}, u32[]{:S(2)}) collective-permute-start(bf16[2048,128]{1,0:T(8,128)(2,1)S(1)} %bitcast_convert_fusion), channel_id=1, source_target_pairs={{16,0},{17,1},{18,2},{19,3},{20,4},{21,5},{22,6},{23,7},{24,8},{25... | collective-permute-start | bytes 1572872 | tf_op jit(solution)/shard_map/ppermute | solution.py:29
  14.9 16.2 %all-to-all-start = ((bf16[4,512,128]{2,1,0:T(8,128)(2,1)}), bf16[4,512,128]{2,1,0:T(8,128)(2,1)S(1)}, u32[]{:S(2)}, u32[]{:S(2)}) async-start(bf16[4,512,128]{2,1,0:T(8,128)(2,1)} %bitcast.3), calls=%async_computation | async-start | bytes 1048576 | tf_op jit(solution)/shard_map/all_to_all | solution.py:147
  19.4 17.4 %collective-permute-start.13 = (bf16[2048,128]{1,0:T(8,128)(2,1)S(1)}, bf16[2048,128]{1,0:T(8,128)(2,1)}, u32[]{:S(2)}, u32[]{:S(2)}) collective-permute-start(bf16[2048,128]{1,0:T(8,128)(2,1)S(1)} %bitcast_convert_fusion), channel_id=1, source_target_pairs={{0,12},{1,13},{2,14},{3,15},{4,0},{5,1},{6,2},{7,3},{8,4},{9,5},{1... | collective-permute-start | bytes 1572872 | tf_op jit(solution)/shard_map/ppermute | solution.py:29
  24.0 14.7 %collective-permute-start.15 = (bf16[2048,128]{1,0:T(8,128)(2,1)S(1)}, bf16[2048,128]{1,0:T(8,128)(2,1)}, u32[]{:S(2)}, u32[]{:S(2)}) collective-permute-start(bf16[2048,128]{1,0:T(8,128)(2,1)S(1)} %bitcast_convert_fusion), channel_id=1, source_target_pairs={{0,8},{1,9},{2,10},{3,11},{4,12},{5,13},{6,14},{7,15},{8,0},{9,1},... | collective-permute-start | bytes 1572872 | tf_op jit(solution)/shard_map/ppermute | solution.py:29
  26.5 26.1 %collective-permute-start.17 = (bf16[2048,128]{1,0:T(8,128)(2,1)S(1)}, bf16[2048,128]{1,0:T(8,128)(2,1)}, u32[]{:S(2)}, u32[]{:S(2)}) collective-permute-start(bf16[2048,128]{1,0:T(8,128)(2,1)S(1)} %bitcast_convert_fusion), channel_id=1, source_target_pairs={{0,4},{1,5},{2,6},{3,7},{4,8},{5,9},{6,10},{7,11},{8,12},{9,13},{1... | collective-permute-start | bytes 1572872 | tf_op jit(solution)/shard_map/ppermute | solution.py:29
  29.0 25.5 %collective-permute-start.5 = (bf16[4,512,128]{2,1,0:T(8,128)(2,1)S(1)}, bf16[4,512,128]{2,1,0:T(8,128)(2,1)S(1)}, u32[]{:S(2)}, u32[]{:S(2)}) collective-permute-start(bf16[4,512,128]{2,1,0:T(8,128)(2,1)S(1)} %all-to-all-done.1.refs_4_), channel_id=1, source_target_pairs={{0,3},{1,0},{2,1},{3,2},{4,7},{5,4},{6,5},{7,6},{8,11},{9,8},{10,9... | collective-permute-start | bytes 1572872 | tf_op jit(solution)/shard_map/ppermute | solution.py:29
  31.2 25.3 %collective-permute-start.2 = (bf16[4,512,128]{2,1,0:T(8,128)(2,1)S(1)}, bf16[4,512,128]{2,1,0:T(8,128)(2,1)S(1)}, u32[]{:S(2)}, u32[]{:S(2)}) collective-permute-start(bf16[4,512,128]{2,1,0:T(8,128)(2,1)S(1)} %all-to-all-done.refs_0_), channel_id=1, source_target_pairs={{0,1},{1,2},{2,3},{3,0},{4,5},{5,6},{6,7},{7,4},{8,9},{9,10},{10,1... | collective-permute-start | bytes 1572872 | tf_op jit(solution)/shard_map/ppermute | solution.py:29
  36.8 23.4 %collective-permute-start.11 = (bf16[4,512,128]{2,1,0:T(8,128)(2,1)S(1)}, bf16[4,512,128]{2,1,0:T(8,128)(2,1)S(1)}, u32[]{:S(2)}, u32[]{:S(2)}) collective-permute-start(bf16[4,512,128]{2,1,0:T(8,128)(2,1)S(1)} %all-to-all-done.1.refs_4_), channel_id=1, source_target_pairs={{0,1},{1,2},{2,3},{3,0},{4,5},{5,6},{6,7},{7,4},{8,9},{9,10},{10,1... | collective-permute-start | bytes 1572872 | tf_op jit(solution)/shard_map/ppermute | solution.py:29
  38.7 24.2 %collective-permute-start.9 = (bf16[4,512,128]{2,1,0:T(8,128)(2,1)S(1)}, bf16[4,512,128]{2,1,0:T(8,128)(2,1)S(1)}, u32[]{:S(2)}, u32[]{:S(2)}) collective-permute-start(bf16[4,512,128]{2,1,0:T(8,128)(2,1)S(1)} %all-to-all-done.refs_0_), channel_id=1, source_target_pairs={{0,3},{1,0},{2,1},{3,2},{4,7},{5,4},{6,5},{7,6},{8,11},{9,8},{10,9... | collective-permute-start | bytes 1572872 | tf_op jit(solution)/shard_map/ppermute | solution.py:29
  52.6 13.1 %collective-permute-start.14 = (bf16[2048,128]{1,0:T(8,128)(2,1)}, bf16[2048,128]{1,0:T(8,128)(2,1)S(1)}, u32[]{:S(2)}, u32[]{:S(2)}) collective-permute-start(bf16[2048,128]{1,0:T(8,128)(2,1)} %collective-permute-done.13), channel_id=1, source_target_pairs={{0,16},{1,17},{2,18},{3,19},{4,20},{5,21},{6,22},{7,23},{8,24},{9,... | collective-permute-start | bytes 1572872 | tf_op jit(solution)/shard_map/ppermute | solution.py:29
  54.5 20.1 %collective-permute-start.16 = (bf16[2048,128]{1,0:T(8,128)(2,1)}, bf16[2048,128]{1,0:T(8,128)(2,1)}, u32[]{:S(2)}, u32[]{:S(2)}) collective-permute-start(bf16[2048,128]{1,0:T(8,128)(2,1)} %collective-permute-done.15), channel_id=1, source_target_pairs={{0,16},{1,17},{2,18},{3,19},{4,20},{5,21},{6,22},{7,23},{8,24},{9,... | collective-permute-start | bytes 1572872 | tf_op jit(solution)/shard_map/ppermute | solution.py:29
  56.4 20.6 %collective-permute-start.18 = (bf16[2048,128]{1,0:T(8,128)(2,1)}, bf16[2048,128]{1,0:T(8,128)(2,1)}, u32[]{:S(2)}, u32[]{:S(2)}) collective-permute-start(bf16[2048,128]{1,0:T(8,128)(2,1)} %collective-permute-done.17), channel_id=1, source_target_pairs={{0,16},{1,17},{2,18},{3,19},{4,20},{5,21},{6,22},{7,23},{8,24},{9,... | collective-permute-start | bytes 1572872 | tf_op jit(solution)/shard_map/ppermute | solution.py:29
  61.0 18.9 %collective-permute-start.20 = (bf16[2048,128]{1,0:T(8,128)(2,1)}, bf16[2048,128]{1,0:T(8,128)(2,1)}, u32[]{:S(2)}, u32[]{:S(2)}) collective-permute-start(bf16[2048,128]{1,0:T(8,128)(2,1)} %collective-permute-done.13), channel_id=1, source_target_pairs={{16,0},{17,1},{18,2},{19,3},{20,4},{21,5},{22,6},{23,7},{24,8},{25... | collective-permute-start | bytes 1572872 | tf_op jit(solution)/shard_map/ppermute | solution.py:29
  63.7 18.1 %collective-permute-start.21 = (bf16[2048,128]{1,0:T(8,128)(2,1)}, bf16[2048,128]{1,0:T(8,128)(2,1)}, u32[]{:S(2)}, u32[]{:S(2)}) collective-permute-start(bf16[2048,128]{1,0:T(8,128)(2,1)} %collective-permute-done.15), channel_id=1, source_target_pairs={{16,0},{17,1},{18,2},{19,3},{20,4},{21,5},{22,6},{23,7},{24,8},{25... | collective-permute-start | bytes 1572872 | tf_op jit(solution)/shard_map/ppermute | solution.py:29
  66.4 20.0 %collective-permute-start.22 = (bf16[2048,128]{1,0:T(8,128)(2,1)}, bf16[2048,128]{1,0:T(8,128)(2,1)}, u32[]{:S(2)}, u32[]{:S(2)}) collective-permute-start(bf16[2048,128]{1,0:T(8,128)(2,1)} %collective-permute-done.17), channel_id=1, source_target_pairs={{16,0},{17,1},{18,2},{19,3},{20,4},{21,5},{22,6},{23,7},{24,8},{25... | collective-permute-start | bytes 1572872 | tf_op jit(solution)/shard_map/ppermute | solution.py:29
  68.4 24.3 %all-to-all-start.2 = ((f32[4,512,128]{2,1,0:T(8,128)}), f32[4,512,128]{2,1,0:T(8,128)S(1)}, u32[]{:S(2)}, u32[]{:S(2)}) async-start(f32[4,512,128]{2,1,0:T(8,128)} %bitcast.7), calls=%async_computation.2 | async-start | bytes 2097152 | tf_op jit(solution)/shard_map/all_to_all | solution.py:147
  74.6 16.2 %collective-permute-start.10 = (bf16[4,512,128]{2,1,0:T(8,128)(2,1)}, bf16[4,512,128]{2,1,0:T(8,128)(2,1)}, u32[]{:S(2)}, u32[]{:S(2)}) collective-permute-start(bf16[4,512,128]{2,1,0:T(8,128)(2,1)} %copy-done), channel_id=1, source_target_pairs={{0,3},{1,0},{2,1},{3,2},{4,7},{5,4},{6,5},{7,6},{8,11},{9,8},{10,9... | collective-permute-start | bytes 1572872 | tf_op jit(solution)/shard_map/ppermute | solution.py:29
  77.0 17.4 %collective-permute-start.3 = (bf16[4,512,128]{2,1,0:T(8,128)(2,1)}, bf16[4,512,128]{2,1,0:T(8,128)(2,1)}, u32[]{:S(2)}, u32[]{:S(2)}) collective-permute-start(bf16[4,512,128]{2,1,0:T(8,128)(2,1)} %copy-done.2), channel_id=1, source_target_pairs={{0,1},{1,2},{2,3},{3,0},{4,5},{5,6},{6,7},{7,4},{8,9},{9,10},{10,1... | collective-permute-start | bytes 1572872 | tf_op jit(solution)/shard_map/ppermute | solution.py:29
  79.9 30.0 %collective-permute-start.1 = (bf16[2048,128]{1,0:T(8,128)(2,1)}, bf16[2048,128]{1,0:T(8,128)(2,1)}, u32[]{:S(2)}, u32[]{:S(2)}) collective-permute-start(bf16[2048,128]{1,0:T(8,128)(2,1)} %bitcast.11), channel_id=1, source_target_pairs={{0,1},{1,2},{2,3},{3,0},{4,5},{5,6},{6,7},{7,4},{8,9},{9,10},{10,1... | collective-permute-start | bytes 1572872 | tf_op jit(solution)/shard_map/ppermute | solution.py:29
  81.8 29.4 %collective-permute-start.6 = (bf16[2048,128]{1,0:T(8,128)(2,1)}, bf16[2048,128]{1,0:T(8,128)(2,1)}, u32[]{:S(2)}, u32[]{:S(2)}) collective-permute-start(bf16[2048,128]{1,0:T(8,128)(2,1)} %bitcast.14), channel_id=1, source_target_pairs={{0,3},{1,0},{2,1},{3,2},{4,7},{5,4},{6,5},{7,6},{8,11},{9,8},{10,9... | collective-permute-start | bytes 1572872 | tf_op jit(solution)/shard_map/ppermute | solution.py:29
  86.4 27.6 %collective-permute-start = (bf16[2048,128]{1,0:T(8,128)(2,1)}, bf16[2048,128]{1,0:T(8,128)(2,1)}, u32[]{:S(2)}, u32[]{:S(2)}) collective-permute-start(bf16[2048,128]{1,0:T(8,128)(2,1)} %bitcast.12), channel_id=1, source_target_pairs={{0,3},{1,0},{2,1},{3,2},{4,7},{5,4},{6,5},{7,6},{8,11},{9,8},{10,9... | collective-permute-start | bytes 1572872 | tf_op jit(solution)/shard_map/ppermute | solution.py:29
  90.8 25.7 %collective-permute-start.8 = (bf16[2048,128]{1,0:T(8,128)(2,1)}, bf16[2048,128]{1,0:T(8,128)(2,1)}, u32[]{:S(2)}, u32[]{:S(2)}) collective-permute-start(bf16[2048,128]{1,0:T(8,128)(2,1)} %bitcast.15), channel_id=1, source_target_pairs={{0,1},{1,2},{2,3},{3,0},{4,5},{5,6},{6,7},{7,4},{8,9},{9,10},{10,1... | collective-permute-start | bytes 1572872 | tf_op jit(solution)/shard_map/ppermute | solution.py:29
  99.6 30.5 %copy-start.11 = (bf16[1,2048,128]{2,1,0:T(8,128)(2,1)S(1)}, bf16[1,2048,128]{2,1,0:T(8,128)(2,1)}, u32[]{:S(2)}) copy-start(bf16[1,2048,128]{2,1,0:T(8,128)(2,1)} %param.9) | copy-start | bytes 1572868
  105.1 15.6 %collective-permute-start.23 = (bf16[4,512,128]{2,1,0:T(8,128)(2,1)S(1)}, bf16[4,512,128]{2,1,0:T(8,128)(2,1)S(1)}, u32[]{:S(2)}, u32[]{:S(2)}) collective-permute-start(bf16[4,512,128]{2,1,0:T(8,128)(2,1)S(1)} %get-tuple-element.19), channel_id=1, source_target_pairs={{0,32},{1,33},{2,34},{3,35},{4,36},{5,37},{6,38},{7,39},{8,40},{9,... | collective-permute-start | bytes 1572872 | tf_op jit(solution)/shard_map/ppermute | solution.py:29
  109.9 13.5 %collective-permute-start.24 = (bf16[4,512,128]{2,1,0:T(8,128)(2,1)S(1)}, bf16[4,512,128]{2,1,0:T(8,128)(2,1)S(1)}, u32[]{:S(2)}, u32[]{:S(2)}) collective-permute-start(bf16[4,512,128]{2,1,0:T(8,128)(2,1)S(1)} %get-tuple-element.19), channel_id=1, source_target_pairs={{32,0},{33,1},{34,2},{35,3},{36,4},{37,5},{38,6},{39,7},{40,8},{41... | collective-permute-start | bytes 1572872 | tf_op jit(solution)/shard_map/ppermute | solution.py:29
  111.2 14.9 %collective-permute-start.7 = (bf16[2048,128]{1,0:T(8,128)(2,1)}, bf16[2048,128]{1,0:T(8,128)(2,1)S(1)}, u32[]{:S(2)}, u32[]{:S(2)}) collective-permute-start(bf16[2048,128]{1,0:T(8,128)(2,1)} %collective-permute-done.6.refs_5_), channel_id=1, source_target_pairs={{0,3},{1,0},{2,1},{3,2},{4,7},{5,4},{6,5},{7,6},{8,11},{9,8},{10,9... | collective-permute-start | bytes 1572872 | tf_op jit(solution)/shard_map/ppermute | solution.py:29
  114.0 16.0 %collective-permute-start.4 = (bf16[2048,128]{1,0:T(8,128)(2,1)}, bf16[2048,128]{1,0:T(8,128)(2,1)S(1)}, u32[]{:S(2)}, u32[]{:S(2)}) collective-permute-start(bf16[2048,128]{1,0:T(8,128)(2,1)} %collective-permute-done.1.refs_3_), channel_id=1, source_target_pairs={{0,1},{1,2},{2,3},{3,0},{4,5},{5,6},{6,7},{7,4},{8,9},{9,10},{10,1... | collective-permute-start | bytes 1572872 | tf_op jit(solution)/shard_map/ppermute | solution.py:29
  135.3 14.9 %collective-permute-start.25 = (bf16[2048,128]{1,0:T(8,128)(2,1)S(1)}, bf16[2048,128]{1,0:T(8,128)(2,1)S(1)}, u32[]{:S(2)}, u32[]{:S(2)}) collective-permute-start(bf16[2048,128]{1,0:T(8,128)(2,1)S(1)} %get-tuple-element.22), channel_id=1, source_target_pairs={{0,4},{1,5},{2,6},{3,7},{4,8},{5,9},{6,10},{7,11},{8,12},{9,13},{1... | collective-permute-start | bytes 1572872 | tf_op jit(solution)/shard_map/ppermute | solution.py:29
  138.7 22.7 %collective-permute-start.26 = (bf16[2048,128]{1,0:T(8,128)(2,1)S(1)}, bf16[2048,128]{1,0:T(8,128)(2,1)S(1)}, u32[]{:S(2)}, u32[]{:S(2)}) collective-permute-start(bf16[2048,128]{1,0:T(8,128)(2,1)S(1)} %get-tuple-element.23), channel_id=1, source_target_pairs={{0,8},{1,9},{2,10},{3,11},{4,12},{5,13},{6,14},{7,15},{8,0},{9,1},... | collective-permute-start | bytes 1572872 | tf_op jit(solution)/shard_map/ppermute | solution.py:29
  142.4 22.6 %collective-permute-start.27 = (bf16[2048,128]{1,0:T(8,128)(2,1)S(1)}, bf16[2048,128]{1,0:T(8,128)(2,1)S(1)}, u32[]{:S(2)}, u32[]{:S(2)}) collective-permute-start(bf16[2048,128]{1,0:T(8,128)(2,1)S(1)} %get-tuple-element.24), channel_id=1, source_target_pairs={{0,12},{1,13},{2,14},{3,15},{4,0},{5,1},{6,2},{7,3},{8,4},{9,5},{1... | collective-permute-start | bytes 1572872 | tf_op jit(solution)/shard_map/ppermute | solution.py:29
  (11 other events, 58.4 us)

commit v3 on v2

v3 whole, which is shorter than its diff:
```python
import jax
import jax.numpy as jnp
from jax import lax
from jax.experimental import pallas as pl
from jax.experimental.pallas import tpu as pltpu
from jax.sharding import Mesh, PartitionSpec as P

Z, CORES, Y, X = 16, 2, 4, 4
PLANES = Z * CORES
M = 2048
BLK = M // Y
COL = 128
AXES = ("z", "core", "y", "x")


def device_index(plane, y, x):
    return (plane * Y + y) * X + x


def moved(value, planes=0, ys=0, xs=0):
    pairs = []
    for plane in range(PLANES):
        if not 0 <= plane + planes < PLANES:
            continue
        for y in range(Y):
            for x in range(X):
                target = device_index(plane + planes, (y + ys) % Y, (x + xs) % X)
                pairs.append((device_index(plane, y, x), target))
    return lax.ppermute(value, AXES, pairs)


def after(value, *before):
    return lax.optimization_barrier((value,) + before)[0]


def rows_in_order(at_ref, ref, row):
    return [
        ref[row + (pl.ds(pl.multiple_of(lax.rem(at_ref[1] + e, X) * COL, COL), COL),)]
        for e in range(X)
    ]


def first_kernel(
    at_ref,
    own_ref,
    left_ref,
    right_ref,
    a_far_ref,
    b_far_ref,
    near_ref,
    down_ref,
    up_ref,
    below_far_ref,
    above_far_ref,
    rhs_ref,
    corr_ref,
    sent_ref,
    acc_ref,
):
    step = pl.program_id(0)

    @pl.when(step == 0)
    def _():
        acc_ref[...] = jnp.zeros_like(acc_ref)

    total = acc_ref[...]
    for side, far_ref in ((0, below_far_ref), (1, above_far_ref)):
        blocks = [
            own_ref[0, side],
            right_ref[0, side],
            jnp.where(step < Y // 2, a_far_ref[0, side], b_far_ref[0, side]),
            left_ref[0, side],
        ]
        left = jnp.concatenate(blocks, axis=1)
        parts = (
            (near_ref, (side,)),
            (up_ref, (side,)),
            (far_ref, ()),
            (down_ref, (side,)),
        )
        right = [
            jnp.concatenate(rows_in_order(at_ref, part, row), axis=0)
            for part, row in parts
        ]
        right = jnp.concatenate(right, axis=1)
        total = total + jnp.dot(left, right, preferred_element_type=jnp.float32)
    acc_ref[...] = total

    @pl.when(step == Y - 1)
    def _():
        for d in range(Y):
            piece = acc_ref[:, d * COL : (d + 1) * COL]
            corr_ref[d] = piece
            owner = lax.rem(at_ref[0] + d, Y)
            sent_ref[d] = (rhs_ref[owner] + piece).astype(jnp.bfloat16)


def first_level(at, pair, left, right, a_far, b_far, near, down, up, below, above, rhs):
    half = Y // 2
    blocks = pl.BlockSpec((1, 2, BLK, COL), lambda k, at: (k, 0, 0, 0))
    a_blocks = pl.BlockSpec(
        (1, 2, BLK, COL), lambda k, at: (jnp.minimum(k, half - 1), 0, 0, 0)
    )
    b_blocks = pl.BlockSpec(
        (1, 2, BLK, COL), lambda k, at: (jnp.maximum(k - half, 0), 0, 0, 0)
    )
    parts = pl.BlockSpec((2, BLK, COL), lambda k, at: (0, k, 0))
    part = pl.BlockSpec((BLK, COL), lambda k, at: (k, 0))
    whole = pl.BlockSpec((Y, BLK, COL), lambda k, at: (0, 0, 0))
    return pl.pallas_call(
        first_kernel,
        name="first_level",
        out_shape=(
            jax.ShapeDtypeStruct((Y, BLK, COL), jnp.float32),
            jax.ShapeDtypeStruct((Y, BLK, COL), jnp.bfloat16),
        ),
        grid_spec=pltpu.PrefetchScalarGridSpec(
            num_scalar_prefetch=1,
            grid=(Y,),
            in_specs=[blocks] * 3
            + [a_blocks, b_blocks]
            + [parts] * 3
            + [part] * 2
            + [whole],
            out_specs=(whole, whole),
            scratch_shapes=[pltpu.VMEM((BLK, Y * COL), jnp.float32)],
        ),
        compiler_params=pltpu.CompilerParams(vmem_limit_bytes=32 << 20),
        cost_estimate=pl.CostEstimate(
            flops=4 * BLK * M * Y * COL, bytes_accessed=11 << 20, transcendentals=0
        ),
    )(at, pair, left, right, a_far, b_far, near, down, up, below, above, rhs)


def second_kernel(
    at_ref, a_ref, below, above, corr_ref, rhs_ref, own_ref, *outs
):
    step = pl.program_id(0)
    total = None
    for side, b_ref in ((0, below), (1, above)):
        left = jnp.concatenate([a_ref[x, side] for x in range(X)], axis=1)
        right = jnp.concatenate([b_ref[d] for d in range(Y)], axis=1)
        term = jnp.dot(left, right, preferred_element_type=jnp.float32)
        total = term if total is None else total + term
    here = step == at_ref[0]
    for d in range(Y):
        piece = total[:, d * COL : (d + 1) * COL]
        piece = piece + jnp.where(here, corr_ref[d], 0.0)
        if d == 0:
            own_ref[...] = piece + rhs_ref[...]
        else:
            outs[d - 1][...] = piece.astype(jnp.bfloat16)


def second_level(at, blocks, below, above, corr, rhs):
    rows = pl.BlockSpec((BLK, COL), lambda m, at: (m, 0))
    pairs = pl.BlockSpec((X, 2, BLK, COL), lambda m, at: (0, 0, m, 0))
    whole = pl.BlockSpec((Y, BLK, COL), lambda m, at: (0, 0, 0))
    return pl.pallas_call(
        second_kernel,
        name="second_level",
        out_shape=(jax.ShapeDtypeStruct((M, COL), jnp.float32),)
        + (jax.ShapeDtypeStruct((M, COL), jnp.bfloat16),) * 3,
        grid_spec=pltpu.PrefetchScalarGridSpec(
            num_scalar_prefetch=1,
            grid=(Y,),
            in_specs=[pairs, whole, whole, whole, rows],
            out_specs=(rows,) * 4,
        ),
        compiler_params=pltpu.CompilerParams(vmem_limit_bytes=56 << 20),
        cost_estimate=pl.CostEstimate(
            flops=4 * BLK * M * Y * COL, bytes_accessed=9 << 20, transcendentals=0
        ),
    )(at, blocks, below, above, corr, rhs)


def relayed(pair, halves, **axis):
    name = "xs" if axis["over"] == "x" else "ys"
    left, right = moved(pair, **{name: 1}), moved(pair, **{name: -1})
    first, second = halves
    far = moved(first(left), **{name: 1}), moved(second(right), **{name: -1})
    return (left, right) + far


def on_device(right_sides, lower_first, upper_first, lower_second, upper_second):
    rhs = right_sides[0]
    at = jnp.stack([lax.axis_index("y"), lax.axis_index("x")]).astype(jnp.int32)
    halves = (lambda v: v[: Y // 2], lambda v: v[Y // 2 :])
    sides = (lambda v: v[0], lambda v: v[1])

    def exchanged(value):
        return lax.all_to_all(value, "y", 0, 0, tiled=True)

    seconds = jnp.stack([lower_second[0], upper_second[0]])
    seconds = lax.all_gather(seconds, "x", axis=0)

    firsts = [v[0].reshape(Y, BLK, COL) for v in (lower_first, upper_first)]
    firsts = jnp.stack(firsts, axis=1)
    sent_one = after(rhs, firsts).astype(jnp.bfloat16)
    pair = exchanged(firsts)
    near = after(jnp.stack([moved(sent_one, 1), moved(sent_one, -1)]), pair)

    left, right, a_far, b_far = relayed(pair, halves, over="x")
    down, up, below_far, above_far = relayed(near, sides, over="y")
    rhs_rows = exchanged(after(rhs, pair).reshape(Y, BLK, COL))

    corr, sent_two = first_level(
        at,
        pair,
        left,
        right,
        a_far,
        b_far,
        near,
        down,
        up,
        below_far,
        above_far,
        rhs_rows,
    )
    below_two, above_two = moved(sent_two, 2), moved(sent_two, -2)
    total, *parts = second_level(at, seconds, below_two, above_two, corr, rhs)
    for d in range(1, Y):
        total = total + moved(parts[d - 1], ys=d).astype(jnp.float32)
    return total[None]


def solution(mesh):
    fine = Mesh(mesh.devices.reshape(Z, CORES, Y, X), AXES)
    spec = P(("z", "core"), None, ("y", "x"))
    return jax.shard_map(
        on_device,
        mesh=fine,
        in_specs=(spec,) * 5,
        out_specs=spec,
        check_vma=False,
    )
```

time: 168 us -> 188 us (1.12)
  the two profiles are of different devices: /device:TPU:1 before, /device:TPU:38 now
where the time goes in v3:
time: 188 us; the launch traced here: 187 us
  waiting for transfers between devices  89 us (47%)
  starting transfers between devices  54.1 us (29%)
  between operations  13.6 us (7%)
  Pallas kernels  13.2 us (7%)
  local copies, waits for them, and re-layouts  9.35 us (5%)
  other arithmetic  7.31 us (4%)
    ppermute x15, waiting for transfers between devices, moved(): return lax.ppermute(value, AXES, pairs)  86.3 us
    ppermute x15, starting transfers between devices, moved(): return lax.ppermute(value, AXES, pairs)  46.1 us
    all_to_all x2, starting transfers between devices, exchanged(): return lax.all_to_all(value, 'y', 0, 0, tiled=True)  7.99 us
    pallas_call x1, Pallas kernels, second_level(): pl.pallas_call(second_kernel, name='second_level', out_shape=(jax.ShapeDt...  7.27 us
    pallas_call x1, Pallas kernels, first_level(): pl.pallas_call(first_kernel, name='first_level', out_shape=(jax.ShapeDtyp...  5.93 us
    slice x2, local copies, waits for them, and re-layouts, on_device(): halves = (lambda v: v[:Y // 2], lambda v: v[Y // 2:])  3.76 us
  transfers between devices with their start and end apart: 18, of which 11 were waited for; matrix products, arithmetic and copies ran while one was open for 5% of the time, Pallas kernels for 3%

profile of v3, /device:TPU:38, one launch (start us, length us, event | category | flops | bytes accessed | tf_op | source)
XLA Modules:
  0.0 186.6 jit_solution(2189264530336007462)
XLA Ops:
  6.5 2.4 %pad_maximum_fusion = bf16[2,2048,128]{2,1,0:T(8,128)(2,1)} fusion(bf16[1,2048,128]{2,1,0:T(8,128)(2,1)} %param.9, bf16[1,2048,128]{2,1,0:T(8,128)(2,1)} %param.8), kind=kLoop, calls=%fused_computation | loop fusion | flops 524288 | bytes 2097152 | tf_op jit(solution)/shard_map/stack | solution.py:194
  8.9 2.3 %pad_maximum_fusion.1 = bf16[4,2,512,128]{3,2,1,0:T(8,128)(2,1)} fusion(bf16[4,1,512,128]{3,2,1,0:T(8,128)(2,1)} %bitcast.18, bf16[4,1,512,128]{3,2,1,0:T(8,128)(2,1)} %bitcast.19), kind=kLoop, calls=%fused_computation.1 | loop fusion | flops 524288 | bytes 2097152 | tf_op jit(solution)/shard_map/stack | solution.py:198
  11.2 4.5 %all-to-all-start = ((bf16[4,2,512,128]{3,2,1,0:T(8,128)(2,1)}), bf16[4,2,512,128]{3,2,1,0:T(8,128)(2,1)S(1)}, u32[]{:S(2)}, u32[]{:S(2)}) async-start(bf16[4,2,512,128]{3,2,1,0:T(8,128)(2,1)} %pad_maximum_fusion.1), calls=%async_computation | async-start | bytes 2097152 | tf_op jit(solution)/shard_map/all_to_all | solution.py:192
  15.8 1.9 %collective-permute-start.4 = (bf16[2048,128]{1,0:T(8,128)(2,1)S(1)}, bf16[2048,128]{1,0:T(8,128)(2,1)S(1)}, u32[]{:S(2)}, u32[]{:S(2)}) collective-permute-start(bf16[2048,128]{1,0:T(8,128)(2,1)S(1)} %convert_element_type.12), channel_id=1, source_target_pairs={{0,16},{1,17},{2,18},{3,19},{4,20},{5,21},{6,22},{7,23},{8,24},{9,... | collective-permute-start | bytes 1572872 | tf_op jit(solution)/shard_map/ppermute | solution.py:29
  17.7 3.6 %collective-permute-start.5 = (bf16[2048,128]{1,0:T(8,128)(2,1)S(1)}, bf16[2048,128]{1,0:T(8,128)(2,1)S(1)}, u32[]{:S(2)}, u32[]{:S(2)}) collective-permute-start(bf16[2048,128]{1,0:T(8,128)(2,1)S(1)} %convert_element_type.12), channel_id=1, source_target_pairs={{16,0},{17,1},{18,2},{19,3},{20,4},{21,5},{22,6},{23,7},{24,8},{25... | collective-permute-start | bytes 1572872 | tf_op jit(solution)/shard_map/ppermute | solution.py:29
  21.3 4.9 %collective-permute-done.4 = bf16[2048,128]{1,0:T(8,128)(2,1)S(1)} collective-permute-done((bf16[2048,128]{1,0:T(8,128)(2,1)S(1)}, bf16[2048,128]{1,0:T(8,128)(2,1)S(1)}, u32[]{:S(2)}, u32[]{:S(2)}) %collective-permute-start.4) | collective-permute-done | bytes 524320 | tf_op jit(solution)/shard_map/ppermute | solution.py:29
  28.1 2.7 %all-to-all-done.own_ref = bf16[4,2,512,128]{3,2,1,0:T(8,128)(2,1)S(1)} async-done(((bf16[4,2,512,128]{3,2,1,0:T(8,128)(2,1)}), bf16[4,2,512,128]{3,2,1,0:T(8,128)(2,1)S(1)}, u32[]{:S(2)}, u32[]{:S(2)}) %all-to-all-start) | async-done | bytes 1048608 | tf_op jit(solution)/shard_map/all_to_all | solution.py:192
  30.8 2.5 %collective-permute-start.6 = (bf16[2,2048,128]{2,1,0:T(8,128)(2,1)S(1)}, bf16[2,2048,128]{2,1,0:T(8,128)(2,1)}, u32[]{:S(2)}, u32[]{:S(2)}) collective-permute-start(bf16[2,2048,128]{2,1,0:T(8,128)(2,1)S(1)} %pad_maximum_fusion.2.near_ref), channel_id=1, source_target_pairs={{0,4},{1,5},{2,6},{3,7},{4,8},{5,9},{6,10},{7,11},{8,12},{9,13},{1... | collective-permute-start | bytes 3145736 | tf_op jit(solution)/shard_map/ppermute | solution.py:29
  33.3 4.6 %collective-permute-start.7 = (bf16[2,2048,128]{2,1,0:T(8,128)(2,1)S(1)}, bf16[2,2048,128]{2,1,0:T(8,128)(2,1)}, u32[]{:S(2)}, u32[]{:S(2)}) collective-permute-start(bf16[2,2048,128]{2,1,0:T(8,128)(2,1)S(1)} %pad_maximum_fusion.2.near_ref), channel_id=1, source_target_pairs={{0,12},{1,13},{2,14},{3,15},{4,0},{5,1},{6,2},{7,3},{8,4},{9,5},{1... | collective-permute-start | bytes 3145736 | tf_op jit(solution)/shard_map/ppermute | solution.py:29
  37.9 2.4 %collective-permute-start = (bf16[4,2,512,128]{3,2,1,0:T(8,128)(2,1)S(1)}, bf16[4,2,512,128]{3,2,1,0:T(8,128)(2,1)}, u32[]{:S(2)}, u32[]{:S(2)}) collective-permute-start(bf16[4,2,512,128]{3,2,1,0:T(8,128)(2,1)S(1)} %all-to-all-done.own_ref), channel_id=1, source_target_pairs={{0,1},{1,2},{2,3},{3,0},{4,5},{5,6},{6,7},{7,4},{8,9},{9,10},{10,1... | collective-permute-start | bytes 3145736 | tf_op jit(solution)/shard_map/ppermute | solution.py:29
  40.2 3.5 %collective-permute-start.1 = (bf16[4,2,512,128]{3,2,1,0:T(8,128)(2,1)S(1)}, bf16[4,2,512,128]{3,2,1,0:T(8,128)(2,1)}, u32[]{:S(2)}, u32[]{:S(2)}) collective-permute-start(bf16[4,2,512,128]{3,2,1,0:T(8,128)(2,1)S(1)} %all-to-all-done.own_ref), channel_id=1, source_target_pairs={{0,3},{1,0},{2,1},{3,2},{4,7},{5,4},{6,5},{7,6},{8,11},{9,8},{10,9... | collective-permute-start | bytes 3145736 | tf_op jit(solution)/shard_map/ppermute | solution.py:29
  43.7 3.5 %all-to-all-start.1 = ((f32[4,512,128]{2,1,0:T(8,128)}), f32[4,512,128]{2,1,0:T(8,128)S(1)}, u32[]{:S(2)}, u32[]{:S(2)}) async-start(f32[4,512,128]{2,1,0:T(8,128)} %bitcast.15), calls=%async_computation.1 | async-start | bytes 2097152 | tf_op jit(solution)/shard_map/all_to_all | solution.py:192
  47.3 12.8 %collective-permute-done.6.down_ref = bf16[2,2048,128]{2,1,0:T(8,128)(2,1)} collective-permute-done((bf16[2,2048,128]{2,1,0:T(8,128)(2,1)S(1)}, bf16[2,2048,128]{2,1,0:T(8,128)(2,1)}, u32[]{:S(2)}, u32[]{:S(2)}) %collective-permute-start.6) | collective-permute-done | bytes 1048608 | tf_op jit(solution)/shard_map/ppermute | solution.py:29
  61.9 1.9 %collective-permute-start.8 = (bf16[2048,128]{1,0:T(8,128)(2,1)}, bf16[2048,128]{1,0:T(8,128)(2,1)}, u32[]{:S(2)}, u32[]{:S(2)}) collective-permute-start(bf16[2048,128]{1,0:T(8,128)(2,1)} %slice_bitcast_fusion.1), channel_id=1, source_target_pairs={{0,4},{1,5},{2,6},{3,7},{4,8},{5,9},{6,10},{7,11},{8,12},{9,13},{1... | collective-permute-start | bytes 1572872 | tf_op jit(solution)/shard_map/ppermute | solution.py:29
  65.7 5.1 %collective-permute-start.9 = (bf16[2048,128]{1,0:T(8,128)(2,1)}, bf16[2048,128]{1,0:T(8,128)(2,1)}, u32[]{:S(2)}, u32[]{:S(2)}) collective-permute-start(bf16[2048,128]{1,0:T(8,128)(2,1)} %slice_bitcast_fusion), channel_id=1, source_target_pairs={{0,12},{1,13},{2,14},{3,15},{4,0},{5,1},{6,2},{7,3},{8,4},{9,5},{1... | collective-permute-start | bytes 1572872 | tf_op jit(solution)/shard_map/ppermute | solution.py:29
  70.9 16.9 %collective-permute-done.left_ref = bf16[4,2,512,128]{3,2,1,0:T(8,128)(2,1)} collective-permute-done((bf16[4,2,512,128]{3,2,1,0:T(8,128)(2,1)S(1)}, bf16[4,2,512,128]{3,2,1,0:T(8,128)(2,1)}, u32[]{:S(2)}, u32[]{:S(2)}) %collective-permute-start) | collective-permute-done | bytes 1048608 | tf_op jit(solution)/shard_map/ppermute | solution.py:29
  89.6 3.6 %collective-permute-start.2 = (bf16[2,2,512,128]{3,2,1,0:T(8,128)(2,1)}, bf16[2,2,512,128]{3,2,1,0:T(8,128)(2,1)}, u32[]{:S(2)}, u32[]{:S(2)}) collective-permute-start(bf16[2,2,512,128]{3,2,1,0:T(8,128)(2,1)} %slice.16), channel_id=1, source_target_pairs={{0,1},{1,2},{2,3},{3,0},{4,5},{5,6},{6,7},{7,4},{8,9},{9,10},{10,1... | collective-permute-start | bytes 1572872 | tf_op jit(solution)/shard_map/ppermute | solution.py:29
  95.1 2.2 %collective-permute-start.3 = (bf16[2,2,512,128]{3,2,1,0:T(8,128)(2,1)}, bf16[2,2,512,128]{3,2,1,0:T(8,128)(2,1)}, u32[]{:S(2)}, u32[]{:S(2)}) collective-permute-start(bf16[2,2,512,128]{3,2,1,0:T(8,128)(2,1)} %slice.17), channel_id=1, source_target_pairs={{0,3},{1,0},{2,1},{3,2},{4,7},{5,4},{6,5},{7,6},{8,11},{9,8},{10,9... | collective-permute-start | bytes 1572872 | tf_op jit(solution)/shard_map/ppermute | solution.py:29
  97.5 6.6 %collective-permute-done.2.a_far_ref = bf16[2,2,512,128]{3,2,1,0:T(8,128)(2,1)} collective-permute-done((bf16[2,2,512,128]{3,2,1,0:T(8,128)(2,1)}, bf16[2,2,512,128]{3,2,1,0:T(8,128)(2,1)}, u32[]{:S(2)}, u32[]{:S(2)}) %collective-permute-start.2) | collective-permute-done | bytes 524320 | tf_op jit(solution)/shard_map/ppermute | solution.py:29
  104.1 6.4 %collective-permute-done.3.b_far_ref = bf16[2,2,512,128]{3,2,1,0:T(8,128)(2,1)} collective-permute-done((bf16[2,2,512,128]{3,2,1,0:T(8,128)(2,1)}, bf16[2,2,512,128]{3,2,1,0:T(8,128)(2,1)}, u32[]{:S(2)}, u32[]{:S(2)}) %collective-permute-start.3) | collective-permute-done | bytes 524320 | tf_op jit(solution)/shard_map/ppermute | solution.py:29
  110.5 5.9 %first_level.1 = (f32[4,512,128]{2,1,0:T(8,128)S(1)}, bf16[4,512,128]{2,1,0:T(8,128)(2,1)S(1)}) custom-call(s32[2]{0:T(128)S(1)} %pad_add_fusion.at_ref, bf16[4,2,512,128]{3,2,1,0:T(8,128)(2,1)S(1)} %all-to-all-done.own_ref, bf16[4,2,512,128]{3,2,1,0:T(8,128)(2,1)} %collective-permute-done.left_ref, ...), custom_call_target="tpu_custom_call" | custom-call | flops 2147483648 | bytes 11534336 | tf_op jit(solution)/shard_map/first_level/pallas_call | solution.py:110
  117.5 3.8 %collective-permute-start.10 = (bf16[4,512,128]{2,1,0:T(8,128)(2,1)S(1)}, bf16[4,512,128]{2,1,0:T(8,128)(2,1)S(1)}, u32[]{:S(2)}, u32[]{:S(2)}) collective-permute-start(bf16[4,512,128]{2,1,0:T(8,128)(2,1)S(1)} %get-tuple-element.17), channel_id=1, source_target_pairs={{0,32},{1,33},{2,34},{3,35},{4,36},{5,37},{6,38},{7,39},{8,40},{9,... | collective-permute-start | bytes 1572872 | tf_op jit(solution)/shard_map/ppermute | solution.py:29
  121.3 2.0 %collective-permute-start.11 = (bf16[4,512,128]{2,1,0:T(8,128)(2,1)S(1)}, bf16[4,512,128]{2,1,0:T(8,128)(2,1)S(1)}, u32[]{:S(2)}, u32[]{:S(2)}) collective-permute-start(bf16[4,512,128]{2,1,0:T(8,128)(2,1)S(1)} %get-tuple-element.17), channel_id=1, source_target_pairs={{32,0},{33,1},{34,2},{35,3},{36,4},{37,5},{38,6},{39,7},{40,8},{41... | collective-permute-start | bytes 1572872 | tf_op jit(solution)/shard_map/ppermute | solution.py:29
  123.3 7.1 %collective-permute-done.10.below = bf16[4,512,128]{2,1,0:T(8,128)(2,1)S(1)} collective-permute-done((bf16[4,512,128]{2,1,0:T(8,128)(2,1)S(1)}, bf16[4,512,128]{2,1,0:T(8,128)(2,1)S(1)}, u32[]{:S(2)}, u32[]{:S(2)}) %collective-permute-start.10) | collective-permute-done | bytes 524320 | tf_op jit(solution)/shard_map/ppermute | solution.py:29
  130.4 9.0 %collective-permute-done.11.above = bf16[4,512,128]{2,1,0:T(8,128)(2,1)S(1)} collective-permute-done((bf16[4,512,128]{2,1,0:T(8,128)(2,1)S(1)}, bf16[4,512,128]{2,1,0:T(8,128)(2,1)S(1)}, u32[]{:S(2)}, u32[]{:S(2)}) %collective-permute-start.11) | collective-permute-done | bytes 524320 | tf_op jit(solution)/shard_map/ppermute | solution.py:29
  140.2 7.3 %second_level.1 = (f32[2048,128]{1,0:T(8,128)}, bf16[2048,128]{1,0:T(8,128)(2,1)}, bf16[2048,128]{1,0:T(8,128)(2,1)}, bf16[2048,128]{1,0:T(8,128)(2,1)}) custom-call(s32[2]{0:T(128)} %copy-done, bf16[4,2,2048,128]{3,2,1,0:T(8,128)(2,1)} %bitcast.22, bf16[4,512,128]{2,1,0:T(8,128)(2,1)} %copy-done.3, bf16[4,512,128]{2,1,0:T(8,128)(2,1)} %copy-done.4, ...), custom_call_target="tpu_custom_call" | custom-call | flops 2147483648 | bytes 9437184 | tf_op jit(solution)/shard_map/second_level/pallas_call | solution.py:159
  147.5 1.9 %collective-permute-start.12 = (bf16[2048,128]{1,0:T(8,128)(2,1)}, bf16[2048,128]{1,0:T(8,128)(2,1)S(1)}, u32[]{:S(2)}, u32[]{:S(2)}) collective-permute-start(bf16[2048,128]{1,0:T(8,128)(2,1)} %get-tuple-element.20), channel_id=1, source_target_pairs={{0,4},{1,5},{2,6},{3,7},{4,8},{5,9},{6,10},{7,11},{8,12},{9,13},{1... | collective-permute-start | bytes 1572872 | tf_op jit(solution)/shard_map/ppermute | solution.py:29
  149.4 3.3 %collective-permute-start.13 = (bf16[2048,128]{1,0:T(8,128)(2,1)}, bf16[2048,128]{1,0:T(8,128)(2,1)S(1)}, u32[]{:S(2)}, u32[]{:S(2)}) collective-permute-start(bf16[2048,128]{1,0:T(8,128)(2,1)} %get-tuple-element.21), channel_id=1, source_target_pairs={{0,8},{1,9},{2,10},{3,11},{4,12},{5,13},{6,14},{7,15},{8,0},{9,1},... | collective-permute-start | bytes 1572872 | tf_op jit(solution)/shard_map/ppermute | solution.py:29
  152.7 3.8 %collective-permute-start.14 = (bf16[2048,128]{1,0:T(8,128)(2,1)}, bf16[2048,128]{1,0:T(8,128)(2,1)S(1)}, u32[]{:S(2)}, u32[]{:S(2)}) collective-permute-start(bf16[2048,128]{1,0:T(8,128)(2,1)} %get-tuple-element.22), channel_id=1, source_target_pairs={{0,12},{1,13},{2,14},{3,15},{4,0},{5,1},{6,2},{7,3},{8,4},{9,5},{1... | collective-permute-start | bytes 1572872 | tf_op jit(solution)/shard_map/ppermute | solution.py:29
  156.5 18.3 %collective-permute-done.12 = bf16[2048,128]{1,0:T(8,128)(2,1)S(1)} collective-permute-done((bf16[2048,128]{1,0:T(8,128)(2,1)}, bf16[2048,128]{1,0:T(8,128)(2,1)S(1)}, u32[]{:S(2)}, u32[]{:S(2)}) %collective-permute-start.12) | collective-permute-done | bytes 524320 | tf_op jit(solution)/shard_map/ppermute | solution.py:29
  174.8 2.5 %collective-permute-done.14 = bf16[2048,128]{1,0:T(8,128)(2,1)S(1)} collective-permute-done((bf16[2048,128]{1,0:T(8,128)(2,1)}, bf16[2048,128]{1,0:T(8,128)(2,1)S(1)}, u32[]{:S(2)}, u32[]{:S(2)}) %collective-permute-start.14) | collective-permute-done | bytes 524320 | tf_op jit(solution)/shard_map/ppermute | solution.py:29
  177.3 2.4 %add_bitcast_fusion = f32[1,2048,128]{2,1,0:T(8,128)} fusion(bf16[2048,128]{1,0:T(8,128)(2,1)S(1)} %collective-permute-done.14, bf16[2048,128]{1,0:T(8,128)(2,1)S(1)} %collective-permute-done.13, f32[2048,128]{1,0:T(8,128)} %get-tuple-element.19, bf16[2048,128]{1,0:T(8,128)(2,1)S(1)} %collective-permute-done.12), kind=kLoop, calls=%fused_computation.3 | loop fusion | flops 1572864 | bytes 3670016 | tf_op jit(solution)/shard_map/broadcast_in_dim | solution.py:225
  (27 shorter events, 11.4 us)
Async XLA Ops:
  6.5 9.2 %copy-start.2 = (f32[1,2048,128]{2,1,0:T(8,128)S(1)}, f32[1,2048,128]{2,1,0:T(8,128)}, u32[]{:S(2)}) copy-start(f32[1,2048,128]{2,1,0:T(8,128)} %param.5) | copy-start | bytes 3145732
  6.5 132.9 %all-gather.3.cloned.1.call-start = ((), (), s32[]{:S(2)}) async-start(), calls=%async_computation.2 | async-start | bytes 5242880 | tf_op jit(solution)/shard_map/all_gather | solution.py:195
  11.2 19.6 %all-to-all-start = ((bf16[4,2,512,128]{3,2,1,0:T(8,128)(2,1)}), bf16[4,2,512,128]{3,2,1,0:T(8,128)(2,1)S(1)}, u32[]{:S(2)}, u32[]{:S(2)}) async-start(bf16[4,2,512,128]{3,2,1,0:T(8,128)(2,1)} %pad_maximum_fusion.1), calls=%async_computation | async-start | bytes 2097152 | tf_op jit(solution)/shard_map/all_to_all | solution.py:192
  15.8 10.5 %collective-permute-start.4 = (bf16[2048,128]{1,0:T(8,128)(2,1)S(1)}, bf16[2048,128]{1,0:T(8,128)(2,1)S(1)}, u32[]{:S(2)}, u32[]{:S(2)}) collective-permute-start(bf16[2048,128]{1,0:T(8,128)(2,1)S(1)} %convert_element_type.12), channel_id=1, source_target_pairs={{0,16},{1,17},{2,18},{3,19},{4,20},{5,21},{6,22},{7,23},{8,24},{9,... | collective-permute-start | bytes 1572872 | tf_op jit(solution)/shard_map/ppermute | solution.py:29
  17.7 10.3 %collective-permute-start.5 = (bf16[2048,128]{1,0:T(8,128)(2,1)S(1)}, bf16[2048,128]{1,0:T(8,128)(2,1)S(1)}, u32[]{:S(2)}, u32[]{:S(2)}) collective-permute-start(bf16[2048,128]{1,0:T(8,128)(2,1)S(1)} %convert_element_type.12), channel_id=1, source_target_pairs={{16,0},{17,1},{18,2},{19,3},{20,4},{21,5},{22,6},{23,7},{24,8},{25... | collective-permute-start | bytes 1572872 | tf_op jit(solution)/shard_map/ppermute | solution.py:29
  30.8 29.2 %collective-permute-start.6 = (bf16[2,2048,128]{2,1,0:T(8,128)(2,1)S(1)}, bf16[2,2048,128]{2,1,0:T(8,128)(2,1)}, u32[]{:S(2)}, u32[]{:S(2)}) collective-permute-start(bf16[2,2048,128]{2,1,0:T(8,128)(2,1)S(1)} %pad_maximum_fusion.2.near_ref), channel_id=1, source_target_pairs={{0,4},{1,5},{2,6},{3,7},{4,8},{5,9},{6,10},{7,11},{8,12},{9,13},{1... | collective-permute-start | bytes 3145736 | tf_op jit(solution)/shard_map/ppermute | solution.py:29
  33.3 30.6 %collective-permute-start.7 = (bf16[2,2048,128]{2,1,0:T(8,128)(2,1)S(1)}, bf16[2,2048,128]{2,1,0:T(8,128)(2,1)}, u32[]{:S(2)}, u32[]{:S(2)}) collective-permute-start(bf16[2,2048,128]{2,1,0:T(8,128)(2,1)S(1)} %pad_maximum_fusion.2.near_ref), channel_id=1, source_target_pairs={{0,12},{1,13},{2,14},{3,15},{4,0},{5,1},{6,2},{7,3},{8,4},{9,5},{1... | collective-permute-start | bytes 3145736 | tf_op jit(solution)/shard_map/ppermute | solution.py:29
  37.9 49.9 %collective-permute-start = (bf16[4,2,512,128]{3,2,1,0:T(8,128)(2,1)S(1)}, bf16[4,2,512,128]{3,2,1,0:T(8,128)(2,1)}, u32[]{:S(2)}, u32[]{:S(2)}) collective-permute-start(bf16[4,2,512,128]{3,2,1,0:T(8,128)(2,1)S(1)} %all-to-all-done.own_ref), channel_id=1, source_target_pairs={{0,1},{1,2},{2,3},{3,0},{4,5},{5,6},{6,7},{7,4},{8,9},{9,10},{10,1... | collective-permute-start | bytes 3145736 | tf_op jit(solution)/shard_map/ppermute | solution.py:29
  40.2 53.0 %collective-permute-start.1 = (bf16[4,2,512,128]{3,2,1,0:T(8,128)(2,1)S(1)}, bf16[4,2,512,128]{3,2,1,0:T(8,128)(2,1)}, u32[]{:S(2)}, u32[]{:S(2)}) collective-permute-start(bf16[4,2,512,128]{3,2,1,0:T(8,128)(2,1)S(1)} %all-to-all-done.own_ref), channel_id=1, source_target_pairs={{0,3},{1,0},{2,1},{3,2},{4,7},{5,4},{6,5},{7,6},{8,11},{9,8},{10,9... | collective-permute-start | bytes 3145736 | tf_op jit(solution)/shard_map/ppermute | solution.py:29
  43.7 53.7 %all-to-all-start.1 = ((f32[4,512,128]{2,1,0:T(8,128)}), f32[4,512,128]{2,1,0:T(8,128)S(1)}, u32[]{:S(2)}, u32[]{:S(2)}) async-start(f32[4,512,128]{2,1,0:T(8,128)} %bitcast.15), calls=%async_computation.1 | async-start | bytes 2097152 | tf_op jit(solution)/shard_map/all_to_all | solution.py:192
  61.9 35.5 %collective-permute-start.8 = (bf16[2048,128]{1,0:T(8,128)(2,1)}, bf16[2048,128]{1,0:T(8,128)(2,1)}, u32[]{:S(2)}, u32[]{:S(2)}) collective-permute-start(bf16[2048,128]{1,0:T(8,128)(2,1)} %slice_bitcast_fusion.1), channel_id=1, source_target_pairs={{0,4},{1,5},{2,6},{3,7},{4,8},{5,9},{6,10},{7,11},{8,12},{9,13},{1... | collective-permute-start | bytes 1572872 | tf_op jit(solution)/shard_map/ppermute | solution.py:29
  65.7 31.7 %collective-permute-start.9 = (bf16[2048,128]{1,0:T(8,128)(2,1)}, bf16[2048,128]{1,0:T(8,128)(2,1)}, u32[]{:S(2)}, u32[]{:S(2)}) collective-permute-start(bf16[2048,128]{1,0:T(8,128)(2,1)} %slice_bitcast_fusion), channel_id=1, source_target_pairs={{0,12},{1,13},{2,14},{3,15},{4,0},{5,1},{6,2},{7,3},{8,4},{9,5},{1... | collective-permute-start | bytes 1572872 | tf_op jit(solution)/shard_map/ppermute | solution.py:29
  89.6 14.5 %collective-permute-start.2 = (bf16[2,2,512,128]{3,2,1,0:T(8,128)(2,1)}, bf16[2,2,512,128]{3,2,1,0:T(8,128)(2,1)}, u32[]{:S(2)}, u32[]{:S(2)}) collective-permute-start(bf16[2,2,512,128]{3,2,1,0:T(8,128)(2,1)} %slice.16), channel_id=1, source_target_pairs={{0,1},{1,2},{2,3},{3,0},{4,5},{5,6},{6,7},{7,4},{8,9},{9,10},{10,1... | collective-permute-start | bytes 1572872 | tf_op jit(solution)/shard_map/ppermute | solution.py:29
  95.1 15.4 %collective-permute-start.3 = (bf16[2,2,512,128]{3,2,1,0:T(8,128)(2,1)}, bf16[2,2,512,128]{3,2,1,0:T(8,128)(2,1)}, u32[]{:S(2)}, u32[]{:S(2)}) collective-permute-start(bf16[2,2,512,128]{3,2,1,0:T(8,128)(2,1)} %slice.17), channel_id=1, source_target_pairs={{0,3},{1,0},{2,1},{3,2},{4,7},{5,4},{6,5},{7,6},{8,11},{9,8},{10,9... | collective-permute-start | bytes 1572872 | tf_op jit(solution)/shard_map/ppermute | solution.py:29
  97.4 19.0 %copy-start = (s32[2]{0:T(128)}, s32[2]{0:T(128)S(1)}, u32[]{:S(2)}) copy-start(s32[2]{0:T(128)S(1)} %pad_add_fusion.at_ref) | copy-start | bytes 28
  116.5 1.0 copy-start.1
  117.5 12.9 %collective-permute-start.10 = (bf16[4,512,128]{2,1,0:T(8,128)(2,1)S(1)}, bf16[4,512,128]{2,1,0:T(8,128)(2,1)S(1)}, u32[]{:S(2)}, u32[]{:S(2)}) collective-permute-start(bf16[4,512,128]{2,1,0:T(8,128)(2,1)S(1)} %get-tuple-element.17), channel_id=1, source_target_pairs={{0,32},{1,33},{2,34},{3,35},{4,36},{5,37},{6,38},{7,39},{8,40},{9,... | collective-permute-start | bytes 1572872 | tf_op jit(solution)/shard_map/ppermute | solution.py:29
  121.3 18.1 %collective-permute-start.11 = (bf16[4,512,128]{2,1,0:T(8,128)(2,1)S(1)}, bf16[4,512,128]{2,1,0:T(8,128)(2,1)S(1)}, u32[]{:S(2)}, u32[]{:S(2)}) collective-permute-start(bf16[4,512,128]{2,1,0:T(8,128)(2,1)S(1)} %get-tuple-element.17), channel_id=1, source_target_pairs={{32,0},{33,1},{34,2},{35,3},{36,4},{37,5},{38,6},{39,7},{40,8},{41... | collective-permute-start | bytes 1572872 | tf_op jit(solution)/shard_map/ppermute | solution.py:29
  130.4 9.0 %copy-start.3 = (bf16[4,512,128]{2,1,0:T(8,128)(2,1)}, bf16[4,512,128]{2,1,0:T(8,128)(2,1)S(1)}, u32[]{:S(2)}) copy-start(bf16[4,512,128]{2,1,0:T(8,128)(2,1)S(1)} %collective-permute-done.10.below) | copy-start | bytes 1572868
  139.4 0.8 copy-start.4
  147.5 27.3 %collective-permute-start.12 = (bf16[2048,128]{1,0:T(8,128)(2,1)}, bf16[2048,128]{1,0:T(8,128)(2,1)S(1)}, u32[]{:S(2)}, u32[]{:S(2)}) collective-permute-start(bf16[2048,128]{1,0:T(8,128)(2,1)} %get-tuple-element.20), channel_id=1, source_target_pairs={{0,4},{1,5},{2,6},{3,7},{4,8},{5,9},{6,10},{7,11},{8,12},{9,13},{1... | collective-permute-start | bytes 1572872 | tf_op jit(solution)/shard_map/ppermute | solution.py:29
  149.4 25.3 %collective-permute-start.13 = (bf16[2048,128]{1,0:T(8,128)(2,1)}, bf16[2048,128]{1,0:T(8,128)(2,1)S(1)}, u32[]{:S(2)}, u32[]{:S(2)}) collective-permute-start(bf16[2048,128]{1,0:T(8,128)(2,1)} %get-tuple-element.21), channel_id=1, source_target_pairs={{0,8},{1,9},{2,10},{3,11},{4,12},{5,13},{6,14},{7,15},{8,0},{9,1},... | collective-permute-start | bytes 1572872 | tf_op jit(solution)/shard_map/ppermute | solution.py:29
  152.7 24.6 %collective-permute-start.14 = (bf16[2048,128]{1,0:T(8,128)(2,1)}, bf16[2048,128]{1,0:T(8,128)(2,1)S(1)}, u32[]{:S(2)}, u32[]{:S(2)}) collective-permute-start(bf16[2048,128]{1,0:T(8,128)(2,1)} %get-tuple-element.22), channel_id=1, source_target_pairs={{0,12},{1,13},{2,14},{3,15},{4,0},{5,1},{6,2},{7,3},{8,4},{9,5},{1... | collective-permute-start | bytes 1572872 | tf_op jit(solution)/shard_map/ppermute | solution.py:29
Sparse Core Ops, SparseCore 0:
  9.5 80.5 all-gather.2

commit v4 on v3

v4 whole, which is shorter than its diff:
```python
import functools

import jax
import jax.numpy as jnp
from jax import lax
from jax.experimental import pallas as pl
from jax.experimental.pallas import tpu as pltpu
from jax.sharding import Mesh, PartitionSpec as P

Z, CORES, Y, X = 16, 2, 4, 4
PLANES = Z * CORES
M = 2048
BLK = M // Y
COL = 128
AXES = ("z", "core", "y", "x")


def device_index(plane, y, x):
    return (plane * Y + y) * X + x


def moved(value, planes=0, ys=0, xs=0):
    pairs = []
    for plane in range(PLANES):
        if not 0 <= plane + planes < PLANES:
            continue
        for y in range(Y):
            for x in range(X):
                target = device_index(plane + planes, (y + ys) % Y, (x + xs) % X)
                pairs.append((device_index(plane, y, x), target))
    return lax.ppermute(value, AXES, pairs)


def after(value, *before):
    return lax.optimization_barrier((value,) + before)[0]


def rows_in_order(at_ref, ref, row):
    return [
        ref[row + (pl.ds(pl.multiple_of(lax.rem(at_ref[1] + e, X) * COL, COL), COL),)]
        for e in range(X)
    ]


FIRST_GROUPS, LAST_GROUPS = (2, 1), (3, 0)


def first_kernel(
    groups,
    at_ref,
    own_ref,
    left_ref,
    right_ref,
    far_ref,
    near_ref,
    down_ref,
    up_ref,
    below_far_ref,
    above_far_ref,
    rhs_ref,
    corr_ref,
    sent_ref,
    acc_ref,
):
    step = pl.program_id(0)

    @pl.when(step == 0)
    def _():
        acc_ref[...] = jnp.zeros_like(acc_ref)

    total = acc_ref[...]
    for side, b_far_ref in ((0, below_far_ref), (1, above_far_ref)):
        blocks = (own_ref, right_ref, far_ref, left_ref)
        left = jnp.concatenate([block[0, side] for block in blocks], axis=1)
        parts = (
            (near_ref, (side,)),
            (up_ref, (side,)),
            (b_far_ref, ()),
            (down_ref, (side,)),
        )
        right = [
            jnp.concatenate(rows_in_order(at_ref, *parts[d]), axis=0) for d in groups
        ]
        right = jnp.concatenate(right, axis=1)
        total = total + jnp.dot(left, right, preferred_element_type=jnp.float32)
    acc_ref[...] = total

    @pl.when(step == Y - 1)
    def _():
        for i, d in enumerate(groups):
            piece = acc_ref[:, i * COL : (i + 1) * COL]
            corr_ref[i] = piece
            owner = lax.rem(at_ref[0] + d, Y)
            sent_ref[i] = (rhs_ref[owner] + piece).astype(jnp.bfloat16)


def first_level(groups, at, blocks, parts, rhs):
    count = len(groups)
    block = pl.BlockSpec((1, 2, BLK, COL), lambda k, at: (k, 0, 0, 0))
    both = pl.BlockSpec((2, BLK, COL), lambda k, at: (0, k, 0))
    part = pl.BlockSpec((BLK, COL), lambda k, at: (k, 0))
    whole = pl.BlockSpec((Y, BLK, COL), lambda k, at: (0, 0, 0))
    out = pl.BlockSpec((count, BLK, COL), lambda k, at: (0, 0, 0))
    return pl.pallas_call(
        functools.partial(first_kernel, groups),
        name="first_level",
        out_shape=(
            jax.ShapeDtypeStruct((count, BLK, COL), jnp.float32),
            jax.ShapeDtypeStruct((count, BLK, COL), jnp.bfloat16),
        ),
        grid_spec=pltpu.PrefetchScalarGridSpec(
            num_scalar_prefetch=1,
            grid=(Y,),
            in_specs=[block] * 4 + [both] * 3 + [part] * 2 + [whole],
            out_specs=(out, out),
            scratch_shapes=[pltpu.VMEM((BLK, count * COL), jnp.float32)],
        ),
        compiler_params=pltpu.CompilerParams(vmem_limit_bytes=32 << 20),
        cost_estimate=pl.CostEstimate(
            flops=4 * BLK * M * count * COL,
            bytes_accessed=9 << 20,
            transcendentals=0,
        ),
    )(at, *blocks, *parts, rhs)


def second_kernel(
    groups,
    at_ref,
    lo_ref,
    up_ref,
    left_ref,
    right_ref,
    lo_far_ref,
    up_far_ref,
    below,
    above,
    corr_ref,
    rhs_ref,
    *outs,
):
    step = pl.program_id(0)
    lower = [lo_ref[...], right_ref[0], lo_far_ref[...], left_ref[0]]
    upper = [up_ref[...], right_ref[1], up_far_ref[...], left_ref[1]]
    total = None
    for blocks, b_ref in ((lower, below), (upper, above)):
        left = jnp.concatenate(blocks, axis=1)
        right = [
            jnp.concatenate(rows_in_order(at_ref, b_ref, (i,)), axis=0)
            for i in range(len(groups))
        ]
        right = jnp.concatenate(right, axis=1)
        term = jnp.dot(left, right, preferred_element_type=jnp.float32)
        total = term if total is None else total + term
    here = step == at_ref[0]
    for i, d in enumerate(groups):
        piece = total[:, i * COL : (i + 1) * COL]
        piece = piece + jnp.where(here, corr_ref[i], 0.0)
        if d == 0:
            piece = piece + rhs_ref[...]
        outs[i][...] = piece.astype(outs[i].dtype)


def second_level(groups, at, blocks, below, above, corr, rhs):
    count = len(groups)
    rows = pl.BlockSpec((BLK, COL), lambda m, at: (m, 0))
    pair = pl.BlockSpec((2, BLK, COL), lambda m, at: (0, m, 0))
    whole = pl.BlockSpec((count, BLK, COL), lambda m, at: (0, 0, 0))
    return pl.pallas_call(
        functools.partial(second_kernel, groups),
        name="second_level",
        out_shape=tuple(
            jax.ShapeDtypeStruct((M, COL), jnp.bfloat16 if d else jnp.float32)
            for d in groups
        ),
        grid_spec=pltpu.PrefetchScalarGridSpec(
            num_scalar_prefetch=1,
            grid=(Y,),
            in_specs=[rows, rows, pair, pair, rows, rows, whole, whole, whole, rows],
            out_specs=(rows,) * count,
        ),
        compiler_params=pltpu.CompilerParams(vmem_limit_bytes=32 << 20),
        cost_estimate=pl.CostEstimate(
            flops=4 * BLK * M * count * COL,
            bytes_accessed=6 << 20,
            transcendentals=0,
        ),
    )(at, *blocks, below, above, corr, rhs)


def on_device(right_sides, lower_first, upper_first, lower_second, upper_second):
    rhs = right_sides[0]
    at = jnp.stack([lax.axis_index("y"), lax.axis_index("x")]).astype(jnp.int32)

    def exchanged(value):
        return lax.all_to_all(value, "y", 0, 0, tiled=True)

    firsts = [v[0].reshape(Y, BLK, COL) for v in (lower_first, upper_first)]
    firsts = jnp.stack(firsts, axis=1)
    sent_one = after(rhs, firsts).astype(jnp.bfloat16)
    own = exchanged(firsts)
    near = jnp.stack([moved(sent_one, 1), moved(sent_one, -1)])

    lo_two, up_two = lower_second[0], upper_second[0]
    seconds = after(jnp.stack([lo_two, up_two]), sent_one)
    two_left, two_right = moved(seconds, xs=1), moved(seconds, xs=-1)

    left, right, far = moved(own, xs=1), moved(own, xs=-1), moved(own, xs=2)
    down, up = moved(near, ys=1), moved(near, ys=-1)
    below_far, above_far = moved(down[0], ys=1), moved(up[1], ys=-1)
    rhs_rows = exchanged(after(rhs, own, two_left, two_right).reshape(Y, BLK, COL))

    lo_far = moved(after(two_left[0], left), xs=1)
    up_far = moved(after(two_right[1], right), xs=-1)

    blocks = (own, left, right, far)
    parts = (near, down, up, below_far, above_far)
    corr_a, sent_a = first_level(FIRST_GROUPS, at, blocks, parts, rhs_rows)
    late = after(at, sent_a)
    corr_b, sent_b = first_level(LAST_GROUPS, late, blocks, parts, rhs_rows)
    below_a, above_a = moved(sent_a, 2), moved(sent_a, -2)
    below_b, above_b = moved(sent_b, 2), moved(sent_b, -2)
    blocks = (lo_two, up_two, two_left, two_right, lo_far, up_far)
    two, one = second_level(FIRST_GROUPS, at, blocks, below_a, above_a, corr_a, rhs)
    late = after(late, two)
    three, total = second_level(
        LAST_GROUPS, late, blocks, below_b, above_b, corr_b, rhs
    )
    for d, part in ((2, two), (1, one), (3, three)):
        total = total + moved(part, ys=d).astype(jnp.float32)
    return total[None]


def solution(mesh):
    fine = Mesh(mesh.devices.reshape(Z, CORES, Y, X), AXES)
    spec = P(("z", "core"), None, ("y", "x"))
    return jax.shard_map(
        on_device,
        mesh=fine,
        in_specs=(spec,) * 5,
        out_specs=spec,
        check_vma=False,
    )
```

time: 188 us -> 153 us (0.81)
  the two profiles are of different devices: /device:TPU:38 before, /device:TPU:32 now
where the time goes in v4:
time: 153 us; the launch traced here: 151 us
  starting transfers between devices  75.7 us (49%)
  waiting for transfers between devices  42.4 us (28%)
  Pallas kernels  18.4 us (12%)
  other arithmetic  7.3 us (5%)
  local copies, waits for them, and re-layouts  7.26 us (5%)
    ppermute x20, starting transfers between devices, moved(): return lax.ppermute(value, AXES, pairs)  67.6 us
    ppermute x20, waiting for transfers between devices, moved(): return lax.ppermute(value, AXES, pairs)  35 us
    pallas_call x2, Pallas kernels, first_level(): pl.pallas_call(functools.partial(first_kernel, groups), name='first_level...  9.74 us
    pallas_call x2, Pallas kernels, second_level(): pl.pallas_call(functools.partial(second_kernel, groups), name='second_lev...  8.65 us
    all_to_all x2, starting transfers between devices, exchanged(): return lax.all_to_all(value, 'y', 0, 0, tiled=True)  8.01 us
    all_to_all x2, waiting for transfers between devices, exchanged(): return lax.all_to_all(value, 'y', 0, 0, tiled=True)  7.41 us
    squeeze x2, local copies, waits for them, and re-layouts, on_device(): below_far, above_far = (moved(down[0], ys=1), moved(up[1], ys=-1))  3.76 us
  transfers between devices with their start and end apart: 22, of which 6 were waited for; matrix products, arithmetic and copies ran while one was open for 6% of the time, Pallas kernels for 12%

profile of v4, /device:TPU:32, one launch (start us, length us, event | category | flops | bytes accessed | tf_op | source)
XLA Modules:
  0.0 151.4 jit_solution(4815197377432610255)
XLA Ops:
  0.0 2.3 %pad_maximum_fusion = bf16[4,2,512,128]{3,2,1,0:T(8,128)(2,1)} fusion(bf16[4,1,512,128]{3,2,1,0:T(8,128)(2,1)} %bitcast.24, bf16[4,1,512,128]{3,2,1,0:T(8,128)(2,1)} %bitcast.25), kind=kLoop, calls=%fused_computation | loop fusion | flops 524288 | bytes 2097152 | tf_op jit(solution)/shard_map/stack | solution.py:199
  3.6 1.9 %collective-permute-start.3 = (bf16[2048,128]{1,0:T(8,128)(2,1)S(1)}, bf16[2048,128]{1,0:T(8,128)(2,1)S(1)}, u32[]{:S(2)}, u32[]{:S(2)}) collective-permute-start(bf16[2048,128]{1,0:T(8,128)(2,1)S(1)} %convert_element_type.12), channel_id=1, source_target_pairs={{0,16},{1,17},{2,18},{3,19},{4,20},{5,21},{6,22},{7,23},{8,24},{9,... | collective-permute-start | bytes 1572872 | tf_op jit(solution)/shard_map/ppermute | solution.py:31
  5.6 3.6 %collective-permute-start.4 = (bf16[2048,128]{1,0:T(8,128)(2,1)S(1)}, bf16[2048,128]{1,0:T(8,128)(2,1)}, u32[]{:S(2)}, u32[]{:S(2)}) collective-permute-start(bf16[2048,128]{1,0:T(8,128)(2,1)S(1)} %convert_element_type.12), channel_id=1, source_target_pairs={{16,0},{17,1},{18,2},{19,3},{20,4},{21,5},{22,6},{23,7},{24,8},{25... | collective-permute-start | bytes 1572872 | tf_op jit(solution)/shard_map/ppermute | solution.py:31
  10.3 4.7 %collective-permute-start.10 = (bf16[2,2048,128]{2,1,0:T(8,128)(2,1)}, bf16[2,2048,128]{2,1,0:T(8,128)(2,1)S(1)}, u32[]{:S(2)}, u32[]{:S(2)}) collective-permute-start(bf16[2,2048,128]{2,1,0:T(8,128)(2,1)} %pad_maximum_fusion.2), channel_id=1, source_target_pairs={{0,3},{1,0},{2,1},{3,2},{4,7},{5,4},{6,5},{7,6},{8,11},{9,8},{10,9... | collective-permute-start | bytes 3145736 | tf_op jit(solution)/shard_map/ppermute | solution.py:31
  15.0 1.9 %collective-permute-start.9 = (bf16[2,2048,128]{2,1,0:T(8,128)(2,1)}, bf16[2,2048,128]{2,1,0:T(8,128)(2,1)}, u32[]{:S(2)}, u32[]{:S(2)}) collective-permute-start(bf16[2,2048,128]{2,1,0:T(8,128)(2,1)} %pad_maximum_fusion.2), channel_id=1, source_target_pairs={{0,1},{1,2},{2,3},{3,0},{4,5},{5,6},{6,7},{7,4},{8,9},{9,10},{10,1... | collective-permute-start | bytes 3145736 | tf_op jit(solution)/shard_map/ppermute | solution.py:31
  16.9 4.5 %all-to-all-start = ((bf16[4,2,512,128]{3,2,1,0:T(8,128)(2,1)}), bf16[4,2,512,128]{3,2,1,0:T(8,128)(2,1)S(1)}, u32[]{:S(2)}, u32[]{:S(2)}) async-start(bf16[4,2,512,128]{3,2,1,0:T(8,128)(2,1)} %pad_maximum_fusion), calls=%async_computation | async-start | bytes 2097152 | tf_op jit(solution)/shard_map/all_to_all | solution.py:196
  23.5 3.9 %collective-permute-start.5 = (bf16[2,2048,128]{2,1,0:T(8,128)(2,1)S(1)}, bf16[2,2048,128]{2,1,0:T(8,128)(2,1)}, u32[]{:S(2)}, u32[]{:S(2)}) collective-permute-start(bf16[2,2048,128]{2,1,0:T(8,128)(2,1)S(1)} %pad_maximum_fusion.1.near_ref), channel_id=1, source_target_pairs={{0,4},{1,5},{2,6},{3,7},{4,8},{5,9},{6,10},{7,11},{8,12},{9,13},{1... | collective-permute-start | bytes 3145736 | tf_op jit(solution)/shard_map/ppermute | solution.py:31
  27.4 3.1 %collective-permute-start.6 = (bf16[2,2048,128]{2,1,0:T(8,128)(2,1)S(1)}, bf16[2,2048,128]{2,1,0:T(8,128)(2,1)}, u32[]{:S(2)}, u32[]{:S(2)}) collective-permute-start(bf16[2,2048,128]{2,1,0:T(8,128)(2,1)S(1)} %pad_maximum_fusion.1.near_ref), channel_id=1, source_target_pairs={{0,12},{1,13},{2,14},{3,15},{4,0},{5,1},{6,2},{7,3},{8,4},{9,5},{1... | collective-permute-start | bytes 3145736 | tf_op jit(solution)/shard_map/ppermute | solution.py:31
  30.5 7.4 %all-to-all-done.own_ref = bf16[4,2,512,128]{3,2,1,0:T(8,128)(2,1)S(1)} async-done(((bf16[4,2,512,128]{3,2,1,0:T(8,128)(2,1)}), bf16[4,2,512,128]{3,2,1,0:T(8,128)(2,1)S(1)}, u32[]{:S(2)}, u32[]{:S(2)}) %all-to-all-start) | async-done | bytes 1048608 | tf_op jit(solution)/shard_map/all_to_all | solution.py:196
  37.9 2.7 %collective-permute-start = (bf16[4,2,512,128]{3,2,1,0:T(8,128)(2,1)S(1)}, bf16[4,2,512,128]{3,2,1,0:T(8,128)(2,1)}, u32[]{:S(2)}, u32[]{:S(2)}) collective-permute-start(bf16[4,2,512,128]{3,2,1,0:T(8,128)(2,1)S(1)} %all-to-all-done.own_ref), channel_id=1, source_target_pairs={{0,1},{1,2},{2,3},{3,0},{4,5},{5,6},{6,7},{7,4},{8,9},{9,10},{10,1... | collective-permute-start | bytes 3145736 | tf_op jit(solution)/shard_map/ppermute | solution.py:31
  40.7 4.4 %collective-permute-start.1 = (bf16[4,2,512,128]{3,2,1,0:T(8,128)(2,1)S(1)}, bf16[4,2,512,128]{3,2,1,0:T(8,128)(2,1)}, u32[]{:S(2)}, u32[]{:S(2)}) collective-permute-start(bf16[4,2,512,128]{3,2,1,0:T(8,128)(2,1)S(1)} %all-to-all-done.own_ref), channel_id=1, source_target_pairs={{0,3},{1,0},{2,1},{3,2},{4,7},{5,4},{6,5},{7,6},{8,11},{9,8},{10,9... | collective-permute-start | bytes 3145736 | tf_op jit(solution)/shard_map/ppermute | solution.py:31
  45.1 3.4 %collective-permute-start.2 = (bf16[4,2,512,128]{3,2,1,0:T(8,128)(2,1)S(1)}, bf16[4,2,512,128]{3,2,1,0:T(8,128)(2,1)}, u32[]{:S(2)}, u32[]{:S(2)}) collective-permute-start(bf16[4,2,512,128]{3,2,1,0:T(8,128)(2,1)S(1)} %all-to-all-done.own_ref), channel_id=1, source_target_pairs={{0,2},{1,3},{2,0},{3,1},{4,6},{5,7},{6,4},{7,5},{8,10},{9,11},{10,... | collective-permute-start | bytes 3145736 | tf_op jit(solution)/shard_map/ppermute | solution.py:31
  48.5 3.5 %all-to-all-start.1 = ((f32[4,512,128]{2,1,0:T(8,128)}), f32[4,512,128]{2,1,0:T(8,128)S(1)}, u32[]{:S(2)}, u32[]{:S(2)}) async-start(f32[4,512,128]{2,1,0:T(8,128)} %bitcast.9), calls=%async_computation.1 | async-start | bytes 2097152 | tf_op jit(solution)/shard_map/all_to_all | solution.py:196
  53.9 6.3 %collective-permute-done.5.down_ref = bf16[2,2048,128]{2,1,0:T(8,128)(2,1)} collective-permute-done((bf16[2,2048,128]{2,1,0:T(8,128)(2,1)S(1)}, bf16[2,2048,128]{2,1,0:T(8,128)(2,1)}, u32[]{:S(2)}, u32[]{:S(2)}) %collective-permute-start.5) | collective-permute-done | bytes 1048608 | tf_op jit(solution)/shard_map/ppermute | solution.py:31
  60.2 1.9 %slice_bitcast_fusion.3 = bf16[2048,128]{1,0:T(8,128)(2,1)} fusion(bf16[2,2048,128]{2,1,0:T(8,128)(2,1)} %collective-permute-done.5.down_ref), kind=kLoop, calls=%fused_computation.7 | loop fusion | bytes 1048576 | tf_op jit(solution)/shard_map/squeeze | solution.py:210
  62.1 1.9 %collective-permute-start.7 = (bf16[2048,128]{1,0:T(8,128)(2,1)}, bf16[2048,128]{1,0:T(8,128)(2,1)}, u32[]{:S(2)}, u32[]{:S(2)}) collective-permute-start(bf16[2048,128]{1,0:T(8,128)(2,1)} %slice_bitcast_fusion.3), channel_id=1, source_target_pairs={{0,4},{1,5},{2,6},{3,7},{4,8},{5,9},{6,10},{7,11},{8,12},{9,13},{1... | collective-permute-start | bytes 1572872 | tf_op jit(solution)/shard_map/ppermute | solution.py:31
  65.9 5.1 %collective-permute-start.8 = (bf16[2048,128]{1,0:T(8,128)(2,1)}, bf16[2048,128]{1,0:T(8,128)(2,1)}, u32[]{:S(2)}, u32[]{:S(2)}) collective-permute-start(bf16[2048,128]{1,0:T(8,128)(2,1)} %slice_bitcast_fusion.2), channel_id=1, source_target_pairs={{0,12},{1,13},{2,14},{3,15},{4,0},{5,1},{6,2},{7,3},{8,4},{9,5},{1... | collective-permute-start | bytes 1572872 | tf_op jit(solution)/shard_map/ppermute | solution.py:31
  71.8 15.3 %collective-permute-done.left_ref = bf16[4,2,512,128]{3,2,1,0:T(8,128)(2,1)} collective-permute-done((bf16[4,2,512,128]{3,2,1,0:T(8,128)(2,1)S(1)}, bf16[4,2,512,128]{3,2,1,0:T(8,128)(2,1)}, u32[]{:S(2)}, u32[]{:S(2)}) %collective-permute-start) | collective-permute-done | bytes 1048608 | tf_op jit(solution)/shard_map/ppermute | solution.py:31
  87.1 1.9 %collective-permute-start.11 = (bf16[2048,128]{1,0:T(8,128)(2,1)}, bf16[2048,128]{1,0:T(8,128)(2,1)}, u32[]{:S(2)}, u32[]{:S(2)}) collective-permute-start(bf16[2048,128]{1,0:T(8,128)(2,1)} %slice_bitcast_fusion.1), channel_id=1, source_target_pairs={{0,1},{1,2},{2,3},{3,0},{4,5},{5,6},{6,7},{7,4},{8,9},{9,10},{10,1... | collective-permute-start | bytes 1572872 | tf_op jit(solution)/shard_map/ppermute | solution.py:31
  90.0 6.0 %collective-permute-start.12 = (bf16[2048,128]{1,0:T(8,128)(2,1)}, bf16[2048,128]{1,0:T(8,128)(2,1)}, u32[]{:S(2)}, u32[]{:S(2)}) collective-permute-start(bf16[2048,128]{1,0:T(8,128)(2,1)} %slice_bitcast_fusion), channel_id=1, source_target_pairs={{0,3},{1,0},{2,1},{3,2},{4,7},{5,4},{6,5},{7,6},{8,11},{9,8},{10,9... | collective-permute-start | bytes 1572872 | tf_op jit(solution)/shard_map/ppermute | solution.py:31
  96.1 4.9 %first_level.2 = (f32[2,512,128]{2,1,0:T(8,128)S(1)}, bf16[2,512,128]{2,1,0:T(8,128)(2,1)S(1)}) custom-call(s32[2]{0:T(128)S(1)} %pad_add_fusion.at_ref, bf16[4,2,512,128]{3,2,1,0:T(8,128)(2,1)S(1)} %all-to-all-done.own_ref, bf16[4,2,512,128]{3,2,1,0:T(8,128)(2,1)} %collective-permute-done.left_ref, ...), custom_call_target="tpu_custom_call" | custom-call | flops 1073741824 | bytes 9437184 | tf_op jit(solution)/shard_map/first_level/pallas_call | solution.py:104
  101.0 4.0 %collective-permute-start.13 = (bf16[2,512,128]{2,1,0:T(8,128)(2,1)S(1)}, bf16[2,512,128]{2,1,0:T(8,128)(2,1)S(1)}, u32[]{:S(2)}, u32[]{:S(2)}) collective-permute-start(bf16[2,512,128]{2,1,0:T(8,128)(2,1)S(1)} %get-tuple-element.23), channel_id=1, source_target_pairs={{0,32},{1,33},{2,34},{3,35},{4,36},{5,37},{6,38},{7,39},{8,40},{9,... | collective-permute-start | bytes 786440 | tf_op jit(solution)/shard_map/ppermute | solution.py:31
  105.0 2.0 %collective-permute-start.14 = (bf16[2,512,128]{2,1,0:T(8,128)(2,1)S(1)}, bf16[2,512,128]{2,1,0:T(8,128)(2,1)S(1)}, u32[]{:S(2)}, u32[]{:S(2)}) collective-permute-start(bf16[2,512,128]{2,1,0:T(8,128)(2,1)S(1)} %get-tuple-element.23), channel_id=1, source_target_pairs={{32,0},{33,1},{34,2},{35,3},{36,4},{37,5},{38,6},{39,7},{40,8},{41... | collective-permute-start | bytes 786440 | tf_op jit(solution)/shard_map/ppermute | solution.py:31
  107.0 4.9 %first_level.3 = (f32[2,512,128]{2,1,0:T(8,128)S(1)}, bf16[2,512,128]{2,1,0:T(8,128)(2,1)S(1)}) custom-call(s32[2]{0:T(128)S(1)} %pad_add_fusion.at_ref, bf16[4,2,512,128]{3,2,1,0:T(8,128)(2,1)S(1)} %all-to-all-done.own_ref, bf16[4,2,512,128]{3,2,1,0:T(8,128)(2,1)} %collective-permute-done.left_ref, ...), custom_call_target="tpu_custom_call" | custom-call | flops 1073741824 | bytes 9437184 | tf_op jit(solution)/shard_map/first_level/pallas_call | solution.py:104
  111.9 3.8 %collective-permute-start.15 = (bf16[2,512,128]{2,1,0:T(8,128)(2,1)S(1)}, bf16[2,512,128]{2,1,0:T(8,128)(2,1)S(1)}, u32[]{:S(2)}, u32[]{:S(2)}) collective-permute-start(bf16[2,512,128]{2,1,0:T(8,128)(2,1)S(1)} %get-tuple-element.30), channel_id=1, source_target_pairs={{0,32},{1,33},{2,34},{3,35},{4,36},{5,37},{6,38},{7,39},{8,40},{9,... | collective-permute-start | bytes 786440 | tf_op jit(solution)/shard_map/ppermute | solution.py:31
  115.8 2.0 %collective-permute-start.16 = (bf16[2,512,128]{2,1,0:T(8,128)(2,1)S(1)}, bf16[2,512,128]{2,1,0:T(8,128)(2,1)S(1)}, u32[]{:S(2)}, u32[]{:S(2)}) collective-permute-start(bf16[2,512,128]{2,1,0:T(8,128)(2,1)S(1)} %get-tuple-element.30), channel_id=1, source_target_pairs={{32,0},{33,1},{34,2},{35,3},{36,4},{37,5},{38,6},{39,7},{40,8},{41... | collective-permute-start | bytes 786440 | tf_op jit(solution)/shard_map/ppermute | solution.py:31
  117.9 4.3 %second_level.2 = (bf16[2048,128]{1,0:T(8,128)(2,1)S(1)}, bf16[2048,128]{1,0:T(8,128)(2,1)S(1)}) custom-call(s32[2]{0:T(128)S(1)} %pad_add_fusion.at_ref, bf16[2048,128]{1,0:T(8,128)(2,1)S(1)} %bitcast.20, bf16[2048,128]{1,0:T(8,128)(2,1)S(1)} %bitcast.22, bf16[2,2048,128]{2,1,0:T(8,128)(2,1)} %collective-permute-done.9.left_ref, ...), custom_call_target="tpu_custom_call" | custom-call | flops 1073741824 | bytes 6291456 | tf_op jit(solution)/shard_map/second_level/pallas_call | solution.py:169
  122.2 5.3 %collective-permute-start.17 = (bf16[2048,128]{1,0:T(8,128)(2,1)S(1)}, bf16[2048,128]{1,0:T(8,128)(2,1)S(1)}, u32[]{:S(2)}, u32[]{:S(2)}) collective-permute-start(bf16[2048,128]{1,0:T(8,128)(2,1)S(1)} %get-tuple-element.28), channel_id=1, source_target_pairs={{0,8},{1,9},{2,10},{3,11},{4,12},{5,13},{6,14},{7,15},{8,0},{9,1},... | collective-permute-start | bytes 1572872 | tf_op jit(solution)/shard_map/ppermute | solution.py:31
  127.6 4.3 %second_level.3 = (bf16[2048,128]{1,0:T(8,128)(2,1)S(1)}, f32[2048,128]{1,0:T(8,128)S(1)}) custom-call(s32[2]{0:T(128)S(1)} %pad_add_fusion.at_ref, bf16[2048,128]{1,0:T(8,128)(2,1)S(1)} %bitcast.21, bf16[2048,128]{1,0:T(8,128)(2,1)S(1)} %bitcast.23, bf16[2,2048,128]{2,1,0:T(8,128)(2,1)} %collective-permute-done.9.left_ref, ...), custom_call_target="tpu_custom_call" | custom-call | flops 1073741824 | bytes 6291456 | tf_op jit(solution)/shard_map/second_level/pallas_call | solution.py:169
  131.9 2.7 %collective-permute-start.19 = (bf16[2048,128]{1,0:T(8,128)(2,1)S(1)}, bf16[2048,128]{1,0:T(8,128)(2,1)S(1)}, u32[]{:S(2)}, u32[]{:S(2)}) collective-permute-start(bf16[2048,128]{1,0:T(8,128)(2,1)S(1)} %get-tuple-element.34), channel_id=1, source_target_pairs={{0,12},{1,13},{2,14},{3,15},{4,0},{5,1},{6,2},{7,3},{8,4},{9,5},{1... | collective-permute-start | bytes 1572872 | tf_op jit(solution)/shard_map/ppermute | solution.py:31
  134.6 3.2 %collective-permute-start.18 = (bf16[2048,128]{1,0:T(8,128)(2,1)S(1)}, bf16[2048,128]{1,0:T(8,128)(2,1)S(1)}, u32[]{:S(2)}, u32[]{:S(2)}) collective-permute-start(bf16[2048,128]{1,0:T(8,128)(2,1)S(1)} %get-tuple-element.33), channel_id=1, source_target_pairs={{0,4},{1,5},{2,6},{3,7},{4,8},{5,9},{6,10},{7,11},{8,12},{9,13},{1... | collective-permute-start | bytes 1572872 | tf_op jit(solution)/shard_map/ppermute | solution.py:31
  137.7 12.2 %collective-permute-done.19 = bf16[2048,128]{1,0:T(8,128)(2,1)S(1)} collective-permute-done((bf16[2048,128]{1,0:T(8,128)(2,1)S(1)}, bf16[2048,128]{1,0:T(8,128)(2,1)S(1)}, u32[]{:S(2)}, u32[]{:S(2)}) %collective-permute-start.19) | collective-permute-done | bytes 524320 | tf_op jit(solution)/shard_map/ppermute | solution.py:31
  (42 shorter events, 11.6 us)
Async XLA Ops:
  2.3 7.0 %copy-start.3 = (bf16[1,2048,128]{2,1,0:T(8,128)(2,1)S(1)}, bf16[1,2048,128]{2,1,0:T(8,128)(2,1)}, u32[]{:S(2)}) copy-start(bf16[1,2048,128]{2,1,0:T(8,128)(2,1)} %param.8) | copy-start | bytes 1572868
  2.3 7.0 %copy-start.5 = (bf16[1,2048,128]{2,1,0:T(8,128)(2,1)S(1)}, bf16[1,2048,128]{2,1,0:T(8,128)(2,1)}, u32[]{:S(2)}) copy-start(bf16[1,2048,128]{2,1,0:T(8,128)(2,1)} %param.9) | copy-start | bytes 1572868
  3.6 17.7 %collective-permute-start.3 = (bf16[2048,128]{1,0:T(8,128)(2,1)S(1)}, bf16[2048,128]{1,0:T(8,128)(2,1)S(1)}, u32[]{:S(2)}, u32[]{:S(2)}) collective-permute-start(bf16[2048,128]{1,0:T(8,128)(2,1)S(1)} %convert_element_type.12), channel_id=1, source_target_pairs={{0,16},{1,17},{2,18},{3,19},{4,20},{5,21},{6,22},{7,23},{8,24},{9,... | collective-permute-start | bytes 1572872 | tf_op jit(solution)/shard_map/ppermute | solution.py:31
  5.6 15.8 %collective-permute-start.4 = (bf16[2048,128]{1,0:T(8,128)(2,1)S(1)}, bf16[2048,128]{1,0:T(8,128)(2,1)}, u32[]{:S(2)}, u32[]{:S(2)}) collective-permute-start(bf16[2048,128]{1,0:T(8,128)(2,1)S(1)} %convert_element_type.12), channel_id=1, source_target_pairs={{16,0},{17,1},{18,2},{19,3},{20,4},{21,5},{22,6},{23,7},{24,8},{25... | collective-permute-start | bytes 1572872 | tf_op jit(solution)/shard_map/ppermute | solution.py:31
  10.3 30.3 %collective-permute-start.10 = (bf16[2,2048,128]{2,1,0:T(8,128)(2,1)}, bf16[2,2048,128]{2,1,0:T(8,128)(2,1)S(1)}, u32[]{:S(2)}, u32[]{:S(2)}) collective-permute-start(bf16[2,2048,128]{2,1,0:T(8,128)(2,1)} %pad_maximum_fusion.2), channel_id=1, source_target_pairs={{0,3},{1,0},{2,1},{3,2},{4,7},{5,4},{6,5},{7,6},{8,11},{9,8},{10,9... | collective-permute-start | bytes 3145736 | tf_op jit(solution)/shard_map/ppermute | solution.py:31
  15.0 30.1 %collective-permute-start.9 = (bf16[2,2048,128]{2,1,0:T(8,128)(2,1)}, bf16[2,2048,128]{2,1,0:T(8,128)(2,1)}, u32[]{:S(2)}, u32[]{:S(2)}) collective-permute-start(bf16[2,2048,128]{2,1,0:T(8,128)(2,1)} %pad_maximum_fusion.2), channel_id=1, source_target_pairs={{0,1},{1,2},{2,3},{3,0},{4,5},{5,6},{6,7},{7,4},{8,9},{9,10},{10,1... | collective-permute-start | bytes 3145736 | tf_op jit(solution)/shard_map/ppermute | solution.py:31
  16.9 21.1 %all-to-all-start = ((bf16[4,2,512,128]{3,2,1,0:T(8,128)(2,1)}), bf16[4,2,512,128]{3,2,1,0:T(8,128)(2,1)S(1)}, u32[]{:S(2)}, u32[]{:S(2)}) async-start(bf16[4,2,512,128]{3,2,1,0:T(8,128)(2,1)} %pad_maximum_fusion), calls=%async_computation | async-start | bytes 2097152 | tf_op jit(solution)/shard_map/all_to_all | solution.py:196
  21.4 0.8 copy-start.7
  23.5 36.7 %collective-permute-start.5 = (bf16[2,2048,128]{2,1,0:T(8,128)(2,1)S(1)}, bf16[2,2048,128]{2,1,0:T(8,128)(2,1)}, u32[]{:S(2)}, u32[]{:S(2)}) collective-permute-start(bf16[2,2048,128]{2,1,0:T(8,128)(2,1)S(1)} %pad_maximum_fusion.1.near_ref), channel_id=1, source_target_pairs={{0,4},{1,5},{2,6},{3,7},{4,8},{5,9},{6,10},{7,11},{8,12},{9,13},{1... | collective-permute-start | bytes 3145736 | tf_op jit(solution)/shard_map/ppermute | solution.py:31
  27.4 36.6 %collective-permute-start.6 = (bf16[2,2048,128]{2,1,0:T(8,128)(2,1)S(1)}, bf16[2,2048,128]{2,1,0:T(8,128)(2,1)}, u32[]{:S(2)}, u32[]{:S(2)}) collective-permute-start(bf16[2,2048,128]{2,1,0:T(8,128)(2,1)S(1)} %pad_maximum_fusion.1.near_ref), channel_id=1, source_target_pairs={{0,12},{1,13},{2,14},{3,15},{4,0},{5,1},{6,2},{7,3},{8,4},{9,5},{1... | collective-permute-start | bytes 3145736 | tf_op jit(solution)/shard_map/ppermute | solution.py:31
  37.9 49.2 %collective-permute-start = (bf16[4,2,512,128]{3,2,1,0:T(8,128)(2,1)S(1)}, bf16[4,2,512,128]{3,2,1,0:T(8,128)(2,1)}, u32[]{:S(2)}, u32[]{:S(2)}) collective-permute-start(bf16[4,2,512,128]{3,2,1,0:T(8,128)(2,1)S(1)} %all-to-all-done.own_ref), channel_id=1, source_target_pairs={{0,1},{1,2},{2,3},{3,0},{4,5},{5,6},{6,7},{7,4},{8,9},{9,10},{10,1... | collective-permute-start | bytes 3145736 | tf_op jit(solution)/shard_map/ppermute | solution.py:31
  40.6 7.8 %copy-start = (bf16[2,2048,128]{2,1,0:T(8,128)(2,1)}, bf16[2,2048,128]{2,1,0:T(8,128)(2,1)S(1)}, u32[]{:S(2)}) copy-start(bf16[2,2048,128]{2,1,0:T(8,128)(2,1)S(1)} %collective-permute-done.10.right_ref) | copy-start | bytes 3145732
  40.7 49.3 %collective-permute-start.1 = (bf16[4,2,512,128]{3,2,1,0:T(8,128)(2,1)S(1)}, bf16[4,2,512,128]{3,2,1,0:T(8,128)(2,1)}, u32[]{:S(2)}, u32[]{:S(2)}) collective-permute-start(bf16[4,2,512,128]{3,2,1,0:T(8,128)(2,1)S(1)} %all-to-all-done.own_ref), channel_id=1, source_target_pairs={{0,3},{1,0},{2,1},{3,2},{4,7},{5,4},{6,5},{7,6},{8,11},{9,8},{10,9... | collective-permute-start | bytes 3145736 | tf_op jit(solution)/shard_map/ppermute | solution.py:31
  45.1 51.0 %collective-permute-start.2 = (bf16[4,2,512,128]{3,2,1,0:T(8,128)(2,1)S(1)}, bf16[4,2,512,128]{3,2,1,0:T(8,128)(2,1)}, u32[]{:S(2)}, u32[]{:S(2)}) collective-permute-start(bf16[4,2,512,128]{3,2,1,0:T(8,128)(2,1)S(1)} %all-to-all-done.own_ref), channel_id=1, source_target_pairs={{0,2},{1,3},{2,0},{3,1},{4,6},{5,7},{6,4},{7,5},{8,10},{9,11},{10,... | collective-permute-start | bytes 3145736 | tf_op jit(solution)/shard_map/ppermute | solution.py:31
  48.5 47.6 %all-to-all-start.1 = ((f32[4,512,128]{2,1,0:T(8,128)}), f32[4,512,128]{2,1,0:T(8,128)S(1)}, u32[]{:S(2)}, u32[]{:S(2)}) async-start(f32[4,512,128]{2,1,0:T(8,128)} %bitcast.9), calls=%async_computation.1 | async-start | bytes 2097152 | tf_op jit(solution)/shard_map/all_to_all | solution.py:196
  53.9 17.1 %copy-start.1 = (bf16[2,2048,128]{2,1,0:T(8,128)(2,1)S(1)}, bf16[2,2048,128]{2,1,0:T(8,128)(2,1)}, u32[]{:S(2)}) copy-start(bf16[2,2048,128]{2,1,0:T(8,128)(2,1)} %copy-done) | copy-start | bytes 3145732
  62.1 34.0 %collective-permute-start.7 = (bf16[2048,128]{1,0:T(8,128)(2,1)}, bf16[2048,128]{1,0:T(8,128)(2,1)}, u32[]{:S(2)}, u32[]{:S(2)}) collective-permute-start(bf16[2048,128]{1,0:T(8,128)(2,1)} %slice_bitcast_fusion.3), channel_id=1, source_target_pairs={{0,4},{1,5},{2,6},{3,7},{4,8},{5,9},{6,10},{7,11},{8,12},{9,13},{1... | collective-permute-start | bytes 1572872 | tf_op jit(solution)/shard_map/ppermute | solution.py:31
  65.9 30.2 %collective-permute-start.8 = (bf16[2048,128]{1,0:T(8,128)(2,1)}, bf16[2048,128]{1,0:T(8,128)(2,1)}, u32[]{:S(2)}, u32[]{:S(2)}) collective-permute-start(bf16[2048,128]{1,0:T(8,128)(2,1)} %slice_bitcast_fusion.2), channel_id=1, source_target_pairs={{0,12},{1,13},{2,14},{3,15},{4,0},{5,1},{6,2},{7,3},{8,4},{9,5},{1... | collective-permute-start | bytes 1572872 | tf_op jit(solution)/shard_map/ppermute | solution.py:31
  87.1 30.7 %collective-permute-start.11 = (bf16[2048,128]{1,0:T(8,128)(2,1)}, bf16[2048,128]{1,0:T(8,128)(2,1)}, u32[]{:S(2)}, u32[]{:S(2)}) collective-permute-start(bf16[2048,128]{1,0:T(8,128)(2,1)} %slice_bitcast_fusion.1), channel_id=1, source_target_pairs={{0,1},{1,2},{2,3},{3,0},{4,5},{5,6},{6,7},{7,4},{8,9},{9,10},{10,1... | collective-permute-start | bytes 1572872 | tf_op jit(solution)/shard_map/ppermute | solution.py:31
  90.0 27.8 %collective-permute-start.12 = (bf16[2048,128]{1,0:T(8,128)(2,1)}, bf16[2048,128]{1,0:T(8,128)(2,1)}, u32[]{:S(2)}, u32[]{:S(2)}) collective-permute-start(bf16[2048,128]{1,0:T(8,128)(2,1)} %slice_bitcast_fusion), channel_id=1, source_target_pairs={{0,3},{1,0},{2,1},{3,2},{4,7},{5,4},{6,5},{7,6},{8,11},{9,8},{10,9... | collective-permute-start | bytes 1572872 | tf_op jit(solution)/shard_map/ppermute | solution.py:31
  101.0 16.8 %copy-start.2 = (bf16[2,2048,128]{2,1,0:T(8,128)(2,1)S(1)}, bf16[2,2048,128]{2,1,0:T(8,128)(2,1)}, u32[]{:S(2)}) copy-start(bf16[2,2048,128]{2,1,0:T(8,128)(2,1)} %copy-done) | copy-start | bytes 3145732
  101.0 16.8 %copy-start.4 = (bf16[1,2048,128]{2,1,0:T(8,128)(2,1)S(1)}, bf16[1,2048,128]{2,1,0:T(8,128)(2,1)}, u32[]{:S(2)}) copy-start(bf16[1,2048,128]{2,1,0:T(8,128)(2,1)} %param.8) | copy-start | bytes 1572868
  101.0 16.8 %copy-start.6 = (bf16[1,2048,128]{2,1,0:T(8,128)(2,1)S(1)}, bf16[1,2048,128]{2,1,0:T(8,128)(2,1)}, u32[]{:S(2)}) copy-start(bf16[1,2048,128]{2,1,0:T(8,128)(2,1)} %param.9) | copy-start | bytes 1572868
  101.0 14.7 %collective-permute-start.13 = (bf16[2,512,128]{2,1,0:T(8,128)(2,1)S(1)}, bf16[2,512,128]{2,1,0:T(8,128)(2,1)S(1)}, u32[]{:S(2)}, u32[]{:S(2)}) collective-permute-start(bf16[2,512,128]{2,1,0:T(8,128)(2,1)S(1)} %get-tuple-element.23), channel_id=1, source_target_pairs={{0,32},{1,33},{2,34},{3,35},{4,36},{5,37},{6,38},{7,39},{8,40},{9,... | collective-permute-start | bytes 786440 | tf_op jit(solution)/shard_map/ppermute | solution.py:31
  105.0 12.8 %collective-permute-start.14 = (bf16[2,512,128]{2,1,0:T(8,128)(2,1)S(1)}, bf16[2,512,128]{2,1,0:T(8,128)(2,1)S(1)}, u32[]{:S(2)}, u32[]{:S(2)}) collective-permute-start(bf16[2,512,128]{2,1,0:T(8,128)(2,1)S(1)} %get-tuple-element.23), channel_id=1, source_target_pairs={{32,0},{33,1},{34,2},{35,3},{36,4},{37,5},{38,6},{39,7},{40,8},{41... | collective-permute-start | bytes 786440 | tf_op jit(solution)/shard_map/ppermute | solution.py:31
  111.9 15.6 %collective-permute-start.15 = (bf16[2,512,128]{2,1,0:T(8,128)(2,1)S(1)}, bf16[2,512,128]{2,1,0:T(8,128)(2,1)S(1)}, u32[]{:S(2)}, u32[]{:S(2)}) collective-permute-start(bf16[2,512,128]{2,1,0:T(8,128)(2,1)S(1)} %get-tuple-element.30), channel_id=1, source_target_pairs={{0,32},{1,33},{2,34},{3,35},{4,36},{5,37},{6,38},{7,39},{8,40},{9,... | collective-permute-start | bytes 786440 | tf_op jit(solution)/shard_map/ppermute | solution.py:31
  115.8 11.8 %collective-permute-start.16 = (bf16[2,512,128]{2,1,0:T(8,128)(2,1)S(1)}, bf16[2,512,128]{2,1,0:T(8,128)(2,1)S(1)}, u32[]{:S(2)}, u32[]{:S(2)}) collective-permute-start(bf16[2,512,128]{2,1,0:T(8,128)(2,1)S(1)} %get-tuple-element.30), channel_id=1, source_target_pairs={{32,0},{33,1},{34,2},{35,3},{36,4},{37,5},{38,6},{39,7},{40,8},{41... | collective-permute-start | bytes 786440 | tf_op jit(solution)/shard_map/ppermute | solution.py:31
  122.2 27.8 %collective-permute-start.17 = (bf16[2048,128]{1,0:T(8,128)(2,1)S(1)}, bf16[2048,128]{1,0:T(8,128)(2,1)S(1)}, u32[]{:S(2)}, u32[]{:S(2)}) collective-permute-start(bf16[2048,128]{1,0:T(8,128)(2,1)S(1)} %get-tuple-element.28), channel_id=1, source_target_pairs={{0,8},{1,9},{2,10},{3,11},{4,12},{5,13},{6,14},{7,15},{8,0},{9,1},... | collective-permute-start | bytes 1572872 | tf_op jit(solution)/shard_map/ppermute | solution.py:31
  131.9 18.1 %collective-permute-start.19 = (bf16[2048,128]{1,0:T(8,128)(2,1)S(1)}, bf16[2048,128]{1,0:T(8,128)(2,1)S(1)}, u32[]{:S(2)}, u32[]{:S(2)}) collective-permute-start(bf16[2048,128]{1,0:T(8,128)(2,1)S(1)} %get-tuple-element.34), channel_id=1, source_target_pairs={{0,12},{1,13},{2,14},{3,15},{4,0},{5,1},{6,2},{7,3},{8,4},{9,5},{1... | collective-permute-start | bytes 1572872 | tf_op jit(solution)/shard_map/ppermute | solution.py:31
  134.6 15.6 %collective-permute-start.18 = (bf16[2048,128]{1,0:T(8,128)(2,1)S(1)}, bf16[2048,128]{1,0:T(8,128)(2,1)S(1)}, u32[]{:S(2)}, u32[]{:S(2)}) collective-permute-start(bf16[2048,128]{1,0:T(8,128)(2,1)S(1)} %get-tuple-element.33), channel_id=1, source_target_pairs={{0,4},{1,5},{2,6},{3,7},{4,8},{5,9},{6,10},{7,11},{8,12},{9,13},{1... | collective-permute-start | bytes 1572872 | tf_op jit(solution)/shard_map/ppermute | solution.py:31

commit v5 on v4

v5 whole, which is shorter than its diff:
```python
import functools
import itertools

import jax
import jax.numpy as jnp
from jax import lax
from jax.experimental import pallas as pl
from jax.experimental.pallas import tpu as pltpu
from jax.sharding import Mesh, PartitionSpec as P

Z, CORES, Y, X = 16, 2, 4, 4
M = 2048
BLK = M // Y
COL = 128
AXES = ("z", "core", "y", "x")


def home(core, x):
    return (core, x) if core == x // 2 else (1 - core, X - 1 - x)


def sent(value, target):
    places = list(itertools.product(range(Z), range(CORES), range(Y), range(X)))
    number = {place: i for i, place in enumerate(places)}
    pairs = [(number[place], number.get(target(*place))) for place in places]
    return lax.ppermute(value, AXES, [pair for pair in pairs if pair[1] is not None])


def along(value, ys=0, zs=0):
    return sent(value, lambda z, core, y, x: (z + zs, core, (y + ys) % Y, x))


def to_home(value, ys=0):
    return sent(
        value,
        lambda z, core, y, x: (z, home(core, x)[0], (y + ys) % Y, home(core, x)[1]),
    )


def to_next_plane(value, step):
    def target(z, core, y, x):
        plane = z * CORES + core + step
        to_core, to_x = home(plane % CORES, x)
        return (plane // CORES, to_core, y, to_x)

    return sent(value, target)


def over_x(value):
    def partner(z, core, y, x):
        to_core, to_x = home(core, x)
        return (z, to_core, y, to_x ^ 1)

    def swapped(part):
        return sent(part, lambda z, core, y, x: (z, 1 - core, y, x))

    near, far = to_home(value), sent(value, partner)
    return near, far, swapped(far), swapped(near)


def after(value, *before):
    return lax.optimization_barrier((value,) + before)[0]


def rows_in_order(at_ref, ref, row):
    starts = [pl.multiple_of((at_ref[1] ^ e) * COL, COL) for e in range(X)]
    return [ref[row + (pl.ds(start, COL),)] for start in starts]


FIRST_GROUPS, LAST_GROUPS = (2, 1), (3, 0)


def first_kernel(groups, at_ref, *refs):
    blocks, parts = refs[:X], refs[X : X + 2 * len(groups)]
    rhs_ref, corr_ref, sent_ref, acc_ref = refs[X + 2 * len(groups) :]
    step = pl.program_id(0)

    @pl.when(step == 0)
    def _():
        acc_ref[...] = jnp.zeros_like(acc_ref)

    total = acc_ref[...]
    for side in (0, 1):
        left = jnp.concatenate([block[0, side] for block in blocks], axis=1)
        right = [
            jnp.concatenate(rows_in_order(at_ref, part, (0,)), axis=0)
            for part in parts[side :: 2]
        ]
        right = jnp.concatenate(right, axis=1)
        total = total + jnp.dot(left, right, preferred_element_type=jnp.float32)
    acc_ref[...] = total

    @pl.when(step == Y - 1)
    def _():
        for i, d in enumerate(groups):
            piece = acc_ref[:, i * COL : (i + 1) * COL]
            corr_ref[i] = piece
            owner = lax.rem(at_ref[0] + d, Y)
            sent_ref[i] = (rhs_ref[owner] + piece).astype(jnp.bfloat16)


def first_level(groups, at, blocks, parts, rhs):
    count = len(groups)
    block = pl.BlockSpec((1, 2, BLK, COL), lambda k, at: (k, 0, 0, 0))
    whole = pl.BlockSpec((Y, BLK, COL), lambda k, at: (0, 0, 0))
    out = pl.BlockSpec((count, BLK, COL), lambda k, at: (0, 0, 0))

    def part(index):
        return pl.BlockSpec((1, BLK, COL), lambda k, at: (index, k, 0))

    return pl.pallas_call(
        functools.partial(first_kernel, groups),
        name="first_level",
        out_shape=(
            jax.ShapeDtypeStruct((count, BLK, COL), jnp.float32),
            jax.ShapeDtypeStruct((count, BLK, COL), jnp.bfloat16),
        ),
        grid_spec=pltpu.PrefetchScalarGridSpec(
            num_scalar_prefetch=1,
            grid=(Y,),
            in_specs=[block] * X + [part(index) for _, index in parts] + [whole],
            out_specs=(out, out),
            scratch_shapes=[pltpu.VMEM((BLK, count * COL), jnp.float32)],
        ),
        compiler_params=pltpu.CompilerParams(vmem_limit_bytes=32 << 20),
        cost_estimate=pl.CostEstimate(
            flops=4 * BLK * M * count * COL,
            bytes_accessed=8 << 20,
            transcendentals=0,
        ),
    )(at, *blocks, *[array for array, _ in parts], rhs)


def second_kernel(groups, at_ref, *refs):
    blocks = refs[:X]
    below, above, corr_ref, *outs = refs[X:]
    step = pl.program_id(0)
    total = None
    for side, b_ref in ((0, below), (1, above)):
        left = jnp.concatenate([block[side] for block in blocks], axis=1)
        right = [
            jnp.concatenate(rows_in_order(at_ref, b_ref, (i,)), axis=0)
            for i in range(len(groups))
        ]
        right = jnp.concatenate(right, axis=1)
        term = jnp.dot(left, right, preferred_element_type=jnp.float32)
        total = term if total is None else total + term
    here = step == at_ref[0]
    for i in range(len(groups)):
        piece = total[:, i * COL : (i + 1) * COL]
        piece = piece + jnp.where(here, corr_ref[i], 0.0)
        outs[i][...] = piece.astype(outs[i].dtype)


def second_level(groups, at, blocks, below, above, corr):
    count = len(groups)
    rows = pl.BlockSpec((BLK, COL), lambda m, at: (m, 0))
    pair = pl.BlockSpec((2, BLK, COL), lambda m, at: (0, m, 0))
    whole = pl.BlockSpec((count, BLK, COL), lambda m, at: (0, 0, 0))
    return pl.pallas_call(
        functools.partial(second_kernel, groups),
        name="second_level",
        out_shape=(jax.ShapeDtypeStruct((M, COL), jnp.bfloat16),) * count,
        grid_spec=pltpu.PrefetchScalarGridSpec(
            num_scalar_prefetch=1,
            grid=(Y,),
            in_specs=[pair] * X + [whole] * 3,
            out_specs=(rows,) * count,
        ),
        compiler_params=pltpu.CompilerParams(vmem_limit_bytes=32 << 20),
        cost_estimate=pl.CostEstimate(
            flops=4 * BLK * M * count * COL,
            bytes_accessed=6 << 20,
            transcendentals=0,
        ),
    )(at, *blocks, below, above, corr)


def on_device(right_sides, lower_first, upper_first, lower_second, upper_second):
    rhs = right_sides[0]
    x = lax.axis_index("x")
    label = jnp.where(lax.axis_index("core") == x >> 1, x, X - 1 - x)
    at = jnp.stack([lax.axis_index("y"), label]).astype(jnp.int32)

    def exchanged(value):
        return lax.all_to_all(value, "y", 0, 0, tiled=True)

    firsts = [v[0].reshape(Y, BLK, COL) for v in (lower_first, upper_first)]
    firsts = jnp.stack(firsts, axis=1)
    sent_one = after(rhs, firsts).astype(jnp.bfloat16)
    own = exchanged(firsts)
    near = jnp.stack([to_next_plane(sent_one, 1), to_next_plane(sent_one, -1)])

    seconds = after(jnp.stack([lower_second[0], upper_second[0]]), sent_one)
    seconds = over_x(seconds)
    firsts = over_x(own)

    down, up = along(near, ys=1), along(near, ys=-1)
    below_far, above_far = along(down[0], ys=1), along(up[1], ys=-1)
    rhs_rows = to_home(exchanged(after(rhs, own).reshape(Y, BLK, COL)))

    parts = ((below_far[None], 0), (above_far[None], 0), (up, 0), (up, 1))
    corr_a, sent_a = first_level(FIRST_GROUPS, at, firsts, parts, rhs_rows)
    late = after(at, sent_a)
    parts = ((down, 0), (down, 1), (near, 0), (near, 1))
    corr_b, sent_b = first_level(LAST_GROUPS, late, firsts, parts, rhs_rows)

    below_a, above_a = along(sent_a, zs=1), along(sent_a, zs=-1)
    below_b, above_b = along(sent_b, zs=1), along(sent_b, zs=-1)
    outs = second_level(FIRST_GROUPS, at, seconds, below_a, above_a, corr_a)
    late = after(late, outs[0])
    outs += second_level(LAST_GROUPS, late, seconds, below_b, above_b, corr_b)
    total = rhs
    for d, part in zip(FIRST_GROUPS + LAST_GROUPS, outs):
        total = total + to_home(part, ys=d).astype(jnp.float32)
    return total[None]


def solution(mesh):
    fine = Mesh(mesh.devices.reshape(Z, CORES, Y, X), AXES)
    spec = P(("z", "core"), None, ("y", "x"))
    return jax.shard_map(
        on_device,
        mesh=fine,
        in_specs=(spec,) * 5,
        out_specs=spec,
        check_vma=False,
    )
```

time: 153 us -> 172 us (1.12)
  the two profiles are of different devices: /device:TPU:32 before, /device:TPU:265 now
where the time goes in v5:
time: 172 us; the launch traced here: 170 us
  starting transfers between devices  86.1 us (50%)
  waiting for transfers between devices  56.3 us (33%)
  Pallas kernels  19 us (11%)
  other arithmetic  6.15 us (4%)
  local copies, waits for them, and re-layouts  1.75 us (1%)
    ppermute x23, starting transfers between devices, sent(): lax.ppermute(value, AXES, [pair for pair in pairs if pair[1] is not None])  74.8 us
    ppermute x23, waiting for transfers between devices, sent(): lax.ppermute(value, AXES, [pair for pair in pairs if pair[1] is not None])  38 us
    all_to_all x2, waiting for transfers between devices, exchanged(): return lax.all_to_all(value, 'y', 0, 0, tiled=True)  18.3 us
    all_to_all x2, starting transfers between devices, exchanged(): return lax.all_to_all(value, 'y', 0, 0, tiled=True)  11.3 us
    pallas_call x2, Pallas kernels, first_level(): pl.pallas_call(functools.partial(first_kernel, groups), name='first_level...  10.1 us
    pallas_call x2, Pallas kernels, second_level(): pl.pallas_call(functools.partial(second_kernel, groups), name='second_lev...  8.83 us
  transfers between devices with their start and end apart: 25, of which 9 were waited for; matrix products, arithmetic and copies ran while one was open for 2% of the time, Pallas kernels for 11%

profile of v5, /device:TPU:265, one launch (start us, length us, event | category | flops | bytes accessed | tf_op | source)
XLA Modules:
  0.0 169.6 jit_solution(5889113180737775237)
XLA Ops:
  0.0 2.4 %pad_maximum_fusion.1 = bf16[4,2,512,128]{3,2,1,0:T(8,128)(2,1)} fusion(bf16[4,1,512,128]{3,2,1,0:T(8,128)(2,1)} %bitcast.19, bf16[4,1,512,128]{3,2,1,0:T(8,128)(2,1)} %bitcast.20), kind=kLoop, calls=%fused_computation.1 | loop fusion | flops 524288 | bytes 2097152 | tf_op jit(solution)/shard_map/stack | solution.py:189
  2.4 3.2 %collective-permute-start.8 = (bf16[2048,128]{1,0:T(8,128)(2,1)S(1)}, bf16[2048,128]{1,0:T(8,128)(2,1)S(1)}, u32[]{:S(2)}, u32[]{:S(2)}) collective-permute-start(bf16[2048,128]{1,0:T(8,128)(2,1)S(1)} %convert_element_type.15), channel_id=1, source_target_pairs={{0,3},{1,2},{2,18},{3,19},{4,7},{5,6},{6,22},{7,23},{8,11},{9,10},... | collective-permute-start | bytes 1572872 | tf_op jit(solution)/shard_map/ppermute | solution.py:26
  5.7 4.0 %collective-permute-start.9 = (bf16[2048,128]{1,0:T(8,128)(2,1)S(1)}, bf16[2048,128]{1,0:T(8,128)(2,1)S(1)}, u32[]{:S(2)}, u32[]{:S(2)}) collective-permute-start(bf16[2048,128]{1,0:T(8,128)(2,1)S(1)} %convert_element_type.15), channel_id=1, source_target_pairs={{16,0},{17,1},{18,17},{19,16},{20,4},{21,5},{22,21},{23,20},{24,8}... | collective-permute-start | bytes 1572872 | tf_op jit(solution)/shard_map/ppermute | solution.py:26
  9.7 6.1 %collective-permute-done.8 = bf16[2048,128]{1,0:T(8,128)(2,1)S(1)} collective-permute-done((bf16[2048,128]{1,0:T(8,128)(2,1)S(1)}, bf16[2048,128]{1,0:T(8,128)(2,1)S(1)}, u32[]{:S(2)}, u32[]{:S(2)}) %collective-permute-start.8) | collective-permute-done | bytes 524320 | tf_op jit(solution)/shard_map/ppermute | solution.py:26
  15.8 5.5 %collective-permute-done.9 = bf16[2048,128]{1,0:T(8,128)(2,1)S(1)} collective-permute-done((bf16[2048,128]{1,0:T(8,128)(2,1)S(1)}, bf16[2048,128]{1,0:T(8,128)(2,1)S(1)}, u32[]{:S(2)}, u32[]{:S(2)}) %collective-permute-start.9) | collective-permute-done | bytes 524320 | tf_op jit(solution)/shard_map/ppermute | solution.py:26
  23.5 7.0 %all-to-all-start = ((bf16[4,2,512,128]{3,2,1,0:T(8,128)(2,1)}), bf16[4,2,512,128]{3,2,1,0:T(8,128)(2,1)}, u32[]{:S(2)}, u32[]{:S(2)}) async-start(bf16[4,2,512,128]{3,2,1,0:T(8,128)(2,1)} %pad_maximum_fusion.1), calls=%async_computation | async-start | bytes 2097152 | tf_op jit(solution)/shard_map/all_to_all | solution.py:186
  30.5 3.1 %collective-permute-start.10 = (bf16[2,2048,128]{2,1,0:T(8,128)(2,1)S(1)}, bf16[2,2048,128]{2,1,0:T(8,128)(2,1)S(1)}, u32[]{:S(2)}, u32[]{:S(2)}) collective-permute-start(bf16[2,2048,128]{2,1,0:T(8,128)(2,1)S(1)} %pad_maximum_fusion.2.refs_6_.refs_7_), channel_id=1, source_target_pairs={{0,4},{1,5},{2,6},{3,7},{4,8},{5,9},{6,10},{7,11},{8,12},{9,13},{1... | collective-permute-start | bytes 3145736 | tf_op jit(solution)/shard_map/ppermute | solution.py:26
  33.5 2.3 %pad_maximum_fusion = bf16[2,2048,128]{2,1,0:T(8,128)(2,1)} fusion(bf16[1,2048,128]{2,1,0:T(8,128)(2,1)} %param.9, bf16[1,2048,128]{2,1,0:T(8,128)(2,1)} %param.8), kind=kLoop, calls=%fused_computation | loop fusion | flops 524288 | bytes 2097152 | tf_op jit(solution)/shard_map/stack | solution.py:194
  35.8 3.9 %collective-permute-start.1 = (bf16[2,2048,128]{2,1,0:T(8,128)(2,1)}, bf16[2,2048,128]{2,1,0:T(8,128)(2,1)}, u32[]{:S(2)}, u32[]{:S(2)}) collective-permute-start(bf16[2,2048,128]{2,1,0:T(8,128)(2,1)} %pad_maximum_fusion), channel_id=1, source_target_pairs={{0,1},{1,0},{2,16},{3,17},{4,5},{5,4},{6,20},{7,21},{8,9},{9,8},{1... | collective-permute-start | bytes 3145736 | tf_op jit(solution)/shard_map/ppermute | solution.py:26
  39.7 2.9 %collective-permute-start = (bf16[2,2048,128]{2,1,0:T(8,128)(2,1)}, bf16[2,2048,128]{2,1,0:T(8,128)(2,1)}, u32[]{:S(2)}, u32[]{:S(2)}) collective-permute-start(bf16[2,2048,128]{2,1,0:T(8,128)(2,1)} %pad_maximum_fusion), channel_id=1, source_target_pairs={{0,0},{1,1},{2,17},{3,16},{4,4},{5,5},{6,21},{7,20},{8,8},{9,9},{1... | collective-permute-start | bytes 3145736 | tf_op jit(solution)/shard_map/ppermute | solution.py:26
  42.6 17.2 %all-to-all-done = bf16[4,2,512,128]{3,2,1,0:T(8,128)(2,1)} async-done(((bf16[4,2,512,128]{3,2,1,0:T(8,128)(2,1)}), bf16[4,2,512,128]{3,2,1,0:T(8,128)(2,1)}, u32[]{:S(2)}, u32[]{:S(2)}) %all-to-all-start) | async-done | bytes 1048608 | tf_op jit(solution)/shard_map/all_to_all | solution.py:186
  59.8 4.4 %all-to-all-start.1 = ((f32[4,512,128]{2,1,0:T(8,128)}), f32[4,512,128]{2,1,0:T(8,128)}, u32[]{:S(2)}, u32[]{:S(2)}) async-start(f32[4,512,128]{2,1,0:T(8,128)} %bitcast.17), calls=%async_computation.1 | async-start | bytes 2097152 | tf_op jit(solution)/shard_map/all_to_all | solution.py:186
  64.1 3.7 %collective-permute-start.5 = (bf16[4,2,512,128]{3,2,1,0:T(8,128)(2,1)}, bf16[4,2,512,128]{3,2,1,0:T(8,128)(2,1)}, u32[]{:S(2)}, u32[]{:S(2)}) collective-permute-start(bf16[4,2,512,128]{3,2,1,0:T(8,128)(2,1)} %all-to-all-done), channel_id=1, source_target_pairs={{0,1},{1,0},{2,16},{3,17},{4,5},{5,4},{6,20},{7,21},{8,9},{9,8},{1... | collective-permute-start | bytes 3145736 | tf_op jit(solution)/shard_map/ppermute | solution.py:26
  67.8 2.8 %collective-permute-start.4 = (bf16[4,2,512,128]{3,2,1,0:T(8,128)(2,1)}, bf16[4,2,512,128]{3,2,1,0:T(8,128)(2,1)}, u32[]{:S(2)}, u32[]{:S(2)}) collective-permute-start(bf16[4,2,512,128]{3,2,1,0:T(8,128)(2,1)} %all-to-all-done), channel_id=1, source_target_pairs={{0,0},{1,1},{2,17},{3,16},{4,4},{5,5},{6,21},{7,20},{8,8},{9,9},{1... | collective-permute-start | bytes 3145736 | tf_op jit(solution)/shard_map/ppermute | solution.py:26
  74.3 3.4 %collective-permute-start.11 = (bf16[2048,128]{1,0:T(8,128)(2,1)}, bf16[2048,128]{1,0:T(8,128)(2,1)}, u32[]{:S(2)}, u32[]{:S(2)}) collective-permute-start(bf16[2048,128]{1,0:T(8,128)(2,1)} %slice_bitcast_fusion.1), channel_id=1, source_target_pairs={{0,4},{1,5},{2,6},{3,7},{4,8},{5,9},{6,10},{7,11},{8,12},{9,13},{1... | collective-permute-start | bytes 1572872 | tf_op jit(solution)/shard_map/ppermute | solution.py:26
  78.7 3.5 %collective-permute-start.14 = (f32[4,512,128]{2,1,0:T(8,128)}, f32[4,512,128]{2,1,0:T(8,128)}, u32[]{:S(2)}, u32[]{:S(2)}) collective-permute-start(f32[4,512,128]{2,1,0:T(8,128)} %all-to-all-done.1), channel_id=1, source_target_pairs={{0,0},{1,1},{2,17},{3,16},{4,4},{5,5},{6,21},{7,20},{8,8},{9,9},{1... | collective-permute-start | bytes 3145736 | tf_op jit(solution)/shard_map/ppermute | solution.py:26
  82.2 8.0 %collective-permute-done.5.refs_1_ = bf16[4,2,512,128]{3,2,1,0:T(8,128)(2,1)} collective-permute-done((bf16[4,2,512,128]{3,2,1,0:T(8,128)(2,1)}, bf16[4,2,512,128]{3,2,1,0:T(8,128)(2,1)}, u32[]{:S(2)}, u32[]{:S(2)}) %collective-permute-start.5) | collective-permute-done | bytes 1048608 | tf_op jit(solution)/shard_map/ppermute | solution.py:26
  90.2 5.1 %collective-permute-start.6 = (bf16[4,2,512,128]{3,2,1,0:T(8,128)(2,1)}, bf16[4,2,512,128]{3,2,1,0:T(8,128)(2,1)}, u32[]{:S(2)}, u32[]{:S(2)}) collective-permute-start(bf16[4,2,512,128]{3,2,1,0:T(8,128)(2,1)} %collective-permute-done.5.refs_1_), channel_id=1, source_target_pairs={{0,16},{1,17},{2,18},{3,19},{4,20},{5,21},{6,22},{7,23},{8,24},{9,... | collective-permute-start | bytes 3145736 | tf_op jit(solution)/shard_map/ppermute | solution.py:26
  97.3 2.4 %collective-permute-start.2 = (bf16[2,2048,128]{2,1,0:T(8,128)(2,1)}, bf16[2,2048,128]{2,1,0:T(8,128)(2,1)}, u32[]{:S(2)}, u32[]{:S(2)}) collective-permute-start(bf16[2,2048,128]{2,1,0:T(8,128)(2,1)} %collective-permute-done.1.refs_1_), channel_id=1, source_target_pairs={{0,16},{1,17},{2,18},{3,19},{4,20},{5,21},{6,22},{7,23},{8,24},{9,... | collective-permute-start | bytes 3145736 | tf_op jit(solution)/shard_map/ppermute | solution.py:26
  101.7 4.6 %collective-permute-done.14.refs_8_ = f32[4,512,128]{2,1,0:T(8,128)} collective-permute-done((f32[4,512,128]{2,1,0:T(8,128)}, f32[4,512,128]{2,1,0:T(8,128)}, u32[]{:S(2)}, u32[]{:S(2)}) %collective-permute-start.14) | collective-permute-done | bytes 1048608 | tf_op jit(solution)/shard_map/ppermute | solution.py:26
  106.3 5.2 %first_level.2 = (f32[2,512,128]{2,1,0:T(8,128)S(1)}, bf16[2,512,128]{2,1,0:T(8,128)(2,1)S(1)}) custom-call(s32[2]{0:T(128)S(1)} %pad_add_fusion.at_ref, bf16[4,2,512,128]{3,2,1,0:T(8,128)(2,1)} %collective-permute-done.4.refs_0_, bf16[4,2,512,128]{3,2,1,0:T(8,128)(2,1)} %collective-permute-done.5.refs_1_, ...), custom_call_target="tpu_custom_call" | custom-call | flops 1073741824 | bytes 8388608 | tf_op jit(solution)/shard_map/first_level/pallas_call | solution.py:111
  113.4 4.6 %collective-permute-start.16 = (bf16[2,512,128]{2,1,0:T(8,128)(2,1)S(1)}, bf16[2,512,128]{2,1,0:T(8,128)(2,1)S(1)}, u32[]{:S(2)}, u32[]{:S(2)}) collective-permute-start(bf16[2,512,128]{2,1,0:T(8,128)(2,1)S(1)} %get-tuple-element.21), channel_id=1, source_target_pairs={{32,0},{33,1},{34,2},{35,3},{36,4},{37,5},{38,6},{39,7},{40,8},{41... | collective-permute-start | bytes 786440 | tf_op jit(solution)/shard_map/ppermute | solution.py:26
  118.0 4.9 %first_level.3 = (f32[2,512,128]{2,1,0:T(8,128)S(1)}, bf16[2,512,128]{2,1,0:T(8,128)(2,1)S(1)}) custom-call(s32[2]{0:T(128)S(1)} %pad_add_fusion.at_ref, bf16[4,2,512,128]{3,2,1,0:T(8,128)(2,1)} %collective-permute-done.4.refs_0_, bf16[4,2,512,128]{3,2,1,0:T(8,128)(2,1)} %collective-permute-done.5.refs_1_, ...), custom_call_target="tpu_custom_call" | custom-call | flops 1073741824 | bytes 8388608 | tf_op jit(solution)/shard_map/first_level/pallas_call | solution.py:111
  124.9 4.6 %collective-permute-start.20 = (bf16[2,512,128]{2,1,0:T(8,128)(2,1)S(1)}, bf16[2,512,128]{2,1,0:T(8,128)(2,1)S(1)}, u32[]{:S(2)}, u32[]{:S(2)}) collective-permute-start(bf16[2,512,128]{2,1,0:T(8,128)(2,1)S(1)} %get-tuple-element.27), channel_id=1, source_target_pairs={{32,0},{33,1},{34,2},{35,3},{36,4},{37,5},{38,6},{39,7},{40,8},{41... | collective-permute-start | bytes 786440 | tf_op jit(solution)/shard_map/ppermute | solution.py:26
  129.5 4.4 %second_level.2 = (bf16[2048,128]{1,0:T(8,128)(2,1)S(1)}, bf16[2048,128]{1,0:T(8,128)(2,1)S(1)}) custom-call(s32[2]{0:T(128)S(1)} %pad_add_fusion.at_ref, bf16[2,2048,128]{2,1,0:T(8,128)(2,1)} %collective-permute-done.refs_0_, bf16[2,2048,128]{2,1,0:T(8,128)(2,1)} %collective-permute-done.1.refs_1_, bf16[2,2048,128]{2,1,0:T(8,128)(2,1)} %collective-permute-done.2.refs_2_, ...), custom_call_target="tpu_custom_call" | custom-call | flops 1073741824 | bytes 6291456 | tf_op jit(solution)/shard_map/second_level/pallas_call | solution.py:160
  133.9 5.7 %collective-permute-start.17 = (bf16[2048,128]{1,0:T(8,128)(2,1)S(1)}, bf16[2048,128]{1,0:T(8,128)(2,1)S(1)}, u32[]{:S(2)}, u32[]{:S(2)}) collective-permute-start(bf16[2048,128]{1,0:T(8,128)(2,1)S(1)} %get-tuple-element.23), channel_id=1, source_target_pairs={{0,8},{1,9},{2,25},{3,24},{4,12},{5,13},{6,29},{7,28},{8,0},{9,1},... | collective-permute-start | bytes 1572872 | tf_op jit(solution)/shard_map/ppermute | solution.py:26
  139.6 4.4 %second_level.3 = (bf16[2048,128]{1,0:T(8,128)(2,1)S(1)}, bf16[2048,128]{1,0:T(8,128)(2,1)S(1)}) custom-call(s32[2]{0:T(128)S(1)} %pad_add_fusion.at_ref, bf16[2,2048,128]{2,1,0:T(8,128)(2,1)} %collective-permute-done.refs_0_, bf16[2,2048,128]{2,1,0:T(8,128)(2,1)} %collective-permute-done.1.refs_1_, bf16[2,2048,128]{2,1,0:T(8,128)(2,1)} %collective-permute-done.2.refs_2_, ...), custom_call_target="tpu_custom_call" | custom-call | flops 1073741824 | bytes 6291456 | tf_op jit(solution)/shard_map/second_level/pallas_call | solution.py:160
  144.0 3.5 %collective-permute-start.21 = (bf16[2048,128]{1,0:T(8,128)(2,1)S(1)}, bf16[2048,128]{1,0:T(8,128)(2,1)S(1)}, u32[]{:S(2)}, u32[]{:S(2)}) collective-permute-start(bf16[2048,128]{1,0:T(8,128)(2,1)S(1)} %get-tuple-element.29), channel_id=1, source_target_pairs={{0,12},{1,13},{2,29},{3,28},{4,0},{5,1},{6,17},{7,16},{8,4},{9,5},... | collective-permute-start | bytes 1572872 | tf_op jit(solution)/shard_map/ppermute | solution.py:26
  147.6 4.0 %collective-permute-start.22 = (bf16[2048,128]{1,0:T(8,128)(2,1)S(1)}, bf16[2048,128]{1,0:T(8,128)(2,1)S(1)}, u32[]{:S(2)}, u32[]{:S(2)}) collective-permute-start(bf16[2048,128]{1,0:T(8,128)(2,1)S(1)} %get-tuple-element.30), channel_id=1, source_target_pairs={{0,0},{1,1},{2,17},{3,16},{4,4},{5,5},{6,21},{7,20},{8,8},{9,9},{1... | collective-permute-start | bytes 1572872 | tf_op jit(solution)/shard_map/ppermute | solution.py:26
  151.5 3.0 %collective-permute-start.18 = (bf16[2048,128]{1,0:T(8,128)(2,1)S(1)}, bf16[2048,128]{1,0:T(8,128)(2,1)S(1)}, u32[]{:S(2)}, u32[]{:S(2)}) collective-permute-start(bf16[2048,128]{1,0:T(8,128)(2,1)S(1)} %get-tuple-element.24), channel_id=1, source_target_pairs={{0,4},{1,5},{2,21},{3,20},{4,8},{5,9},{6,25},{7,24},{8,12},{9,13},... | collective-permute-start | bytes 1572872 | tf_op jit(solution)/shard_map/ppermute | solution.py:26
  156.7 5.4 %collective-permute-done.22 = bf16[2048,128]{1,0:T(8,128)(2,1)S(1)} collective-permute-done((bf16[2048,128]{1,0:T(8,128)(2,1)S(1)}, bf16[2048,128]{1,0:T(8,128)(2,1)S(1)}, u32[]{:S(2)}, u32[]{:S(2)}) %collective-permute-start.22) | collective-permute-done | bytes 524320 | tf_op jit(solution)/shard_map/ppermute | solution.py:26
  162.1 6.2 %collective-permute-done.18 = bf16[2048,128]{1,0:T(8,128)(2,1)S(1)} collective-permute-done((bf16[2048,128]{1,0:T(8,128)(2,1)S(1)}, bf16[2048,128]{1,0:T(8,128)(2,1)S(1)}, u32[]{:S(2)}, u32[]{:S(2)}) %collective-permute-start.18) | collective-permute-done | bytes 524320 | tf_op jit(solution)/shard_map/ppermute | solution.py:26
  (34 shorter events, 18.3 us)
Async XLA Ops:
  0.0 2.4 %copy-start = (f32[1,2048,128]{2,1,0:T(8,128)S(1)}, f32[1,2048,128]{2,1,0:T(8,128)}, u32[]{:S(2)}) copy-start(f32[1,2048,128]{2,1,0:T(8,128)} %param.5) | copy-start | bytes 3145732
  2.4 13.3 %collective-permute-start.8 = (bf16[2048,128]{1,0:T(8,128)(2,1)S(1)}, bf16[2048,128]{1,0:T(8,128)(2,1)S(1)}, u32[]{:S(2)}, u32[]{:S(2)}) collective-permute-start(bf16[2048,128]{1,0:T(8,128)(2,1)S(1)} %convert_element_type.15), channel_id=1, source_target_pairs={{0,3},{1,2},{2,18},{3,19},{4,7},{5,6},{6,22},{7,23},{8,11},{9,10},... | collective-permute-start | bytes 1572872 | tf_op jit(solution)/shard_map/ppermute | solution.py:26
  5.7 15.6 %collective-permute-start.9 = (bf16[2048,128]{1,0:T(8,128)(2,1)S(1)}, bf16[2048,128]{1,0:T(8,128)(2,1)S(1)}, u32[]{:S(2)}, u32[]{:S(2)}) collective-permute-start(bf16[2048,128]{1,0:T(8,128)(2,1)S(1)} %convert_element_type.15), channel_id=1, source_target_pairs={{16,0},{17,1},{18,17},{19,16},{20,4},{21,5},{22,21},{23,20},{24,8}... | collective-permute-start | bytes 1572872 | tf_op jit(solution)/shard_map/ppermute | solution.py:26
  21.4 46.4 %collective-permute-start.12 = (bf16[2,2048,128]{2,1,0:T(8,128)(2,1)S(1)}, bf16[2,2048,128]{2,1,0:T(8,128)(2,1)S(1)}, u32[]{:S(2)}, u32[]{:S(2)}) collective-permute-start(bf16[2,2048,128]{2,1,0:T(8,128)(2,1)S(1)} %pad_maximum_fusion.2.refs_6_.refs_7_), channel_id=1, source_target_pairs={{0,12},{1,13},{2,14},{3,15},{4,0},{5,1},{6,2},{7,3},{8,4},{9,5},{1... | collective-permute-start | bytes 3145736 | tf_op jit(solution)/shard_map/ppermute | solution.py:26
  23.5 36.3 %all-to-all-start = ((bf16[4,2,512,128]{3,2,1,0:T(8,128)(2,1)}), bf16[4,2,512,128]{3,2,1,0:T(8,128)(2,1)}, u32[]{:S(2)}, u32[]{:S(2)}) async-start(bf16[4,2,512,128]{3,2,1,0:T(8,128)(2,1)} %pad_maximum_fusion.1), calls=%async_computation | async-start | bytes 2097152 | tf_op jit(solution)/shard_map/all_to_all | solution.py:186
  30.5 41.0 %collective-permute-start.10 = (bf16[2,2048,128]{2,1,0:T(8,128)(2,1)S(1)}, bf16[2,2048,128]{2,1,0:T(8,128)(2,1)S(1)}, u32[]{:S(2)}, u32[]{:S(2)}) collective-permute-start(bf16[2,2048,128]{2,1,0:T(8,128)(2,1)S(1)} %pad_maximum_fusion.2.refs_6_.refs_7_), channel_id=1, source_target_pairs={{0,4},{1,5},{2,6},{3,7},{4,8},{5,9},{6,10},{7,11},{8,12},{9,13},{1... | collective-permute-start | bytes 3145736 | tf_op jit(solution)/shard_map/ppermute | solution.py:26
  35.8 38.4 %collective-permute-start.1 = (bf16[2,2048,128]{2,1,0:T(8,128)(2,1)}, bf16[2,2048,128]{2,1,0:T(8,128)(2,1)}, u32[]{:S(2)}, u32[]{:S(2)}) collective-permute-start(bf16[2,2048,128]{2,1,0:T(8,128)(2,1)} %pad_maximum_fusion), channel_id=1, source_target_pairs={{0,1},{1,0},{2,16},{3,17},{4,5},{5,4},{6,20},{7,21},{8,9},{9,8},{1... | collective-permute-start | bytes 3145736 | tf_op jit(solution)/shard_map/ppermute | solution.py:26
  39.7 37.9 %collective-permute-start = (bf16[2,2048,128]{2,1,0:T(8,128)(2,1)}, bf16[2,2048,128]{2,1,0:T(8,128)(2,1)}, u32[]{:S(2)}, u32[]{:S(2)}) collective-permute-start(bf16[2,2048,128]{2,1,0:T(8,128)(2,1)} %pad_maximum_fusion), channel_id=1, source_target_pairs={{0,0},{1,1},{2,17},{3,16},{4,4},{5,5},{6,21},{7,20},{8,8},{9,9},{1... | collective-permute-start | bytes 3145736 | tf_op jit(solution)/shard_map/ppermute | solution.py:26
  59.8 19.0 %all-to-all-start.1 = ((f32[4,512,128]{2,1,0:T(8,128)}), f32[4,512,128]{2,1,0:T(8,128)}, u32[]{:S(2)}, u32[]{:S(2)}) async-start(f32[4,512,128]{2,1,0:T(8,128)} %bitcast.17), calls=%async_computation.1 | async-start | bytes 2097152 | tf_op jit(solution)/shard_map/all_to_all | solution.py:186
  64.1 26.0 %collective-permute-start.5 = (bf16[4,2,512,128]{3,2,1,0:T(8,128)(2,1)}, bf16[4,2,512,128]{3,2,1,0:T(8,128)(2,1)}, u32[]{:S(2)}, u32[]{:S(2)}) collective-permute-start(bf16[4,2,512,128]{3,2,1,0:T(8,128)(2,1)} %all-to-all-done), channel_id=1, source_target_pairs={{0,1},{1,0},{2,16},{3,17},{4,5},{5,4},{6,20},{7,21},{8,9},{9,8},{1... | collective-permute-start | bytes 3145736 | tf_op jit(solution)/shard_map/ppermute | solution.py:26
  67.8 27.5 %collective-permute-start.4 = (bf16[4,2,512,128]{3,2,1,0:T(8,128)(2,1)}, bf16[4,2,512,128]{3,2,1,0:T(8,128)(2,1)}, u32[]{:S(2)}, u32[]{:S(2)}) collective-permute-start(bf16[4,2,512,128]{3,2,1,0:T(8,128)(2,1)} %all-to-all-done), channel_id=1, source_target_pairs={{0,0},{1,1},{2,17},{3,16},{4,4},{5,5},{6,21},{7,20},{8,8},{9,9},{1... | collective-permute-start | bytes 3145736 | tf_op jit(solution)/shard_map/ppermute | solution.py:26
  71.4 25.8 %collective-permute-start.13 = (bf16[2048,128]{1,0:T(8,128)(2,1)}, bf16[2048,128]{1,0:T(8,128)(2,1)}, u32[]{:S(2)}, u32[]{:S(2)}) collective-permute-start(bf16[2048,128]{1,0:T(8,128)(2,1)} %slice_bitcast_fusion), channel_id=1, source_target_pairs={{0,12},{1,13},{2,14},{3,15},{4,0},{5,1},{6,2},{7,3},{8,4},{9,5},{1... | collective-permute-start | bytes 1572872 | tf_op jit(solution)/shard_map/ppermute | solution.py:26
  74.3 25.4 %collective-permute-start.11 = (bf16[2048,128]{1,0:T(8,128)(2,1)}, bf16[2048,128]{1,0:T(8,128)(2,1)}, u32[]{:S(2)}, u32[]{:S(2)}) collective-permute-start(bf16[2048,128]{1,0:T(8,128)(2,1)} %slice_bitcast_fusion.1), channel_id=1, source_target_pairs={{0,4},{1,5},{2,6},{3,7},{4,8},{5,9},{6,10},{7,11},{8,12},{9,13},{1... | collective-permute-start | bytes 1572872 | tf_op jit(solution)/shard_map/ppermute | solution.py:26
  78.7 27.5 %collective-permute-start.14 = (f32[4,512,128]{2,1,0:T(8,128)}, f32[4,512,128]{2,1,0:T(8,128)}, u32[]{:S(2)}, u32[]{:S(2)}) collective-permute-start(f32[4,512,128]{2,1,0:T(8,128)} %all-to-all-done.1), channel_id=1, source_target_pairs={{0,0},{1,1},{2,17},{3,16},{4,4},{5,5},{6,21},{7,20},{8,8},{9,9},{1... | collective-permute-start | bytes 3145736 | tf_op jit(solution)/shard_map/ppermute | solution.py:26
  90.2 16.1 %collective-permute-start.6 = (bf16[4,2,512,128]{3,2,1,0:T(8,128)(2,1)}, bf16[4,2,512,128]{3,2,1,0:T(8,128)(2,1)}, u32[]{:S(2)}, u32[]{:S(2)}) collective-permute-start(bf16[4,2,512,128]{3,2,1,0:T(8,128)(2,1)} %collective-permute-done.5.refs_1_), channel_id=1, source_target_pairs={{0,16},{1,17},{2,18},{3,19},{4,20},{5,21},{6,22},{7,23},{8,24},{9,... | collective-permute-start | bytes 3145736 | tf_op jit(solution)/shard_map/ppermute | solution.py:26
  95.3 11.0 %collective-permute-start.7 = (bf16[4,2,512,128]{3,2,1,0:T(8,128)(2,1)}, bf16[4,2,512,128]{3,2,1,0:T(8,128)(2,1)}, u32[]{:S(2)}, u32[]{:S(2)}) collective-permute-start(bf16[4,2,512,128]{3,2,1,0:T(8,128)(2,1)} %collective-permute-done.4.refs_0_), channel_id=1, source_target_pairs={{0,16},{1,17},{2,18},{3,19},{4,20},{5,21},{6,22},{7,23},{8,24},{9,... | collective-permute-start | bytes 3145736 | tf_op jit(solution)/shard_map/ppermute | solution.py:26
  97.3 27.6 %collective-permute-start.2 = (bf16[2,2048,128]{2,1,0:T(8,128)(2,1)}, bf16[2,2048,128]{2,1,0:T(8,128)(2,1)}, u32[]{:S(2)}, u32[]{:S(2)}) collective-permute-start(bf16[2,2048,128]{2,1,0:T(8,128)(2,1)} %collective-permute-done.1.refs_1_), channel_id=1, source_target_pairs={{0,16},{1,17},{2,18},{3,19},{4,20},{5,21},{6,22},{7,23},{8,24},{9,... | collective-permute-start | bytes 3145736 | tf_op jit(solution)/shard_map/ppermute | solution.py:26
  99.7 29.8 %collective-permute-start.3 = (bf16[2,2048,128]{2,1,0:T(8,128)(2,1)}, bf16[2,2048,128]{2,1,0:T(8,128)(2,1)}, u32[]{:S(2)}, u32[]{:S(2)}) collective-permute-start(bf16[2,2048,128]{2,1,0:T(8,128)(2,1)} %collective-permute-done.refs_0_), channel_id=1, source_target_pairs={{0,16},{1,17},{2,18},{3,19},{4,20},{5,21},{6,22},{7,23},{8,24},{9,... | collective-permute-start | bytes 3145736 | tf_op jit(solution)/shard_map/ppermute | solution.py:26
  111.5 18.0 %collective-permute-start.15 = (bf16[2,512,128]{2,1,0:T(8,128)(2,1)S(1)}, bf16[2,512,128]{2,1,0:T(8,128)(2,1)S(1)}, u32[]{:S(2)}, u32[]{:S(2)}) collective-permute-start(bf16[2,512,128]{2,1,0:T(8,128)(2,1)S(1)} %get-tuple-element.21), channel_id=1, source_target_pairs={{0,32},{1,33},{2,34},{3,35},{4,36},{5,37},{6,38},{7,39},{8,40},{9,... | collective-permute-start | bytes 786440 | tf_op jit(solution)/shard_map/ppermute | solution.py:26
  113.4 16.1 %collective-permute-start.16 = (bf16[2,512,128]{2,1,0:T(8,128)(2,1)S(1)}, bf16[2,512,128]{2,1,0:T(8,128)(2,1)S(1)}, u32[]{:S(2)}, u32[]{:S(2)}) collective-permute-start(bf16[2,512,128]{2,1,0:T(8,128)(2,1)S(1)} %get-tuple-element.21), channel_id=1, source_target_pairs={{32,0},{33,1},{34,2},{35,3},{36,4},{37,5},{38,6},{39,7},{40,8},{41... | collective-permute-start | bytes 786440 | tf_op jit(solution)/shard_map/ppermute | solution.py:26
  122.9 16.6 %collective-permute-start.19 = (bf16[2,512,128]{2,1,0:T(8,128)(2,1)S(1)}, bf16[2,512,128]{2,1,0:T(8,128)(2,1)S(1)}, u32[]{:S(2)}, u32[]{:S(2)}) collective-permute-start(bf16[2,512,128]{2,1,0:T(8,128)(2,1)S(1)} %get-tuple-element.27), channel_id=1, source_target_pairs={{0,32},{1,33},{2,34},{3,35},{4,36},{5,37},{6,38},{7,39},{8,40},{9,... | collective-permute-start | bytes 786440 | tf_op jit(solution)/shard_map/ppermute | solution.py:26
  124.9 14.7 %collective-permute-start.20 = (bf16[2,512,128]{2,1,0:T(8,128)(2,1)S(1)}, bf16[2,512,128]{2,1,0:T(8,128)(2,1)S(1)}, u32[]{:S(2)}, u32[]{:S(2)}) collective-permute-start(bf16[2,512,128]{2,1,0:T(8,128)(2,1)S(1)} %get-tuple-element.27), channel_id=1, source_target_pairs={{32,0},{33,1},{34,2},{35,3},{36,4},{37,5},{38,6},{39,7},{40,8},{41... | collective-permute-start | bytes 786440 | tf_op jit(solution)/shard_map/ppermute | solution.py:26
  133.9 28.2 %collective-permute-start.17 = (bf16[2048,128]{1,0:T(8,128)(2,1)S(1)}, bf16[2048,128]{1,0:T(8,128)(2,1)S(1)}, u32[]{:S(2)}, u32[]{:S(2)}) collective-permute-start(bf16[2048,128]{1,0:T(8,128)(2,1)S(1)} %get-tuple-element.23), channel_id=1, source_target_pairs={{0,8},{1,9},{2,25},{3,24},{4,12},{5,13},{6,29},{7,28},{8,0},{9,1},... | collective-permute-start | bytes 1572872 | tf_op jit(solution)/shard_map/ppermute | solution.py:26
  139.6 28.8 %copy-start.1 = (f32[1,2048,128]{2,1,0:T(8,128)S(1)}, f32[1,2048,128]{2,1,0:T(8,128)}, u32[]{:S(2)}) copy-start(f32[1,2048,128]{2,1,0:T(8,128)} %param.5) | copy-start | bytes 3145732
  144.0 12.7 %collective-permute-start.21 = (bf16[2048,128]{1,0:T(8,128)(2,1)S(1)}, bf16[2048,128]{1,0:T(8,128)(2,1)S(1)}, u32[]{:S(2)}, u32[]{:S(2)}) collective-permute-start(bf16[2048,128]{1,0:T(8,128)(2,1)S(1)} %get-tuple-element.29), channel_id=1, source_target_pairs={{0,12},{1,13},{2,29},{3,28},{4,0},{5,1},{6,17},{7,16},{8,4},{9,5},... | collective-permute-start | bytes 1572872 | tf_op jit(solution)/shard_map/ppermute | solution.py:26
  147.6 14.6 %collective-permute-start.22 = (bf16[2048,128]{1,0:T(8,128)(2,1)S(1)}, bf16[2048,128]{1,0:T(8,128)(2,1)S(1)}, u32[]{:S(2)}, u32[]{:S(2)}) collective-permute-start(bf16[2048,128]{1,0:T(8,128)(2,1)S(1)} %get-tuple-element.30), channel_id=1, source_target_pairs={{0,0},{1,1},{2,17},{3,16},{4,4},{5,5},{6,21},{7,20},{8,8},{9,9},{1... | collective-permute-start | bytes 1572872 | tf_op jit(solution)/shard_map/ppermute | solution.py:26
  151.5 16.8 %collective-permute-start.18 = (bf16[2048,128]{1,0:T(8,128)(2,1)S(1)}, bf16[2048,128]{1,0:T(8,128)(2,1)S(1)}, u32[]{:S(2)}, u32[]{:S(2)}) collective-permute-start(bf16[2048,128]{1,0:T(8,128)(2,1)S(1)} %get-tuple-element.24), channel_id=1, source_target_pairs={{0,4},{1,5},{2,21},{3,20},{4,8},{5,9},{6,25},{7,24},{8,12},{9,13},... | collective-permute-start | bytes 1572872 | tf_op jit(solution)/shard_map/ppermute | solution.py:26

commit v6 on v5

--- a/solution.py
+++ b/solution.py
@@ -30,11 +30,14 @@
     return sent(value, lambda z, core, y, x: (z + zs, core, (y + ys) % Y, x))
 
 
-def to_home(value, ys=0):
-    return sent(
-        value,
-        lambda z, core, y, x: (z, home(core, x)[0], (y + ys) % Y, home(core, x)[1]),
-    )
+def to_home(value, ys=0, itself=True):
+    def target(z, core, y, x):
+        to_core, to_x = home(core, x)
+        if to_core == core and not itself:
+            return None
+        return (z, to_core, (y + ys) % Y, to_x)
+
+    return sent(value, target)
 
 
 def to_next_plane(value, step):
@@ -47,15 +50,36 @@
 
 
 def over_x(value):
-    def partner(z, core, y, x):
-        to_core, to_x = home(core, x)
-        return (z, to_core, y, to_x ^ 1)
-
-    def swapped(part):
-        return sent(part, lambda z, core, y, x: (z, 1 - core, y, x))
-
-    near, far = to_home(value), sent(value, partner)
-    return near, far, swapped(far), swapped(near)
+    def at_home(core, x):
+        return core == x // 2
+
+    def near(z, core, y, x):
+        return (z, core, y, x ^ 1) if at_home(core, x) else (z, 1 - core, y, x ^ 3)
+
+    def far(z, core, y, x):
+        return None if at_home(core, x) else (z, 1 - core, y, x ^ 2)
+
+    def swapped(part, kept=None):
+        def target(z, core, y, x):
+            if kept is None or at_home(core, x) == kept:
+                return (z, 1 - core, y, x)
+            return None
+
+        return sent(part, target)
+
+    first, second = sent(value, near), sent(value, far)
+    return value, second, first, swapped(value, True), swapped(second, False), swapped(first)
+
+
+def in_order(at_ref, pieces):
+    own, far, near, core_own, core_far, core_near = pieces
+    kept = at_ref[2] == 1
+    return [
+        jnp.where(kept, own, far),
+        near,
+        jnp.where(kept, core_far, core_own),
+        core_near,
+    ]
 
 
 def after(value, *before):
@@ -68,11 +92,12 @@
 
 
 FIRST_GROUPS, LAST_GROUPS = (2, 1), (3, 0)
+BLOCKS = 6
 
 
 def first_kernel(groups, at_ref, *refs):
-    blocks, parts = refs[:X], refs[X : X + 2 * len(groups)]
-    rhs_ref, corr_ref, sent_ref, acc_ref = refs[X + 2 * len(groups) :]
+    blocks, parts = refs[:BLOCKS], refs[BLOCKS : BLOCKS + 2 * len(groups)]
+    rhs_ref, rhs_home_ref, corr_ref, sent_ref, acc_ref = refs[BLOCKS + 2 * len(groups) :]
     step = pl.program_id(0)
 
     @pl.when(step == 0)
@@ -81,7 +106,8 @@
 
     total = acc_ref[...]
     for side in (0, 1):
-        left = jnp.concatenate([block[0, side] for block in blocks], axis=1)
+        left = in_order(at_ref, [block[0, side] for block in blocks])
+        left = jnp.concatenate(left, axis=1)
         right = [
             jnp.concatenate(rows_in_order(at_ref, part, (0,)), axis=0)
             for part in parts[side :: 2]
@@ -96,7 +122,8 @@
             piece = acc_ref[:, i * COL : (i + 1) * COL]
             corr_ref[i] = piece
             owner = lax.rem(at_ref[0] + d, Y)
-            sent_ref[i] = (rhs_ref[owner] + piece).astype(jnp.bfloat16)
+            rhs = jnp.where(at_ref[2] == 1, rhs_ref[owner], rhs_home_ref[owner])
+            sent_ref[i] = (rhs + piece).astype(jnp.bfloat16)
 
 
 def first_level(groups, at, blocks, parts, rhs):
@@ -118,7 +145,9 @@
         grid_spec=pltpu.PrefetchScalarGridSpec(
             num_scalar_prefetch=1,
             grid=(Y,),
-            in_specs=[block] * X + [part(index) for _, index in parts] + [whole],
+            in_specs=[block] * BLOCKS
+            + [part(index) for _, index in parts]
+            + [whole, whole],
             out_specs=(out, out),
             scratch_shapes=[pltpu.VMEM((BLK, count * COL), jnp.float32)],
         ),
@@ -128,16 +157,17 @@
             bytes_accessed=8 << 20,
             transcendentals=0,
         ),
-    )(at, *blocks, *[array for array, _ in parts], rhs)
+    )(at, *blocks, *[array for array, _ in parts], *rhs)
 
 
 def second_kernel(groups, at_ref, *refs):
-    blocks = refs[:X]
-    below, above, corr_ref, *outs = refs[X:]
+    blocks = refs[:BLOCKS]
+    below, above, corr_ref, *outs = refs[BLOCKS:]
     step = pl.program_id(0)
     total = None
     for side, b_ref in ((0, below), (1, above)):
-        left = jnp.concatenate([block[side] for block in blocks], axis=1)
+        left = in_order(at_ref, [block[side] for block in blocks])
+        left = jnp.concatenate(left, axis=1)
         right = [
             jnp.concatenate(rows_in_order(at_ref, b_ref, (i,)), axis=0)
             for i in range(len(groups))
@@ -164,7 +194,7 @@
         grid_spec=pltpu.PrefetchScalarGridSpec(
             num_scalar_prefetch=1,
             grid=(Y,),
-            in_specs=[pair] * X + [whole] * 3,
+            in_specs=[pair] * BLOCKS + [whole] * 3,
             out_specs=(rows,) * count,
         ),
         compiler_params=pltpu.CompilerParams(vmem_limit_bytes=32 << 20),
@@ -179,8 +209,9 @@
 def on_device(right_sides, lower_first, upper_first, lower_second, upper_second):
     rhs = right_sides[0]
     x = lax.axis_index("x")
-    label = jnp.where(lax.axis_index("core") == x >> 1, x, X - 1 - x)
-    at = jnp.stack([lax.axis_index("y"), label]).astype(jnp.int32)
+    kept = (lax.axis_index("core") == x >> 1).astype(jnp.int32)
+    label = x ^ (2 - 2 * kept)
+    at = jnp.stack([lax.axis_index("y"), label, kept]).astype(jnp.int32)
 
     def exchanged(value):
         return lax.all_to_all(value, "y", 0, 0, tiled=True)
@@ -189,7 +220,8 @@
     firsts = jnp.stack(firsts, axis=1)
     sent_one = after(rhs, firsts).astype(jnp.bfloat16)
     own = exchanged(firsts)
-    near = jnp.stack([to_next_plane(sent_one, 1), to_next_plane(sent_one, -1)])
+    near = [to_next_plane(sent_one, 1), to_next_plane(sent_one, -1)]
+    near = after(jnp.stack(near), own)
 
     seconds = after(jnp.stack([lower_second[0], upper_second[0]]), sent_one)
     seconds = over_x(seconds)
@@ -197,7 +229,8 @@
 
     down, up = along(near, ys=1), along(near, ys=-1)
     below_far, above_far = along(down[0], ys=1), along(up[1], ys=-1)
-    rhs_rows = to_home(exchanged(after(rhs, own).reshape(Y, BLK, COL)))
+    rhs_rows = exchanged(after(rhs, own).reshape(Y, BLK, COL))
+    rhs_rows = (rhs_rows, to_home(rhs_rows, itself=False))
 
     parts = ((below_far[None], 0), (above_far[None], 0), (up, 0), (up, 1))
     corr_a, sent_a = first_level(FIRST_GROUPS, at, firsts, parts, rhs_rows)

time: 172 us -> 177 us (1.029)
  the two profiles are of different devices: /device:TPU:265 before, /device:TPU:386 now
where the time goes in v6:
time: 177 us; the launch traced here: 176 us
  starting transfers between devices  80.3 us (45%)
  waiting for transfers between devices  62.2 us (35%)
  Pallas kernels  19.5 us (11%)
  local copies, waits for them, and re-layouts  8.9 us (5%)
  other arithmetic  4.82 us (3%)
    ppermute x25, starting transfers between devices, sent(): lax.ppermute(value, AXES, [pair for pair in pairs if pair[1] is not None])  71.2 us
    ppermute x25, waiting for transfers between devices, sent(): lax.ppermute(value, AXES, [pair for pair in pairs if pair[1] is not None])  47 us
    all_to_all x2, waiting for transfers between devices, exchanged(): return lax.all_to_all(value, 'y', 0, 0, tiled=True)  15.2 us
    pallas_call x2, Pallas kernels, first_level(): pl.pallas_call(functools.partial(first_kernel, groups), name='first_level...  9.83 us
    pallas_call x2, Pallas kernels, second_level(): pl.pallas_call(functools.partial(second_kernel, groups), name='second_lev...  9.63 us
    all_to_all x2, starting transfers between devices, exchanged(): return lax.all_to_all(value, 'y', 0, 0, tiled=True)  9.1 us
    unnamed x20, local copies, waits for them, and re-layouts  5.89 us
  transfers between devices with their start and end apart: 27, of which 6 were waited for; matrix products, arithmetic and copies ran while one was open for 2% of the time, Pallas kernels for 11%

profile of v6, /device:TPU:386, one launch (start us, length us, event | category | flops | bytes accessed | tf_op | source)
XLA Modules:
  0.0 176.1 jit_solution(8019028487384806489)
XLA Ops:
  0.0 2.3 %pad_maximum_fusion.1 = bf16[4,2,512,128]{3,2,1,0:T(8,128)(2,1)} fusion(bf16[4,1,512,128]{3,2,1,0:T(8,128)(2,1)} %bitcast.22, bf16[4,1,512,128]{3,2,1,0:T(8,128)(2,1)} %bitcast.23), kind=kLoop, calls=%fused_computation.1 | loop fusion | flops 524288 | bytes 2097152 | tf_op jit(solution)/shard_map/stack | solution.py:220
  2.3 4.6 %all-to-all-start = ((bf16[4,2,512,128]{3,2,1,0:T(8,128)(2,1)}), bf16[4,2,512,128]{3,2,1,0:T(8,128)(2,1)S(1)}, u32[]{:S(2)}, u32[]{:S(2)}) async-start(bf16[4,2,512,128]{3,2,1,0:T(8,128)(2,1)} %pad_maximum_fusion.1), calls=%async_computation | async-start | bytes 2097152 | tf_op jit(solution)/shard_map/all_to_all | solution.py:217
  6.9 3.5 %collective-permute-start.10 = (bf16[2048,128]{1,0:T(8,128)(2,1)S(1)}, bf16[2048,128]{1,0:T(8,128)(2,1)S(1)}, u32[]{:S(2)}, u32[]{:S(2)}) collective-permute-start(bf16[2048,128]{1,0:T(8,128)(2,1)S(1)} %convert_element_type.16), channel_id=1, source_target_pairs={{0,3},{1,2},{2,18},{3,19},{4,7},{5,6},{6,22},{7,23},{8,11},{9,10},... | collective-permute-start | bytes 1572872 | tf_op jit(solution)/shard_map/ppermute | solution.py:26
  10.5 3.6 %collective-permute-start.11 = (bf16[2048,128]{1,0:T(8,128)(2,1)S(1)}, bf16[2048,128]{1,0:T(8,128)(2,1)S(1)}, u32[]{:S(2)}, u32[]{:S(2)}) collective-permute-start(bf16[2048,128]{1,0:T(8,128)(2,1)S(1)} %convert_element_type.16), channel_id=1, source_target_pairs={{16,0},{17,1},{18,17},{19,16},{20,4},{21,5},{22,21},{23,20},{24,8}... | collective-permute-start | bytes 1572872 | tf_op jit(solution)/shard_map/ppermute | solution.py:26
  16.8 17.2 %collective-permute-done.10 = bf16[2048,128]{1,0:T(8,128)(2,1)S(1)} collective-permute-done((bf16[2048,128]{1,0:T(8,128)(2,1)S(1)}, bf16[2048,128]{1,0:T(8,128)(2,1)S(1)}, u32[]{:S(2)}, u32[]{:S(2)}) %collective-permute-start.10) | collective-permute-done | bytes 524320 | tf_op jit(solution)/shard_map/ppermute | solution.py:26
  34.1 5.1 %collective-permute-start.14 = (bf16[2,2048,128]{2,1,0:T(8,128)(2,1)S(1)}, bf16[2,2048,128]{2,1,0:T(8,128)(2,1)}, u32[]{:S(2)}, u32[]{:S(2)}) collective-permute-start(bf16[2,2048,128]{2,1,0:T(8,128)(2,1)S(1)} %pad_maximum_fusion.2.refs_8_.refs_9_), channel_id=1, source_target_pairs={{0,12},{1,13},{2,14},{3,15},{4,0},{5,1},{6,2},{7,3},{8,4},{9,5},{1... | collective-permute-start | bytes 3145736 | tf_op jit(solution)/shard_map/ppermute | solution.py:26
  39.3 3.7 %collective-permute-start.1 = (bf16[2,2048,128]{2,1,0:T(8,128)(2,1)}, bf16[2,2048,128]{2,1,0:T(8,128)(2,1)}, u32[]{:S(2)}, u32[]{:S(2)}) collective-permute-start(bf16[2,2048,128]{2,1,0:T(8,128)(2,1)} %pad_maximum_fusion.refs_0_), channel_id=1, source_target_pairs={{0,1},{1,0},{2,17},{3,16},{4,5},{5,4},{6,21},{7,20},{8,9},{9,8},{1... | collective-permute-start | bytes 3145736 | tf_op jit(solution)/shard_map/ppermute | solution.py:26
  43.0 1.9 %collective-permute-start.12 = (bf16[2,2048,128]{2,1,0:T(8,128)(2,1)S(1)}, bf16[2,2048,128]{2,1,0:T(8,128)(2,1)}, u32[]{:S(2)}, u32[]{:S(2)}) collective-permute-start(bf16[2,2048,128]{2,1,0:T(8,128)(2,1)S(1)} %pad_maximum_fusion.2.refs_8_.refs_9_), channel_id=1, source_target_pairs={{0,4},{1,5},{2,6},{3,7},{4,8},{5,9},{6,10},{7,11},{8,12},{9,13},{1... | collective-permute-start | bytes 3145736 | tf_op jit(solution)/shard_map/ppermute | solution.py:26
  44.9 4.5 %all-to-all-start.1 = ((f32[4,512,128]{2,1,0:T(8,128)}), f32[4,512,128]{2,1,0:T(8,128)S(1)}, u32[]{:S(2)}, u32[]{:S(2)}) async-start(f32[4,512,128]{2,1,0:T(8,128)} %bitcast.20), calls=%async_computation.1 | async-start | bytes 2097152 | tf_op jit(solution)/shard_map/all_to_all | solution.py:217
  51.1 2.1 %collective-permute-start.6 = (bf16[4,2,512,128]{3,2,1,0:T(8,128)(2,1)S(1)}, bf16[4,2,512,128]{3,2,1,0:T(8,128)(2,1)}, u32[]{:S(2)}, u32[]{:S(2)}) collective-permute-start(bf16[4,2,512,128]{3,2,1,0:T(8,128)(2,1)S(1)} %all-to-all-done.refs_0_), channel_id=1, source_target_pairs={{0,1},{1,0},{2,17},{3,16},{4,5},{5,4},{6,21},{7,20},{8,9},{9,8},{1... | collective-permute-start | bytes 3145736 | tf_op jit(solution)/shard_map/ppermute | solution.py:26
  53.2 9.3 %collective-permute-done.14.refs_8_.refs_9_ = bf16[2,2048,128]{2,1,0:T(8,128)(2,1)} collective-permute-done((bf16[2,2048,128]{2,1,0:T(8,128)(2,1)S(1)}, bf16[2,2048,128]{2,1,0:T(8,128)(2,1)}, u32[]{:S(2)}, u32[]{:S(2)}) %collective-permute-start.14) | collective-permute-done | bytes 1048608 | tf_op jit(solution)/shard_map/ppermute | solution.py:26
  62.6 3.5 %collective-permute-start.7 = (bf16[4,2,512,128]{3,2,1,0:T(8,128)(2,1)S(1)}, bf16[4,2,512,128]{3,2,1,0:T(8,128)(2,1)}, u32[]{:S(2)}, u32[]{:S(2)}) collective-permute-start(bf16[4,2,512,128]{3,2,1,0:T(8,128)(2,1)S(1)} %all-to-all-done.refs_0_), channel_id=1, source_target_pairs={{0,16},{1,17},{4,20},{5,21},{8,24},{9,25},{12,28},{13,29},{18,2},{... | collective-permute-start | bytes 3145736 | tf_op jit(solution)/shard_map/ppermute | solution.py:26
  66.1 1.9 %slice_bitcast_fusion = bf16[2048,128]{1,0:T(8,128)(2,1)} fusion(bf16[2,2048,128]{2,1,0:T(8,128)(2,1)} %collective-permute-done.14.refs_8_.refs_9_), kind=kLoop, calls=%fused_computation.4 | loop fusion | bytes 1048576 | tf_op jit(solution)/shard_map/squeeze | solution.py:231
  68.0 15.2 %all-to-all-done.1.refs_10_ = f32[4,512,128]{2,1,0:T(8,128)S(1)} async-done(((f32[4,512,128]{2,1,0:T(8,128)}), f32[4,512,128]{2,1,0:T(8,128)S(1)}, u32[]{:S(2)}, u32[]{:S(2)}) %all-to-all-start.1) | async-done | bytes 1048608 | tf_op jit(solution)/shard_map/all_to_all | solution.py:217
  86.9 3.9 %collective-permute-start.13 = (bf16[2048,128]{1,0:T(8,128)(2,1)S(1)}, bf16[2048,128]{1,0:T(8,128)(2,1)S(1)}, u32[]{:S(2)}, u32[]{:S(2)}) collective-permute-start(bf16[2048,128]{1,0:T(8,128)(2,1)S(1)} %slice_bitcast_fusion.1), channel_id=1, source_target_pairs={{0,4},{1,5},{2,6},{3,7},{4,8},{5,9},{6,10},{7,11},{8,12},{9,13},{1... | collective-permute-start | bytes 1572872 | tf_op jit(solution)/shard_map/ppermute | solution.py:26
  92.2 4.0 %collective-permute-start.9 = (bf16[4,2,512,128]{3,2,1,0:T(8,128)(2,1)}, bf16[4,2,512,128]{3,2,1,0:T(8,128)(2,1)}, u32[]{:S(2)}, u32[]{:S(2)}) collective-permute-start(bf16[4,2,512,128]{3,2,1,0:T(8,128)(2,1)} %collective-permute-done.6.refs_2_), channel_id=1, source_target_pairs={{0,16},{1,17},{2,18},{3,19},{4,20},{5,21},{6,22},{7,23},{8,24},{9,... | collective-permute-start | bytes 3145736 | tf_op jit(solution)/shard_map/ppermute | solution.py:26
  96.2 4.5 %collective-permute-done.15 = bf16[2048,128]{1,0:T(8,128)(2,1)S(1)} collective-permute-done((bf16[2048,128]{1,0:T(8,128)(2,1)}, bf16[2048,128]{1,0:T(8,128)(2,1)S(1)}, u32[]{:S(2)}, u32[]{:S(2)}) %collective-permute-start.15) | collective-permute-done | bytes 524320 | tf_op jit(solution)/shard_map/ppermute | solution.py:26
  101.5 3.3 %collective-permute-start.2 = (bf16[2,2048,128]{2,1,0:T(8,128)(2,1)}, bf16[2,2048,128]{2,1,0:T(8,128)(2,1)}, u32[]{:S(2)}, u32[]{:S(2)}) collective-permute-start(bf16[2,2048,128]{2,1,0:T(8,128)(2,1)} %pad_maximum_fusion.refs_0_), channel_id=1, source_target_pairs={{0,16},{1,17},{4,20},{5,21},{8,24},{9,25},{12,28},{13,29},{18,2},{... | collective-permute-start | bytes 3145736 | tf_op jit(solution)/shard_map/ppermute | solution.py:26
  107.8 4.0 %collective-permute-start.4 = (bf16[2,2048,128]{2,1,0:T(8,128)(2,1)}, bf16[2,2048,128]{2,1,0:T(8,128)(2,1)}, u32[]{:S(2)}, u32[]{:S(2)}) collective-permute-start(bf16[2,2048,128]{2,1,0:T(8,128)(2,1)} %collective-permute-done.1.refs_2_), channel_id=1, source_target_pairs={{0,16},{1,17},{2,18},{3,19},{4,20},{5,21},{6,22},{7,23},{8,24},{9,... | collective-permute-start | bytes 3145736 | tf_op jit(solution)/shard_map/ppermute | solution.py:26
  115.2 4.9 %first_level.2 = (f32[2,512,128]{2,1,0:T(8,128)S(1)}, bf16[2,512,128]{2,1,0:T(8,128)(2,1)S(1)}) custom-call(s32[3]{0:T(128)S(1)} %pad_add_fusion.at_ref, bf16[4,2,512,128]{3,2,1,0:T(8,128)(2,1)S(1)} %all-to-all-done.refs_0_, bf16[4,2,512,128]{3,2,1,0:T(8,128)(2,1)} %collective-permute-done.5.refs_1_, ...), custom_call_target="tpu_custom_call" | custom-call | flops 1073741824 | bytes 8388608 | tf_op jit(solution)/shard_map/first_level/pallas_call | solution.py:138
  120.1 2.9 %collective-permute-start.17 = (bf16[2,512,128]{2,1,0:T(8,128)(2,1)S(1)}, bf16[2,512,128]{2,1,0:T(8,128)(2,1)S(1)}, u32[]{:S(2)}, u32[]{:S(2)}) collective-permute-start(bf16[2,512,128]{2,1,0:T(8,128)(2,1)S(1)} %get-tuple-element.23), channel_id=1, source_target_pairs={{0,32},{1,33},{2,34},{3,35},{4,36},{5,37},{6,38},{7,39},{8,40},{9,... | collective-permute-start | bytes 786440 | tf_op jit(solution)/shard_map/ppermute | solution.py:26
  123.1 4.1 %collective-permute-start.18 = (bf16[2,512,128]{2,1,0:T(8,128)(2,1)S(1)}, bf16[2,512,128]{2,1,0:T(8,128)(2,1)S(1)}, u32[]{:S(2)}, u32[]{:S(2)}) collective-permute-start(bf16[2,512,128]{2,1,0:T(8,128)(2,1)S(1)} %get-tuple-element.23), channel_id=1, source_target_pairs={{32,0},{33,1},{34,2},{35,3},{36,4},{37,5},{38,6},{39,7},{40,8},{41... | collective-permute-start | bytes 786440 | tf_op jit(solution)/shard_map/ppermute | solution.py:26
  127.2 4.9 %first_level.3 = (f32[2,512,128]{2,1,0:T(8,128)S(1)}, bf16[2,512,128]{2,1,0:T(8,128)(2,1)S(1)}) custom-call(s32[3]{0:T(128)S(1)} %pad_add_fusion.at_ref, bf16[4,2,512,128]{3,2,1,0:T(8,128)(2,1)S(1)} %all-to-all-done.refs_0_, bf16[4,2,512,128]{3,2,1,0:T(8,128)(2,1)} %collective-permute-done.5.refs_1_, ...), custom_call_target="tpu_custom_call" | custom-call | flops 1073741824 | bytes 8388608 | tf_op jit(solution)/shard_map/first_level/pallas_call | solution.py:138
  132.1 1.9 %collective-permute-start.21 = (bf16[2,512,128]{2,1,0:T(8,128)(2,1)S(1)}, bf16[2,512,128]{2,1,0:T(8,128)(2,1)S(1)}, u32[]{:S(2)}, u32[]{:S(2)}) collective-permute-start(bf16[2,512,128]{2,1,0:T(8,128)(2,1)S(1)} %get-tuple-element.29), channel_id=1, source_target_pairs={{0,32},{1,33},{2,34},{3,35},{4,36},{5,37},{6,38},{7,39},{8,40},{9,... | collective-permute-start | bytes 786440 | tf_op jit(solution)/shard_map/ppermute | solution.py:26
  134.1 5.1 %collective-permute-start.22 = (bf16[2,512,128]{2,1,0:T(8,128)(2,1)S(1)}, bf16[2,512,128]{2,1,0:T(8,128)(2,1)S(1)}, u32[]{:S(2)}, u32[]{:S(2)}) collective-permute-start(bf16[2,512,128]{2,1,0:T(8,128)(2,1)S(1)} %get-tuple-element.29), channel_id=1, source_target_pairs={{32,0},{33,1},{34,2},{35,3},{36,4},{37,5},{38,6},{39,7},{40,8},{41... | collective-permute-start | bytes 786440 | tf_op jit(solution)/shard_map/ppermute | solution.py:26
  139.2 4.8 %second_level.2 = (bf16[2048,128]{1,0:T(8,128)(2,1)S(1)}, bf16[2048,128]{1,0:T(8,128)(2,1)S(1)}) custom-call(s32[3]{0:T(128)S(1)} %pad_add_fusion.at_ref, bf16[2,2048,128]{2,1,0:T(8,128)(2,1)} %pad_maximum_fusion.refs_0_, bf16[2,2048,128]{2,1,0:T(8,128)(2,1)} %collective-permute-done.refs_1_, bf16[2,2048,128]{2,1,0:T(8,128)(2,1)} %collective-permute-done.1.refs_2_, ...), custom_call_target="tpu_custom_call" | custom-call | flops 1073741824 | bytes 6291456 | tf_op jit(solution)/shard_map/second_level/pallas_call | solution.py:190
  144.1 2.7 %collective-permute-start.19 = (bf16[2048,128]{1,0:T(8,128)(2,1)S(1)}, bf16[2048,128]{1,0:T(8,128)(2,1)S(1)}, u32[]{:S(2)}, u32[]{:S(2)}) collective-permute-start(bf16[2048,128]{1,0:T(8,128)(2,1)S(1)} %get-tuple-element.25), channel_id=1, source_target_pairs={{0,8},{1,9},{2,25},{3,24},{4,12},{5,13},{6,29},{7,28},{8,0},{9,1},... | collective-permute-start | bytes 1572872 | tf_op jit(solution)/shard_map/ppermute | solution.py:26
  146.9 4.8 %second_level.3 = (bf16[2048,128]{1,0:T(8,128)(2,1)S(1)}, bf16[2048,128]{1,0:T(8,128)(2,1)S(1)}) custom-call(s32[3]{0:T(128)S(1)} %pad_add_fusion.at_ref, bf16[2,2048,128]{2,1,0:T(8,128)(2,1)} %pad_maximum_fusion.refs_0_, bf16[2,2048,128]{2,1,0:T(8,128)(2,1)} %collective-permute-done.refs_1_, bf16[2,2048,128]{2,1,0:T(8,128)(2,1)} %collective-permute-done.1.refs_2_, ...), custom_call_target="tpu_custom_call" | custom-call | flops 1073741824 | bytes 6291456 | tf_op jit(solution)/shard_map/second_level/pallas_call | solution.py:190
  151.7 4.6 %collective-permute-start.23 = (bf16[2048,128]{1,0:T(8,128)(2,1)S(1)}, bf16[2048,128]{1,0:T(8,128)(2,1)S(1)}, u32[]{:S(2)}, u32[]{:S(2)}) collective-permute-start(bf16[2048,128]{1,0:T(8,128)(2,1)S(1)} %get-tuple-element.31), channel_id=1, source_target_pairs={{0,12},{1,13},{2,29},{3,28},{4,0},{5,1},{6,17},{7,16},{8,4},{9,5},... | collective-permute-start | bytes 1572872 | tf_op jit(solution)/shard_map/ppermute | solution.py:26
  156.9 1.9 %collective-permute-start.20 = (bf16[2048,128]{1,0:T(8,128)(2,1)S(1)}, bf16[2048,128]{1,0:T(8,128)(2,1)S(1)}, u32[]{:S(2)}, u32[]{:S(2)}) collective-permute-start(bf16[2048,128]{1,0:T(8,128)(2,1)S(1)} %get-tuple-element.26), channel_id=1, source_target_pairs={{0,4},{1,5},{2,21},{3,20},{4,8},{5,9},{6,25},{7,24},{8,12},{9,13},... | collective-permute-start | bytes 1572872 | tf_op jit(solution)/shard_map/ppermute | solution.py:26
  158.9 12.3 %collective-permute-done.23 = bf16[2048,128]{1,0:T(8,128)(2,1)S(1)} collective-permute-done((bf16[2048,128]{1,0:T(8,128)(2,1)S(1)}, bf16[2048,128]{1,0:T(8,128)(2,1)S(1)}, u32[]{:S(2)}, u32[]{:S(2)}) %collective-permute-start.23) | collective-permute-done | bytes 524320 | tf_op jit(solution)/shard_map/ppermute | solution.py:26
  171.2 3.6 %collective-permute-done.20 = bf16[2048,128]{1,0:T(8,128)(2,1)S(1)} collective-permute-done((bf16[2048,128]{1,0:T(8,128)(2,1)S(1)}, bf16[2048,128]{1,0:T(8,128)(2,1)S(1)}, u32[]{:S(2)}, u32[]{:S(2)}) %collective-permute-start.20) | collective-permute-done | bytes 524320 | tf_op jit(solution)/shard_map/ppermute | solution.py:26
  (54 shorter events, 18.8 us)
Async XLA Ops:
  2.3 4.6 %copy-start.6 = (f32[1,2048,128]{2,1,0:T(8,128)S(1)}, f32[1,2048,128]{2,1,0:T(8,128)}, u32[]{:S(2)}) copy-start(f32[1,2048,128]{2,1,0:T(8,128)} %param.5) | copy-start | bytes 3145732
  2.3 31.8 %all-to-all-start = ((bf16[4,2,512,128]{3,2,1,0:T(8,128)(2,1)}), bf16[4,2,512,128]{3,2,1,0:T(8,128)(2,1)S(1)}, u32[]{:S(2)}, u32[]{:S(2)}) async-start(bf16[4,2,512,128]{3,2,1,0:T(8,128)(2,1)} %pad_maximum_fusion.1), calls=%async_computation | async-start | bytes 2097152 | tf_op jit(solution)/shard_map/all_to_all | solution.py:217
  6.9 7.2 %copy-start.8 = (bf16[1,2048,128]{2,1,0:T(8,128)(2,1)S(1)}, bf16[1,2048,128]{2,1,0:T(8,128)(2,1)}, u32[]{:S(2)}) copy-start(bf16[1,2048,128]{2,1,0:T(8,128)(2,1)} %param.9) | copy-start | bytes 1572868
  6.9 7.2 %copy-start.9 = (bf16[1,2048,128]{2,1,0:T(8,128)(2,1)S(1)}, bf16[1,2048,128]{2,1,0:T(8,128)(2,1)}, u32[]{:S(2)}) copy-start(bf16[1,2048,128]{2,1,0:T(8,128)(2,1)} %param.8) | copy-start | bytes 1572868
  6.9 27.1 %collective-permute-start.10 = (bf16[2048,128]{1,0:T(8,128)(2,1)S(1)}, bf16[2048,128]{1,0:T(8,128)(2,1)S(1)}, u32[]{:S(2)}, u32[]{:S(2)}) collective-permute-start(bf16[2048,128]{1,0:T(8,128)(2,1)S(1)} %convert_element_type.16), channel_id=1, source_target_pairs={{0,3},{1,2},{2,18},{3,19},{4,7},{5,6},{6,22},{7,23},{8,11},{9,10},... | collective-permute-start | bytes 1572872 | tf_op jit(solution)/shard_map/ppermute | solution.py:26
  10.5 23.5 %collective-permute-start.11 = (bf16[2048,128]{1,0:T(8,128)(2,1)S(1)}, bf16[2048,128]{1,0:T(8,128)(2,1)S(1)}, u32[]{:S(2)}, u32[]{:S(2)}) collective-permute-start(bf16[2048,128]{1,0:T(8,128)(2,1)S(1)} %convert_element_type.16), channel_id=1, source_target_pairs={{16,0},{17,1},{18,17},{19,16},{20,4},{21,5},{22,21},{23,20},{24,8}... | collective-permute-start | bytes 1572872 | tf_op jit(solution)/shard_map/ppermute | solution.py:26
  15.2 35.9 %collective-permute-start = (bf16[2,2048,128]{2,1,0:T(8,128)(2,1)}, bf16[2,2048,128]{2,1,0:T(8,128)(2,1)}, u32[]{:S(2)}, u32[]{:S(2)}) collective-permute-start(bf16[2,2048,128]{2,1,0:T(8,128)(2,1)} %pad_maximum_fusion.refs_0_), channel_id=1, source_target_pairs={{2,16},{3,17},{6,20},{7,21},{10,24},{11,25},{14,28},{15,29},{16,2}... | collective-permute-start | bytes 3145736 | tf_op jit(solution)/shard_map/ppermute | solution.py:26
  34.1 28.4 %collective-permute-start.14 = (bf16[2,2048,128]{2,1,0:T(8,128)(2,1)S(1)}, bf16[2,2048,128]{2,1,0:T(8,128)(2,1)}, u32[]{:S(2)}, u32[]{:S(2)}) collective-permute-start(bf16[2,2048,128]{2,1,0:T(8,128)(2,1)S(1)} %pad_maximum_fusion.2.refs_8_.refs_9_), channel_id=1, source_target_pairs={{0,12},{1,13},{2,14},{3,15},{4,0},{5,1},{6,2},{7,3},{8,4},{9,5},{1... | collective-permute-start | bytes 3145736 | tf_op jit(solution)/shard_map/ppermute | solution.py:26
  39.3 28.7 %collective-permute-start.1 = (bf16[2,2048,128]{2,1,0:T(8,128)(2,1)}, bf16[2,2048,128]{2,1,0:T(8,128)(2,1)}, u32[]{:S(2)}, u32[]{:S(2)}) collective-permute-start(bf16[2,2048,128]{2,1,0:T(8,128)(2,1)} %pad_maximum_fusion.refs_0_), channel_id=1, source_target_pairs={{0,1},{1,0},{2,17},{3,16},{4,5},{5,4},{6,21},{7,20},{8,9},{9,8},{1... | collective-permute-start | bytes 3145736 | tf_op jit(solution)/shard_map/ppermute | solution.py:26
  43.0 40.9 %collective-permute-start.12 = (bf16[2,2048,128]{2,1,0:T(8,128)(2,1)S(1)}, bf16[2,2048,128]{2,1,0:T(8,128)(2,1)}, u32[]{:S(2)}, u32[]{:S(2)}) collective-permute-start(bf16[2,2048,128]{2,1,0:T(8,128)(2,1)S(1)} %pad_maximum_fusion.2.refs_8_.refs_9_), channel_id=1, source_target_pairs={{0,4},{1,5},{2,6},{3,7},{4,8},{5,9},{6,10},{7,11},{8,12},{9,13},{1... | collective-permute-start | bytes 3145736 | tf_op jit(solution)/shard_map/ppermute | solution.py:26
  44.9 38.3 %all-to-all-start.1 = ((f32[4,512,128]{2,1,0:T(8,128)}), f32[4,512,128]{2,1,0:T(8,128)S(1)}, u32[]{:S(2)}, u32[]{:S(2)}) async-start(f32[4,512,128]{2,1,0:T(8,128)} %bitcast.20), calls=%async_computation.1 | async-start | bytes 2097152 | tf_op jit(solution)/shard_map/all_to_all | solution.py:217
  49.4 37.5 %collective-permute-start.5 = (bf16[4,2,512,128]{3,2,1,0:T(8,128)(2,1)S(1)}, bf16[4,2,512,128]{3,2,1,0:T(8,128)(2,1)}, u32[]{:S(2)}, u32[]{:S(2)}) collective-permute-start(bf16[4,2,512,128]{3,2,1,0:T(8,128)(2,1)S(1)} %all-to-all-done.refs_0_), channel_id=1, source_target_pairs={{2,16},{3,17},{6,20},{7,21},{10,24},{11,25},{14,28},{15,29},{16,2}... | collective-permute-start | bytes 3145736 | tf_op jit(solution)/shard_map/ppermute | solution.py:26
  51.1 39.8 %collective-permute-start.6 = (bf16[4,2,512,128]{3,2,1,0:T(8,128)(2,1)S(1)}, bf16[4,2,512,128]{3,2,1,0:T(8,128)(2,1)}, u32[]{:S(2)}, u32[]{:S(2)}) collective-permute-start(bf16[4,2,512,128]{3,2,1,0:T(8,128)(2,1)S(1)} %all-to-all-done.refs_0_), channel_id=1, source_target_pairs={{0,1},{1,0},{2,17},{3,16},{4,5},{5,4},{6,21},{7,20},{8,9},{9,8},{1... | collective-permute-start | bytes 3145736 | tf_op jit(solution)/shard_map/ppermute | solution.py:26
  62.6 29.6 %collective-permute-start.7 = (bf16[4,2,512,128]{3,2,1,0:T(8,128)(2,1)S(1)}, bf16[4,2,512,128]{3,2,1,0:T(8,128)(2,1)}, u32[]{:S(2)}, u32[]{:S(2)}) collective-permute-start(bf16[4,2,512,128]{3,2,1,0:T(8,128)(2,1)S(1)} %all-to-all-done.refs_0_), channel_id=1, source_target_pairs={{0,16},{1,17},{4,20},{5,21},{8,24},{9,25},{12,28},{13,29},{18,2},{... | collective-permute-start | bytes 3145736 | tf_op jit(solution)/shard_map/ppermute | solution.py:26
  83.2 23.6 %collective-permute-start.16 = (f32[4,512,128]{2,1,0:T(8,128)S(1)}, f32[4,512,128]{2,1,0:T(8,128)S(1)}, u32[]{:S(2)}, u32[]{:S(2)}) collective-permute-start(f32[4,512,128]{2,1,0:T(8,128)S(1)} %all-to-all-done.1.refs_10_), channel_id=1, source_target_pairs={{2,17},{3,16},{6,21},{7,20},{10,25},{11,24},{14,29},{15,28},{16,3}... | collective-permute-start | bytes 3145736 | tf_op jit(solution)/shard_map/ppermute | solution.py:26
  83.9 16.7 %collective-permute-start.15 = (bf16[2048,128]{1,0:T(8,128)(2,1)}, bf16[2048,128]{1,0:T(8,128)(2,1)S(1)}, u32[]{:S(2)}, u32[]{:S(2)}) collective-permute-start(bf16[2048,128]{1,0:T(8,128)(2,1)} %slice_bitcast_fusion), channel_id=1, source_target_pairs={{0,12},{1,13},{2,14},{3,15},{4,0},{5,1},{6,2},{7,3},{8,4},{9,5},{1... | collective-permute-start | bytes 1572872 | tf_op jit(solution)/shard_map/ppermute | solution.py:26
  86.9 17.8 %collective-permute-start.13 = (bf16[2048,128]{1,0:T(8,128)(2,1)S(1)}, bf16[2048,128]{1,0:T(8,128)(2,1)S(1)}, u32[]{:S(2)}, u32[]{:S(2)}) collective-permute-start(bf16[2048,128]{1,0:T(8,128)(2,1)S(1)} %slice_bitcast_fusion.1), channel_id=1, source_target_pairs={{0,4},{1,5},{2,6},{3,7},{4,8},{5,9},{6,10},{7,11},{8,12},{9,13},{1... | collective-permute-start | bytes 1572872 | tf_op jit(solution)/shard_map/ppermute | solution.py:26
  90.9 21.0 %collective-permute-start.8 = (bf16[4,2,512,128]{3,2,1,0:T(8,128)(2,1)}, bf16[4,2,512,128]{3,2,1,0:T(8,128)(2,1)}, u32[]{:S(2)}, u32[]{:S(2)}) collective-permute-start(bf16[4,2,512,128]{3,2,1,0:T(8,128)(2,1)} %collective-permute-done.5.refs_1_), channel_id=1, source_target_pairs={{2,18},{3,19},{6,22},{7,23},{10,26},{11,27},{14,30},{15,31},{16,0}... | collective-permute-start | bytes 3145736 | tf_op jit(solution)/shard_map/ppermute | solution.py:26
  92.2 19.7 %collective-permute-start.9 = (bf16[4,2,512,128]{3,2,1,0:T(8,128)(2,1)}, bf16[4,2,512,128]{3,2,1,0:T(8,128)(2,1)}, u32[]{:S(2)}, u32[]{:S(2)}) collective-permute-start(bf16[4,2,512,128]{3,2,1,0:T(8,128)(2,1)} %collective-permute-done.6.refs_2_), channel_id=1, source_target_pairs={{0,16},{1,17},{2,18},{3,19},{4,20},{5,21},{6,22},{7,23},{8,24},{9,... | collective-permute-start | bytes 3145736 | tf_op jit(solution)/shard_map/ppermute | solution.py:26
  101.5 30.7 %collective-permute-start.2 = (bf16[2,2048,128]{2,1,0:T(8,128)(2,1)}, bf16[2,2048,128]{2,1,0:T(8,128)(2,1)}, u32[]{:S(2)}, u32[]{:S(2)}) collective-permute-start(bf16[2,2048,128]{2,1,0:T(8,128)(2,1)} %pad_maximum_fusion.refs_0_), channel_id=1, source_target_pairs={{0,16},{1,17},{4,20},{5,21},{8,24},{9,25},{12,28},{13,29},{18,2},{... | collective-permute-start | bytes 3145736 | tf_op jit(solution)/shard_map/ppermute | solution.py:26
  105.5 28.5 %collective-permute-start.3 = (bf16[2,2048,128]{2,1,0:T(8,128)(2,1)}, bf16[2,2048,128]{2,1,0:T(8,128)(2,1)}, u32[]{:S(2)}, u32[]{:S(2)}) collective-permute-start(bf16[2,2048,128]{2,1,0:T(8,128)(2,1)} %collective-permute-done.refs_1_), channel_id=1, source_target_pairs={{2,18},{3,19},{6,22},{7,23},{10,26},{11,27},{14,30},{15,31},{16,0}... | collective-permute-start | bytes 3145736 | tf_op jit(solution)/shard_map/ppermute | solution.py:26
  107.8 31.4 %collective-permute-start.4 = (bf16[2,2048,128]{2,1,0:T(8,128)(2,1)}, bf16[2,2048,128]{2,1,0:T(8,128)(2,1)}, u32[]{:S(2)}, u32[]{:S(2)}) collective-permute-start(bf16[2,2048,128]{2,1,0:T(8,128)(2,1)} %collective-permute-done.1.refs_2_), channel_id=1, source_target_pairs={{0,16},{1,17},{2,18},{3,19},{4,20},{5,21},{6,22},{7,23},{8,24},{9,... | collective-permute-start | bytes 3145736 | tf_op jit(solution)/shard_map/ppermute | solution.py:26
  111.9 1.2 copy-start.1
  120.1 19.1 %collective-permute-start.17 = (bf16[2,512,128]{2,1,0:T(8,128)(2,1)S(1)}, bf16[2,512,128]{2,1,0:T(8,128)(2,1)S(1)}, u32[]{:S(2)}, u32[]{:S(2)}) collective-permute-start(bf16[2,512,128]{2,1,0:T(8,128)(2,1)S(1)} %get-tuple-element.23), channel_id=1, source_target_pairs={{0,32},{1,33},{2,34},{3,35},{4,36},{5,37},{6,38},{7,39},{8,40},{9,... | collective-permute-start | bytes 786440 | tf_op jit(solution)/shard_map/ppermute | solution.py:26
  123.1 16.2 %collective-permute-start.18 = (bf16[2,512,128]{2,1,0:T(8,128)(2,1)S(1)}, bf16[2,512,128]{2,1,0:T(8,128)(2,1)S(1)}, u32[]{:S(2)}, u32[]{:S(2)}) collective-permute-start(bf16[2,512,128]{2,1,0:T(8,128)(2,1)S(1)} %get-tuple-element.23), channel_id=1, source_target_pairs={{32,0},{33,1},{34,2},{35,3},{36,4},{37,5},{38,6},{39,7},{40,8},{41... | collective-permute-start | bytes 786440 | tf_op jit(solution)/shard_map/ppermute | solution.py:26
  132.1 14.7 %collective-permute-start.21 = (bf16[2,512,128]{2,1,0:T(8,128)(2,1)S(1)}, bf16[2,512,128]{2,1,0:T(8,128)(2,1)S(1)}, u32[]{:S(2)}, u32[]{:S(2)}) collective-permute-start(bf16[2,512,128]{2,1,0:T(8,128)(2,1)S(1)} %get-tuple-element.29), channel_id=1, source_target_pairs={{0,32},{1,33},{2,34},{3,35},{4,36},{5,37},{6,38},{7,39},{8,40},{9,... | collective-permute-start | bytes 786440 | tf_op jit(solution)/shard_map/ppermute | solution.py:26
  134.1 12.8 %collective-permute-start.22 = (bf16[2,512,128]{2,1,0:T(8,128)(2,1)S(1)}, bf16[2,512,128]{2,1,0:T(8,128)(2,1)S(1)}, u32[]{:S(2)}, u32[]{:S(2)}) collective-permute-start(bf16[2,512,128]{2,1,0:T(8,128)(2,1)S(1)} %get-tuple-element.29), channel_id=1, source_target_pairs={{32,0},{33,1},{34,2},{35,3},{36,4},{37,5},{38,6},{39,7},{40,8},{41... | collective-permute-start | bytes 786440 | tf_op jit(solution)/shard_map/ppermute | solution.py:26
  144.1 27.1 %collective-permute-start.19 = (bf16[2048,128]{1,0:T(8,128)(2,1)S(1)}, bf16[2048,128]{1,0:T(8,128)(2,1)S(1)}, u32[]{:S(2)}, u32[]{:S(2)}) collective-permute-start(bf16[2048,128]{1,0:T(8,128)(2,1)S(1)} %get-tuple-element.25), channel_id=1, source_target_pairs={{0,8},{1,9},{2,25},{3,24},{4,12},{5,13},{6,29},{7,28},{8,0},{9,1},... | collective-permute-start | bytes 1572872 | tf_op jit(solution)/shard_map/ppermute | solution.py:26
  146.8 28.0 %copy-start.7 = (f32[1,2048,128]{2,1,0:T(8,128)S(1)}, f32[1,2048,128]{2,1,0:T(8,128)}, u32[]{:S(2)}) copy-start(f32[1,2048,128]{2,1,0:T(8,128)} %param.5) | copy-start | bytes 3145732
  151.7 19.5 %collective-permute-start.23 = (bf16[2048,128]{1,0:T(8,128)(2,1)S(1)}, bf16[2048,128]{1,0:T(8,128)(2,1)S(1)}, u32[]{:S(2)}, u32[]{:S(2)}) collective-permute-start(bf16[2048,128]{1,0:T(8,128)(2,1)S(1)} %get-tuple-element.31), channel_id=1, source_target_pairs={{0,12},{1,13},{2,29},{3,28},{4,0},{5,1},{6,17},{7,16},{8,4},{9,5},... | collective-permute-start | bytes 1572872 | tf_op jit(solution)/shard_map/ppermute | solution.py:26
  156.2 15.0 %collective-permute-start.24 = (bf16[2048,128]{1,0:T(8,128)(2,1)S(1)}, bf16[2048,128]{1,0:T(8,128)(2,1)S(1)}, u32[]{:S(2)}, u32[]{:S(2)}) collective-permute-start(bf16[2048,128]{1,0:T(8,128)(2,1)S(1)} %get-tuple-element.32), channel_id=1, source_target_pairs={{0,0},{1,1},{2,17},{3,16},{4,4},{5,5},{6,21},{7,20},{8,8},{9,9},{1... | collective-permute-start | bytes 1572872 | tf_op jit(solution)/shard_map/ppermute | solution.py:26
  156.9 17.9 %collective-permute-start.20 = (bf16[2048,128]{1,0:T(8,128)(2,1)S(1)}, bf16[2048,128]{1,0:T(8,128)(2,1)S(1)}, u32[]{:S(2)}, u32[]{:S(2)}) collective-permute-start(bf16[2048,128]{1,0:T(8,128)(2,1)S(1)} %get-tuple-element.26), channel_id=1, source_target_pairs={{0,4},{1,5},{2,21},{3,20},{4,8},{5,9},{6,25},{7,24},{8,12},{9,13},... | collective-permute-start | bytes 1572872 | tf_op jit(solution)/shard_map/ppermute | solution.py:26
  (5 other events, 4.7 us)

commit v7 on v0

v7 whole, which is shorter than its diff:
```python
import functools

import jax
import jax.numpy as jnp
from jax import lax
from jax.experimental import pallas as pl
from jax.experimental.pallas import tpu as pltpu
from jax.sharding import Mesh, PartitionSpec as P

Z, CORES, Y, X = 16, 2, 4, 4
PLANES = Z * CORES
M = 2048
BLK = M // Y
COL = 128
AXES = ("z", "core", "y", "x")


def device_index(plane, y, x):
    return (plane * Y + y) * X + x


def moved(value, planes=0, ys=0, xs=0):
    pairs = []
    for plane in range(PLANES):
        if not 0 <= plane + planes < PLANES:
            continue
        for y in range(Y):
            for x in range(X):
                target = device_index(plane + planes, (y + ys) % Y, (x + xs) % X)
                pairs.append((device_index(plane, y, x), target))
    return lax.ppermute(value, AXES, pairs)


def after(value, *before):
    return lax.optimization_barrier((value,) + before)[0]


def rows_in_order(at_ref, ref, index, start):
    starts = [start + lax.rem(at_ref[1] + e, X) * COL for e in range(X)]
    return [ref[index + (pl.ds(pl.multiple_of(at, COL), COL),)] for at in starts]


FIRST_GROUPS, LAST_GROUPS = (2, 1), (3, 0)


def first_kernel(groups, at_ref, *refs):
    blocks, parts = refs[:X], refs[X : X + 2 * len(groups)]
    rhs_ref, corr_ref, sent_ref = refs[X + 2 * len(groups) :]
    indices = [index for _, index in part_places(groups)]

    total = jnp.zeros((BLK, len(groups) * COL), jnp.float32)
    for k in range(Y):
        for side in (0, 1):
            left = jnp.concatenate([block[k, side] for block in blocks], axis=1)
            right = []
            for part, index in list(zip(parts, indices))[side::2]:
                rows = rows_in_order(at_ref, part, index, k * BLK)
                right.append(jnp.concatenate(rows, axis=0))
            right = jnp.concatenate(right, axis=1)
            total = total + jnp.dot(left, right, preferred_element_type=jnp.float32)

    for i, d in enumerate(groups):
        piece = total[:, i * COL : (i + 1) * COL]
        corr_ref[i] = piece
        owner = lax.rem(at_ref[0] + d, Y)
        sent_ref[i] = (rhs_ref[owner] + piece).astype(jnp.bfloat16)


def part_places(groups):
    places = {
        0: (("near", (0,)), ("near", (1,))),
        1: (("up", (0,)), ("up", (1,))),
        2: (("below_far", ()), ("above_far", ())),
        3: (("down", (0,)), ("down", (1,))),
    }
    return [place for d in groups for place in places[d]]


IN_SMEM = pl.BlockSpec(memory_space=pltpu.SMEM)
IN_VMEM = pl.BlockSpec(memory_space=pltpu.VMEM)


def first_level(groups, at, blocks, parts, rhs):
    count = len(groups)
    parts = [parts[name] for name, _ in part_places(groups)]
    return pl.pallas_call(
        functools.partial(first_kernel, groups),
        name="first_level",
        out_shape=(
            jax.ShapeDtypeStruct((count, BLK, COL), jnp.float32),
            jax.ShapeDtypeStruct((count, BLK, COL), jnp.bfloat16),
        ),
        in_specs=[IN_SMEM] + [IN_VMEM] * (X + len(parts) + 1),
        out_specs=(IN_VMEM, IN_VMEM),
        compiler_params=pltpu.CompilerParams(vmem_limit_bytes=24 << 20),
        cost_estimate=pl.CostEstimate(
            flops=4 * BLK * M * count * COL,
            bytes_accessed=8 << 20,
            transcendentals=0,
        ),
    )(at, *blocks, *parts, rhs)


def second_kernel(groups, at_ref, *refs):
    lower, upper = refs[:X], refs[X : 2 * X]
    below, above, corr_ref, *outs = refs[2 * X :]

    for m in range(Y):
        rows = pl.ds(m * BLK, BLK)
        total = None
        for blocks, b_ref in ((lower, below), (upper, above)):
            left = jnp.concatenate([block[rows, :] for block in blocks], axis=1)
            right = [
                jnp.concatenate(rows_in_order(at_ref, b_ref, (i,), 0), axis=0)
                for i in range(len(groups))
            ]
            right = jnp.concatenate(right, axis=1)
            term = jnp.dot(left, right, preferred_element_type=jnp.float32)
            total = term if total is None else total + term
        here = m == at_ref[0]
        for i in range(len(groups)):
            piece = total[:, i * COL : (i + 1) * COL]
            piece = piece + jnp.where(here, corr_ref[i], 0.0)
            outs[i][rows, :] = piece.astype(outs[i].dtype)


def second_level(groups, at, blocks, below, above, corr):
    return pl.pallas_call(
        functools.partial(second_kernel, groups),
        name="second_level",
        out_shape=tuple(
            jax.ShapeDtypeStruct((M, COL), jnp.bfloat16 if d else jnp.float32)
            for d in groups
        ),
        in_specs=[IN_SMEM] + [IN_VMEM] * (2 * X + 3),
        out_specs=(IN_VMEM,) * len(groups),
        compiler_params=pltpu.CompilerParams(vmem_limit_bytes=24 << 20),
        cost_estimate=pl.CostEstimate(
            flops=4 * BLK * M * len(groups) * COL,
            bytes_accessed=6 << 20,
            transcendentals=0,
        ),
    )(at, *blocks, below, above, corr)


def on_device(right_sides, lower_first, upper_first, lower_second, upper_second):
    rhs = right_sides[0]
    at = jnp.stack([lax.axis_index("y"), lax.axis_index("x")]).astype(jnp.int32)

    def exchanged(value):
        return lax.all_to_all(value, "y", 0, 0, tiled=True)

    firsts = [v[0].reshape(Y, BLK, COL) for v in (lower_first, upper_first)]
    firsts = jnp.stack(firsts, axis=1)
    sent_one = after(rhs, firsts).astype(jnp.bfloat16)
    own = exchanged(firsts)
    near = jnp.stack([moved(sent_one, 1), moved(sent_one, -1)])
    near = after(near, own)

    lo, up = after(lower_second[0], sent_one), upper_second[0]
    lo_left, lo_right = moved(lo, xs=1), moved(lo, xs=-1)

    sent_own = after(own, lo_left, lo_right)
    left, right = moved(sent_own, xs=1), moved(sent_own, xs=-1)
    far = moved(sent_own, xs=2)
    from_down, from_up = moved(near, ys=1), moved(near, ys=-1)
    below_far = moved(from_down[0], ys=1)
    above_far = moved(from_up[1], ys=-1)
    rhs_rows = exchanged(after(rhs, own).reshape(Y, BLK, COL))

    up = after(up, from_down, from_up)
    up_left, up_right = moved(up, xs=1), moved(up, xs=-1)
    lo_far = moved(after(lo_left, from_down, from_up), xs=1)
    up_far = moved(up_right, xs=-1)

    blocks = (own, right, far, left)
    parts = dict(near=near, up=from_up, down=from_down)
    parts.update(below_far=below_far, above_far=above_far)
    corr_a, sent_a = first_level(FIRST_GROUPS, at, blocks, parts, rhs_rows)
    late = after(at, sent_a)
    corr_b, sent_b = first_level(LAST_GROUPS, late, blocks, parts, rhs_rows)
    below_a, above_a = moved(sent_a, 2), moved(sent_a, -2)
    below_b, above_b = moved(sent_b, 2), moved(sent_b, -2)
    blocks = (lo, lo_right, lo_far, lo_left, up, up_right, up_far, up_left)
    two, one = second_level(FIRST_GROUPS, at, blocks, below_a, above_a, corr_a)
    late = after(late, two)
    three, total = second_level(LAST_GROUPS, late, blocks, below_b, above_b, corr_b)
    total = total + rhs
    for d, part in ((2, two), (1, one), (3, three)):
        total = total + moved(part, ys=d).astype(jnp.float32)
    return total[None]


def solution(mesh):
    fine = Mesh(mesh.devices.reshape(Z, CORES, Y, X), AXES)
    spec = P(("z", "core"), None, ("y", "x"))
    return jax.shard_map(
        on_device,
        mesh=fine,
        in_specs=(spec,) * 5,
        out_specs=spec,
        check_vma=False,
    )
```

time: 410 us -> 167 us (0.41)
  the two profiles are of different devices: /device:TPU:1 before, /device:TPU:390 now
where the time goes in v7:
time: 167 us; the launch traced here: 166 us
  starting transfers between devices  76.4 us (46%)
  waiting for transfers between devices  66.8 us (40%)
  Pallas kernels  14.1 us (8%)
  local copies, waits for them, and re-layouts  4.53 us (3%)
  other arithmetic  3.7 us (2%)
    ppermute x22, starting transfers between devices, moved(): return lax.ppermute(value, AXES, pairs)  68.3 us
    ppermute x22, waiting for transfers between devices, moved(): return lax.ppermute(value, AXES, pairs)  65.3 us
    all_to_all x2, starting transfers between devices, exchanged(): return lax.all_to_all(value, 'y', 0, 0, tiled=True)  8.12 us
    pallas_call x2, Pallas kernels, first_level(): pl.pallas_call(functools.partial(first_kernel, groups), name='first_level...  7.82 us
    pallas_call x2, Pallas kernels, second_level(): pl.pallas_call(functools.partial(second_kernel, groups), name='second_lev...  6.29 us
  transfers between devices with their start and end apart: 24, of which 10 were waited for; matrix products, arithmetic and copies ran while one was open for 2% of the time, Pallas kernels for 9%

profile of v7, /device:TPU:390, one launch (start us, length us, event | category | flops | bytes accessed | tf_op | source)
XLA Modules:
  0.0 165.9 jit_solution(16623409425625440213)
XLA Ops:
  0.0 2.3 %pad_maximum_fusion = bf16[4,2,512,128]{3,2,1,0:T(8,128)(2,1)} fusion(bf16[4,1,512,128]{3,2,1,0:T(8,128)(2,1)} %bitcast.23, bf16[4,1,512,128]{3,2,1,0:T(8,128)(2,1)} %bitcast.24), kind=kLoop, calls=%fused_computation | loop fusion | flops 524288 | bytes 2097152 | tf_op jit(solution)/shard_map/stack | solution.py:154
  2.3 4.6 %all-to-all-start = ((bf16[4,2,512,128]{3,2,1,0:T(8,128)(2,1)}), bf16[4,2,512,128]{3,2,1,0:T(8,128)(2,1)S(1)}, u32[]{:S(2)}, u32[]{:S(2)}) async-start(bf16[4,2,512,128]{3,2,1,0:T(8,128)(2,1)} %pad_maximum_fusion), calls=%async_computation | async-start | bytes 2097152 | tf_op jit(solution)/shard_map/all_to_all | solution.py:151
  6.9 1.9 %collective-permute-start.5 = (bf16[2048,128]{1,0:T(8,128)(2,1)S(1)}, bf16[2048,128]{1,0:T(8,128)(2,1)S(1)}, u32[]{:S(2)}, u32[]{:S(2)}) collective-permute-start(bf16[2048,128]{1,0:T(8,128)(2,1)S(1)} %convert_element_type.12), channel_id=1, source_target_pairs={{0,16},{1,17},{2,18},{3,19},{4,20},{5,21},{6,22},{7,23},{8,24},{9,... | collective-permute-start | bytes 1572872 | tf_op jit(solution)/shard_map/ppermute | solution.py:31
  8.9 4.9 %collective-permute-start.6 = (bf16[2048,128]{1,0:T(8,128)(2,1)S(1)}, bf16[2048,128]{1,0:T(8,128)(2,1)S(1)}, u32[]{:S(2)}, u32[]{:S(2)}) collective-permute-start(bf16[2048,128]{1,0:T(8,128)(2,1)S(1)} %convert_element_type.12), channel_id=1, source_target_pairs={{16,0},{17,1},{18,2},{19,3},{20,4},{21,5},{22,6},{23,7},{24,8},{25... | collective-permute-start | bytes 1572872 | tf_op jit(solution)/shard_map/ppermute | solution.py:31
  13.7 4.9 %collective-permute-done.5 = bf16[2048,128]{1,0:T(8,128)(2,1)S(1)} collective-permute-done((bf16[2048,128]{1,0:T(8,128)(2,1)S(1)}, bf16[2048,128]{1,0:T(8,128)(2,1)S(1)}, u32[]{:S(2)}, u32[]{:S(2)}) %collective-permute-start.5) | collective-permute-done | bytes 524320 | tf_op jit(solution)/shard_map/ppermute | solution.py:31
  22.0 3.8 %collective-permute-start.9 = (bf16[2,2048,128]{2,1,0:T(8,128)(2,1)S(1)}, bf16[2,2048,128]{2,1,0:T(8,128)(2,1)}, u32[]{:S(2)}, u32[]{:S(2)}) collective-permute-start(bf16[2,2048,128]{2,1,0:T(8,128)(2,1)S(1)} %pad_maximum_fusion.1.refs_6_.refs_7_), channel_id=1, source_target_pairs={{0,12},{1,13},{2,14},{3,15},{4,0},{5,1},{6,2},{7,3},{8,4},{9,5},{1... | collective-permute-start | bytes 3145736 | tf_op jit(solution)/shard_map/ppermute | solution.py:31
  25.8 2.4 %collective-permute-start = (bf16[2048,128]{1,0:T(8,128)(2,1)S(1)}, bf16[2048,128]{1,0:T(8,128)(2,1)}, u32[]{:S(2)}, u32[]{:S(2)}) collective-permute-start(bf16[2048,128]{1,0:T(8,128)(2,1)S(1)} %bitcast.17), channel_id=1, source_target_pairs={{0,1},{1,2},{2,3},{3,0},{4,5},{5,6},{6,7},{7,4},{8,9},{9,10},{10,1... | collective-permute-start | bytes 1572872 | tf_op jit(solution)/shard_map/ppermute | solution.py:31
  28.2 3.5 %collective-permute-start.1 = (bf16[2048,128]{1,0:T(8,128)(2,1)S(1)}, bf16[2048,128]{1,0:T(8,128)(2,1)S(1)}, u32[]{:S(2)}, u32[]{:S(2)}) collective-permute-start(bf16[2048,128]{1,0:T(8,128)(2,1)S(1)} %bitcast.18), channel_id=1, source_target_pairs={{0,3},{1,0},{2,1},{3,2},{4,7},{5,4},{6,5},{7,6},{8,11},{9,8},{10,9... | collective-permute-start | bytes 1572872 | tf_op jit(solution)/shard_map/ppermute | solution.py:31
  31.7 2.0 %collective-permute-start.7 = (bf16[2,2048,128]{2,1,0:T(8,128)(2,1)S(1)}, bf16[2,2048,128]{2,1,0:T(8,128)(2,1)}, u32[]{:S(2)}, u32[]{:S(2)}) collective-permute-start(bf16[2,2048,128]{2,1,0:T(8,128)(2,1)S(1)} %pad_maximum_fusion.1.refs_6_.refs_7_), channel_id=1, source_target_pairs={{0,4},{1,5},{2,6},{3,7},{4,8},{5,9},{6,10},{7,11},{8,12},{9,13},{1... | collective-permute-start | bytes 3145736 | tf_op jit(solution)/shard_map/ppermute | solution.py:31
  33.7 7.8 %collective-permute-done.refs_3_ = bf16[2048,128]{1,0:T(8,128)(2,1)} collective-permute-done((bf16[2048,128]{1,0:T(8,128)(2,1)S(1)}, bf16[2048,128]{1,0:T(8,128)(2,1)}, u32[]{:S(2)}, u32[]{:S(2)}) %collective-permute-start) | collective-permute-done | bytes 524320 | tf_op jit(solution)/shard_map/ppermute | solution.py:31
  41.4 3.2 %collective-permute-done.1.refs_1_ = bf16[2048,128]{1,0:T(8,128)(2,1)S(1)} collective-permute-done((bf16[2048,128]{1,0:T(8,128)(2,1)S(1)}, bf16[2048,128]{1,0:T(8,128)(2,1)S(1)}, u32[]{:S(2)}, u32[]{:S(2)}) %collective-permute-start.1) | collective-permute-done | bytes 524320 | tf_op jit(solution)/shard_map/ppermute | solution.py:31
  45.4 2.2 %collective-permute-start.2 = (bf16[4,2,512,128]{3,2,1,0:T(8,128)(2,1)S(1)}, bf16[4,2,512,128]{3,2,1,0:T(8,128)(2,1)}, u32[]{:S(2)}, u32[]{:S(2)}) collective-permute-start(bf16[4,2,512,128]{3,2,1,0:T(8,128)(2,1)S(1)} %all-to-all-done.refs_0_), channel_id=1, source_target_pairs={{0,3},{1,0},{2,1},{3,2},{4,7},{5,4},{6,5},{7,6},{8,11},{9,8},{10,9... | collective-permute-start | bytes 3145736 | tf_op jit(solution)/shard_map/ppermute | solution.py:31
  47.7 3.3 %collective-permute-start.3 = (bf16[4,2,512,128]{3,2,1,0:T(8,128)(2,1)S(1)}, bf16[4,2,512,128]{3,2,1,0:T(8,128)(2,1)}, u32[]{:S(2)}, u32[]{:S(2)}) collective-permute-start(bf16[4,2,512,128]{3,2,1,0:T(8,128)(2,1)S(1)} %all-to-all-done.refs_0_), channel_id=1, source_target_pairs={{0,2},{1,3},{2,0},{3,1},{4,6},{5,7},{6,4},{7,5},{8,10},{9,11},{10,... | collective-permute-start | bytes 3145736 | tf_op jit(solution)/shard_map/ppermute | solution.py:31
  51.0 4.0 %collective-permute-start.4 = (bf16[4,2,512,128]{3,2,1,0:T(8,128)(2,1)S(1)}, bf16[4,2,512,128]{3,2,1,0:T(8,128)(2,1)}, u32[]{:S(2)}, u32[]{:S(2)}) collective-permute-start(bf16[4,2,512,128]{3,2,1,0:T(8,128)(2,1)S(1)} %all-to-all-done.refs_0_), channel_id=1, source_target_pairs={{0,1},{1,2},{2,3},{3,0},{4,5},{5,6},{6,7},{7,4},{8,9},{9,10},{10,1... | collective-permute-start | bytes 3145736 | tf_op jit(solution)/shard_map/ppermute | solution.py:31
  55.0 3.5 %all-to-all-start.1 = ((f32[4,512,128]{2,1,0:T(8,128)}), f32[4,512,128]{2,1,0:T(8,128)S(1)}, u32[]{:S(2)}, u32[]{:S(2)}) async-start(f32[4,512,128]{2,1,0:T(8,128)} %bitcast.21), calls=%async_computation.1 | async-start | bytes 2097152 | tf_op jit(solution)/shard_map/all_to_all | solution.py:151
  60.4 5.1 %collective-permute-start.10 = (bf16[2048,128]{1,0:T(8,128)(2,1)}, bf16[2048,128]{1,0:T(8,128)(2,1)}, u32[]{:S(2)}, u32[]{:S(2)}) collective-permute-start(bf16[2048,128]{1,0:T(8,128)(2,1)} %slice_bitcast_fusion), channel_id=1, source_target_pairs={{0,12},{1,13},{2,14},{3,15},{4,0},{5,1},{6,2},{7,3},{8,4},{9,5},{1... | collective-permute-start | bytes 1572872 | tf_op jit(solution)/shard_map/ppermute | solution.py:31
  65.5 2.2 %collective-permute-start.12 = (bf16[2048,128]{1,0:T(8,128)(2,1)}, bf16[2048,128]{1,0:T(8,128)(2,1)}, u32[]{:S(2)}, u32[]{:S(2)}) collective-permute-start(bf16[2048,128]{1,0:T(8,128)(2,1)} %bitcast.11.refs_4_), channel_id=1, source_target_pairs={{0,3},{1,0},{2,1},{3,2},{4,7},{5,4},{6,5},{7,6},{8,11},{9,8},{10,9... | collective-permute-start | bytes 1572872 | tf_op jit(solution)/shard_map/ppermute | solution.py:31
  69.6 27.6 %collective-permute-done.2.refs_1_ = bf16[4,2,512,128]{3,2,1,0:T(8,128)(2,1)} collective-permute-done((bf16[4,2,512,128]{3,2,1,0:T(8,128)(2,1)S(1)}, bf16[4,2,512,128]{3,2,1,0:T(8,128)(2,1)}, u32[]{:S(2)}, u32[]{:S(2)}) %collective-permute-start.2) | collective-permute-done | bytes 1048608 | tf_op jit(solution)/shard_map/ppermute | solution.py:31
  99.1 1.9 %collective-permute-start.11 = (bf16[2048,128]{1,0:T(8,128)(2,1)}, bf16[2048,128]{1,0:T(8,128)(2,1)}, u32[]{:S(2)}, u32[]{:S(2)}) collective-permute-start(bf16[2048,128]{1,0:T(8,128)(2,1)} %collective-permute-done.refs_3_), channel_id=1, source_target_pairs={{0,1},{1,2},{2,3},{3,0},{4,5},{5,6},{6,7},{7,4},{8,9},{9,10},{10,1... | collective-permute-start | bytes 1572872 | tf_op jit(solution)/shard_map/ppermute | solution.py:31
  101.1 1.9 %collective-permute-start.14 = (bf16[2048,128]{1,0:T(8,128)(2,1)}, bf16[2048,128]{1,0:T(8,128)(2,1)}, u32[]{:S(2)}, u32[]{:S(2)}) collective-permute-start(bf16[2048,128]{1,0:T(8,128)(2,1)} %bitcast.11.refs_4_), channel_id=1, source_target_pairs={{0,1},{1,2},{2,3},{3,0},{4,5},{5,6},{6,7},{7,4},{8,9},{9,10},{10,1... | collective-permute-start | bytes 1572872 | tf_op jit(solution)/shard_map/ppermute | solution.py:31
  103.0 3.1 %collective-permute-done.12.refs_5_ = bf16[2048,128]{1,0:T(8,128)(2,1)} collective-permute-done((bf16[2048,128]{1,0:T(8,128)(2,1)}, bf16[2048,128]{1,0:T(8,128)(2,1)}, u32[]{:S(2)}, u32[]{:S(2)}) %collective-permute-start.12) | collective-permute-done | bytes 524320 | tf_op jit(solution)/shard_map/ppermute | solution.py:31
  109.8 4.1 %first_level.2 = (f32[2,512,128]{2,1,0:T(8,128)S(1)}, bf16[2,512,128]{2,1,0:T(8,128)(2,1)S(1)}) custom-call(s32[2]{0:T(128)S(1)} %pad_add_fusion.at_ref, bf16[4,2,512,128]{3,2,1,0:T(8,128)(2,1)S(1)} %all-to-all-done.refs_0_, bf16[4,2,512,128]{3,2,1,0:T(8,128)(2,1)} %collective-permute-done.2.refs_1_, ...), custom_call_target="tpu_custom_call" | custom-call | flops 1073741824 | bytes 8388608 | tf_op jit(solution)/shard_map/first_level/pallas_call | solution.py:86
  113.9 3.2 %collective-permute-start.15 = (bf16[2,512,128]{2,1,0:T(8,128)(2,1)S(1)}, bf16[2,512,128]{2,1,0:T(8,128)(2,1)S(1)}, u32[]{:S(2)}, u32[]{:S(2)}) collective-permute-start(bf16[2,512,128]{2,1,0:T(8,128)(2,1)S(1)} %get-tuple-element.27), channel_id=1, source_target_pairs={{0,32},{1,33},{2,34},{3,35},{4,36},{5,37},{6,38},{7,39},{8,40},{9,... | collective-permute-start | bytes 786440 | tf_op jit(solution)/shard_map/ppermute | solution.py:31
  117.1 7.3 %collective-permute-start.16 = (bf16[2,512,128]{2,1,0:T(8,128)(2,1)S(1)}, bf16[2,512,128]{2,1,0:T(8,128)(2,1)S(1)}, u32[]{:S(2)}, u32[]{:S(2)}) collective-permute-start(bf16[2,512,128]{2,1,0:T(8,128)(2,1)S(1)} %get-tuple-element.27), channel_id=1, source_target_pairs={{32,0},{33,1},{34,2},{35,3},{36,4},{37,5},{38,6},{39,7},{40,8},{41... | collective-permute-start | bytes 786440 | tf_op jit(solution)/shard_map/ppermute | solution.py:31
  124.4 3.8 %first_level.3 = (f32[2,512,128]{2,1,0:T(8,128)S(1)}, bf16[2,512,128]{2,1,0:T(8,128)(2,1)S(1)}) custom-call(s32[2]{0:T(128)S(1)} %pad_add_fusion.at_ref, bf16[4,2,512,128]{3,2,1,0:T(8,128)(2,1)S(1)} %all-to-all-done.refs_0_, bf16[4,2,512,128]{3,2,1,0:T(8,128)(2,1)} %collective-permute-done.2.refs_1_, ...), custom_call_target="tpu_custom_call" | custom-call | flops 1073741824 | bytes 8388608 | tf_op jit(solution)/shard_map/first_level/pallas_call | solution.py:86
  130.1 5.1 %collective-permute-start.18 = (bf16[2,512,128]{2,1,0:T(8,128)(2,1)S(1)}, bf16[2,512,128]{2,1,0:T(8,128)(2,1)S(1)}, u32[]{:S(2)}, u32[]{:S(2)}) collective-permute-start(bf16[2,512,128]{2,1,0:T(8,128)(2,1)S(1)} %get-tuple-element.34), channel_id=1, source_target_pairs={{32,0},{33,1},{34,2},{35,3},{36,4},{37,5},{38,6},{39,7},{40,8},{41... | collective-permute-start | bytes 786440 | tf_op jit(solution)/shard_map/ppermute | solution.py:31
  135.3 3.1 %second_level.2 = (bf16[2048,128]{1,0:T(8,128)(2,1)S(1)}, bf16[2048,128]{1,0:T(8,128)(2,1)S(1)}) custom-call(s32[2]{0:T(128)S(1)} %pad_add_fusion.at_ref, bf16[2048,128]{1,0:T(8,128)(2,1)S(1)} %bitcast.19, bf16[2048,128]{1,0:T(8,128)(2,1)S(1)} %copy-done.3, bf16[2048,128]{1,0:T(8,128)(2,1)} %collective-permute-done.11.refs_2_, ...), custom_call_target="tpu_custom_call" | custom-call | flops 1073741824 | bytes 6291456 | tf_op jit(solution)/shard_map/second_level/pallas_call | solution.py:128
  140.4 3.2 %second_level.3 = (bf16[2048,128]{1,0:T(8,128)(2,1)S(1)}, f32[2048,128]{1,0:T(8,128)S(1)}) custom-call(s32[2]{0:T(128)S(1)} %pad_add_fusion.at_ref, bf16[2048,128]{1,0:T(8,128)(2,1)S(1)} %bitcast.20, bf16[2048,128]{1,0:T(8,128)(2,1)S(1)} %copy-done.3, bf16[2048,128]{1,0:T(8,128)(2,1)} %collective-permute-done.11.refs_2_, ...), custom_call_target="tpu_custom_call" | custom-call | flops 1073741824 | bytes 6291456 | tf_op jit(solution)/shard_map/second_level/pallas_call | solution.py:128
  143.6 3.7 %collective-permute-start.21 = (bf16[2048,128]{1,0:T(8,128)(2,1)S(1)}, bf16[2048,128]{1,0:T(8,128)(2,1)S(1)}, u32[]{:S(2)}, u32[]{:S(2)}) collective-permute-start(bf16[2048,128]{1,0:T(8,128)(2,1)S(1)} %get-tuple-element.38), channel_id=1, source_target_pairs={{0,12},{1,13},{2,14},{3,15},{4,0},{5,1},{6,2},{7,3},{8,4},{9,5},{1... | collective-permute-start | bytes 1572872 | tf_op jit(solution)/shard_map/ppermute | solution.py:31
  147.3 2.2 %collective-permute-start.20 = (bf16[2048,128]{1,0:T(8,128)(2,1)S(1)}, bf16[2048,128]{1,0:T(8,128)(2,1)S(1)}, u32[]{:S(2)}, u32[]{:S(2)}) collective-permute-start(bf16[2048,128]{1,0:T(8,128)(2,1)S(1)} %get-tuple-element.37), channel_id=1, source_target_pairs={{0,4},{1,5},{2,6},{3,7},{4,8},{5,9},{6,10},{7,11},{8,12},{9,13},{1... | collective-permute-start | bytes 1572872 | tf_op jit(solution)/shard_map/ppermute | solution.py:31
  149.5 12.4 %collective-permute-done.21 = bf16[2048,128]{1,0:T(8,128)(2,1)S(1)} collective-permute-done((bf16[2048,128]{1,0:T(8,128)(2,1)S(1)}, bf16[2048,128]{1,0:T(8,128)(2,1)S(1)}, u32[]{:S(2)}, u32[]{:S(2)}) %collective-permute-start.21) | collective-permute-done | bytes 524320 | tf_op jit(solution)/shard_map/ppermute | solution.py:31
  161.9 2.8 %collective-permute-done.20 = bf16[2048,128]{1,0:T(8,128)(2,1)S(1)} collective-permute-done((bf16[2048,128]{1,0:T(8,128)(2,1)S(1)}, bf16[2048,128]{1,0:T(8,128)(2,1)S(1)}, u32[]{:S(2)}, u32[]{:S(2)}) %collective-permute-start.20) | collective-permute-done | bytes 524320 | tf_op jit(solution)/shard_map/ppermute | solution.py:31
  (39 shorter events, 18.6 us)
Async XLA Ops:
  2.3 4.6 %copy-start.4 = (f32[1,2048,128]{2,1,0:T(8,128)S(1)}, f32[1,2048,128]{2,1,0:T(8,128)}, u32[]{:S(2)}) copy-start(f32[1,2048,128]{2,1,0:T(8,128)} %param.5) | copy-start | bytes 3145732
  2.3 19.7 %all-to-all-start = ((bf16[4,2,512,128]{3,2,1,0:T(8,128)(2,1)}), bf16[4,2,512,128]{3,2,1,0:T(8,128)(2,1)S(1)}, u32[]{:S(2)}, u32[]{:S(2)}) async-start(bf16[4,2,512,128]{3,2,1,0:T(8,128)(2,1)} %pad_maximum_fusion), calls=%async_computation | async-start | bytes 2097152 | tf_op jit(solution)/shard_map/all_to_all | solution.py:151
  6.9 11.7 %collective-permute-start.5 = (bf16[2048,128]{1,0:T(8,128)(2,1)S(1)}, bf16[2048,128]{1,0:T(8,128)(2,1)S(1)}, u32[]{:S(2)}, u32[]{:S(2)}) collective-permute-start(bf16[2048,128]{1,0:T(8,128)(2,1)S(1)} %convert_element_type.12), channel_id=1, source_target_pairs={{0,16},{1,17},{2,18},{3,19},{4,20},{5,21},{6,22},{7,23},{8,24},{9,... | collective-permute-start | bytes 1572872 | tf_op jit(solution)/shard_map/ppermute | solution.py:31
  8.9 11.5 %collective-permute-start.6 = (bf16[2048,128]{1,0:T(8,128)(2,1)S(1)}, bf16[2048,128]{1,0:T(8,128)(2,1)S(1)}, u32[]{:S(2)}, u32[]{:S(2)}) collective-permute-start(bf16[2048,128]{1,0:T(8,128)(2,1)S(1)} %convert_element_type.12), channel_id=1, source_target_pairs={{16,0},{17,1},{18,2},{19,3},{20,4},{21,5},{22,6},{23,7},{24,8},{25... | collective-permute-start | bytes 1572872 | tf_op jit(solution)/shard_map/ppermute | solution.py:31
  20.4 5.4 %copy-start = (bf16[1,2048,128]{2,1,0:T(8,128)(2,1)S(1)}, bf16[1,2048,128]{2,1,0:T(8,128)(2,1)}, u32[]{:S(2)}) copy-start(bf16[1,2048,128]{2,1,0:T(8,128)(2,1)} %param.8) | copy-start | bytes 1572868
  22.0 36.6 %collective-permute-start.9 = (bf16[2,2048,128]{2,1,0:T(8,128)(2,1)S(1)}, bf16[2,2048,128]{2,1,0:T(8,128)(2,1)}, u32[]{:S(2)}, u32[]{:S(2)}) collective-permute-start(bf16[2,2048,128]{2,1,0:T(8,128)(2,1)S(1)} %pad_maximum_fusion.1.refs_6_.refs_7_), channel_id=1, source_target_pairs={{0,12},{1,13},{2,14},{3,15},{4,0},{5,1},{6,2},{7,3},{8,4},{9,5},{1... | collective-permute-start | bytes 3145736 | tf_op jit(solution)/shard_map/ppermute | solution.py:31
  25.8 15.6 %collective-permute-start = (bf16[2048,128]{1,0:T(8,128)(2,1)S(1)}, bf16[2048,128]{1,0:T(8,128)(2,1)}, u32[]{:S(2)}, u32[]{:S(2)}) collective-permute-start(bf16[2048,128]{1,0:T(8,128)(2,1)S(1)} %bitcast.17), channel_id=1, source_target_pairs={{0,1},{1,2},{2,3},{3,0},{4,5},{5,6},{6,7},{7,4},{8,9},{9,10},{10,1... | collective-permute-start | bytes 1572872 | tf_op jit(solution)/shard_map/ppermute | solution.py:31
  28.2 16.5 %collective-permute-start.1 = (bf16[2048,128]{1,0:T(8,128)(2,1)S(1)}, bf16[2048,128]{1,0:T(8,128)(2,1)S(1)}, u32[]{:S(2)}, u32[]{:S(2)}) collective-permute-start(bf16[2048,128]{1,0:T(8,128)(2,1)S(1)} %bitcast.18), channel_id=1, source_target_pairs={{0,3},{1,0},{2,1},{3,2},{4,7},{5,4},{6,5},{7,6},{8,11},{9,8},{10,9... | collective-permute-start | bytes 1572872 | tf_op jit(solution)/shard_map/ppermute | solution.py:31
  31.7 33.9 %collective-permute-start.7 = (bf16[2,2048,128]{2,1,0:T(8,128)(2,1)S(1)}, bf16[2,2048,128]{2,1,0:T(8,128)(2,1)}, u32[]{:S(2)}, u32[]{:S(2)}) collective-permute-start(bf16[2,2048,128]{2,1,0:T(8,128)(2,1)S(1)} %pad_maximum_fusion.1.refs_6_.refs_7_), channel_id=1, source_target_pairs={{0,4},{1,5},{2,6},{3,7},{4,8},{5,9},{6,10},{7,11},{8,12},{9,13},{1... | collective-permute-start | bytes 3145736 | tf_op jit(solution)/shard_map/ppermute | solution.py:31
  44.7 0.8 copy-start.2
  45.4 51.8 %collective-permute-start.2 = (bf16[4,2,512,128]{3,2,1,0:T(8,128)(2,1)S(1)}, bf16[4,2,512,128]{3,2,1,0:T(8,128)(2,1)}, u32[]{:S(2)}, u32[]{:S(2)}) collective-permute-start(bf16[4,2,512,128]{3,2,1,0:T(8,128)(2,1)S(1)} %all-to-all-done.refs_0_), channel_id=1, source_target_pairs={{0,3},{1,0},{2,1},{3,2},{4,7},{5,4},{6,5},{7,6},{8,11},{9,8},{10,9... | collective-permute-start | bytes 3145736 | tf_op jit(solution)/shard_map/ppermute | solution.py:31
  47.7 51.4 %collective-permute-start.3 = (bf16[4,2,512,128]{3,2,1,0:T(8,128)(2,1)S(1)}, bf16[4,2,512,128]{3,2,1,0:T(8,128)(2,1)}, u32[]{:S(2)}, u32[]{:S(2)}) collective-permute-start(bf16[4,2,512,128]{3,2,1,0:T(8,128)(2,1)S(1)} %all-to-all-done.refs_0_), channel_id=1, source_target_pairs={{0,2},{1,3},{2,0},{3,1},{4,6},{5,7},{6,4},{7,5},{8,10},{9,11},{10,... | collective-permute-start | bytes 3145736 | tf_op jit(solution)/shard_map/ppermute | solution.py:31
  51.0 50.1 %collective-permute-start.4 = (bf16[4,2,512,128]{3,2,1,0:T(8,128)(2,1)S(1)}, bf16[4,2,512,128]{3,2,1,0:T(8,128)(2,1)}, u32[]{:S(2)}, u32[]{:S(2)}) collective-permute-start(bf16[4,2,512,128]{3,2,1,0:T(8,128)(2,1)S(1)} %all-to-all-done.refs_0_), channel_id=1, source_target_pairs={{0,1},{1,2},{2,3},{3,0},{4,5},{5,6},{6,7},{7,4},{8,9},{9,10},{10,1... | collective-permute-start | bytes 3145736 | tf_op jit(solution)/shard_map/ppermute | solution.py:31
  55.0 53.1 %all-to-all-start.1 = ((f32[4,512,128]{2,1,0:T(8,128)}), f32[4,512,128]{2,1,0:T(8,128)S(1)}, u32[]{:S(2)}, u32[]{:S(2)}) async-start(f32[4,512,128]{2,1,0:T(8,128)} %bitcast.21), calls=%async_computation.1 | async-start | bytes 2097152 | tf_op jit(solution)/shard_map/all_to_all | solution.py:151
  60.4 47.7 %collective-permute-start.10 = (bf16[2048,128]{1,0:T(8,128)(2,1)}, bf16[2048,128]{1,0:T(8,128)(2,1)}, u32[]{:S(2)}, u32[]{:S(2)}) collective-permute-start(bf16[2048,128]{1,0:T(8,128)(2,1)} %slice_bitcast_fusion), channel_id=1, source_target_pairs={{0,12},{1,13},{2,14},{3,15},{4,0},{5,1},{6,2},{7,3},{8,4},{9,5},{1... | collective-permute-start | bytes 1572872 | tf_op jit(solution)/shard_map/ppermute | solution.py:31
  65.5 40.6 %collective-permute-start.12 = (bf16[2048,128]{1,0:T(8,128)(2,1)}, bf16[2048,128]{1,0:T(8,128)(2,1)}, u32[]{:S(2)}, u32[]{:S(2)}) collective-permute-start(bf16[2048,128]{1,0:T(8,128)(2,1)} %bitcast.11.refs_4_), channel_id=1, source_target_pairs={{0,3},{1,0},{2,1},{3,2},{4,7},{5,4},{6,5},{7,6},{8,11},{9,8},{10,9... | collective-permute-start | bytes 1572872 | tf_op jit(solution)/shard_map/ppermute | solution.py:31
  97.2 12.6 %collective-permute-start.8 = (bf16[2048,128]{1,0:T(8,128)(2,1)}, bf16[2048,128]{1,0:T(8,128)(2,1)}, u32[]{:S(2)}, u32[]{:S(2)}) collective-permute-start(bf16[2048,128]{1,0:T(8,128)(2,1)} %slice_bitcast_fusion.1), channel_id=1, source_target_pairs={{0,4},{1,5},{2,6},{3,7},{4,8},{5,9},{6,10},{7,11},{8,12},{9,13},{1... | collective-permute-start | bytes 1572872 | tf_op jit(solution)/shard_map/ppermute | solution.py:31
  99.1 29.1 %collective-permute-start.11 = (bf16[2048,128]{1,0:T(8,128)(2,1)}, bf16[2048,128]{1,0:T(8,128)(2,1)}, u32[]{:S(2)}, u32[]{:S(2)}) collective-permute-start(bf16[2048,128]{1,0:T(8,128)(2,1)} %collective-permute-done.refs_3_), channel_id=1, source_target_pairs={{0,1},{1,2},{2,3},{3,0},{4,5},{5,6},{6,7},{7,4},{8,9},{9,10},{10,1... | collective-permute-start | bytes 1572872 | tf_op jit(solution)/shard_map/ppermute | solution.py:31
  101.1 29.1 %collective-permute-start.14 = (bf16[2048,128]{1,0:T(8,128)(2,1)}, bf16[2048,128]{1,0:T(8,128)(2,1)}, u32[]{:S(2)}, u32[]{:S(2)}) collective-permute-start(bf16[2048,128]{1,0:T(8,128)(2,1)} %bitcast.11.refs_4_), channel_id=1, source_target_pairs={{0,1},{1,2},{2,3},{3,0},{4,5},{5,6},{6,7},{7,4},{8,9},{9,10},{10,1... | collective-permute-start | bytes 1572872 | tf_op jit(solution)/shard_map/ppermute | solution.py:31
  106.1 29.2 %collective-permute-start.13 = (bf16[2048,128]{1,0:T(8,128)(2,1)}, bf16[2048,128]{1,0:T(8,128)(2,1)}, u32[]{:S(2)}, u32[]{:S(2)}) collective-permute-start(bf16[2048,128]{1,0:T(8,128)(2,1)} %collective-permute-done.12.refs_5_), channel_id=1, source_target_pairs={{0,3},{1,0},{2,1},{3,2},{4,7},{5,4},{6,5},{7,6},{8,11},{9,8},{10,9... | collective-permute-start | bytes 1572872 | tf_op jit(solution)/shard_map/ppermute | solution.py:31
  113.9 21.4 %copy-start.1 = (bf16[1,2048,128]{2,1,0:T(8,128)(2,1)S(1)}, bf16[1,2048,128]{2,1,0:T(8,128)(2,1)}, u32[]{:S(2)}) copy-start(bf16[1,2048,128]{2,1,0:T(8,128)(2,1)} %param.8) | copy-start | bytes 1572868
  113.9 21.4 %copy-start.3 = (bf16[2048,128]{1,0:T(8,128)(2,1)S(1)}, bf16[2048,128]{1,0:T(8,128)(2,1)}, u32[]{:S(2)}) copy-start(bf16[2048,128]{1,0:T(8,128)(2,1)} %copy-done.2) | copy-start | bytes 1572868
  113.9 21.4 %collective-permute-start.15 = (bf16[2,512,128]{2,1,0:T(8,128)(2,1)S(1)}, bf16[2,512,128]{2,1,0:T(8,128)(2,1)S(1)}, u32[]{:S(2)}, u32[]{:S(2)}) collective-permute-start(bf16[2,512,128]{2,1,0:T(8,128)(2,1)S(1)} %get-tuple-element.27), channel_id=1, source_target_pairs={{0,32},{1,33},{2,34},{3,35},{4,36},{5,37},{6,38},{7,39},{8,40},{9,... | collective-permute-start | bytes 786440 | tf_op jit(solution)/shard_map/ppermute | solution.py:31
  117.1 18.2 %collective-permute-start.16 = (bf16[2,512,128]{2,1,0:T(8,128)(2,1)S(1)}, bf16[2,512,128]{2,1,0:T(8,128)(2,1)S(1)}, u32[]{:S(2)}, u32[]{:S(2)}) collective-permute-start(bf16[2,512,128]{2,1,0:T(8,128)(2,1)S(1)} %get-tuple-element.27), channel_id=1, source_target_pairs={{32,0},{33,1},{34,2},{35,3},{36,4},{37,5},{38,6},{39,7},{40,8},{41... | collective-permute-start | bytes 786440 | tf_op jit(solution)/shard_map/ppermute | solution.py:31
  128.2 12.2 %collective-permute-start.17 = (bf16[2,512,128]{2,1,0:T(8,128)(2,1)S(1)}, bf16[2,512,128]{2,1,0:T(8,128)(2,1)S(1)}, u32[]{:S(2)}, u32[]{:S(2)}) collective-permute-start(bf16[2,512,128]{2,1,0:T(8,128)(2,1)S(1)} %get-tuple-element.34), channel_id=1, source_target_pairs={{0,32},{1,33},{2,34},{3,35},{4,36},{5,37},{6,38},{7,39},{8,40},{9,... | collective-permute-start | bytes 786440 | tf_op jit(solution)/shard_map/ppermute | solution.py:31
  130.1 10.2 %collective-permute-start.18 = (bf16[2,512,128]{2,1,0:T(8,128)(2,1)S(1)}, bf16[2,512,128]{2,1,0:T(8,128)(2,1)S(1)}, u32[]{:S(2)}, u32[]{:S(2)}) collective-permute-start(bf16[2,512,128]{2,1,0:T(8,128)(2,1)S(1)} %get-tuple-element.34), channel_id=1, source_target_pairs={{32,0},{33,1},{34,2},{35,3},{36,4},{37,5},{38,6},{39,7},{40,8},{41... | collective-permute-start | bytes 786440 | tf_op jit(solution)/shard_map/ppermute | solution.py:31
  138.4 23.4 %collective-permute-start.19 = (bf16[2048,128]{1,0:T(8,128)(2,1)S(1)}, bf16[2048,128]{1,0:T(8,128)(2,1)S(1)}, u32[]{:S(2)}, u32[]{:S(2)}) collective-permute-start(bf16[2048,128]{1,0:T(8,128)(2,1)S(1)} %get-tuple-element.32), channel_id=1, source_target_pairs={{0,8},{1,9},{2,10},{3,11},{4,12},{5,13},{6,14},{7,15},{8,0},{9,1},... | collective-permute-start | bytes 1572872 | tf_op jit(solution)/shard_map/ppermute | solution.py:31
  140.4 24.3 %copy-start.5 = (f32[1,2048,128]{2,1,0:T(8,128)S(1)}, f32[1,2048,128]{2,1,0:T(8,128)}, u32[]{:S(2)}) copy-start(f32[1,2048,128]{2,1,0:T(8,128)} %param.5) | copy-start | bytes 3145732
  143.6 18.3 %collective-permute-start.21 = (bf16[2048,128]{1,0:T(8,128)(2,1)S(1)}, bf16[2048,128]{1,0:T(8,128)(2,1)S(1)}, u32[]{:S(2)}, u32[]{:S(2)}) collective-permute-start(bf16[2048,128]{1,0:T(8,128)(2,1)S(1)} %get-tuple-element.38), channel_id=1, source_target_pairs={{0,12},{1,13},{2,14},{3,15},{4,0},{5,1},{6,2},{7,3},{8,4},{9,5},{1... | collective-permute-start | bytes 1572872 | tf_op jit(solution)/shard_map/ppermute | solution.py:31
  147.3 17.4 %collective-permute-start.20 = (bf16[2048,128]{1,0:T(8,128)(2,1)S(1)}, bf16[2048,128]{1,0:T(8,128)(2,1)S(1)}, u32[]{:S(2)}, u32[]{:S(2)}) collective-permute-start(bf16[2048,128]{1,0:T(8,128)(2,1)S(1)} %get-tuple-element.37), channel_id=1, source_target_pairs={{0,4},{1,5},{2,6},{3,7},{4,8},{5,9},{6,10},{7,11},{8,12},{9,13},{1... | collective-permute-start | bytes 1572872 | tf_op jit(solution)/shard_map/ppermute | solution.py:31

commit v8 on v7

--- a/solution.py
+++ b/solution.py
@@ -70,7 +70,7 @@
     places = {
         0: (("near", (0,)), ("near", (1,))),
         1: (("up", (0,)), ("up", (1,))),
-        2: (("below_far", ()), ("above_far", ())),
+        2: (("far", (0,)), ("far", (1,))),
         3: (("down", (0,)), ("down", (1,))),
     }
     return [place for d in groups for place in places[d]]
@@ -102,14 +102,14 @@
 
 
 def second_kernel(groups, at_ref, *refs):
-    lower, upper = refs[:X], refs[X : 2 * X]
-    below, above, corr_ref, *outs = refs[2 * X :]
+    blocks = refs[:X]
+    below, above, corr_ref, *outs = refs[X:]
 
     for m in range(Y):
         rows = pl.ds(m * BLK, BLK)
         total = None
-        for blocks, b_ref in ((lower, below), (upper, above)):
-            left = jnp.concatenate([block[rows, :] for block in blocks], axis=1)
+        for side, b_ref in ((0, below), (1, above)):
+            left = jnp.concatenate([block[side, rows, :] for block in blocks], axis=1)
             right = [
                 jnp.concatenate(rows_in_order(at_ref, b_ref, (i,), 0), axis=0)
                 for i in range(len(groups))
@@ -132,7 +132,7 @@
             jax.ShapeDtypeStruct((M, COL), jnp.bfloat16 if d else jnp.float32)
             for d in groups
         ),
-        in_specs=[IN_SMEM] + [IN_VMEM] * (2 * X + 3),
+        in_specs=[IN_SMEM] + [IN_VMEM] * (X + 3),
         out_specs=(IN_VMEM,) * len(groups),
         compiler_params=pltpu.CompilerParams(vmem_limit_bytes=24 << 20),
         cost_estimate=pl.CostEstimate(
@@ -155,33 +155,25 @@
     sent_one = after(rhs, firsts).astype(jnp.bfloat16)
     own = exchanged(firsts)
     near = jnp.stack([moved(sent_one, 1), moved(sent_one, -1)])
-    near = after(near, own)
 
-    lo, up = after(lower_second[0], sent_one), upper_second[0]
-    lo_left, lo_right = moved(lo, xs=1), moved(lo, xs=-1)
+    seconds = jnp.stack([lower_second[0], upper_second[0]])
+    seconds = after(seconds, sent_one)
+    two_left, two_right = moved(seconds, xs=1), moved(seconds, xs=-1)
 
-    sent_own = after(own, lo_left, lo_right)
-    left, right = moved(sent_own, xs=1), moved(sent_own, xs=-1)
-    far = moved(sent_own, xs=2)
-    from_down, from_up = moved(near, ys=1), moved(near, ys=-1)
-    below_far = moved(from_down[0], ys=1)
-    above_far = moved(from_up[1], ys=-1)
-    rhs_rows = exchanged(after(rhs, own).reshape(Y, BLK, COL))
-
-    up = after(up, from_down, from_up)
-    up_left, up_right = moved(up, xs=1), moved(up, xs=-1)
-    lo_far = moved(after(lo_left, from_down, from_up), xs=1)
-    up_far = moved(up_right, xs=-1)
+    ready = after(own, near)
+    left, right, far = moved(ready, xs=1), moved(ready, xs=-1), moved(ready, xs=2)
+    parts = dict(near=near, down=moved(near, ys=1), up=moved(near, ys=-1))
+    parts["far"] = moved(after(near, own), ys=2)
+    rhs_rows = exchanged(after(rhs, own, two_left, two_right).reshape(Y, BLK, COL))
+    two_far = moved(after(seconds, left, right), xs=2)
 
     blocks = (own, right, far, left)
-    parts = dict(near=near, up=from_up, down=from_down)
-    parts.update(below_far=below_far, above_far=above_far)
     corr_a, sent_a = first_level(FIRST_GROUPS, at, blocks, parts, rhs_rows)
     late = after(at, sent_a)
     corr_b, sent_b = first_level(LAST_GROUPS, late, blocks, parts, rhs_rows)
     below_a, above_a = moved(sent_a, 2), moved(sent_a, -2)
     below_b, above_b = moved(sent_b, 2), moved(sent_b, -2)
-    blocks = (lo, lo_right, lo_far, lo_left, up, up_right, up_far, up_left)
+    blocks = (seconds, two_right, two_far, two_left)
     two, one = second_level(FIRST_GROUPS, at, blocks, below_a, above_a, corr_a)
     late = after(late, two)
     three, total = second_level(LAST_GROUPS, late, blocks, below_b, above_b, corr_b)

time: 167 us -> 183 us (1.096)
  the two profiles are of different devices: /device:TPU:390 before, /device:TPU:1 now
where the time goes in v8:
time: 183 us; the launch traced here: 180 us
  waiting for transfers between devices  96.3 us (53%)
  starting transfers between devices  63.5 us (35%)
  Pallas kernels  14.1 us (8%)
  other arithmetic  3.82 us (2%)
  local copies, waits for them, and re-layouts  2.28 us (1%)
    ppermute x18, waiting for transfers between devices, moved(): return lax.ppermute(value, AXES, pairs)  65.6 us
    ppermute x18, starting transfers between devices, moved(): return lax.ppermute(value, AXES, pairs)  54.7 us
    all_to_all x2, waiting for transfers between devices, exchanged(): return lax.all_to_all(value, 'y', 0, 0, tiled=True)  30.7 us
    all_to_all x2, starting transfers between devices, exchanged(): return lax.all_to_all(value, 'y', 0, 0, tiled=True)  8.82 us
    pallas_call x2, Pallas kernels, first_level(): pl.pallas_call(functools.partial(first_kernel, groups), name='first_level...  7.72 us
    pallas_call x2, Pallas kernels, second_level(): pl.pallas_call(functools.partial(second_kernel, groups), name='second_lev...  6.33 us
  transfers between devices with their start and end apart: 20, of which 6 were waited for; matrix products, arithmetic and copies ran while one was open for 0% of the time, Pallas kernels for 8%

profile of v8, /device:TPU:1, one launch (start us, length us, event | category | flops | bytes accessed | tf_op | source)
XLA Modules:
  0.0 180.3 jit_solution(8093465408520856467)
XLA Ops:
  0.0 2.3 %pad_maximum_fusion = bf16[4,2,512,128]{3,2,1,0:T(8,128)(2,1)} fusion(bf16[4,1,512,128]{3,2,1,0:T(8,128)(2,1)} %bitcast.13, bf16[4,1,512,128]{3,2,1,0:T(8,128)(2,1)} %bitcast.14), kind=kLoop, calls=%fused_computation | loop fusion | flops 524288 | bytes 2097152 | tf_op jit(solution)/shard_map/stack | solution.py:154
  2.3 5.1 %all-to-all-start = ((bf16[4,2,512,128]{3,2,1,0:T(8,128)(2,1)}), bf16[4,2,512,128]{3,2,1,0:T(8,128)(2,1)S(1)}, u32[]{:S(2)}, u32[]{:S(2)}) async-start(bf16[4,2,512,128]{3,2,1,0:T(8,128)(2,1)} %pad_maximum_fusion), calls=%async_computation | async-start | bytes 2097152 | tf_op jit(solution)/shard_map/all_to_all | solution.py:151
  7.5 4.5 %collective-permute-start = (bf16[2048,128]{1,0:T(8,128)(2,1)S(1)}, bf16[2048,128]{1,0:T(8,128)(2,1)S(1)}, u32[]{:S(2)}, u32[]{:S(2)}) collective-permute-start(bf16[2048,128]{1,0:T(8,128)(2,1)S(1)} %convert_element_type.12), channel_id=1, source_target_pairs={{0,16},{1,17},{2,18},{3,19},{4,20},{5,21},{6,22},{7,23},{8,24},{9,... | collective-permute-start | bytes 1572872 | tf_op jit(solution)/shard_map/ppermute | solution.py:31
  12.0 4.3 %collective-permute-start.1 = (bf16[2048,128]{1,0:T(8,128)(2,1)S(1)}, bf16[2048,128]{1,0:T(8,128)(2,1)S(1)}, u32[]{:S(2)}, u32[]{:S(2)}) collective-permute-start(bf16[2048,128]{1,0:T(8,128)(2,1)S(1)} %convert_element_type.12), channel_id=1, source_target_pairs={{16,0},{17,1},{18,2},{19,3},{20,4},{21,5},{22,6},{23,7},{24,8},{25... | collective-permute-start | bytes 1572872 | tf_op jit(solution)/shard_map/ppermute | solution.py:31
  16.4 1.9 %collective-permute-start.7 = (bf16[2,2048,128]{2,1,0:T(8,128)(2,1)S(1)}, bf16[2,2048,128]{2,1,0:T(8,128)(2,1)}, u32[]{:S(2)}, u32[]{:S(2)}) collective-permute-start(bf16[2,2048,128]{2,1,0:T(8,128)(2,1)S(1)} %pad_maximum_fusion.2.refs_0_), channel_id=1, source_target_pairs={{0,1},{1,2},{2,3},{3,0},{4,5},{5,6},{6,7},{7,4},{8,9},{9,10},{10,1... | collective-permute-start | bytes 3145736 | tf_op jit(solution)/shard_map/ppermute | solution.py:31
  18.4 4.6 %collective-permute-start.8 = (bf16[2,2048,128]{2,1,0:T(8,128)(2,1)S(1)}, bf16[2,2048,128]{2,1,0:T(8,128)(2,1)}, u32[]{:S(2)}, u32[]{:S(2)}) collective-permute-start(bf16[2,2048,128]{2,1,0:T(8,128)(2,1)S(1)} %pad_maximum_fusion.2.refs_0_), channel_id=1, source_target_pairs={{0,3},{1,0},{2,1},{3,2},{4,7},{5,4},{6,5},{7,6},{8,11},{9,8},{10,9... | collective-permute-start | bytes 3145736 | tf_op jit(solution)/shard_map/ppermute | solution.py:31
  23.1 4.3 %collective-permute-start.2 = (bf16[4,2,512,128]{3,2,1,0:T(8,128)(2,1)S(1)}, bf16[4,2,512,128]{3,2,1,0:T(8,128)(2,1)S(1)}, u32[]{:S(2)}, u32[]{:S(2)}) collective-permute-start(bf16[4,2,512,128]{3,2,1,0:T(8,128)(2,1)S(1)} %all-to-all-done.refs_0_), channel_id=1, source_target_pairs={{0,3},{1,0},{2,1},{3,2},{4,7},{5,4},{6,5},{7,6},{8,11},{9,8},{10,9... | collective-permute-start | bytes 3145736 | tf_op jit(solution)/shard_map/ppermute | solution.py:31
  27.4 1.9 %collective-permute-start.4 = (bf16[4,2,512,128]{3,2,1,0:T(8,128)(2,1)S(1)}, bf16[4,2,512,128]{3,2,1,0:T(8,128)(2,1)}, u32[]{:S(2)}, u32[]{:S(2)}) collective-permute-start(bf16[4,2,512,128]{3,2,1,0:T(8,128)(2,1)S(1)} %all-to-all-done.refs_0_), channel_id=1, source_target_pairs={{0,1},{1,2},{2,3},{3,0},{4,5},{5,6},{6,7},{7,4},{8,9},{9,10},{10,1... | collective-permute-start | bytes 3145736 | tf_op jit(solution)/shard_map/ppermute | solution.py:31
  29.4 4.9 %collective-permute-start.6 = (bf16[2,2048,128]{2,1,0:T(8,128)(2,1)S(1)}, bf16[2,2048,128]{2,1,0:T(8,128)(2,1)}, u32[]{:S(2)}, u32[]{:S(2)}) collective-permute-start(bf16[2,2048,128]{2,1,0:T(8,128)(2,1)S(1)} %pad_maximum_fusion.1.refs_6_.refs_7_), channel_id=1, source_target_pairs={{0,12},{1,13},{2,14},{3,15},{4,0},{5,1},{6,2},{7,3},{8,4},{9,5},{1... | collective-permute-start | bytes 3145736 | tf_op jit(solution)/shard_map/ppermute | solution.py:31
  34.2 10.6 %collective-permute-done.7.refs_3_ = bf16[2,2048,128]{2,1,0:T(8,128)(2,1)} collective-permute-done((bf16[2,2048,128]{2,1,0:T(8,128)(2,1)S(1)}, bf16[2,2048,128]{2,1,0:T(8,128)(2,1)}, u32[]{:S(2)}, u32[]{:S(2)}) %collective-permute-start.7) | collective-permute-done | bytes 1048608 | tf_op jit(solution)/shard_map/ppermute | solution.py:31
  44.8 1.9 %collective-permute-start.3 = (bf16[4,2,512,128]{3,2,1,0:T(8,128)(2,1)S(1)}, bf16[4,2,512,128]{3,2,1,0:T(8,128)(2,1)}, u32[]{:S(2)}, u32[]{:S(2)}) collective-permute-start(bf16[4,2,512,128]{3,2,1,0:T(8,128)(2,1)S(1)} %all-to-all-done.refs_0_), channel_id=1, source_target_pairs={{0,2},{1,3},{2,0},{3,1},{4,6},{5,7},{6,4},{7,5},{8,10},{9,11},{10,... | collective-permute-start | bytes 3145736 | tf_op jit(solution)/shard_map/ppermute | solution.py:31
  46.7 5.1 %collective-permute-start.5 = (bf16[2,2048,128]{2,1,0:T(8,128)(2,1)S(1)}, bf16[2,2048,128]{2,1,0:T(8,128)(2,1)}, u32[]{:S(2)}, u32[]{:S(2)}) collective-permute-start(bf16[2,2048,128]{2,1,0:T(8,128)(2,1)S(1)} %pad_maximum_fusion.1.refs_6_.refs_7_), channel_id=1, source_target_pairs={{0,8},{1,9},{2,10},{3,11},{4,12},{5,13},{6,14},{7,15},{8,0},{9,1},... | collective-permute-start | bytes 3145736 | tf_op jit(solution)/shard_map/ppermute | solution.py:31
  51.9 38.9 %collective-permute-done.2.refs_1_ = bf16[4,2,512,128]{3,2,1,0:T(8,128)(2,1)S(1)} collective-permute-done((bf16[4,2,512,128]{3,2,1,0:T(8,128)(2,1)S(1)}, bf16[4,2,512,128]{3,2,1,0:T(8,128)(2,1)S(1)}, u32[]{:S(2)}, u32[]{:S(2)}) %collective-permute-start.2) | collective-permute-done | bytes 1048608 | tf_op jit(solution)/shard_map/ppermute | solution.py:31
  91.7 3.6 %collective-permute-start.12 = (bf16[2,2048,128]{2,1,0:T(8,128)(2,1)S(1)}, bf16[2,2048,128]{2,1,0:T(8,128)(2,1)}, u32[]{:S(2)}, u32[]{:S(2)}) collective-permute-start(bf16[2,2048,128]{2,1,0:T(8,128)(2,1)S(1)} %pad_maximum_fusion.1.refs_6_.refs_7_), channel_id=1, source_target_pairs={{0,4},{1,5},{2,6},{3,7},{4,8},{5,9},{6,10},{7,11},{8,12},{9,13},{1... | collective-permute-start | bytes 3145736 | tf_op jit(solution)/shard_map/ppermute | solution.py:31
  95.3 3.7 %all-to-all-start.1 = ((f32[4,512,128]{2,1,0:T(8,128)}), f32[4,512,128]{2,1,0:T(8,128)S(1)}, u32[]{:S(2)}, u32[]{:S(2)}) async-start(f32[4,512,128]{2,1,0:T(8,128)} %bitcast.11), calls=%async_computation.1 | async-start | bytes 2097152 | tf_op jit(solution)/shard_map/all_to_all | solution.py:151
  99.0 1.9 %collective-permute-start.9 = (bf16[2,2048,128]{2,1,0:T(8,128)(2,1)}, bf16[2,2048,128]{2,1,0:T(8,128)(2,1)}, u32[]{:S(2)}, u32[]{:S(2)}) collective-permute-start(bf16[2,2048,128]{2,1,0:T(8,128)(2,1)} %copy-done), channel_id=1, source_target_pairs={{0,2},{1,3},{2,0},{3,1},{4,6},{5,7},{6,4},{7,5},{8,10},{9,11},{10,... | collective-permute-start | bytes 3145736 | tf_op jit(solution)/shard_map/ppermute | solution.py:31
  101.0 30.7 %all-to-all-done.1.refs_8_ = f32[4,512,128]{2,1,0:T(8,128)S(1)} async-done(((f32[4,512,128]{2,1,0:T(8,128)}), f32[4,512,128]{2,1,0:T(8,128)S(1)}, u32[]{:S(2)}, u32[]{:S(2)}) %all-to-all-start.1) | async-done | bytes 1048608 | tf_op jit(solution)/shard_map/all_to_all | solution.py:151
  131.7 1.2 copy-done.3
  132.9 4.2 %first_level.2 = (f32[2,512,128]{2,1,0:T(8,128)S(1)}, bf16[2,512,128]{2,1,0:T(8,128)(2,1)S(1)}) custom-call(s32[2]{0:T(128)S(1)} %pad_add_fusion.at_ref, bf16[4,2,512,128]{3,2,1,0:T(8,128)(2,1)S(1)} %all-to-all-done.refs_0_, bf16[4,2,512,128]{3,2,1,0:T(8,128)(2,1)S(1)} %copy-done.3, bf16[4,2,512,128]{3,2,1,0:T(8,128)(2,1)} %collective-permute-done.3.refs_2_, ...), custom_call_target="tpu_custom_call" | custom-call | flops 1073741824 | bytes 8388608 | tf_op jit(solution)/shard_map/first_level/pallas_call | solution.py:86
  137.2 1.4 collective-permute-start.10
  138.6 1.3 collective-permute-start.11
  139.9 3.5 %first_level.3 = (f32[2,512,128]{2,1,0:T(8,128)S(1)}, bf16[2,512,128]{2,1,0:T(8,128)(2,1)S(1)}) custom-call(s32[2]{0:T(128)S(1)} %pad_add_fusion.at_ref, bf16[4,2,512,128]{3,2,1,0:T(8,128)(2,1)S(1)} %all-to-all-done.refs_0_, bf16[4,2,512,128]{3,2,1,0:T(8,128)(2,1)S(1)} %copy-done.3, bf16[4,2,512,128]{3,2,1,0:T(8,128)(2,1)} %collective-permute-done.3.refs_2_, ...), custom_call_target="tpu_custom_call" | custom-call | flops 1073741824 | bytes 8388608 | tf_op jit(solution)/shard_map/first_level/pallas_call | solution.py:86
  143.4 4.0 %collective-permute-start.13 = (bf16[2,512,128]{2,1,0:T(8,128)(2,1)S(1)}, bf16[2,512,128]{2,1,0:T(8,128)(2,1)S(1)}, u32[]{:S(2)}, u32[]{:S(2)}) collective-permute-start(bf16[2,512,128]{2,1,0:T(8,128)(2,1)S(1)} %get-tuple-element.32), channel_id=1, source_target_pairs={{0,32},{1,33},{2,34},{3,35},{4,36},{5,37},{6,38},{7,39},{8,40},{9,... | collective-permute-start | bytes 786440 | tf_op jit(solution)/shard_map/ppermute | solution.py:31
  147.4 1.3 collective-permute-start.14
  148.8 3.1 %second_level.2 = (bf16[2048,128]{1,0:T(8,128)(2,1)S(1)}, bf16[2048,128]{1,0:T(8,128)(2,1)S(1)}) custom-call(s32[2]{0:T(128)S(1)} %pad_add_fusion.at_ref, bf16[2,2048,128]{2,1,0:T(8,128)(2,1)S(1)} %copy-done.1, bf16[2,2048,128]{2,1,0:T(8,128)(2,1)} %collective-permute-done.8.refs_1_, bf16[2,2048,128]{2,1,0:T(8,128)(2,1)} %collective-permute-done.9.refs_2_, ...), custom_call_target="tpu_custom_call" | custom-call | flops 1073741824 | bytes 6291456 | tf_op jit(solution)/shard_map/second_level/pallas_call | solution.py:128
  151.9 2.5 %collective-permute-start.15 = (bf16[2048,128]{1,0:T(8,128)(2,1)S(1)}, bf16[2048,128]{1,0:T(8,128)(2,1)S(1)}, u32[]{:S(2)}, u32[]{:S(2)}) collective-permute-start(bf16[2048,128]{1,0:T(8,128)(2,1)S(1)} %get-tuple-element.30), channel_id=1, source_target_pairs={{0,8},{1,9},{2,10},{3,11},{4,12},{5,13},{6,14},{7,15},{8,0},{9,1},... | collective-permute-start | bytes 1572872 | tf_op jit(solution)/shard_map/ppermute | solution.py:31
  155.2 3.2 %second_level.3 = (bf16[2048,128]{1,0:T(8,128)(2,1)S(1)}, f32[2048,128]{1,0:T(8,128)S(1)}) custom-call(s32[2]{0:T(128)S(1)} %pad_add_fusion.at_ref, bf16[2,2048,128]{2,1,0:T(8,128)(2,1)S(1)} %copy-done.1, bf16[2,2048,128]{2,1,0:T(8,128)(2,1)} %collective-permute-done.8.refs_1_, bf16[2,2048,128]{2,1,0:T(8,128)(2,1)} %collective-permute-done.9.refs_2_, ...), custom_call_target="tpu_custom_call" | custom-call | flops 1073741824 | bytes 6291456 | tf_op jit(solution)/shard_map/second_level/pallas_call | solution.py:128
  158.4 1.9 %collective-permute-start.17 = (bf16[2048,128]{1,0:T(8,128)(2,1)S(1)}, bf16[2048,128]{1,0:T(8,128)(2,1)S(1)}, u32[]{:S(2)}, u32[]{:S(2)}) collective-permute-start(bf16[2048,128]{1,0:T(8,128)(2,1)S(1)} %get-tuple-element.36), channel_id=1, source_target_pairs={{0,12},{1,13},{2,14},{3,15},{4,0},{5,1},{6,2},{7,3},{8,4},{9,5},{1... | collective-permute-start | bytes 1572872 | tf_op jit(solution)/shard_map/ppermute | solution.py:31
  160.3 3.4 %collective-permute-start.16 = (bf16[2048,128]{1,0:T(8,128)(2,1)S(1)}, bf16[2048,128]{1,0:T(8,128)(2,1)S(1)}, u32[]{:S(2)}, u32[]{:S(2)}) collective-permute-start(bf16[2048,128]{1,0:T(8,128)(2,1)S(1)} %get-tuple-element.35), channel_id=1, source_target_pairs={{0,4},{1,5},{2,6},{3,7},{4,8},{5,9},{6,10},{7,11},{8,12},{9,13},{1... | collective-permute-start | bytes 1572872 | tf_op jit(solution)/shard_map/ppermute | solution.py:31
  163.7 7.2 %collective-permute-done.17 = bf16[2048,128]{1,0:T(8,128)(2,1)S(1)} collective-permute-done((bf16[2048,128]{1,0:T(8,128)(2,1)S(1)}, bf16[2048,128]{1,0:T(8,128)(2,1)S(1)}, u32[]{:S(2)}, u32[]{:S(2)}) %collective-permute-start.17) | collective-permute-done | bytes 524320 | tf_op jit(solution)/shard_map/ppermute | solution.py:31
  170.9 8.2 %collective-permute-done.16 = bf16[2048,128]{1,0:T(8,128)(2,1)S(1)} collective-permute-done((bf16[2048,128]{1,0:T(8,128)(2,1)S(1)}, bf16[2048,128]{1,0:T(8,128)(2,1)S(1)}, u32[]{:S(2)}, u32[]{:S(2)}) %collective-permute-start.16) | collective-permute-done | bytes 524320 | tf_op jit(solution)/shard_map/ppermute | solution.py:31
  179.1 1.2 add_bitcast_fusion
  (34 shorter events, 2.2 us)
Async XLA Ops:
  2.3 5.1 %copy-start.4 = (f32[1,2048,128]{2,1,0:T(8,128)S(1)}, f32[1,2048,128]{2,1,0:T(8,128)}, u32[]{:S(2)}) copy-start(f32[1,2048,128]{2,1,0:T(8,128)} %param.5) | copy-start | bytes 3145732
  2.3 20.8 %all-to-all-start = ((bf16[4,2,512,128]{3,2,1,0:T(8,128)(2,1)}), bf16[4,2,512,128]{3,2,1,0:T(8,128)(2,1)S(1)}, u32[]{:S(2)}, u32[]{:S(2)}) async-start(bf16[4,2,512,128]{3,2,1,0:T(8,128)(2,1)} %pad_maximum_fusion), calls=%async_computation | async-start | bytes 2097152 | tf_op jit(solution)/shard_map/all_to_all | solution.py:151
  7.4 8.9 %copy-start.6 = (bf16[1,2048,128]{2,1,0:T(8,128)(2,1)S(1)}, bf16[1,2048,128]{2,1,0:T(8,128)(2,1)}, u32[]{:S(2)}) copy-start(bf16[1,2048,128]{2,1,0:T(8,128)(2,1)} %param.9) | copy-start | bytes 1572868
  7.4 8.9 %copy-start.7 = (bf16[1,2048,128]{2,1,0:T(8,128)(2,1)S(1)}, bf16[1,2048,128]{2,1,0:T(8,128)(2,1)}, u32[]{:S(2)}) copy-start(bf16[1,2048,128]{2,1,0:T(8,128)(2,1)} %param.8) | copy-start | bytes 1572868
  7.5 15.4 %collective-permute-start = (bf16[2048,128]{1,0:T(8,128)(2,1)S(1)}, bf16[2048,128]{1,0:T(8,128)(2,1)S(1)}, u32[]{:S(2)}, u32[]{:S(2)}) collective-permute-start(bf16[2048,128]{1,0:T(8,128)(2,1)S(1)} %convert_element_type.12), channel_id=1, source_target_pairs={{0,16},{1,17},{2,18},{3,19},{4,20},{5,21},{6,22},{7,23},{8,24},{9,... | collective-permute-start | bytes 1572872 | tf_op jit(solution)/shard_map/ppermute | solution.py:31
  12.0 10.9 %collective-permute-start.1 = (bf16[2048,128]{1,0:T(8,128)(2,1)S(1)}, bf16[2048,128]{1,0:T(8,128)(2,1)S(1)}, u32[]{:S(2)}, u32[]{:S(2)}) collective-permute-start(bf16[2048,128]{1,0:T(8,128)(2,1)S(1)} %convert_element_type.12), channel_id=1, source_target_pairs={{16,0},{17,1},{18,2},{19,3},{20,4},{21,5},{22,6},{23,7},{24,8},{25... | collective-permute-start | bytes 1572872 | tf_op jit(solution)/shard_map/ppermute | solution.py:31
  16.4 6.7 %copy-start = (bf16[2,2048,128]{2,1,0:T(8,128)(2,1)}, bf16[2,2048,128]{2,1,0:T(8,128)(2,1)S(1)}, u32[]{:S(2)}) copy-start(bf16[2,2048,128]{2,1,0:T(8,128)(2,1)S(1)} %pad_maximum_fusion.2.refs_0_) | copy-start | bytes 3145732
  16.4 28.4 %collective-permute-start.7 = (bf16[2,2048,128]{2,1,0:T(8,128)(2,1)S(1)}, bf16[2,2048,128]{2,1,0:T(8,128)(2,1)}, u32[]{:S(2)}, u32[]{:S(2)}) collective-permute-start(bf16[2,2048,128]{2,1,0:T(8,128)(2,1)S(1)} %pad_maximum_fusion.2.refs_0_), channel_id=1, source_target_pairs={{0,1},{1,2},{2,3},{3,0},{4,5},{5,6},{6,7},{7,4},{8,9},{9,10},{10,1... | collective-permute-start | bytes 3145736 | tf_op jit(solution)/shard_map/ppermute | solution.py:31
  18.4 28.4 %collective-permute-start.8 = (bf16[2,2048,128]{2,1,0:T(8,128)(2,1)S(1)}, bf16[2,2048,128]{2,1,0:T(8,128)(2,1)}, u32[]{:S(2)}, u32[]{:S(2)}) collective-permute-start(bf16[2,2048,128]{2,1,0:T(8,128)(2,1)S(1)} %pad_maximum_fusion.2.refs_0_), channel_id=1, source_target_pairs={{0,3},{1,0},{2,1},{3,2},{4,7},{5,4},{6,5},{7,6},{8,11},{9,8},{10,9... | collective-permute-start | bytes 3145736 | tf_op jit(solution)/shard_map/ppermute | solution.py:31
  23.1 67.6 %collective-permute-start.2 = (bf16[4,2,512,128]{3,2,1,0:T(8,128)(2,1)S(1)}, bf16[4,2,512,128]{3,2,1,0:T(8,128)(2,1)S(1)}, u32[]{:S(2)}, u32[]{:S(2)}) collective-permute-start(bf16[4,2,512,128]{3,2,1,0:T(8,128)(2,1)S(1)} %all-to-all-done.refs_0_), channel_id=1, source_target_pairs={{0,3},{1,0},{2,1},{3,2},{4,7},{5,4},{6,5},{7,6},{8,11},{9,8},{10,9... | collective-permute-start | bytes 3145736 | tf_op jit(solution)/shard_map/ppermute | solution.py:31
  27.4 71.6 %collective-permute-start.4 = (bf16[4,2,512,128]{3,2,1,0:T(8,128)(2,1)S(1)}, bf16[4,2,512,128]{3,2,1,0:T(8,128)(2,1)}, u32[]{:S(2)}, u32[]{:S(2)}) collective-permute-start(bf16[4,2,512,128]{3,2,1,0:T(8,128)(2,1)S(1)} %all-to-all-done.refs_0_), channel_id=1, source_target_pairs={{0,1},{1,2},{2,3},{3,0},{4,5},{5,6},{6,7},{7,4},{8,9},{9,10},{10,1... | collective-permute-start | bytes 3145736 | tf_op jit(solution)/shard_map/ppermute | solution.py:31
  29.4 71.6 %collective-permute-start.6 = (bf16[2,2048,128]{2,1,0:T(8,128)(2,1)S(1)}, bf16[2,2048,128]{2,1,0:T(8,128)(2,1)}, u32[]{:S(2)}, u32[]{:S(2)}) collective-permute-start(bf16[2,2048,128]{2,1,0:T(8,128)(2,1)S(1)} %pad_maximum_fusion.1.refs_6_.refs_7_), channel_id=1, source_target_pairs={{0,12},{1,13},{2,14},{3,15},{4,0},{5,1},{6,2},{7,3},{8,4},{9,5},{1... | collective-permute-start | bytes 3145736 | tf_op jit(solution)/shard_map/ppermute | solution.py:31
  44.8 86.9 %collective-permute-start.3 = (bf16[4,2,512,128]{3,2,1,0:T(8,128)(2,1)S(1)}, bf16[4,2,512,128]{3,2,1,0:T(8,128)(2,1)}, u32[]{:S(2)}, u32[]{:S(2)}) collective-permute-start(bf16[4,2,512,128]{3,2,1,0:T(8,128)(2,1)S(1)} %all-to-all-done.refs_0_), channel_id=1, source_target_pairs={{0,2},{1,3},{2,0},{3,1},{4,6},{5,7},{6,4},{7,5},{8,10},{9,11},{10,... | collective-permute-start | bytes 3145736 | tf_op jit(solution)/shard_map/ppermute | solution.py:31
  46.7 84.9 %collective-permute-start.5 = (bf16[2,2048,128]{2,1,0:T(8,128)(2,1)S(1)}, bf16[2,2048,128]{2,1,0:T(8,128)(2,1)}, u32[]{:S(2)}, u32[]{:S(2)}) collective-permute-start(bf16[2,2048,128]{2,1,0:T(8,128)(2,1)S(1)} %pad_maximum_fusion.1.refs_6_.refs_7_), channel_id=1, source_target_pairs={{0,8},{1,9},{2,10},{3,11},{4,12},{5,13},{6,14},{7,15},{8,0},{9,1},... | collective-permute-start | bytes 3145736 | tf_op jit(solution)/shard_map/ppermute | solution.py:31
  90.7 1.0 copy-start.2
  91.7 48.2 %collective-permute-start.12 = (bf16[2,2048,128]{2,1,0:T(8,128)(2,1)S(1)}, bf16[2,2048,128]{2,1,0:T(8,128)(2,1)}, u32[]{:S(2)}, u32[]{:S(2)}) collective-permute-start(bf16[2,2048,128]{2,1,0:T(8,128)(2,1)S(1)} %pad_maximum_fusion.1.refs_6_.refs_7_), channel_id=1, source_target_pairs={{0,4},{1,5},{2,6},{3,7},{4,8},{5,9},{6,10},{7,11},{8,12},{9,13},{1... | collective-permute-start | bytes 3145736 | tf_op jit(solution)/shard_map/ppermute | solution.py:31
  95.3 36.3 %all-to-all-start.1 = ((f32[4,512,128]{2,1,0:T(8,128)}), f32[4,512,128]{2,1,0:T(8,128)S(1)}, u32[]{:S(2)}, u32[]{:S(2)}) async-start(f32[4,512,128]{2,1,0:T(8,128)} %bitcast.11), calls=%async_computation.1 | async-start | bytes 2097152 | tf_op jit(solution)/shard_map/all_to_all | solution.py:151
  99.0 49.7 %collective-permute-start.9 = (bf16[2,2048,128]{2,1,0:T(8,128)(2,1)}, bf16[2,2048,128]{2,1,0:T(8,128)(2,1)}, u32[]{:S(2)}, u32[]{:S(2)}) collective-permute-start(bf16[2,2048,128]{2,1,0:T(8,128)(2,1)} %copy-done), channel_id=1, source_target_pairs={{0,2},{1,3},{2,0},{3,1},{4,6},{5,7},{6,4},{7,5},{8,10},{9,11},{10,... | collective-permute-start | bytes 3145736 | tf_op jit(solution)/shard_map/ppermute | solution.py:31
  131.7 1.2 copy-start.3
  137.2 11.6 %copy-start.1 = (bf16[2,2048,128]{2,1,0:T(8,128)(2,1)S(1)}, bf16[2,2048,128]{2,1,0:T(8,128)(2,1)}, u32[]{:S(2)}) copy-start(bf16[2,2048,128]{2,1,0:T(8,128)(2,1)} %copy-done) | copy-start | bytes 3145732
  137.2 11.5 %collective-permute-start.10 = (bf16[2,512,128]{2,1,0:T(8,128)(2,1)S(1)}, bf16[2,512,128]{2,1,0:T(8,128)(2,1)S(1)}, u32[]{:S(2)}, u32[]{:S(2)}) collective-permute-start(bf16[2,512,128]{2,1,0:T(8,128)(2,1)S(1)} %get-tuple-element.26), channel_id=1, source_target_pairs={{0,32},{1,33},{2,34},{3,35},{4,36},{5,37},{6,38},{7,39},{8,40},{9,... | collective-permute-start | bytes 786440 | tf_op jit(solution)/shard_map/ppermute | solution.py:31
  138.6 10.1 %collective-permute-start.11 = (bf16[2,512,128]{2,1,0:T(8,128)(2,1)S(1)}, bf16[2,512,128]{2,1,0:T(8,128)(2,1)S(1)}, u32[]{:S(2)}, u32[]{:S(2)}) collective-permute-start(bf16[2,512,128]{2,1,0:T(8,128)(2,1)S(1)} %get-tuple-element.26), channel_id=1, source_target_pairs={{32,0},{33,1},{34,2},{35,3},{36,4},{37,5},{38,6},{39,7},{40,8},{41... | collective-permute-start | bytes 786440 | tf_op jit(solution)/shard_map/ppermute | solution.py:31
  143.4 11.0 %collective-permute-start.13 = (bf16[2,512,128]{2,1,0:T(8,128)(2,1)S(1)}, bf16[2,512,128]{2,1,0:T(8,128)(2,1)S(1)}, u32[]{:S(2)}, u32[]{:S(2)}) collective-permute-start(bf16[2,512,128]{2,1,0:T(8,128)(2,1)S(1)} %get-tuple-element.32), channel_id=1, source_target_pairs={{0,32},{1,33},{2,34},{3,35},{4,36},{5,37},{6,38},{7,39},{8,40},{9,... | collective-permute-start | bytes 786440 | tf_op jit(solution)/shard_map/ppermute | solution.py:31
  147.4 7.8 %collective-permute-start.14 = (bf16[2,512,128]{2,1,0:T(8,128)(2,1)S(1)}, bf16[2,512,128]{2,1,0:T(8,128)(2,1)S(1)}, u32[]{:S(2)}, u32[]{:S(2)}) collective-permute-start(bf16[2,512,128]{2,1,0:T(8,128)(2,1)S(1)} %get-tuple-element.32), channel_id=1, source_target_pairs={{32,0},{33,1},{34,2},{35,3},{36,4},{37,5},{38,6},{39,7},{40,8},{41... | collective-permute-start | bytes 786440 | tf_op jit(solution)/shard_map/ppermute | solution.py:31
  151.9 19.0 %collective-permute-start.15 = (bf16[2048,128]{1,0:T(8,128)(2,1)S(1)}, bf16[2048,128]{1,0:T(8,128)(2,1)S(1)}, u32[]{:S(2)}, u32[]{:S(2)}) collective-permute-start(bf16[2048,128]{1,0:T(8,128)(2,1)S(1)} %get-tuple-element.30), channel_id=1, source_target_pairs={{0,8},{1,9},{2,10},{3,11},{4,12},{5,13},{6,14},{7,15},{8,0},{9,1},... | collective-permute-start | bytes 1572872 | tf_op jit(solution)/shard_map/ppermute | solution.py:31
  155.2 23.9 %copy-start.5 = (f32[1,2048,128]{2,1,0:T(8,128)S(1)}, f32[1,2048,128]{2,1,0:T(8,128)}, u32[]{:S(2)}) copy-start(f32[1,2048,128]{2,1,0:T(8,128)} %param.5) | copy-start | bytes 3145732
  158.4 12.5 %collective-permute-start.17 = (bf16[2048,128]{1,0:T(8,128)(2,1)S(1)}, bf16[2048,128]{1,0:T(8,128)(2,1)S(1)}, u32[]{:S(2)}, u32[]{:S(2)}) collective-permute-start(bf16[2048,128]{1,0:T(8,128)(2,1)S(1)} %get-tuple-element.36), channel_id=1, source_target_pairs={{0,12},{1,13},{2,14},{3,15},{4,0},{5,1},{6,2},{7,3},{8,4},{9,5},{1... | collective-permute-start | bytes 1572872 | tf_op jit(solution)/shard_map/ppermute | solution.py:31
  160.3 18.7 %collective-permute-start.16 = (bf16[2048,128]{1,0:T(8,128)(2,1)S(1)}, bf16[2048,128]{1,0:T(8,128)(2,1)S(1)}, u32[]{:S(2)}, u32[]{:S(2)}) collective-permute-start(bf16[2048,128]{1,0:T(8,128)(2,1)S(1)} %get-tuple-element.35), channel_id=1, source_target_pairs={{0,4},{1,5},{2,6},{3,7},{4,8},{5,9},{6,10},{7,11},{8,12},{9,13},{1... | collective-permute-start | bytes 1572872 | tf_op jit(solution)/shard_map/ppermute | solution.py:31

commit v9 on v8

--- a/solution.py
+++ b/solution.py
@@ -70,7 +70,7 @@
     places = {
         0: (("near", (0,)), ("near", (1,))),
         1: (("up", (0,)), ("up", (1,))),
-        2: (("far", (0,)), ("far", (1,))),
+        2: (("below_far", ()), ("above_far", ())),
         3: (("down", (0,)), ("down", (1,))),
     }
     return [place for d in groups for place in places[d]]
@@ -102,14 +102,17 @@
 
 
 def second_kernel(groups, at_ref, *refs):
-    blocks = refs[:X]
-    below, above, corr_ref, *outs = refs[X:]
+    lo, up, left, right, lo_far, up_far = refs[:6]
+    lower = (lo, right.at[0], lo_far, left.at[0])
+    upper = (up, right.at[1], up_far, left.at[1])
+    below, above, corr_ref, *outs = refs[6:]
 
     for m in range(Y):
         rows = pl.ds(m * BLK, BLK)
         total = None
-        for side, b_ref in ((0, below), (1, above)):
-            left = jnp.concatenate([block[side, rows, :] for block in blocks], axis=1)
+        for blocks, b_ref in ((lower, below), (upper, above)):
+            blocks = [block[rows, :] for block in blocks]
+            left = jnp.concatenate(blocks, axis=1)
             right = [
                 jnp.concatenate(rows_in_order(at_ref, b_ref, (i,), 0), axis=0)
                 for i in range(len(groups))
@@ -132,7 +135,7 @@
             jax.ShapeDtypeStruct((M, COL), jnp.bfloat16 if d else jnp.float32)
             for d in groups
         ),
-        in_specs=[IN_SMEM] + [IN_VMEM] * (X + 3),
+        in_specs=[IN_SMEM] + [IN_VMEM] * 9,
         out_specs=(IN_VMEM,) * len(groups),
         compiler_params=pltpu.CompilerParams(vmem_limit_bytes=24 << 20),
         cost_estimate=pl.CostEstimate(
@@ -156,24 +159,27 @@
     own = exchanged(firsts)
     near = jnp.stack([moved(sent_one, 1), moved(sent_one, -1)])
 
-    seconds = jnp.stack([lower_second[0], upper_second[0]])
-    seconds = after(seconds, sent_one)
+    lo_two, up_two = lower_second[0], upper_second[0]
+    seconds = after(jnp.stack([lo_two, up_two]), sent_one)
     two_left, two_right = moved(seconds, xs=1), moved(seconds, xs=-1)
 
-    ready = after(own, near)
-    left, right, far = moved(ready, xs=1), moved(ready, xs=-1), moved(ready, xs=2)
-    parts = dict(near=near, down=moved(near, ys=1), up=moved(near, ys=-1))
-    parts["far"] = moved(after(near, own), ys=2)
+    left, right, far = moved(own, xs=1), moved(own, xs=-1), moved(own, xs=2)
+    down, up = moved(near, ys=1), moved(near, ys=-1)
+    below_far, above_far = moved(down[0], ys=1), moved(up[1], ys=-1)
     rhs_rows = exchanged(after(rhs, own, two_left, two_right).reshape(Y, BLK, COL))
-    two_far = moved(after(seconds, left, right), xs=2)
+
+    lo_far = moved(after(two_left[0], left), xs=1)
+    up_far = moved(after(two_right[1], right), xs=-1)
 
     blocks = (own, right, far, left)
+    parts = dict(near=near, down=down, up=up)
+    parts.update(below_far=below_far, above_far=above_far)
     corr_a, sent_a = first_level(FIRST_GROUPS, at, blocks, parts, rhs_rows)
     late = after(at, sent_a)
     corr_b, sent_b = first_level(LAST_GROUPS, late, blocks, parts, rhs_rows)
     below_a, above_a = moved(sent_a, 2), moved(sent_a, -2)
     below_b, above_b = moved(sent_b, 2), moved(sent_b, -2)
-    blocks = (seconds, two_right, two_far, two_left)
+    blocks = (lo_two, up_two, two_left, two_right, lo_far, up_far)
     two, one = second_level(FIRST_GROUPS, at, blocks, below_a, above_a, corr_a)
     late = after(late, two)
     three, total = second_level(LAST_GROUPS, late, blocks, below_b, above_b, corr_b)

time: 183 us -> 148 us (0.81)
  the two profiles are of different devices: /device:TPU:1 before, /device:TPU:128 now
where the time goes in v9:
time: 148 us; the launch traced here: 147 us
  starting transfers between devices  79.1 us (53%)
  waiting for transfers between devices  40.4 us (27%)
  Pallas kernels  13.5 us (9%)
  local copies, waits for them, and re-layouts  7.32 us (5%)
  other arithmetic  6.08 us (4%)
    ppermute x20, starting transfers between devices, moved(): return lax.ppermute(value, AXES, pairs)  71.1 us
    ppermute x20, waiting for transfers between devices, moved(): return lax.ppermute(value, AXES, pairs)  33 us
    all_to_all x2, starting transfers between devices, exchanged(): return lax.all_to_all(value, 'y', 0, 0, tiled=True)  8.03 us
    pallas_call x2, Pallas kernels, first_level(): pl.pallas_call(functools.partial(first_kernel, groups), name='first_level...  7.83 us
    all_to_all x2, waiting for transfers between devices, exchanged(): return lax.all_to_all(value, 'y', 0, 0, tiled=True)  7.4 us
    pallas_call x2, Pallas kernels, second_level(): pl.pallas_call(functools.partial(second_kernel, groups), name='second_lev...  5.65 us
    squeeze x2, local copies, waits for them, and re-layouts, on_device(): below_far, above_far = (moved(down[0], ys=1), moved(up[1], ys=-1))  3.76 us
  transfers between devices with their start and end apart: 22, of which 7 were waited for; matrix products, arithmetic and copies ran while one was open for 6% of the time, Pallas kernels for 9%

profile of v9, /device:TPU:128, one launch (start us, length us, event | category | flops | bytes accessed | tf_op | source)
XLA Modules:
  0.0 146.7 jit_solution(10979047147185562492)
XLA Ops:
  0.0 2.4 %pad_maximum_fusion = bf16[4,2,512,128]{3,2,1,0:T(8,128)(2,1)} fusion(bf16[4,1,512,128]{3,2,1,0:T(8,128)(2,1)} %bitcast.27, bf16[4,1,512,128]{3,2,1,0:T(8,128)(2,1)} %bitcast.28), kind=kLoop, calls=%fused_computation | loop fusion | flops 524288 | bytes 2097152 | tf_op jit(solution)/shard_map/stack | solution.py:157
  2.4 2.1 %collective-permute-start.3 = (bf16[2048,128]{1,0:T(8,128)(2,1)S(1)}, bf16[2048,128]{1,0:T(8,128)(2,1)S(1)}, u32[]{:S(2)}, u32[]{:S(2)}) collective-permute-start(bf16[2048,128]{1,0:T(8,128)(2,1)S(1)} %convert_element_type.12), channel_id=1, source_target_pairs={{0,16},{1,17},{2,18},{3,19},{4,20},{5,21},{6,22},{7,23},{8,24},{9,... | collective-permute-start | bytes 1572872 | tf_op jit(solution)/shard_map/ppermute | solution.py:31
  4.5 4.9 %collective-permute-start.4 = (bf16[2048,128]{1,0:T(8,128)(2,1)S(1)}, bf16[2048,128]{1,0:T(8,128)(2,1)}, u32[]{:S(2)}, u32[]{:S(2)}) collective-permute-start(bf16[2048,128]{1,0:T(8,128)(2,1)S(1)} %convert_element_type.12), channel_id=1, source_target_pairs={{16,0},{17,1},{18,2},{19,3},{20,4},{21,5},{22,6},{23,7},{24,8},{25... | collective-permute-start | bytes 1572872 | tf_op jit(solution)/shard_map/ppermute | solution.py:31
  10.5 4.7 %collective-permute-start.10 = (bf16[2,2048,128]{2,1,0:T(8,128)(2,1)}, bf16[2,2048,128]{2,1,0:T(8,128)(2,1)S(1)}, u32[]{:S(2)}, u32[]{:S(2)}) collective-permute-start(bf16[2,2048,128]{2,1,0:T(8,128)(2,1)} %pad_maximum_fusion.2), channel_id=1, source_target_pairs={{0,3},{1,0},{2,1},{3,2},{4,7},{5,4},{6,5},{7,6},{8,11},{9,8},{10,9... | collective-permute-start | bytes 3145736 | tf_op jit(solution)/shard_map/ppermute | solution.py:31
  15.1 1.9 %collective-permute-start.9 = (bf16[2,2048,128]{2,1,0:T(8,128)(2,1)}, bf16[2,2048,128]{2,1,0:T(8,128)(2,1)}, u32[]{:S(2)}, u32[]{:S(2)}) collective-permute-start(bf16[2,2048,128]{2,1,0:T(8,128)(2,1)} %pad_maximum_fusion.2), channel_id=1, source_target_pairs={{0,1},{1,2},{2,3},{3,0},{4,5},{5,6},{6,7},{7,4},{8,9},{9,10},{10,1... | collective-permute-start | bytes 3145736 | tf_op jit(solution)/shard_map/ppermute | solution.py:31
  17.0 4.5 %all-to-all-start = ((bf16[4,2,512,128]{3,2,1,0:T(8,128)(2,1)}), bf16[4,2,512,128]{3,2,1,0:T(8,128)(2,1)S(1)}, u32[]{:S(2)}, u32[]{:S(2)}) async-start(bf16[4,2,512,128]{3,2,1,0:T(8,128)(2,1)} %pad_maximum_fusion), calls=%async_computation | async-start | bytes 2097152 | tf_op jit(solution)/shard_map/all_to_all | solution.py:154
  23.6 3.9 %collective-permute-start.5 = (bf16[2,2048,128]{2,1,0:T(8,128)(2,1)S(1)}, bf16[2,2048,128]{2,1,0:T(8,128)(2,1)}, u32[]{:S(2)}, u32[]{:S(2)}) collective-permute-start(bf16[2,2048,128]{2,1,0:T(8,128)(2,1)S(1)} %pad_maximum_fusion.1.refs_6_.refs_7_), channel_id=1, source_target_pairs={{0,4},{1,5},{2,6},{3,7},{4,8},{5,9},{6,10},{7,11},{8,12},{9,13},{1... | collective-permute-start | bytes 3145736 | tf_op jit(solution)/shard_map/ppermute | solution.py:31
  27.6 3.1 %collective-permute-start.7 = (bf16[2,2048,128]{2,1,0:T(8,128)(2,1)S(1)}, bf16[2,2048,128]{2,1,0:T(8,128)(2,1)}, u32[]{:S(2)}, u32[]{:S(2)}) collective-permute-start(bf16[2,2048,128]{2,1,0:T(8,128)(2,1)S(1)} %pad_maximum_fusion.1.refs_6_.refs_7_), channel_id=1, source_target_pairs={{0,12},{1,13},{2,14},{3,15},{4,0},{5,1},{6,2},{7,3},{8,4},{9,5},{1... | collective-permute-start | bytes 3145736 | tf_op jit(solution)/shard_map/ppermute | solution.py:31
  30.7 7.4 %all-to-all-done.refs_0_ = bf16[4,2,512,128]{3,2,1,0:T(8,128)(2,1)S(1)} async-done(((bf16[4,2,512,128]{3,2,1,0:T(8,128)(2,1)}), bf16[4,2,512,128]{3,2,1,0:T(8,128)(2,1)S(1)}, u32[]{:S(2)}, u32[]{:S(2)}) %all-to-all-start) | async-done | bytes 1048608 | tf_op jit(solution)/shard_map/all_to_all | solution.py:154
  38.1 5.1 %collective-permute-start = (bf16[4,2,512,128]{3,2,1,0:T(8,128)(2,1)S(1)}, bf16[4,2,512,128]{3,2,1,0:T(8,128)(2,1)}, u32[]{:S(2)}, u32[]{:S(2)}) collective-permute-start(bf16[4,2,512,128]{3,2,1,0:T(8,128)(2,1)S(1)} %all-to-all-done.refs_0_), channel_id=1, source_target_pairs={{0,3},{1,0},{2,1},{3,2},{4,7},{5,4},{6,5},{7,6},{8,11},{9,8},{10,9... | collective-permute-start | bytes 3145736 | tf_op jit(solution)/shard_map/ppermute | solution.py:31
  43.2 1.9 %collective-permute-start.2 = (bf16[4,2,512,128]{3,2,1,0:T(8,128)(2,1)S(1)}, bf16[4,2,512,128]{3,2,1,0:T(8,128)(2,1)}, u32[]{:S(2)}, u32[]{:S(2)}) collective-permute-start(bf16[4,2,512,128]{3,2,1,0:T(8,128)(2,1)S(1)} %all-to-all-done.refs_0_), channel_id=1, source_target_pairs={{0,1},{1,2},{2,3},{3,0},{4,5},{5,6},{6,7},{7,4},{8,9},{9,10},{10,1... | collective-permute-start | bytes 3145736 | tf_op jit(solution)/shard_map/ppermute | solution.py:31
  45.2 3.4 %collective-permute-start.1 = (bf16[4,2,512,128]{3,2,1,0:T(8,128)(2,1)S(1)}, bf16[4,2,512,128]{3,2,1,0:T(8,128)(2,1)}, u32[]{:S(2)}, u32[]{:S(2)}) collective-permute-start(bf16[4,2,512,128]{3,2,1,0:T(8,128)(2,1)S(1)} %all-to-all-done.refs_0_), channel_id=1, source_target_pairs={{0,2},{1,3},{2,0},{3,1},{4,6},{5,7},{6,4},{7,5},{8,10},{9,11},{10,... | collective-permute-start | bytes 3145736 | tf_op jit(solution)/shard_map/ppermute | solution.py:31
  48.6 3.6 %all-to-all-start.1 = ((f32[4,512,128]{2,1,0:T(8,128)}), f32[4,512,128]{2,1,0:T(8,128)S(1)}, u32[]{:S(2)}, u32[]{:S(2)}) async-start(f32[4,512,128]{2,1,0:T(8,128)} %bitcast.25), calls=%async_computation.1 | async-start | bytes 2097152 | tf_op jit(solution)/shard_map/all_to_all | solution.py:154
  54.0 5.8 %collective-permute-done.5.refs_4_.refs_5_ = bf16[2,2048,128]{2,1,0:T(8,128)(2,1)} collective-permute-done((bf16[2,2048,128]{2,1,0:T(8,128)(2,1)S(1)}, bf16[2,2048,128]{2,1,0:T(8,128)(2,1)}, u32[]{:S(2)}, u32[]{:S(2)}) %collective-permute-start.5) | collective-permute-done | bytes 1048608 | tf_op jit(solution)/shard_map/ppermute | solution.py:31
  65.5 5.1 %collective-permute-start.8 = (bf16[2048,128]{1,0:T(8,128)(2,1)}, bf16[2048,128]{1,0:T(8,128)(2,1)}, u32[]{:S(2)}, u32[]{:S(2)}) collective-permute-start(bf16[2048,128]{1,0:T(8,128)(2,1)} %slice_bitcast_fusion.2), channel_id=1, source_target_pairs={{0,12},{1,13},{2,14},{3,15},{4,0},{5,1},{6,2},{7,3},{8,4},{9,5},{1... | collective-permute-start | bytes 1572872 | tf_op jit(solution)/shard_map/ppermute | solution.py:31
  71.5 12.2 %collective-permute-done.2.refs_3_ = bf16[4,2,512,128]{3,2,1,0:T(8,128)(2,1)} collective-permute-done((bf16[4,2,512,128]{3,2,1,0:T(8,128)(2,1)S(1)}, bf16[4,2,512,128]{3,2,1,0:T(8,128)(2,1)}, u32[]{:S(2)}, u32[]{:S(2)}) %collective-permute-start.2) | collective-permute-done | bytes 1048608 | tf_op jit(solution)/shard_map/ppermute | solution.py:31
  85.7 5.1 %collective-permute-start.12 = (bf16[2048,128]{1,0:T(8,128)(2,1)}, bf16[2048,128]{1,0:T(8,128)(2,1)}, u32[]{:S(2)}, u32[]{:S(2)}) collective-permute-start(bf16[2048,128]{1,0:T(8,128)(2,1)} %slice_bitcast_fusion), channel_id=1, source_target_pairs={{0,3},{1,0},{2,1},{3,2},{4,7},{5,4},{6,5},{7,6},{8,11},{9,8},{10,9... | collective-permute-start | bytes 1572872 | tf_op jit(solution)/shard_map/ppermute | solution.py:31
  90.9 2.4 %collective-permute-done.1.refs_2_ = bf16[4,2,512,128]{3,2,1,0:T(8,128)(2,1)} collective-permute-done((bf16[4,2,512,128]{3,2,1,0:T(8,128)(2,1)S(1)}, bf16[4,2,512,128]{3,2,1,0:T(8,128)(2,1)}, u32[]{:S(2)}, u32[]{:S(2)}) %collective-permute-start.1) | collective-permute-done | bytes 1048608 | tf_op jit(solution)/shard_map/ppermute | solution.py:31
  93.3 4.1 %first_level.2 = (f32[2,512,128]{2,1,0:T(8,128)S(1)}, bf16[2,512,128]{2,1,0:T(8,128)(2,1)S(1)}) custom-call(s32[2]{0:T(128)S(1)} %pad_add_fusion.at_ref, bf16[4,2,512,128]{3,2,1,0:T(8,128)(2,1)S(1)} %all-to-all-done.refs_0_, bf16[4,2,512,128]{3,2,1,0:T(8,128)(2,1)} %collective-permute-done.refs_1_, bf16[4,2,512,128]{3,2,1,0:T(8,128)(2,1)} %collective-permute-done.1.refs_2_, ...), custom_call_target="tpu_custom_call" | custom-call | flops 1073741824 | bytes 8388608 | tf_op jit(solution)/shard_map/first_level/pallas_call | solution.py:86
  97.4 4.9 %collective-permute-start.13 = (bf16[2,512,128]{2,1,0:T(8,128)(2,1)S(1)}, bf16[2,512,128]{2,1,0:T(8,128)(2,1)S(1)}, u32[]{:S(2)}, u32[]{:S(2)}) collective-permute-start(bf16[2,512,128]{2,1,0:T(8,128)(2,1)S(1)} %get-tuple-element.23), channel_id=1, source_target_pairs={{0,32},{1,33},{2,34},{3,35},{4,36},{5,37},{6,38},{7,39},{8,40},{9,... | collective-permute-start | bytes 786440 | tf_op jit(solution)/shard_map/ppermute | solution.py:31
  102.3 6.3 %collective-permute-start.14 = (bf16[2,512,128]{2,1,0:T(8,128)(2,1)S(1)}, bf16[2,512,128]{2,1,0:T(8,128)(2,1)S(1)}, u32[]{:S(2)}, u32[]{:S(2)}) collective-permute-start(bf16[2,512,128]{2,1,0:T(8,128)(2,1)S(1)} %get-tuple-element.23), channel_id=1, source_target_pairs={{32,0},{33,1},{34,2},{35,3},{36,4},{37,5},{38,6},{39,7},{40,8},{41... | collective-permute-start | bytes 786440 | tf_op jit(solution)/shard_map/ppermute | solution.py:31
  108.7 3.8 %first_level.3 = (f32[2,512,128]{2,1,0:T(8,128)S(1)}, bf16[2,512,128]{2,1,0:T(8,128)(2,1)S(1)}) custom-call(s32[2]{0:T(128)S(1)} %pad_add_fusion.at_ref, bf16[4,2,512,128]{3,2,1,0:T(8,128)(2,1)S(1)} %all-to-all-done.refs_0_, bf16[4,2,512,128]{3,2,1,0:T(8,128)(2,1)} %collective-permute-done.refs_1_, bf16[4,2,512,128]{3,2,1,0:T(8,128)(2,1)} %collective-permute-done.1.refs_2_, ...), custom_call_target="tpu_custom_call" | custom-call | flops 1073741824 | bytes 8388608 | tf_op jit(solution)/shard_map/first_level/pallas_call | solution.py:86
  112.4 1.9 %collective-permute-start.15 = (bf16[2,512,128]{2,1,0:T(8,128)(2,1)S(1)}, bf16[2,512,128]{2,1,0:T(8,128)(2,1)S(1)}, u32[]{:S(2)}, u32[]{:S(2)}) collective-permute-start(bf16[2,512,128]{2,1,0:T(8,128)(2,1)S(1)} %get-tuple-element.30), channel_id=1, source_target_pairs={{0,32},{1,33},{2,34},{3,35},{4,36},{5,37},{6,38},{7,39},{8,40},{9,... | collective-permute-start | bytes 786440 | tf_op jit(solution)/shard_map/ppermute | solution.py:31
  114.4 5.1 %collective-permute-start.16 = (bf16[2,512,128]{2,1,0:T(8,128)(2,1)S(1)}, bf16[2,512,128]{2,1,0:T(8,128)(2,1)S(1)}, u32[]{:S(2)}, u32[]{:S(2)}) collective-permute-start(bf16[2,512,128]{2,1,0:T(8,128)(2,1)S(1)} %get-tuple-element.30), channel_id=1, source_target_pairs={{32,0},{33,1},{34,2},{35,3},{36,4},{37,5},{38,6},{39,7},{40,8},{41... | collective-permute-start | bytes 786440 | tf_op jit(solution)/shard_map/ppermute | solution.py:31
  119.6 2.8 %second_level.2 = (bf16[2048,128]{1,0:T(8,128)(2,1)S(1)}, bf16[2048,128]{1,0:T(8,128)(2,1)S(1)}) custom-call(s32[2]{0:T(128)S(1)} %pad_add_fusion.at_ref, bf16[2048,128]{1,0:T(8,128)(2,1)S(1)} %bitcast.21, bf16[2048,128]{1,0:T(8,128)(2,1)S(1)} %bitcast.23, bf16[2,2048,128]{2,1,0:T(8,128)(2,1)} %collective-permute-done.9.refs_2_, ...), custom_call_target="tpu_custom_call" | custom-call | flops 1073741824 | bytes 6291456 | tf_op jit(solution)/shard_map/second_level/pallas_call | solution.py:131
  122.4 1.9 %collective-permute-start.17 = (bf16[2048,128]{1,0:T(8,128)(2,1)S(1)}, bf16[2048,128]{1,0:T(8,128)(2,1)S(1)}, u32[]{:S(2)}, u32[]{:S(2)}) collective-permute-start(bf16[2048,128]{1,0:T(8,128)(2,1)S(1)} %get-tuple-element.28), channel_id=1, source_target_pairs={{0,8},{1,9},{2,10},{3,11},{4,12},{5,13},{6,14},{7,15},{8,0},{9,1},... | collective-permute-start | bytes 1572872 | tf_op jit(solution)/shard_map/ppermute | solution.py:31
  124.3 1.9 %collective-permute-done.16.refs_7_ = bf16[2,512,128]{2,1,0:T(8,128)(2,1)S(1)} collective-permute-done((bf16[2,512,128]{2,1,0:T(8,128)(2,1)S(1)}, bf16[2,512,128]{2,1,0:T(8,128)(2,1)S(1)}, u32[]{:S(2)}, u32[]{:S(2)}) %collective-permute-start.16) | collective-permute-done | bytes 262176 | tf_op jit(solution)/shard_map/ppermute | solution.py:31
  126.3 2.9 %second_level.3 = (bf16[2048,128]{1,0:T(8,128)(2,1)S(1)}, f32[2048,128]{1,0:T(8,128)S(1)}) custom-call(s32[2]{0:T(128)S(1)} %pad_add_fusion.at_ref, bf16[2048,128]{1,0:T(8,128)(2,1)S(1)} %bitcast.22, bf16[2048,128]{1,0:T(8,128)(2,1)S(1)} %bitcast.24, bf16[2,2048,128]{2,1,0:T(8,128)(2,1)} %collective-permute-done.9.refs_2_, ...), custom_call_target="tpu_custom_call" | custom-call | flops 1073741824 | bytes 6291456 | tf_op jit(solution)/shard_map/second_level/pallas_call | solution.py:131
  129.1 2.6 %collective-permute-start.19 = (bf16[2048,128]{1,0:T(8,128)(2,1)S(1)}, bf16[2048,128]{1,0:T(8,128)(2,1)S(1)}, u32[]{:S(2)}, u32[]{:S(2)}) collective-permute-start(bf16[2048,128]{1,0:T(8,128)(2,1)S(1)} %get-tuple-element.34), channel_id=1, source_target_pairs={{0,12},{1,13},{2,14},{3,15},{4,0},{5,1},{6,2},{7,3},{8,4},{9,5},{1... | collective-permute-start | bytes 1572872 | tf_op jit(solution)/shard_map/ppermute | solution.py:31
  131.7 3.3 %collective-permute-start.18 = (bf16[2048,128]{1,0:T(8,128)(2,1)S(1)}, bf16[2048,128]{1,0:T(8,128)(2,1)S(1)}, u32[]{:S(2)}, u32[]{:S(2)}) collective-permute-start(bf16[2048,128]{1,0:T(8,128)(2,1)S(1)} %get-tuple-element.33), channel_id=1, source_target_pairs={{0,4},{1,5},{2,6},{3,7},{4,8},{5,9},{6,10},{7,11},{8,12},{9,13},{1... | collective-permute-start | bytes 1572872 | tf_op jit(solution)/shard_map/ppermute | solution.py:31
  135.0 5.3 %collective-permute-done.19 = bf16[2048,128]{1,0:T(8,128)(2,1)S(1)} collective-permute-done((bf16[2048,128]{1,0:T(8,128)(2,1)S(1)}, bf16[2048,128]{1,0:T(8,128)(2,1)S(1)}, u32[]{:S(2)}, u32[]{:S(2)}) %collective-permute-start.19) | collective-permute-done | bytes 524320 | tf_op jit(solution)/shard_map/ppermute | solution.py:31
  140.3 5.2 %collective-permute-done.18 = bf16[2048,128]{1,0:T(8,128)(2,1)S(1)} collective-permute-done((bf16[2048,128]{1,0:T(8,128)(2,1)S(1)}, bf16[2048,128]{1,0:T(8,128)(2,1)S(1)}, u32[]{:S(2)}, u32[]{:S(2)}) %collective-permute-start.18) | collective-permute-done | bytes 524320 | tf_op jit(solution)/shard_map/ppermute | solution.py:31
  (46 shorter events, 14.9 us)
Async XLA Ops:
  0.0 2.4 %copy-start.7 = (f32[1,2048,128]{2,1,0:T(8,128)S(1)}, f32[1,2048,128]{2,1,0:T(8,128)}, u32[]{:S(2)}) copy-start(f32[1,2048,128]{2,1,0:T(8,128)} %param.5) | copy-start | bytes 3145732
  2.4 7.0 %copy-start.3 = (bf16[1,2048,128]{2,1,0:T(8,128)(2,1)S(1)}, bf16[1,2048,128]{2,1,0:T(8,128)(2,1)}, u32[]{:S(2)}) copy-start(bf16[1,2048,128]{2,1,0:T(8,128)(2,1)} %param.8) | copy-start | bytes 1572868
  2.4 7.0 %copy-start.5 = (bf16[1,2048,128]{2,1,0:T(8,128)(2,1)S(1)}, bf16[1,2048,128]{2,1,0:T(8,128)(2,1)}, u32[]{:S(2)}) copy-start(bf16[1,2048,128]{2,1,0:T(8,128)(2,1)} %param.9) | copy-start | bytes 1572868
  2.4 19.1 %collective-permute-start.3 = (bf16[2048,128]{1,0:T(8,128)(2,1)S(1)}, bf16[2048,128]{1,0:T(8,128)(2,1)S(1)}, u32[]{:S(2)}, u32[]{:S(2)}) collective-permute-start(bf16[2048,128]{1,0:T(8,128)(2,1)S(1)} %convert_element_type.12), channel_id=1, source_target_pairs={{0,16},{1,17},{2,18},{3,19},{4,20},{5,21},{6,22},{7,23},{8,24},{9,... | collective-permute-start | bytes 1572872 | tf_op jit(solution)/shard_map/ppermute | solution.py:31
  4.5 17.0 %collective-permute-start.4 = (bf16[2048,128]{1,0:T(8,128)(2,1)S(1)}, bf16[2048,128]{1,0:T(8,128)(2,1)}, u32[]{:S(2)}, u32[]{:S(2)}) collective-permute-start(bf16[2048,128]{1,0:T(8,128)(2,1)S(1)} %convert_element_type.12), channel_id=1, source_target_pairs={{16,0},{17,1},{18,2},{19,3},{20,4},{21,5},{22,6},{23,7},{24,8},{25... | collective-permute-start | bytes 1572872 | tf_op jit(solution)/shard_map/ppermute | solution.py:31
  10.5 32.8 %collective-permute-start.10 = (bf16[2,2048,128]{2,1,0:T(8,128)(2,1)}, bf16[2,2048,128]{2,1,0:T(8,128)(2,1)S(1)}, u32[]{:S(2)}, u32[]{:S(2)}) collective-permute-start(bf16[2,2048,128]{2,1,0:T(8,128)(2,1)} %pad_maximum_fusion.2), channel_id=1, source_target_pairs={{0,3},{1,0},{2,1},{3,2},{4,7},{5,4},{6,5},{7,6},{8,11},{9,8},{10,9... | collective-permute-start | bytes 3145736 | tf_op jit(solution)/shard_map/ppermute | solution.py:31
  15.1 30.1 %collective-permute-start.9 = (bf16[2,2048,128]{2,1,0:T(8,128)(2,1)}, bf16[2,2048,128]{2,1,0:T(8,128)(2,1)}, u32[]{:S(2)}, u32[]{:S(2)}) collective-permute-start(bf16[2,2048,128]{2,1,0:T(8,128)(2,1)} %pad_maximum_fusion.2), channel_id=1, source_target_pairs={{0,1},{1,2},{2,3},{3,0},{4,5},{5,6},{6,7},{7,4},{8,9},{9,10},{10,1... | collective-permute-start | bytes 3145736 | tf_op jit(solution)/shard_map/ppermute | solution.py:31
  17.0 21.1 %all-to-all-start = ((bf16[4,2,512,128]{3,2,1,0:T(8,128)(2,1)}), bf16[4,2,512,128]{3,2,1,0:T(8,128)(2,1)S(1)}, u32[]{:S(2)}, u32[]{:S(2)}) async-start(bf16[4,2,512,128]{3,2,1,0:T(8,128)(2,1)} %pad_maximum_fusion), calls=%async_computation | async-start | bytes 2097152 | tf_op jit(solution)/shard_map/all_to_all | solution.py:154
  21.5 0.8 copy-start.9
  23.6 36.2 %collective-permute-start.5 = (bf16[2,2048,128]{2,1,0:T(8,128)(2,1)S(1)}, bf16[2,2048,128]{2,1,0:T(8,128)(2,1)}, u32[]{:S(2)}, u32[]{:S(2)}) collective-permute-start(bf16[2,2048,128]{2,1,0:T(8,128)(2,1)S(1)} %pad_maximum_fusion.1.refs_6_.refs_7_), channel_id=1, source_target_pairs={{0,4},{1,5},{2,6},{3,7},{4,8},{5,9},{6,10},{7,11},{8,12},{9,13},{1... | collective-permute-start | bytes 3145736 | tf_op jit(solution)/shard_map/ppermute | solution.py:31
  27.6 36.1 %collective-permute-start.7 = (bf16[2,2048,128]{2,1,0:T(8,128)(2,1)S(1)}, bf16[2,2048,128]{2,1,0:T(8,128)(2,1)}, u32[]{:S(2)}, u32[]{:S(2)}) collective-permute-start(bf16[2,2048,128]{2,1,0:T(8,128)(2,1)S(1)} %pad_maximum_fusion.1.refs_6_.refs_7_), channel_id=1, source_target_pairs={{0,12},{1,13},{2,14},{3,15},{4,0},{5,1},{6,2},{7,3},{8,4},{9,5},{1... | collective-permute-start | bytes 3145736 | tf_op jit(solution)/shard_map/ppermute | solution.py:31
  38.1 47.6 %collective-permute-start = (bf16[4,2,512,128]{3,2,1,0:T(8,128)(2,1)S(1)}, bf16[4,2,512,128]{3,2,1,0:T(8,128)(2,1)}, u32[]{:S(2)}, u32[]{:S(2)}) collective-permute-start(bf16[4,2,512,128]{3,2,1,0:T(8,128)(2,1)S(1)} %all-to-all-done.refs_0_), channel_id=1, source_target_pairs={{0,3},{1,0},{2,1},{3,2},{4,7},{5,4},{6,5},{7,6},{8,11},{9,8},{10,9... | collective-permute-start | bytes 3145736 | tf_op jit(solution)/shard_map/ppermute | solution.py:31
  43.2 5.3 %copy-start = (bf16[2,2048,128]{2,1,0:T(8,128)(2,1)}, bf16[2,2048,128]{2,1,0:T(8,128)(2,1)S(1)}, u32[]{:S(2)}) copy-start(bf16[2,2048,128]{2,1,0:T(8,128)(2,1)S(1)} %collective-permute-done.10.refs_3_) | copy-start | bytes 3145732
  43.2 40.5 %collective-permute-start.2 = (bf16[4,2,512,128]{3,2,1,0:T(8,128)(2,1)S(1)}, bf16[4,2,512,128]{3,2,1,0:T(8,128)(2,1)}, u32[]{:S(2)}, u32[]{:S(2)}) collective-permute-start(bf16[4,2,512,128]{3,2,1,0:T(8,128)(2,1)S(1)} %all-to-all-done.refs_0_), channel_id=1, source_target_pairs={{0,1},{1,2},{2,3},{3,0},{4,5},{5,6},{6,7},{7,4},{8,9},{9,10},{10,1... | collective-permute-start | bytes 3145736 | tf_op jit(solution)/shard_map/ppermute | solution.py:31
  45.2 48.1 %collective-permute-start.1 = (bf16[4,2,512,128]{3,2,1,0:T(8,128)(2,1)S(1)}, bf16[4,2,512,128]{3,2,1,0:T(8,128)(2,1)}, u32[]{:S(2)}, u32[]{:S(2)}) collective-permute-start(bf16[4,2,512,128]{3,2,1,0:T(8,128)(2,1)S(1)} %all-to-all-done.refs_0_), channel_id=1, source_target_pairs={{0,2},{1,3},{2,0},{3,1},{4,6},{5,7},{6,4},{7,5},{8,10},{9,11},{10,... | collective-permute-start | bytes 3145736 | tf_op jit(solution)/shard_map/ppermute | solution.py:31
  48.6 42.3 %all-to-all-start.1 = ((f32[4,512,128]{2,1,0:T(8,128)}), f32[4,512,128]{2,1,0:T(8,128)S(1)}, u32[]{:S(2)}, u32[]{:S(2)}) async-start(f32[4,512,128]{2,1,0:T(8,128)} %bitcast.25), calls=%async_computation.1 | async-start | bytes 2097152 | tf_op jit(solution)/shard_map/all_to_all | solution.py:154
  54.0 16.7 %copy-start.1 = (bf16[2,2048,128]{2,1,0:T(8,128)(2,1)S(1)}, bf16[2,2048,128]{2,1,0:T(8,128)(2,1)}, u32[]{:S(2)}) copy-start(bf16[2,2048,128]{2,1,0:T(8,128)(2,1)} %copy-done) | copy-start | bytes 3145732
  61.7 31.6 %collective-permute-start.6 = (bf16[2048,128]{1,0:T(8,128)(2,1)}, bf16[2048,128]{1,0:T(8,128)(2,1)}, u32[]{:S(2)}, u32[]{:S(2)}) collective-permute-start(bf16[2048,128]{1,0:T(8,128)(2,1)} %slice_bitcast_fusion.3), channel_id=1, source_target_pairs={{0,4},{1,5},{2,6},{3,7},{4,8},{5,9},{6,10},{7,11},{8,12},{9,13},{1... | collective-permute-start | bytes 1572872 | tf_op jit(solution)/shard_map/ppermute | solution.py:31
  65.5 27.8 %collective-permute-start.8 = (bf16[2048,128]{1,0:T(8,128)(2,1)}, bf16[2048,128]{1,0:T(8,128)(2,1)}, u32[]{:S(2)}, u32[]{:S(2)}) collective-permute-start(bf16[2048,128]{1,0:T(8,128)(2,1)} %slice_bitcast_fusion.2), channel_id=1, source_target_pairs={{0,12},{1,13},{2,14},{3,15},{4,0},{5,1},{6,2},{7,3},{8,4},{9,5},{1... | collective-permute-start | bytes 1572872 | tf_op jit(solution)/shard_map/ppermute | solution.py:31
  83.7 35.8 %collective-permute-start.11 = (bf16[2048,128]{1,0:T(8,128)(2,1)}, bf16[2048,128]{1,0:T(8,128)(2,1)}, u32[]{:S(2)}, u32[]{:S(2)}) collective-permute-start(bf16[2048,128]{1,0:T(8,128)(2,1)} %slice_bitcast_fusion.1), channel_id=1, source_target_pairs={{0,1},{1,2},{2,3},{3,0},{4,5},{5,6},{6,7},{7,4},{8,9},{9,10},{10,1... | collective-permute-start | bytes 1572872 | tf_op jit(solution)/shard_map/ppermute | solution.py:31
  85.7 33.9 %collective-permute-start.12 = (bf16[2048,128]{1,0:T(8,128)(2,1)}, bf16[2048,128]{1,0:T(8,128)(2,1)}, u32[]{:S(2)}, u32[]{:S(2)}) collective-permute-start(bf16[2048,128]{1,0:T(8,128)(2,1)} %slice_bitcast_fusion), channel_id=1, source_target_pairs={{0,3},{1,0},{2,1},{3,2},{4,7},{5,4},{6,5},{7,6},{8,11},{9,8},{10,9... | collective-permute-start | bytes 1572872 | tf_op jit(solution)/shard_map/ppermute | solution.py:31
  97.4 22.2 %copy-start.2 = (bf16[2,2048,128]{2,1,0:T(8,128)(2,1)S(1)}, bf16[2,2048,128]{2,1,0:T(8,128)(2,1)}, u32[]{:S(2)}) copy-start(bf16[2,2048,128]{2,1,0:T(8,128)(2,1)} %copy-done) | copy-start | bytes 3145732
  97.4 22.2 %copy-start.4 = (bf16[1,2048,128]{2,1,0:T(8,128)(2,1)S(1)}, bf16[1,2048,128]{2,1,0:T(8,128)(2,1)}, u32[]{:S(2)}) copy-start(bf16[1,2048,128]{2,1,0:T(8,128)(2,1)} %param.8) | copy-start | bytes 1572868
  97.4 22.2 %copy-start.6 = (bf16[1,2048,128]{2,1,0:T(8,128)(2,1)S(1)}, bf16[1,2048,128]{2,1,0:T(8,128)(2,1)}, u32[]{:S(2)}) copy-start(bf16[1,2048,128]{2,1,0:T(8,128)(2,1)} %param.9) | copy-start | bytes 1572868
  97.4 16.9 %collective-permute-start.13 = (bf16[2,512,128]{2,1,0:T(8,128)(2,1)S(1)}, bf16[2,512,128]{2,1,0:T(8,128)(2,1)S(1)}, u32[]{:S(2)}, u32[]{:S(2)}) collective-permute-start(bf16[2,512,128]{2,1,0:T(8,128)(2,1)S(1)} %get-tuple-element.23), channel_id=1, source_target_pairs={{0,32},{1,33},{2,34},{3,35},{4,36},{5,37},{6,38},{7,39},{8,40},{9,... | collective-permute-start | bytes 786440 | tf_op jit(solution)/shard_map/ppermute | solution.py:31
  102.3 17.2 %collective-permute-start.14 = (bf16[2,512,128]{2,1,0:T(8,128)(2,1)S(1)}, bf16[2,512,128]{2,1,0:T(8,128)(2,1)S(1)}, u32[]{:S(2)}, u32[]{:S(2)}) collective-permute-start(bf16[2,512,128]{2,1,0:T(8,128)(2,1)S(1)} %get-tuple-element.23), channel_id=1, source_target_pairs={{32,0},{33,1},{34,2},{35,3},{36,4},{37,5},{38,6},{39,7},{40,8},{41... | collective-permute-start | bytes 786440 | tf_op jit(solution)/shard_map/ppermute | solution.py:31
  112.4 11.9 %collective-permute-start.15 = (bf16[2,512,128]{2,1,0:T(8,128)(2,1)S(1)}, bf16[2,512,128]{2,1,0:T(8,128)(2,1)S(1)}, u32[]{:S(2)}, u32[]{:S(2)}) collective-permute-start(bf16[2,512,128]{2,1,0:T(8,128)(2,1)S(1)} %get-tuple-element.30), channel_id=1, source_target_pairs={{0,32},{1,33},{2,34},{3,35},{4,36},{5,37},{6,38},{7,39},{8,40},{9,... | collective-permute-start | bytes 786440 | tf_op jit(solution)/shard_map/ppermute | solution.py:31
  114.4 11.9 %collective-permute-start.16 = (bf16[2,512,128]{2,1,0:T(8,128)(2,1)S(1)}, bf16[2,512,128]{2,1,0:T(8,128)(2,1)S(1)}, u32[]{:S(2)}, u32[]{:S(2)}) collective-permute-start(bf16[2,512,128]{2,1,0:T(8,128)(2,1)S(1)} %get-tuple-element.30), channel_id=1, source_target_pairs={{32,0},{33,1},{34,2},{35,3},{36,4},{37,5},{38,6},{39,7},{40,8},{41... | collective-permute-start | bytes 786440 | tf_op jit(solution)/shard_map/ppermute | solution.py:31
  122.4 17.9 %collective-permute-start.17 = (bf16[2048,128]{1,0:T(8,128)(2,1)S(1)}, bf16[2048,128]{1,0:T(8,128)(2,1)S(1)}, u32[]{:S(2)}, u32[]{:S(2)}) collective-permute-start(bf16[2048,128]{1,0:T(8,128)(2,1)S(1)} %get-tuple-element.28), channel_id=1, source_target_pairs={{0,8},{1,9},{2,10},{3,11},{4,12},{5,13},{6,14},{7,15},{8,0},{9,1},... | collective-permute-start | bytes 1572872 | tf_op jit(solution)/shard_map/ppermute | solution.py:31
  126.3 19.3 %copy-start.8 = (f32[1,2048,128]{2,1,0:T(8,128)S(1)}, f32[1,2048,128]{2,1,0:T(8,128)}, u32[]{:S(2)}) copy-start(f32[1,2048,128]{2,1,0:T(8,128)} %param.5) | copy-start | bytes 3145732
  129.1 11.2 %collective-permute-start.19 = (bf16[2048,128]{1,0:T(8,128)(2,1)S(1)}, bf16[2048,128]{1,0:T(8,128)(2,1)S(1)}, u32[]{:S(2)}, u32[]{:S(2)}) collective-permute-start(bf16[2048,128]{1,0:T(8,128)(2,1)S(1)} %get-tuple-element.34), channel_id=1, source_target_pairs={{0,12},{1,13},{2,14},{3,15},{4,0},{5,1},{6,2},{7,3},{8,4},{9,5},{1... | collective-permute-start | bytes 1572872 | tf_op jit(solution)/shard_map/ppermute | solution.py:31
  131.7 13.8 %collective-permute-start.18 = (bf16[2048,128]{1,0:T(8,128)(2,1)S(1)}, bf16[2048,128]{1,0:T(8,128)(2,1)S(1)}, u32[]{:S(2)}, u32[]{:S(2)}) collective-permute-start(bf16[2048,128]{1,0:T(8,128)(2,1)S(1)} %get-tuple-element.33), channel_id=1, source_target_pairs={{0,4},{1,5},{2,6},{3,7},{4,8},{5,9},{6,10},{7,11},{8,12},{9,13},{1... | collective-permute-start | bytes 1572872 | tf_op jit(solution)/shard_map/ppermute | solution.py:31

commit v10 on v9

--- a/solution.py
+++ b/solution.py
@@ -164,7 +164,8 @@
     two_left, two_right = moved(seconds, xs=1), moved(seconds, xs=-1)
 
     left, right, far = moved(own, xs=1), moved(own, xs=-1), moved(own, xs=2)
-    down, up = moved(near, ys=1), moved(near, ys=-1)
+    shared = after(near, own)
+    down, up = moved(shared, ys=1), moved(shared, ys=-1)
     below_far, above_far = moved(down[0], ys=1), moved(up[1], ys=-1)
     rhs_rows = exchanged(after(rhs, own, two_left, two_right).reshape(Y, BLK, COL))
 

time: 148 us -> 152 us (1.027)
  the two profiles are of different devices: /device:TPU:128 before, /device:TPU:1 now
where the time goes in v10:
time: 152 us; the launch traced here: 150 us
  starting transfers between devices  71.6 us (47%)
  waiting for transfers between devices  53.5 us (35%)
  Pallas kernels  13.5 us (9%)
  local copies, waits for them, and re-layouts  6.63 us (4%)
  other arithmetic  4.75 us (3%)
    ppermute x20, starting transfers between devices, moved(): return lax.ppermute(value, AXES, pairs)  61.9 us
    ppermute x20, waiting for transfers between devices, moved(): return lax.ppermute(value, AXES, pairs)  53.5 us
    all_to_all x2, starting transfers between devices, exchanged(): return lax.all_to_all(value, 'y', 0, 0, tiled=True)  9.67 us
    pallas_call x2, Pallas kernels, first_level(): pl.pallas_call(functools.partial(first_kernel, groups), name='first_level...  7.83 us
    pallas_call x2, Pallas kernels, second_level(): pl.pallas_call(functools.partial(second_kernel, groups), name='second_lev...  5.65 us
    squeeze x2, local copies, waits for them, and re-layouts, on_device(): below_far, above_far = (moved(down[0], ys=1), moved(up[1], ys=-1))  3.85 us
  transfers between devices with their start and end apart: 22, of which 5 were waited for; matrix products, arithmetic and copies ran while one was open for 5% of the time, Pallas kernels for 9%

profile of v10, /device:TPU:1, one launch (start us, length us, event | category | flops | bytes accessed | tf_op | source)
XLA Modules:
  0.0 150.3 jit_solution(2739988574418835227)
XLA Ops:
  0.0 2.2 %pad_maximum_fusion = bf16[4,2,512,128]{3,2,1,0:T(8,128)(2,1)} fusion(bf16[4,1,512,128]{3,2,1,0:T(8,128)(2,1)} %bitcast.27, bf16[4,1,512,128]{3,2,1,0:T(8,128)(2,1)} %bitcast.28), kind=kLoop, calls=%fused_computation | loop fusion | flops 524288 | bytes 2097152 | tf_op jit(solution)/shard_map/stack | solution.py:157
  2.3 5.1 %all-to-all-start = ((bf16[4,2,512,128]{3,2,1,0:T(8,128)(2,1)}), bf16[4,2,512,128]{3,2,1,0:T(8,128)(2,1)S(1)}, u32[]{:S(2)}, u32[]{:S(2)}) async-start(bf16[4,2,512,128]{3,2,1,0:T(8,128)(2,1)} %pad_maximum_fusion), calls=%async_computation | async-start | bytes 2097152 | tf_op jit(solution)/shard_map/all_to_all | solution.py:154
  7.5 4.5 %collective-permute-start.3 = (bf16[2048,128]{1,0:T(8,128)(2,1)S(1)}, bf16[2048,128]{1,0:T(8,128)(2,1)S(1)}, u32[]{:S(2)}, u32[]{:S(2)}) collective-permute-start(bf16[2048,128]{1,0:T(8,128)(2,1)S(1)} %convert_element_type.12), channel_id=1, source_target_pairs={{0,16},{1,17},{2,18},{3,19},{4,20},{5,21},{6,22},{7,23},{8,24},{9,... | collective-permute-start | bytes 1572872 | tf_op jit(solution)/shard_map/ppermute | solution.py:31
  12.0 4.3 %collective-permute-start.4 = (bf16[2048,128]{1,0:T(8,128)(2,1)S(1)}, bf16[2048,128]{1,0:T(8,128)(2,1)S(1)}, u32[]{:S(2)}, u32[]{:S(2)}) collective-permute-start(bf16[2048,128]{1,0:T(8,128)(2,1)S(1)} %convert_element_type.12), channel_id=1, source_target_pairs={{16,0},{17,1},{18,2},{19,3},{20,4},{21,5},{22,6},{23,7},{24,8},{25... | collective-permute-start | bytes 1572872 | tf_op jit(solution)/shard_map/ppermute | solution.py:31
  17.3 2.0 %collective-permute-start.10 = (bf16[2,2048,128]{2,1,0:T(8,128)(2,1)}, bf16[2,2048,128]{2,1,0:T(8,128)(2,1)S(1)}, u32[]{:S(2)}, u32[]{:S(2)}) collective-permute-start(bf16[2,2048,128]{2,1,0:T(8,128)(2,1)} %pad_maximum_fusion.2), channel_id=1, source_target_pairs={{0,3},{1,0},{2,1},{3,2},{4,7},{5,4},{6,5},{7,6},{8,11},{9,8},{10,9... | collective-permute-start | bytes 3145736 | tf_op jit(solution)/shard_map/ppermute | solution.py:31
  19.4 3.2 %collective-permute-start.9 = (bf16[2,2048,128]{2,1,0:T(8,128)(2,1)}, bf16[2,2048,128]{2,1,0:T(8,128)(2,1)}, u32[]{:S(2)}, u32[]{:S(2)}) collective-permute-start(bf16[2,2048,128]{2,1,0:T(8,128)(2,1)} %pad_maximum_fusion.2), channel_id=1, source_target_pairs={{0,1},{1,2},{2,3},{3,0},{4,5},{5,6},{6,7},{7,4},{8,9},{9,10},{10,1... | collective-permute-start | bytes 3145736 | tf_op jit(solution)/shard_map/ppermute | solution.py:31
  22.9 3.6 %collective-permute-start.5 = (bf16[2,2048,128]{2,1,0:T(8,128)(2,1)S(1)}, bf16[2,2048,128]{2,1,0:T(8,128)(2,1)}, u32[]{:S(2)}, u32[]{:S(2)}) collective-permute-start(bf16[2,2048,128]{2,1,0:T(8,128)(2,1)S(1)} %pad_maximum_fusion.1.refs_6_.refs_7_), channel_id=1, source_target_pairs={{0,4},{1,5},{2,6},{3,7},{4,8},{5,9},{6,10},{7,11},{8,12},{9,13},{1... | collective-permute-start | bytes 3145736 | tf_op jit(solution)/shard_map/ppermute | solution.py:31
  26.6 3.1 %collective-permute-start.7 = (bf16[2,2048,128]{2,1,0:T(8,128)(2,1)S(1)}, bf16[2,2048,128]{2,1,0:T(8,128)(2,1)}, u32[]{:S(2)}, u32[]{:S(2)}) collective-permute-start(bf16[2,2048,128]{2,1,0:T(8,128)(2,1)S(1)} %pad_maximum_fusion.1.refs_6_.refs_7_), channel_id=1, source_target_pairs={{0,12},{1,13},{2,14},{3,15},{4,0},{5,1},{6,2},{7,3},{8,4},{9,5},{1... | collective-permute-start | bytes 3145736 | tf_op jit(solution)/shard_map/ppermute | solution.py:31
  29.7 4.5 %collective-permute-start = (bf16[4,2,512,128]{3,2,1,0:T(8,128)(2,1)S(1)}, bf16[4,2,512,128]{3,2,1,0:T(8,128)(2,1)}, u32[]{:S(2)}, u32[]{:S(2)}) collective-permute-start(bf16[4,2,512,128]{3,2,1,0:T(8,128)(2,1)S(1)} %all-to-all-done.refs_0_), channel_id=1, source_target_pairs={{0,3},{1,0},{2,1},{3,2},{4,7},{5,4},{6,5},{7,6},{8,11},{9,8},{10,9... | collective-permute-start | bytes 3145736 | tf_op jit(solution)/shard_map/ppermute | solution.py:31
  34.2 10.5 %collective-permute-done.10.refs_3_ = bf16[2,2048,128]{2,1,0:T(8,128)(2,1)S(1)} collective-permute-done((bf16[2,2048,128]{2,1,0:T(8,128)(2,1)}, bf16[2,2048,128]{2,1,0:T(8,128)(2,1)S(1)}, u32[]{:S(2)}, u32[]{:S(2)}) %collective-permute-start.10) | collective-permute-done | bytes 1048608 | tf_op jit(solution)/shard_map/ppermute | solution.py:31
  44.7 1.9 %collective-permute-start.2 = (bf16[4,2,512,128]{3,2,1,0:T(8,128)(2,1)S(1)}, bf16[4,2,512,128]{3,2,1,0:T(8,128)(2,1)}, u32[]{:S(2)}, u32[]{:S(2)}) collective-permute-start(bf16[4,2,512,128]{3,2,1,0:T(8,128)(2,1)S(1)} %all-to-all-done.refs_0_), channel_id=1, source_target_pairs={{0,1},{1,2},{2,3},{3,0},{4,5},{5,6},{6,7},{7,4},{8,9},{9,10},{10,1... | collective-permute-start | bytes 3145736 | tf_op jit(solution)/shard_map/ppermute | solution.py:31
  47.7 3.3 %collective-permute-start.1 = (bf16[4,2,512,128]{3,2,1,0:T(8,128)(2,1)S(1)}, bf16[4,2,512,128]{3,2,1,0:T(8,128)(2,1)}, u32[]{:S(2)}, u32[]{:S(2)}) collective-permute-start(bf16[4,2,512,128]{3,2,1,0:T(8,128)(2,1)S(1)} %all-to-all-done.refs_0_), channel_id=1, source_target_pairs={{0,2},{1,3},{2,0},{3,1},{4,6},{5,7},{6,4},{7,5},{8,10},{9,11},{10,... | collective-permute-start | bytes 3145736 | tf_op jit(solution)/shard_map/ppermute | solution.py:31
  51.0 4.5 %all-to-all-start.1 = ((f32[4,512,128]{2,1,0:T(8,128)}), f32[4,512,128]{2,1,0:T(8,128)S(1)}, u32[]{:S(2)}, u32[]{:S(2)}) async-start(f32[4,512,128]{2,1,0:T(8,128)} %bitcast.25), calls=%async_computation.1 | async-start | bytes 2097152 | tf_op jit(solution)/shard_map/all_to_all | solution.py:154
  55.6 1.9 %slice_bitcast_fusion.1 = bf16[2048,128]{1,0:T(8,128)(2,1)} fusion(bf16[2,2048,128]{2,1,0:T(8,128)(2,1)} %collective-permute-done.9.refs_2_), kind=kLoop, calls=%fused_computation.5 | loop fusion | bytes 1048576 | tf_op jit(solution)/shard_map/squeeze | solution.py:172
  57.4 2.0 %slice_bitcast_fusion.3 = bf16[2048,128]{1,0:T(8,128)(2,1)} fusion(bf16[2,2048,128]{2,1,0:T(8,128)(2,1)} %collective-permute-done.5.refs_4_.refs_5_), kind=kLoop, calls=%fused_computation.7 | loop fusion | bytes 1048576 | tf_op jit(solution)/shard_map/squeeze | solution.py:169
  59.4 3.4 %collective-permute-start.6 = (bf16[2048,128]{1,0:T(8,128)(2,1)}, bf16[2048,128]{1,0:T(8,128)(2,1)}, u32[]{:S(2)}, u32[]{:S(2)}) collective-permute-start(bf16[2048,128]{1,0:T(8,128)(2,1)} %slice_bitcast_fusion.3), channel_id=1, source_target_pairs={{0,4},{1,5},{2,6},{3,7},{4,8},{5,9},{6,10},{7,11},{8,12},{9,13},{1... | collective-permute-start | bytes 1572872 | tf_op jit(solution)/shard_map/ppermute | solution.py:31
  62.8 1.9 %slice_bitcast_fusion.2 = bf16[2048,128]{1,0:T(8,128)(2,1)} fusion(bf16[2,2048,128]{2,1,0:T(8,128)(2,1)} %collective-permute-done.7.refs_6_.refs_7_), kind=kLoop, calls=%fused_computation.6 | loop fusion | bytes 1048576 | tf_op jit(solution)/shard_map/squeeze | solution.py:169
  64.7 3.1 %collective-permute-start.8 = (bf16[2048,128]{1,0:T(8,128)(2,1)}, bf16[2048,128]{1,0:T(8,128)(2,1)}, u32[]{:S(2)}, u32[]{:S(2)}) collective-permute-start(bf16[2048,128]{1,0:T(8,128)(2,1)} %slice_bitcast_fusion.2), channel_id=1, source_target_pairs={{0,12},{1,13},{2,14},{3,15},{4,0},{5,1},{6,2},{7,3},{8,4},{9,5},{1... | collective-permute-start | bytes 1572872 | tf_op jit(solution)/shard_map/ppermute | solution.py:31
  67.8 27.4 %collective-permute-done.2.refs_3_ = bf16[4,2,512,128]{3,2,1,0:T(8,128)(2,1)} collective-permute-done((bf16[4,2,512,128]{3,2,1,0:T(8,128)(2,1)S(1)}, bf16[4,2,512,128]{3,2,1,0:T(8,128)(2,1)}, u32[]{:S(2)}, u32[]{:S(2)}) %collective-permute-start.2) | collective-permute-done | bytes 1048608 | tf_op jit(solution)/shard_map/ppermute | solution.py:31
  95.2 1.9 %collective-permute-start.11 = (bf16[2048,128]{1,0:T(8,128)(2,1)}, bf16[2048,128]{1,0:T(8,128)(2,1)}, u32[]{:S(2)}, u32[]{:S(2)}) collective-permute-start(bf16[2048,128]{1,0:T(8,128)(2,1)} %slice_bitcast_fusion.1), channel_id=1, source_target_pairs={{0,1},{1,2},{2,3},{3,0},{4,5},{5,6},{6,7},{7,4},{8,9},{9,10},{10,1... | collective-permute-start | bytes 1572872 | tf_op jit(solution)/shard_map/ppermute | solution.py:31
  98.0 4.6 %collective-permute-start.12 = (bf16[2048,128]{1,0:T(8,128)(2,1)}, bf16[2048,128]{1,0:T(8,128)(2,1)}, u32[]{:S(2)}, u32[]{:S(2)}) collective-permute-start(bf16[2048,128]{1,0:T(8,128)(2,1)} %slice_bitcast_fusion), channel_id=1, source_target_pairs={{0,3},{1,0},{2,1},{3,2},{4,7},{5,4},{6,5},{7,6},{8,11},{9,8},{10,9... | collective-permute-start | bytes 1572872 | tf_op jit(solution)/shard_map/ppermute | solution.py:31
  102.7 4.1 %first_level.2 = (f32[2,512,128]{2,1,0:T(8,128)S(1)}, bf16[2,512,128]{2,1,0:T(8,128)(2,1)S(1)}) custom-call(s32[2]{0:T(128)S(1)} %pad_add_fusion.at_ref, bf16[4,2,512,128]{3,2,1,0:T(8,128)(2,1)S(1)} %all-to-all-done.refs_0_, bf16[4,2,512,128]{3,2,1,0:T(8,128)(2,1)} %collective-permute-done.refs_1_, bf16[4,2,512,128]{3,2,1,0:T(8,128)(2,1)} %collective-permute-done.1.refs_2_, ...), custom_call_target="tpu_custom_call" | custom-call | flops 1073741824 | bytes 8388608 | tf_op jit(solution)/shard_map/first_level/pallas_call | solution.py:86
  106.8 1.4 collective-permute-start.13
  108.2 1.3 collective-permute-start.14
  109.5 3.8 %first_level.3 = (f32[2,512,128]{2,1,0:T(8,128)S(1)}, bf16[2,512,128]{2,1,0:T(8,128)(2,1)S(1)}) custom-call(s32[2]{0:T(128)S(1)} %pad_add_fusion.at_ref, bf16[4,2,512,128]{3,2,1,0:T(8,128)(2,1)S(1)} %all-to-all-done.refs_0_, bf16[4,2,512,128]{3,2,1,0:T(8,128)(2,1)} %collective-permute-done.refs_1_, bf16[4,2,512,128]{3,2,1,0:T(8,128)(2,1)} %collective-permute-done.1.refs_2_, ...), custom_call_target="tpu_custom_call" | custom-call | flops 1073741824 | bytes 8388608 | tf_op jit(solution)/shard_map/first_level/pallas_call | solution.py:86
  113.3 4.0 %collective-permute-start.15 = (bf16[2,512,128]{2,1,0:T(8,128)(2,1)S(1)}, bf16[2,512,128]{2,1,0:T(8,128)(2,1)S(1)}, u32[]{:S(2)}, u32[]{:S(2)}) collective-permute-start(bf16[2,512,128]{2,1,0:T(8,128)(2,1)S(1)} %get-tuple-element.32), channel_id=1, source_target_pairs={{0,32},{1,33},{2,34},{3,35},{4,36},{5,37},{6,38},{7,39},{8,40},{9,... | collective-permute-start | bytes 786440 | tf_op jit(solution)/shard_map/ppermute | solution.py:31
  118.7 2.8 %second_level.2 = (bf16[2048,128]{1,0:T(8,128)(2,1)S(1)}, bf16[2048,128]{1,0:T(8,128)(2,1)S(1)}) custom-call(s32[2]{0:T(128)S(1)} %pad_add_fusion.at_ref, bf16[2048,128]{1,0:T(8,128)(2,1)S(1)} %bitcast.21, bf16[2048,128]{1,0:T(8,128)(2,1)S(1)} %bitcast.23, bf16[2,2048,128]{2,1,0:T(8,128)(2,1)} %collective-permute-done.9.refs_2_, ...), custom_call_target="tpu_custom_call" | custom-call | flops 1073741824 | bytes 6291456 | tf_op jit(solution)/shard_map/second_level/pallas_call | solution.py:131
  121.5 5.1 %collective-permute-start.17 = (bf16[2048,128]{1,0:T(8,128)(2,1)S(1)}, bf16[2048,128]{1,0:T(8,128)(2,1)S(1)}, u32[]{:S(2)}, u32[]{:S(2)}) collective-permute-start(bf16[2048,128]{1,0:T(8,128)(2,1)S(1)} %get-tuple-element.30), channel_id=1, source_target_pairs={{0,8},{1,9},{2,10},{3,11},{4,12},{5,13},{6,14},{7,15},{8,0},{9,1},... | collective-permute-start | bytes 1572872 | tf_op jit(solution)/shard_map/ppermute | solution.py:31
  126.6 2.9 %second_level.3 = (bf16[2048,128]{1,0:T(8,128)(2,1)S(1)}, f32[2048,128]{1,0:T(8,128)S(1)}) custom-call(s32[2]{0:T(128)S(1)} %pad_add_fusion.at_ref, bf16[2048,128]{1,0:T(8,128)(2,1)S(1)} %bitcast.22, bf16[2048,128]{1,0:T(8,128)(2,1)S(1)} %bitcast.24, bf16[2,2048,128]{2,1,0:T(8,128)(2,1)} %collective-permute-done.9.refs_2_, ...), custom_call_target="tpu_custom_call" | custom-call | flops 1073741824 | bytes 6291456 | tf_op jit(solution)/shard_map/second_level/pallas_call | solution.py:131
  129.5 3.3 %collective-permute-start.19 = (bf16[2048,128]{1,0:T(8,128)(2,1)S(1)}, bf16[2048,128]{1,0:T(8,128)(2,1)S(1)}, u32[]{:S(2)}, u32[]{:S(2)}) collective-permute-start(bf16[2048,128]{1,0:T(8,128)(2,1)S(1)} %get-tuple-element.36), channel_id=1, source_target_pairs={{0,12},{1,13},{2,14},{3,15},{4,0},{5,1},{6,2},{7,3},{8,4},{9,5},{1... | collective-permute-start | bytes 1572872 | tf_op jit(solution)/shard_map/ppermute | solution.py:31
  132.8 2.0 %collective-permute-start.18 = (bf16[2048,128]{1,0:T(8,128)(2,1)S(1)}, bf16[2048,128]{1,0:T(8,128)(2,1)S(1)}, u32[]{:S(2)}, u32[]{:S(2)}) collective-permute-start(bf16[2048,128]{1,0:T(8,128)(2,1)S(1)} %get-tuple-element.35), channel_id=1, source_target_pairs={{0,4},{1,5},{2,6},{3,7},{4,8},{5,9},{6,10},{7,11},{8,12},{9,13},{1... | collective-permute-start | bytes 1572872 | tf_op jit(solution)/shard_map/ppermute | solution.py:31
  134.8 14.3 %collective-permute-done.19 = bf16[2048,128]{1,0:T(8,128)(2,1)S(1)} collective-permute-done((bf16[2048,128]{1,0:T(8,128)(2,1)S(1)}, bf16[2048,128]{1,0:T(8,128)(2,1)S(1)}, u32[]{:S(2)}, u32[]{:S(2)}) %collective-permute-start.19) | collective-permute-done | bytes 524320 | tf_op jit(solution)/shard_map/ppermute | solution.py:31
  (44 shorter events, 6.0 us)
Async XLA Ops:
  2.3 5.1 %copy-start.7 = (f32[1,2048,128]{2,1,0:T(8,128)S(1)}, f32[1,2048,128]{2,1,0:T(8,128)}, u32[]{:S(2)}) copy-start(f32[1,2048,128]{2,1,0:T(8,128)} %param.5) | copy-start | bytes 3145732
  2.3 20.6 %all-to-all-start = ((bf16[4,2,512,128]{3,2,1,0:T(8,128)(2,1)}), bf16[4,2,512,128]{3,2,1,0:T(8,128)(2,1)S(1)}, u32[]{:S(2)}, u32[]{:S(2)}) async-start(bf16[4,2,512,128]{3,2,1,0:T(8,128)(2,1)} %pad_maximum_fusion), calls=%async_computation | async-start | bytes 2097152 | tf_op jit(solution)/shard_map/all_to_all | solution.py:154
  7.4 8.9 %copy-start.3 = (bf16[1,2048,128]{2,1,0:T(8,128)(2,1)S(1)}, bf16[1,2048,128]{2,1,0:T(8,128)(2,1)}, u32[]{:S(2)}) copy-start(bf16[1,2048,128]{2,1,0:T(8,128)(2,1)} %param.8) | copy-start | bytes 1572868
  7.4 8.9 %copy-start.5 = (bf16[1,2048,128]{2,1,0:T(8,128)(2,1)S(1)}, bf16[1,2048,128]{2,1,0:T(8,128)(2,1)}, u32[]{:S(2)}) copy-start(bf16[1,2048,128]{2,1,0:T(8,128)(2,1)} %param.9) | copy-start | bytes 1572868
  7.5 15.2 %collective-permute-start.3 = (bf16[2048,128]{1,0:T(8,128)(2,1)S(1)}, bf16[2048,128]{1,0:T(8,128)(2,1)S(1)}, u32[]{:S(2)}, u32[]{:S(2)}) collective-permute-start(bf16[2048,128]{1,0:T(8,128)(2,1)S(1)} %convert_element_type.12), channel_id=1, source_target_pairs={{0,16},{1,17},{2,18},{3,19},{4,20},{5,21},{6,22},{7,23},{8,24},{9,... | collective-permute-start | bytes 1572872 | tf_op jit(solution)/shard_map/ppermute | solution.py:31
  12.0 10.8 %collective-permute-start.4 = (bf16[2048,128]{1,0:T(8,128)(2,1)S(1)}, bf16[2048,128]{1,0:T(8,128)(2,1)S(1)}, u32[]{:S(2)}, u32[]{:S(2)}) collective-permute-start(bf16[2048,128]{1,0:T(8,128)(2,1)S(1)} %convert_element_type.12), channel_id=1, source_target_pairs={{16,0},{17,1},{18,2},{19,3},{20,4},{21,5},{22,6},{23,7},{24,8},{25... | collective-permute-start | bytes 1572872 | tf_op jit(solution)/shard_map/ppermute | solution.py:31
  17.3 27.4 %collective-permute-start.10 = (bf16[2,2048,128]{2,1,0:T(8,128)(2,1)}, bf16[2,2048,128]{2,1,0:T(8,128)(2,1)S(1)}, u32[]{:S(2)}, u32[]{:S(2)}) collective-permute-start(bf16[2,2048,128]{2,1,0:T(8,128)(2,1)} %pad_maximum_fusion.2), channel_id=1, source_target_pairs={{0,3},{1,0},{2,1},{3,2},{4,7},{5,4},{6,5},{7,6},{8,11},{9,8},{10,9... | collective-permute-start | bytes 3145736 | tf_op jit(solution)/shard_map/ppermute | solution.py:31
  19.4 28.3 %collective-permute-start.9 = (bf16[2,2048,128]{2,1,0:T(8,128)(2,1)}, bf16[2,2048,128]{2,1,0:T(8,128)(2,1)}, u32[]{:S(2)}, u32[]{:S(2)}) collective-permute-start(bf16[2,2048,128]{2,1,0:T(8,128)(2,1)} %pad_maximum_fusion.2), channel_id=1, source_target_pairs={{0,1},{1,2},{2,3},{3,0},{4,5},{5,6},{6,7},{7,4},{8,9},{9,10},{10,1... | collective-permute-start | bytes 3145736 | tf_op jit(solution)/shard_map/ppermute | solution.py:31
  22.9 34.5 %collective-permute-start.5 = (bf16[2,2048,128]{2,1,0:T(8,128)(2,1)S(1)}, bf16[2,2048,128]{2,1,0:T(8,128)(2,1)}, u32[]{:S(2)}, u32[]{:S(2)}) collective-permute-start(bf16[2,2048,128]{2,1,0:T(8,128)(2,1)S(1)} %pad_maximum_fusion.1.refs_6_.refs_7_), channel_id=1, source_target_pairs={{0,4},{1,5},{2,6},{3,7},{4,8},{5,9},{6,10},{7,11},{8,12},{9,13},{1... | collective-permute-start | bytes 3145736 | tf_op jit(solution)/shard_map/ppermute | solution.py:31
  26.6 36.2 %collective-permute-start.7 = (bf16[2,2048,128]{2,1,0:T(8,128)(2,1)S(1)}, bf16[2,2048,128]{2,1,0:T(8,128)(2,1)}, u32[]{:S(2)}, u32[]{:S(2)}) collective-permute-start(bf16[2,2048,128]{2,1,0:T(8,128)(2,1)S(1)} %pad_maximum_fusion.1.refs_6_.refs_7_), channel_id=1, source_target_pairs={{0,12},{1,13},{2,14},{3,15},{4,0},{5,1},{6,2},{7,3},{8,4},{9,5},{1... | collective-permute-start | bytes 3145736 | tf_op jit(solution)/shard_map/ppermute | solution.py:31
  29.7 68.3 %collective-permute-start = (bf16[4,2,512,128]{3,2,1,0:T(8,128)(2,1)S(1)}, bf16[4,2,512,128]{3,2,1,0:T(8,128)(2,1)}, u32[]{:S(2)}, u32[]{:S(2)}) collective-permute-start(bf16[4,2,512,128]{3,2,1,0:T(8,128)(2,1)S(1)} %all-to-all-done.refs_0_), channel_id=1, source_target_pairs={{0,3},{1,0},{2,1},{3,2},{4,7},{5,4},{6,5},{7,6},{8,11},{9,8},{10,9... | collective-permute-start | bytes 3145736 | tf_op jit(solution)/shard_map/ppermute | solution.py:31
  44.7 6.3 %copy-start = (bf16[2,2048,128]{2,1,0:T(8,128)(2,1)}, bf16[2,2048,128]{2,1,0:T(8,128)(2,1)S(1)}, u32[]{:S(2)}) copy-start(bf16[2,2048,128]{2,1,0:T(8,128)(2,1)S(1)} %collective-permute-done.10.refs_3_) | copy-start | bytes 3145732
  44.7 50.5 %collective-permute-start.2 = (bf16[4,2,512,128]{3,2,1,0:T(8,128)(2,1)S(1)}, bf16[4,2,512,128]{3,2,1,0:T(8,128)(2,1)}, u32[]{:S(2)}, u32[]{:S(2)}) collective-permute-start(bf16[4,2,512,128]{3,2,1,0:T(8,128)(2,1)S(1)} %all-to-all-done.refs_0_), channel_id=1, source_target_pairs={{0,1},{1,2},{2,3},{3,0},{4,5},{5,6},{6,7},{7,4},{8,9},{9,10},{10,1... | collective-permute-start | bytes 3145736 | tf_op jit(solution)/shard_map/ppermute | solution.py:31
  47.7 55.0 %collective-permute-start.1 = (bf16[4,2,512,128]{3,2,1,0:T(8,128)(2,1)S(1)}, bf16[4,2,512,128]{3,2,1,0:T(8,128)(2,1)}, u32[]{:S(2)}, u32[]{:S(2)}) collective-permute-start(bf16[4,2,512,128]{3,2,1,0:T(8,128)(2,1)S(1)} %all-to-all-done.refs_0_), channel_id=1, source_target_pairs={{0,2},{1,3},{2,0},{3,1},{4,6},{5,7},{6,4},{7,5},{8,10},{9,11},{10,... | collective-permute-start | bytes 3145736 | tf_op jit(solution)/shard_map/ppermute | solution.py:31
  51.0 51.6 %all-to-all-start.1 = ((f32[4,512,128]{2,1,0:T(8,128)}), f32[4,512,128]{2,1,0:T(8,128)S(1)}, u32[]{:S(2)}, u32[]{:S(2)}) async-start(f32[4,512,128]{2,1,0:T(8,128)} %bitcast.25), calls=%async_computation.1 | async-start | bytes 2097152 | tf_op jit(solution)/shard_map/all_to_all | solution.py:154
  57.4 39.7 %copy-start.1 = (bf16[2,2048,128]{2,1,0:T(8,128)(2,1)S(1)}, bf16[2,2048,128]{2,1,0:T(8,128)(2,1)}, u32[]{:S(2)}) copy-start(bf16[2,2048,128]{2,1,0:T(8,128)(2,1)} %copy-done) | copy-start | bytes 3145732
  59.4 43.3 %collective-permute-start.6 = (bf16[2048,128]{1,0:T(8,128)(2,1)}, bf16[2048,128]{1,0:T(8,128)(2,1)}, u32[]{:S(2)}, u32[]{:S(2)}) collective-permute-start(bf16[2048,128]{1,0:T(8,128)(2,1)} %slice_bitcast_fusion.3), channel_id=1, source_target_pairs={{0,4},{1,5},{2,6},{3,7},{4,8},{5,9},{6,10},{7,11},{8,12},{9,13},{1... | collective-permute-start | bytes 1572872 | tf_op jit(solution)/shard_map/ppermute | solution.py:31
  64.7 38.0 %collective-permute-start.8 = (bf16[2048,128]{1,0:T(8,128)(2,1)}, bf16[2048,128]{1,0:T(8,128)(2,1)}, u32[]{:S(2)}, u32[]{:S(2)}) collective-permute-start(bf16[2048,128]{1,0:T(8,128)(2,1)} %slice_bitcast_fusion.2), channel_id=1, source_target_pairs={{0,12},{1,13},{2,14},{3,15},{4,0},{5,1},{6,2},{7,3},{8,4},{9,5},{1... | collective-permute-start | bytes 1572872 | tf_op jit(solution)/shard_map/ppermute | solution.py:31
  95.2 22.1 %collective-permute-start.11 = (bf16[2048,128]{1,0:T(8,128)(2,1)}, bf16[2048,128]{1,0:T(8,128)(2,1)}, u32[]{:S(2)}, u32[]{:S(2)}) collective-permute-start(bf16[2048,128]{1,0:T(8,128)(2,1)} %slice_bitcast_fusion.1), channel_id=1, source_target_pairs={{0,1},{1,2},{2,3},{3,0},{4,5},{5,6},{6,7},{7,4},{8,9},{9,10},{10,1... | collective-permute-start | bytes 1572872 | tf_op jit(solution)/shard_map/ppermute | solution.py:31
  98.0 20.6 %collective-permute-start.12 = (bf16[2048,128]{1,0:T(8,128)(2,1)}, bf16[2048,128]{1,0:T(8,128)(2,1)}, u32[]{:S(2)}, u32[]{:S(2)}) collective-permute-start(bf16[2048,128]{1,0:T(8,128)(2,1)} %slice_bitcast_fusion), channel_id=1, source_target_pairs={{0,3},{1,0},{2,1},{3,2},{4,7},{5,4},{6,5},{7,6},{8,11},{9,8},{10,9... | collective-permute-start | bytes 1572872 | tf_op jit(solution)/shard_map/ppermute | solution.py:31
  106.8 11.9 %copy-start.2 = (bf16[2,2048,128]{2,1,0:T(8,128)(2,1)S(1)}, bf16[2,2048,128]{2,1,0:T(8,128)(2,1)}, u32[]{:S(2)}) copy-start(bf16[2,2048,128]{2,1,0:T(8,128)(2,1)} %copy-done) | copy-start | bytes 3145732
  106.8 11.9 %copy-start.4 = (bf16[1,2048,128]{2,1,0:T(8,128)(2,1)S(1)}, bf16[1,2048,128]{2,1,0:T(8,128)(2,1)}, u32[]{:S(2)}) copy-start(bf16[1,2048,128]{2,1,0:T(8,128)(2,1)} %param.8) | copy-start | bytes 1572868
  106.8 11.9 %copy-start.6 = (bf16[1,2048,128]{2,1,0:T(8,128)(2,1)S(1)}, bf16[1,2048,128]{2,1,0:T(8,128)(2,1)}, u32[]{:S(2)}) copy-start(bf16[1,2048,128]{2,1,0:T(8,128)(2,1)} %param.9) | copy-start | bytes 1572868
  106.8 11.8 %collective-permute-start.13 = (bf16[2,512,128]{2,1,0:T(8,128)(2,1)S(1)}, bf16[2,512,128]{2,1,0:T(8,128)(2,1)S(1)}, u32[]{:S(2)}, u32[]{:S(2)}) collective-permute-start(bf16[2,512,128]{2,1,0:T(8,128)(2,1)S(1)} %get-tuple-element.25), channel_id=1, source_target_pairs={{0,32},{1,33},{2,34},{3,35},{4,36},{5,37},{6,38},{7,39},{8,40},{9,... | collective-permute-start | bytes 786440 | tf_op jit(solution)/shard_map/ppermute | solution.py:31
  108.2 10.4 %collective-permute-start.14 = (bf16[2,512,128]{2,1,0:T(8,128)(2,1)S(1)}, bf16[2,512,128]{2,1,0:T(8,128)(2,1)S(1)}, u32[]{:S(2)}, u32[]{:S(2)}) collective-permute-start(bf16[2,512,128]{2,1,0:T(8,128)(2,1)S(1)} %get-tuple-element.25), channel_id=1, source_target_pairs={{32,0},{33,1},{34,2},{35,3},{36,4},{37,5},{38,6},{39,7},{40,8},{41... | collective-permute-start | bytes 786440 | tf_op jit(solution)/shard_map/ppermute | solution.py:31
  113.3 13.3 %collective-permute-start.15 = (bf16[2,512,128]{2,1,0:T(8,128)(2,1)S(1)}, bf16[2,512,128]{2,1,0:T(8,128)(2,1)S(1)}, u32[]{:S(2)}, u32[]{:S(2)}) collective-permute-start(bf16[2,512,128]{2,1,0:T(8,128)(2,1)S(1)} %get-tuple-element.32), channel_id=1, source_target_pairs={{0,32},{1,33},{2,34},{3,35},{4,36},{5,37},{6,38},{7,39},{8,40},{9,... | collective-permute-start | bytes 786440 | tf_op jit(solution)/shard_map/ppermute | solution.py:31
  117.3 9.3 %collective-permute-start.16 = (bf16[2,512,128]{2,1,0:T(8,128)(2,1)S(1)}, bf16[2,512,128]{2,1,0:T(8,128)(2,1)S(1)}, u32[]{:S(2)}, u32[]{:S(2)}) collective-permute-start(bf16[2,512,128]{2,1,0:T(8,128)(2,1)S(1)} %get-tuple-element.32), channel_id=1, source_target_pairs={{32,0},{33,1},{34,2},{35,3},{36,4},{37,5},{38,6},{39,7},{40,8},{41... | collective-permute-start | bytes 786440 | tf_op jit(solution)/shard_map/ppermute | solution.py:31
  121.5 27.6 %collective-permute-start.17 = (bf16[2048,128]{1,0:T(8,128)(2,1)S(1)}, bf16[2048,128]{1,0:T(8,128)(2,1)S(1)}, u32[]{:S(2)}, u32[]{:S(2)}) collective-permute-start(bf16[2048,128]{1,0:T(8,128)(2,1)S(1)} %get-tuple-element.30), channel_id=1, source_target_pairs={{0,8},{1,9},{2,10},{3,11},{4,12},{5,13},{6,14},{7,15},{8,0},{9,1},... | collective-permute-start | bytes 1572872 | tf_op jit(solution)/shard_map/ppermute | solution.py:31
  126.6 22.5 %copy-start.8 = (f32[1,2048,128]{2,1,0:T(8,128)S(1)}, f32[1,2048,128]{2,1,0:T(8,128)}, u32[]{:S(2)}) copy-start(f32[1,2048,128]{2,1,0:T(8,128)} %param.5) | copy-start | bytes 3145732
  129.5 19.6 %collective-permute-start.19 = (bf16[2048,128]{1,0:T(8,128)(2,1)S(1)}, bf16[2048,128]{1,0:T(8,128)(2,1)S(1)}, u32[]{:S(2)}, u32[]{:S(2)}) collective-permute-start(bf16[2048,128]{1,0:T(8,128)(2,1)S(1)} %get-tuple-element.36), channel_id=1, source_target_pairs={{0,12},{1,13},{2,14},{3,15},{4,0},{5,1},{6,2},{7,3},{8,4},{9,5},{1... | collective-permute-start | bytes 1572872 | tf_op jit(solution)/shard_map/ppermute | solution.py:31
  132.8 16.3 %collective-permute-start.18 = (bf16[2048,128]{1,0:T(8,128)(2,1)S(1)}, bf16[2048,128]{1,0:T(8,128)(2,1)S(1)}, u32[]{:S(2)}, u32[]{:S(2)}) collective-permute-start(bf16[2048,128]{1,0:T(8,128)(2,1)S(1)} %get-tuple-element.35), channel_id=1, source_target_pairs={{0,4},{1,5},{2,6},{3,7},{4,8},{5,9},{6,10},{7,11},{8,12},{9,13},{1... | collective-permute-start | bytes 1572872 | tf_op jit(solution)/shard_map/ppermute | solution.py:31

commit v11 on v9

--- a/solution.py
+++ b/solution.py
@@ -44,14 +44,19 @@
 
 
 def first_kernel(groups, at_ref, *refs):
-    blocks, parts = refs[:X], refs[X : X + 2 * len(groups)]
-    rhs_ref, corr_ref, sent_ref = refs[X + 2 * len(groups) :]
+    own, right_ref, *far, left_ref = refs[: X + 1]
+    refs = refs[X + 1 :]
+    parts = refs[: 2 * len(groups)]
+    rhs_ref, corr_ref, sent_ref = refs[2 * len(groups) :]
     indices = [index for _, index in part_places(groups)]
 
     total = jnp.zeros((BLK, len(groups) * COL), jnp.float32)
     for k in range(Y):
         for side in (0, 1):
-            left = jnp.concatenate([block[k, side] for block in blocks], axis=1)
+            half, row = divmod(k, Y // 2)
+            left = [own[k, side], right_ref[k, side]]
+            left += [far[half][row, side], left_ref[k, side]]
+            left = jnp.concatenate(left, axis=1)
             right = []
             for part, index in list(zip(parts, indices))[side::2]:
                 rows = rows_in_order(at_ref, part, index, k * BLK)
@@ -70,7 +75,7 @@
     places = {
         0: (("near", (0,)), ("near", (1,))),
         1: (("up", (0,)), ("up", (1,))),
-        2: (("below_far", ()), ("above_far", ())),
+        2: (("far", (0,)), ("far", (1,))),
         3: (("down", (0,)), ("down", (1,))),
     }
     return [place for d in groups for place in places[d]]
@@ -90,7 +95,7 @@
             jax.ShapeDtypeStruct((count, BLK, COL), jnp.float32),
             jax.ShapeDtypeStruct((count, BLK, COL), jnp.bfloat16),
         ),
-        in_specs=[IN_SMEM] + [IN_VMEM] * (X + len(parts) + 1),
+        in_specs=[IN_SMEM] + [IN_VMEM] * (X + len(parts) + 2),
         out_specs=(IN_VMEM, IN_VMEM),
         compiler_params=pltpu.CompilerParams(vmem_limit_bytes=24 << 20),
         cost_estimate=pl.CostEstimate(
@@ -163,17 +168,18 @@
     seconds = after(jnp.stack([lo_two, up_two]), sent_one)
     two_left, two_right = moved(seconds, xs=1), moved(seconds, xs=-1)
 
-    left, right, far = moved(own, xs=1), moved(own, xs=-1), moved(own, xs=2)
+    left, right = moved(own, xs=1), moved(own, xs=-1)
+    far = moved(left[: Y // 2], xs=1), moved(right[Y // 2 :], xs=-1)
     down, up = moved(near, ys=1), moved(near, ys=-1)
-    below_far, above_far = moved(down[0], ys=1), moved(up[1], ys=-1)
+    distant = moved(after(near, down, up), ys=2)
     rhs_rows = exchanged(after(rhs, own, two_left, two_right).reshape(Y, BLK, COL))
 
     lo_far = moved(after(two_left[0], left), xs=1)
     up_far = moved(after(two_right[1], right), xs=-1)
 
-    blocks = (own, right, far, left)
+    blocks = (own, right, *far, left)
     parts = dict(near=near, down=down, up=up)
-    parts.update(below_far=below_far, above_far=above_far)
+    parts["far"] = distant
     corr_a, sent_a = first_level(FIRST_GROUPS, at, blocks, parts, rhs_rows)
     late = after(at, sent_a)
     corr_b, sent_b = first_level(LAST_GROUPS, late, blocks, parts, rhs_rows)

time: 148 us -> 146 us (0.986)
  the two profiles are of different devices: /device:TPU:128 before, /device:TPU:166 now
where the time goes in v11:
time: 146 us; the launch traced here: 145 us
  starting transfers between devices  78.2 us (54%)
  waiting for transfers between devices  39.3 us (27%)
  Pallas kernels  13.8 us (9%)
  local copies, waits for them, and re-layouts  7.27 us (5%)
  other arithmetic  6.05 us (4%)
    ppermute x20, starting transfers between devices, moved(): return lax.ppermute(value, AXES, pairs)  68.9 us
    ppermute x20, waiting for transfers between devices, moved(): return lax.ppermute(value, AXES, pairs)  36.2 us
    all_to_all x2, starting transfers between devices, exchanged(): return lax.all_to_all(value, 'y', 0, 0, tiled=True)  9.31 us
    pallas_call x2, Pallas kernels, first_level(): pl.pallas_call(functools.partial(first_kernel, groups), name='first_level...  8.14 us
    pallas_call x2, Pallas kernels, second_level(): pl.pallas_call(functools.partial(second_kernel, groups), name='second_lev...  5.65 us
    slice x2, local copies, waits for them, and re-layouts, on_device(): far = (moved(left[:Y // 2], xs=1), moved(right[Y // 2:], xs=-1))  3.76 us
    all_to_all x2, waiting for transfers between devices, exchanged(): return lax.all_to_all(value, 'y', 0, 0, tiled=True)  3.08 us
  transfers between devices with their start and end apart: 22, of which 10 were waited for; matrix products, arithmetic and copies ran while one was open for 6% of the time, Pallas kernels for 10%

profile of v11, /device:TPU:166, one launch (start us, length us, event | category | flops | bytes accessed | tf_op | source)
XLA Modules:
  0.0 144.9 jit_solution(11702258114837814931)
XLA Ops:
  0.0 2.4 %pad_maximum_fusion = bf16[4,2,512,128]{3,2,1,0:T(8,128)(2,1)} fusion(bf16[4,1,512,128]{3,2,1,0:T(8,128)(2,1)} %bitcast.23, bf16[4,1,512,128]{3,2,1,0:T(8,128)(2,1)} %bitcast.24), kind=kLoop, calls=%fused_computation | loop fusion | flops 524288 | bytes 2097152 | tf_op jit(solution)/shard_map/stack | solution.py:162
  2.4 2.1 %collective-permute-start.4 = (bf16[2048,128]{1,0:T(8,128)(2,1)S(1)}, bf16[2048,128]{1,0:T(8,128)(2,1)S(1)}, u32[]{:S(2)}, u32[]{:S(2)}) collective-permute-start(bf16[2048,128]{1,0:T(8,128)(2,1)S(1)} %convert_element_type.12), channel_id=1, source_target_pairs={{0,16},{1,17},{2,18},{3,19},{4,20},{5,21},{6,22},{7,23},{8,24},{9,... | collective-permute-start | bytes 1572872 | tf_op jit(solution)/shard_map/ppermute | solution.py:31
  4.5 3.6 %collective-permute-start.5 = (bf16[2048,128]{1,0:T(8,128)(2,1)S(1)}, bf16[2048,128]{1,0:T(8,128)(2,1)}, u32[]{:S(2)}, u32[]{:S(2)}) collective-permute-start(bf16[2048,128]{1,0:T(8,128)(2,1)S(1)} %convert_element_type.12), channel_id=1, source_target_pairs={{16,0},{17,1},{18,2},{19,3},{20,4},{21,5},{22,6},{23,7},{24,8},{25... | collective-permute-start | bytes 1572872 | tf_op jit(solution)/shard_map/ppermute | solution.py:31
  9.2 2.7 %collective-permute-start.10 = (bf16[2,2048,128]{2,1,0:T(8,128)(2,1)}, bf16[2,2048,128]{2,1,0:T(8,128)(2,1)S(1)}, u32[]{:S(2)}, u32[]{:S(2)}) collective-permute-start(bf16[2,2048,128]{2,1,0:T(8,128)(2,1)} %pad_maximum_fusion.2), channel_id=1, source_target_pairs={{0,3},{1,0},{2,1},{3,2},{4,7},{5,4},{6,5},{7,6},{8,11},{9,8},{10,9... | collective-permute-start | bytes 3145736 | tf_op jit(solution)/shard_map/ppermute | solution.py:31
  11.9 4.5 %all-to-all-start = ((bf16[4,2,512,128]{3,2,1,0:T(8,128)(2,1)}), bf16[4,2,512,128]{3,2,1,0:T(8,128)(2,1)S(1)}, u32[]{:S(2)}, u32[]{:S(2)}) async-start(bf16[4,2,512,128]{3,2,1,0:T(8,128)(2,1)} %pad_maximum_fusion), calls=%async_computation | async-start | bytes 2097152 | tf_op jit(solution)/shard_map/all_to_all | solution.py:159
  16.4 4.3 %collective-permute-start.9 = (bf16[2,2048,128]{2,1,0:T(8,128)(2,1)}, bf16[2,2048,128]{2,1,0:T(8,128)(2,1)}, u32[]{:S(2)}, u32[]{:S(2)}) collective-permute-start(bf16[2,2048,128]{2,1,0:T(8,128)(2,1)} %pad_maximum_fusion.2), channel_id=1, source_target_pairs={{0,1},{1,2},{2,3},{3,0},{4,5},{5,6},{6,7},{7,4},{8,9},{9,10},{10,1... | collective-permute-start | bytes 3145736 | tf_op jit(solution)/shard_map/ppermute | solution.py:31
  22.8 3.9 %collective-permute-start.6 = (bf16[2,2048,128]{2,1,0:T(8,128)(2,1)S(1)}, bf16[2,2048,128]{2,1,0:T(8,128)(2,1)}, u32[]{:S(2)}, u32[]{:S(2)}) collective-permute-start(bf16[2,2048,128]{2,1,0:T(8,128)(2,1)S(1)} %pad_maximum_fusion.1.refs_7_.refs_8_), channel_id=1, source_target_pairs={{0,4},{1,5},{2,6},{3,7},{4,8},{5,9},{6,10},{7,11},{8,12},{9,13},{1... | collective-permute-start | bytes 3145736 | tf_op jit(solution)/shard_map/ppermute | solution.py:31
  26.8 3.1 %collective-permute-start.7 = (bf16[2,2048,128]{2,1,0:T(8,128)(2,1)S(1)}, bf16[2,2048,128]{2,1,0:T(8,128)(2,1)}, u32[]{:S(2)}, u32[]{:S(2)}) collective-permute-start(bf16[2,2048,128]{2,1,0:T(8,128)(2,1)S(1)} %pad_maximum_fusion.1.refs_7_.refs_8_), channel_id=1, source_target_pairs={{0,12},{1,13},{2,14},{3,15},{4,0},{5,1},{6,2},{7,3},{8,4},{9,5},{1... | collective-permute-start | bytes 3145736 | tf_op jit(solution)/shard_map/ppermute | solution.py:31
  29.9 3.1 %all-to-all-done.refs_0_ = bf16[4,2,512,128]{3,2,1,0:T(8,128)(2,1)S(1)} async-done(((bf16[4,2,512,128]{3,2,1,0:T(8,128)(2,1)}), bf16[4,2,512,128]{3,2,1,0:T(8,128)(2,1)S(1)}, u32[]{:S(2)}, u32[]{:S(2)}) %all-to-all-start) | async-done | bytes 1048608 | tf_op jit(solution)/shard_map/all_to_all | solution.py:159
  33.0 4.3 %collective-permute-start.1 = (bf16[4,2,512,128]{3,2,1,0:T(8,128)(2,1)S(1)}, bf16[4,2,512,128]{3,2,1,0:T(8,128)(2,1)}, u32[]{:S(2)}, u32[]{:S(2)}) collective-permute-start(bf16[4,2,512,128]{3,2,1,0:T(8,128)(2,1)S(1)} %all-to-all-done.refs_0_), channel_id=1, source_target_pairs={{0,1},{1,2},{2,3},{3,0},{4,5},{5,6},{6,7},{7,4},{8,9},{9,10},{10,1... | collective-permute-start | bytes 3145736 | tf_op jit(solution)/shard_map/ppermute | solution.py:31
  37.9 1.9 %collective-permute-start = (bf16[4,2,512,128]{3,2,1,0:T(8,128)(2,1)S(1)}, bf16[4,2,512,128]{3,2,1,0:T(8,128)(2,1)}, u32[]{:S(2)}, u32[]{:S(2)}) collective-permute-start(bf16[4,2,512,128]{3,2,1,0:T(8,128)(2,1)S(1)} %all-to-all-done.refs_0_), channel_id=1, source_target_pairs={{0,3},{1,0},{2,1},{3,2},{4,7},{5,4},{6,5},{7,6},{8,11},{9,8},{10,9... | collective-permute-start | bytes 3145736 | tf_op jit(solution)/shard_map/ppermute | solution.py:31
  39.8 4.9 %collective-permute-done.9.refs_2_ = bf16[2,2048,128]{2,1,0:T(8,128)(2,1)} collective-permute-done((bf16[2,2048,128]{2,1,0:T(8,128)(2,1)}, bf16[2,2048,128]{2,1,0:T(8,128)(2,1)}, u32[]{:S(2)}, u32[]{:S(2)}) %collective-permute-start.9) | collective-permute-done | bytes 1048608 | tf_op jit(solution)/shard_map/ppermute | solution.py:31
  44.7 4.8 %all-to-all-start.1 = ((f32[4,512,128]{2,1,0:T(8,128)}), f32[4,512,128]{2,1,0:T(8,128)S(1)}, u32[]{:S(2)}, u32[]{:S(2)}) async-start(f32[4,512,128]{2,1,0:T(8,128)} %bitcast.21), calls=%async_computation.1 | async-start | bytes 2097152 | tf_op jit(solution)/shard_map/all_to_all | solution.py:159
  49.5 4.8 %collective-permute-done.6.refs_5_.refs_6_ = bf16[2,2048,128]{2,1,0:T(8,128)(2,1)} collective-permute-done((bf16[2,2048,128]{2,1,0:T(8,128)(2,1)S(1)}, bf16[2,2048,128]{2,1,0:T(8,128)(2,1)}, u32[]{:S(2)}, u32[]{:S(2)}) %collective-permute-start.6) | collective-permute-done | bytes 1048608 | tf_op jit(solution)/shard_map/ppermute | solution.py:31
  54.9 4.6 %collective-permute-start.8 = (bf16[2,2048,128]{2,1,0:T(8,128)(2,1)S(1)}, bf16[2,2048,128]{2,1,0:T(8,128)(2,1)}, u32[]{:S(2)}, u32[]{:S(2)}) collective-permute-start(bf16[2,2048,128]{2,1,0:T(8,128)(2,1)S(1)} %pad_maximum_fusion.1.refs_7_.refs_8_), channel_id=1, source_target_pairs={{0,8},{1,9},{2,10},{3,11},{4,12},{5,13},{6,14},{7,15},{8,0},{9,1},... | collective-permute-start | bytes 3145736 | tf_op jit(solution)/shard_map/ppermute | solution.py:31
  61.3 4.6 %collective-permute-done.1.refs_4_ = bf16[4,2,512,128]{3,2,1,0:T(8,128)(2,1)} collective-permute-done((bf16[4,2,512,128]{3,2,1,0:T(8,128)(2,1)S(1)}, bf16[4,2,512,128]{3,2,1,0:T(8,128)(2,1)}, u32[]{:S(2)}, u32[]{:S(2)}) %collective-permute-start.1) | collective-permute-done | bytes 1048608 | tf_op jit(solution)/shard_map/ppermute | solution.py:31
  67.8 5.5 %collective-permute-start.2 = (bf16[2,2,512,128]{3,2,1,0:T(8,128)(2,1)}, bf16[2,2,512,128]{3,2,1,0:T(8,128)(2,1)}, u32[]{:S(2)}, u32[]{:S(2)}) collective-permute-start(bf16[2,2,512,128]{3,2,1,0:T(8,128)(2,1)} %slice.16), channel_id=1, source_target_pairs={{0,1},{1,2},{2,3},{3,0},{4,5},{5,6},{6,7},{7,4},{8,9},{9,10},{10,1... | collective-permute-start | bytes 1572872 | tf_op jit(solution)/shard_map/ppermute | solution.py:31
  77.1 5.1 %collective-permute-start.11 = (bf16[2048,128]{1,0:T(8,128)(2,1)}, bf16[2048,128]{1,0:T(8,128)(2,1)}, u32[]{:S(2)}, u32[]{:S(2)}) collective-permute-start(bf16[2048,128]{1,0:T(8,128)(2,1)} %slice_bitcast_fusion.1), channel_id=1, source_target_pairs={{0,1},{1,2},{2,3},{3,0},{4,5},{5,6},{6,7},{7,4},{8,9},{9,10},{10,1... | collective-permute-start | bytes 1572872 | tf_op jit(solution)/shard_map/ppermute | solution.py:31
  83.1 1.9 %collective-permute-start.12 = (bf16[2048,128]{1,0:T(8,128)(2,1)}, bf16[2048,128]{1,0:T(8,128)(2,1)}, u32[]{:S(2)}, u32[]{:S(2)}) collective-permute-start(bf16[2048,128]{1,0:T(8,128)(2,1)} %slice_bitcast_fusion), channel_id=1, source_target_pairs={{0,3},{1,0},{2,1},{3,2},{4,7},{5,4},{6,5},{7,6},{8,11},{9,8},{10,9... | collective-permute-start | bytes 1572872 | tf_op jit(solution)/shard_map/ppermute | solution.py:31
  86.0 7.5 %collective-permute-done.3.refs_3_ = bf16[2,2,512,128]{3,2,1,0:T(8,128)(2,1)} collective-permute-done((bf16[2,2,512,128]{3,2,1,0:T(8,128)(2,1)}, bf16[2,2,512,128]{3,2,1,0:T(8,128)(2,1)}, u32[]{:S(2)}, u32[]{:S(2)}) %collective-permute-start.3) | collective-permute-done | bytes 524320 | tf_op jit(solution)/shard_map/ppermute | solution.py:31
  93.5 4.4 %first_level.2 = (f32[2,512,128]{2,1,0:T(8,128)S(1)}, bf16[2,512,128]{2,1,0:T(8,128)(2,1)S(1)}) custom-call(s32[2]{0:T(128)S(1)} %pad_add_fusion.at_ref, bf16[4,2,512,128]{3,2,1,0:T(8,128)(2,1)S(1)} %all-to-all-done.refs_0_, bf16[4,2,512,128]{3,2,1,0:T(8,128)(2,1)} %collective-permute-done.refs_1_, bf16[2,2,512,128]{3,2,1,0:T(8,128)(2,1)} %collective-permute-done.2.refs_2_, ...), custom_call_target="tpu_custom_call" | custom-call | flops 1073741824 | bytes 8388608 | tf_op jit(solution)/shard_map/first_level/pallas_call | solution.py:91
  97.9 4.0 %collective-permute-start.13 = (bf16[2,512,128]{2,1,0:T(8,128)(2,1)S(1)}, bf16[2,512,128]{2,1,0:T(8,128)(2,1)S(1)}, u32[]{:S(2)}, u32[]{:S(2)}) collective-permute-start(bf16[2,512,128]{2,1,0:T(8,128)(2,1)S(1)} %get-tuple-element.25), channel_id=1, source_target_pairs={{0,32},{1,33},{2,34},{3,35},{4,36},{5,37},{6,38},{7,39},{8,40},{9,... | collective-permute-start | bytes 786440 | tf_op jit(solution)/shard_map/ppermute | solution.py:31
  101.8 2.0 %collective-permute-start.14 = (bf16[2,512,128]{2,1,0:T(8,128)(2,1)S(1)}, bf16[2,512,128]{2,1,0:T(8,128)(2,1)S(1)}, u32[]{:S(2)}, u32[]{:S(2)}) collective-permute-start(bf16[2,512,128]{2,1,0:T(8,128)(2,1)S(1)} %get-tuple-element.25), channel_id=1, source_target_pairs={{32,0},{33,1},{34,2},{35,3},{36,4},{37,5},{38,6},{39,7},{40,8},{41... | collective-permute-start | bytes 786440 | tf_op jit(solution)/shard_map/ppermute | solution.py:31
  103.9 3.8 %first_level.3 = (f32[2,512,128]{2,1,0:T(8,128)S(1)}, bf16[2,512,128]{2,1,0:T(8,128)(2,1)S(1)}) custom-call(s32[2]{0:T(128)S(1)} %pad_add_fusion.at_ref, bf16[4,2,512,128]{3,2,1,0:T(8,128)(2,1)S(1)} %all-to-all-done.refs_0_, bf16[4,2,512,128]{3,2,1,0:T(8,128)(2,1)} %collective-permute-done.refs_1_, bf16[2,2,512,128]{3,2,1,0:T(8,128)(2,1)} %collective-permute-done.2.refs_2_, ...), custom_call_target="tpu_custom_call" | custom-call | flops 1073741824 | bytes 8388608 | tf_op jit(solution)/shard_map/first_level/pallas_call | solution.py:91
  107.6 4.9 %collective-permute-start.15 = (bf16[2,512,128]{2,1,0:T(8,128)(2,1)S(1)}, bf16[2,512,128]{2,1,0:T(8,128)(2,1)S(1)}, u32[]{:S(2)}, u32[]{:S(2)}) collective-permute-start(bf16[2,512,128]{2,1,0:T(8,128)(2,1)S(1)} %get-tuple-element.32), channel_id=1, source_target_pairs={{0,32},{1,33},{2,34},{3,35},{4,36},{5,37},{6,38},{7,39},{8,40},{9,... | collective-permute-start | bytes 786440 | tf_op jit(solution)/shard_map/ppermute | solution.py:31
  112.6 1.9 %collective-permute-start.16 = (bf16[2,512,128]{2,1,0:T(8,128)(2,1)S(1)}, bf16[2,512,128]{2,1,0:T(8,128)(2,1)S(1)}, u32[]{:S(2)}, u32[]{:S(2)}) collective-permute-start(bf16[2,512,128]{2,1,0:T(8,128)(2,1)S(1)} %get-tuple-element.32), channel_id=1, source_target_pairs={{32,0},{33,1},{34,2},{35,3},{36,4},{37,5},{38,6},{39,7},{40,8},{41... | collective-permute-start | bytes 786440 | tf_op jit(solution)/shard_map/ppermute | solution.py:31
  114.5 2.8 %second_level.2 = (bf16[2048,128]{1,0:T(8,128)(2,1)S(1)}, bf16[2048,128]{1,0:T(8,128)(2,1)S(1)}) custom-call(s32[2]{0:T(128)S(1)} %pad_add_fusion.at_ref, bf16[2048,128]{1,0:T(8,128)(2,1)S(1)} %bitcast.17, bf16[2048,128]{1,0:T(8,128)(2,1)S(1)} %bitcast.19, bf16[2,2048,128]{2,1,0:T(8,128)(2,1)} %collective-permute-done.9.refs_2_, ...), custom_call_target="tpu_custom_call" | custom-call | flops 1073741824 | bytes 6291456 | tf_op jit(solution)/shard_map/second_level/pallas_call | solution.py:136
  117.3 5.2 %collective-permute-start.17 = (bf16[2048,128]{1,0:T(8,128)(2,1)S(1)}, bf16[2048,128]{1,0:T(8,128)(2,1)S(1)}, u32[]{:S(2)}, u32[]{:S(2)}) collective-permute-start(bf16[2048,128]{1,0:T(8,128)(2,1)S(1)} %get-tuple-element.30), channel_id=1, source_target_pairs={{0,8},{1,9},{2,10},{3,11},{4,12},{5,13},{6,14},{7,15},{8,0},{9,1},... | collective-permute-start | bytes 1572872 | tf_op jit(solution)/shard_map/ppermute | solution.py:31
  122.6 2.9 %second_level.3 = (bf16[2048,128]{1,0:T(8,128)(2,1)S(1)}, f32[2048,128]{1,0:T(8,128)S(1)}) custom-call(s32[2]{0:T(128)S(1)} %pad_add_fusion.at_ref, bf16[2048,128]{1,0:T(8,128)(2,1)S(1)} %bitcast.18, bf16[2048,128]{1,0:T(8,128)(2,1)S(1)} %bitcast.20, bf16[2,2048,128]{2,1,0:T(8,128)(2,1)} %collective-permute-done.9.refs_2_, ...), custom_call_target="tpu_custom_call" | custom-call | flops 1073741824 | bytes 6291456 | tf_op jit(solution)/shard_map/second_level/pallas_call | solution.py:136
  125.5 3.2 %collective-permute-start.19 = (bf16[2048,128]{1,0:T(8,128)(2,1)S(1)}, bf16[2048,128]{1,0:T(8,128)(2,1)S(1)}, u32[]{:S(2)}, u32[]{:S(2)}) collective-permute-start(bf16[2048,128]{1,0:T(8,128)(2,1)S(1)} %get-tuple-element.36), channel_id=1, source_target_pairs={{0,12},{1,13},{2,14},{3,15},{4,0},{5,1},{6,2},{7,3},{8,4},{9,5},{1... | collective-permute-start | bytes 1572872 | tf_op jit(solution)/shard_map/ppermute | solution.py:31
  128.6 2.7 %collective-permute-start.18 = (bf16[2048,128]{1,0:T(8,128)(2,1)S(1)}, bf16[2048,128]{1,0:T(8,128)(2,1)S(1)}, u32[]{:S(2)}, u32[]{:S(2)}) collective-permute-start(bf16[2048,128]{1,0:T(8,128)(2,1)S(1)} %get-tuple-element.35), channel_id=1, source_target_pairs={{0,4},{1,5},{2,6},{3,7},{4,8},{5,9},{6,10},{7,11},{8,12},{9,13},{1... | collective-permute-start | bytes 1572872 | tf_op jit(solution)/shard_map/ppermute | solution.py:31
  131.3 11.4 %collective-permute-done.19 = bf16[2048,128]{1,0:T(8,128)(2,1)S(1)} collective-permute-done((bf16[2048,128]{1,0:T(8,128)(2,1)S(1)}, bf16[2048,128]{1,0:T(8,128)(2,1)S(1)}, u32[]{:S(2)}, u32[]{:S(2)}) %collective-permute-start.19) | collective-permute-done | bytes 524320 | tf_op jit(solution)/shard_map/ppermute | solution.py:31
  (46 shorter events, 15.9 us)
Async XLA Ops:
  0.0 2.4 %copy-start.7 = (f32[1,2048,128]{2,1,0:T(8,128)S(1)}, f32[1,2048,128]{2,1,0:T(8,128)}, u32[]{:S(2)}) copy-start(f32[1,2048,128]{2,1,0:T(8,128)} %param.5) | copy-start | bytes 3145732
  2.4 5.8 %copy-start.3 = (bf16[1,2048,128]{2,1,0:T(8,128)(2,1)S(1)}, bf16[1,2048,128]{2,1,0:T(8,128)(2,1)}, u32[]{:S(2)}) copy-start(bf16[1,2048,128]{2,1,0:T(8,128)(2,1)} %param.8) | copy-start | bytes 1572868
  2.4 5.8 %copy-start.5 = (bf16[1,2048,128]{2,1,0:T(8,128)(2,1)S(1)}, bf16[1,2048,128]{2,1,0:T(8,128)(2,1)}, u32[]{:S(2)}) copy-start(bf16[1,2048,128]{2,1,0:T(8,128)(2,1)} %param.9) | copy-start | bytes 1572868
  2.4 18.3 %collective-permute-start.4 = (bf16[2048,128]{1,0:T(8,128)(2,1)S(1)}, bf16[2048,128]{1,0:T(8,128)(2,1)S(1)}, u32[]{:S(2)}, u32[]{:S(2)}) collective-permute-start(bf16[2048,128]{1,0:T(8,128)(2,1)S(1)} %convert_element_type.12), channel_id=1, source_target_pairs={{0,16},{1,17},{2,18},{3,19},{4,20},{5,21},{6,22},{7,23},{8,24},{9,... | collective-permute-start | bytes 1572872 | tf_op jit(solution)/shard_map/ppermute | solution.py:31
  4.5 16.3 %collective-permute-start.5 = (bf16[2048,128]{1,0:T(8,128)(2,1)S(1)}, bf16[2048,128]{1,0:T(8,128)(2,1)}, u32[]{:S(2)}, u32[]{:S(2)}) collective-permute-start(bf16[2048,128]{1,0:T(8,128)(2,1)S(1)} %convert_element_type.12), channel_id=1, source_target_pairs={{16,0},{17,1},{18,2},{19,3},{20,4},{21,5},{22,6},{23,7},{24,8},{25... | collective-permute-start | bytes 1572872 | tf_op jit(solution)/shard_map/ppermute | solution.py:31
  9.2 28.7 %collective-permute-start.10 = (bf16[2,2048,128]{2,1,0:T(8,128)(2,1)}, bf16[2,2048,128]{2,1,0:T(8,128)(2,1)S(1)}, u32[]{:S(2)}, u32[]{:S(2)}) collective-permute-start(bf16[2,2048,128]{2,1,0:T(8,128)(2,1)} %pad_maximum_fusion.2), channel_id=1, source_target_pairs={{0,3},{1,0},{2,1},{3,2},{4,7},{5,4},{6,5},{7,6},{8,11},{9,8},{10,9... | collective-permute-start | bytes 3145736 | tf_op jit(solution)/shard_map/ppermute | solution.py:31
  11.9 21.1 %all-to-all-start = ((bf16[4,2,512,128]{3,2,1,0:T(8,128)(2,1)}), bf16[4,2,512,128]{3,2,1,0:T(8,128)(2,1)S(1)}, u32[]{:S(2)}, u32[]{:S(2)}) async-start(bf16[4,2,512,128]{3,2,1,0:T(8,128)(2,1)} %pad_maximum_fusion), calls=%async_computation | async-start | bytes 2097152 | tf_op jit(solution)/shard_map/all_to_all | solution.py:159
  16.4 28.3 %collective-permute-start.9 = (bf16[2,2048,128]{2,1,0:T(8,128)(2,1)}, bf16[2,2048,128]{2,1,0:T(8,128)(2,1)}, u32[]{:S(2)}, u32[]{:S(2)}) collective-permute-start(bf16[2,2048,128]{2,1,0:T(8,128)(2,1)} %pad_maximum_fusion.2), channel_id=1, source_target_pairs={{0,1},{1,2},{2,3},{3,0},{4,5},{5,6},{6,7},{7,4},{8,9},{9,10},{10,1... | collective-permute-start | bytes 3145736 | tf_op jit(solution)/shard_map/ppermute | solution.py:31
  20.7 0.8 copy-start.9
  22.8 31.5 %collective-permute-start.6 = (bf16[2,2048,128]{2,1,0:T(8,128)(2,1)S(1)}, bf16[2,2048,128]{2,1,0:T(8,128)(2,1)}, u32[]{:S(2)}, u32[]{:S(2)}) collective-permute-start(bf16[2,2048,128]{2,1,0:T(8,128)(2,1)S(1)} %pad_maximum_fusion.1.refs_7_.refs_8_), channel_id=1, source_target_pairs={{0,4},{1,5},{2,6},{3,7},{4,8},{5,9},{6,10},{7,11},{8,12},{9,13},{1... | collective-permute-start | bytes 3145736 | tf_op jit(solution)/shard_map/ppermute | solution.py:31
  26.8 28.1 %collective-permute-start.7 = (bf16[2,2048,128]{2,1,0:T(8,128)(2,1)S(1)}, bf16[2,2048,128]{2,1,0:T(8,128)(2,1)}, u32[]{:S(2)}, u32[]{:S(2)}) collective-permute-start(bf16[2,2048,128]{2,1,0:T(8,128)(2,1)S(1)} %pad_maximum_fusion.1.refs_7_.refs_8_), channel_id=1, source_target_pairs={{0,12},{1,13},{2,14},{3,15},{4,0},{5,1},{6,2},{7,3},{8,4},{9,5},{1... | collective-permute-start | bytes 3145736 | tf_op jit(solution)/shard_map/ppermute | solution.py:31
  33.0 32.9 %collective-permute-start.1 = (bf16[4,2,512,128]{3,2,1,0:T(8,128)(2,1)S(1)}, bf16[4,2,512,128]{3,2,1,0:T(8,128)(2,1)}, u32[]{:S(2)}, u32[]{:S(2)}) collective-permute-start(bf16[4,2,512,128]{3,2,1,0:T(8,128)(2,1)S(1)} %all-to-all-done.refs_0_), channel_id=1, source_target_pairs={{0,1},{1,2},{2,3},{3,0},{4,5},{5,6},{6,7},{7,4},{8,9},{9,10},{10,1... | collective-permute-start | bytes 3145736 | tf_op jit(solution)/shard_map/ppermute | solution.py:31
  37.9 6.8 %copy-start = (bf16[2,2048,128]{2,1,0:T(8,128)(2,1)}, bf16[2,2048,128]{2,1,0:T(8,128)(2,1)S(1)}, u32[]{:S(2)}) copy-start(bf16[2,2048,128]{2,1,0:T(8,128)(2,1)S(1)} %collective-permute-done.10.refs_3_) | copy-start | bytes 3145732
  37.9 35.4 %collective-permute-start = (bf16[4,2,512,128]{3,2,1,0:T(8,128)(2,1)S(1)}, bf16[4,2,512,128]{3,2,1,0:T(8,128)(2,1)}, u32[]{:S(2)}, u32[]{:S(2)}) collective-permute-start(bf16[4,2,512,128]{3,2,1,0:T(8,128)(2,1)S(1)} %all-to-all-done.refs_0_), channel_id=1, source_target_pairs={{0,3},{1,0},{2,1},{3,2},{4,7},{5,4},{6,5},{7,6},{8,11},{9,8},{10,9... | collective-permute-start | bytes 3145736 | tf_op jit(solution)/shard_map/ppermute | solution.py:31
  44.7 40.4 %all-to-all-start.1 = ((f32[4,512,128]{2,1,0:T(8,128)}), f32[4,512,128]{2,1,0:T(8,128)S(1)}, u32[]{:S(2)}, u32[]{:S(2)}) async-start(f32[4,512,128]{2,1,0:T(8,128)} %bitcast.21), calls=%async_computation.1 | async-start | bytes 2097152 | tf_op jit(solution)/shard_map/all_to_all | solution.py:159
  54.9 38.6 %collective-permute-start.8 = (bf16[2,2048,128]{2,1,0:T(8,128)(2,1)S(1)}, bf16[2,2048,128]{2,1,0:T(8,128)(2,1)}, u32[]{:S(2)}, u32[]{:S(2)}) collective-permute-start(bf16[2,2048,128]{2,1,0:T(8,128)(2,1)S(1)} %pad_maximum_fusion.1.refs_7_.refs_8_), channel_id=1, source_target_pairs={{0,8},{1,9},{2,10},{3,11},{4,12},{5,13},{6,14},{7,15},{8,0},{9,1},... | collective-permute-start | bytes 3145736 | tf_op jit(solution)/shard_map/ppermute | solution.py:31
  61.3 20.9 %copy-start.1 = (bf16[2,2048,128]{2,1,0:T(8,128)(2,1)S(1)}, bf16[2,2048,128]{2,1,0:T(8,128)(2,1)}, u32[]{:S(2)}) copy-start(bf16[2,2048,128]{2,1,0:T(8,128)(2,1)} %copy-done) | copy-start | bytes 3145732
  67.8 18.2 %collective-permute-start.2 = (bf16[2,2,512,128]{3,2,1,0:T(8,128)(2,1)}, bf16[2,2,512,128]{3,2,1,0:T(8,128)(2,1)}, u32[]{:S(2)}, u32[]{:S(2)}) collective-permute-start(bf16[2,2,512,128]{3,2,1,0:T(8,128)(2,1)} %slice.16), channel_id=1, source_target_pairs={{0,1},{1,2},{2,3},{3,0},{4,5},{5,6},{6,7},{7,4},{8,9},{9,10},{10,1... | collective-permute-start | bytes 1572872 | tf_op jit(solution)/shard_map/ppermute | solution.py:31
  75.2 18.3 %collective-permute-start.3 = (bf16[2,2,512,128]{3,2,1,0:T(8,128)(2,1)}, bf16[2,2,512,128]{3,2,1,0:T(8,128)(2,1)}, u32[]{:S(2)}, u32[]{:S(2)}) collective-permute-start(bf16[2,2,512,128]{3,2,1,0:T(8,128)(2,1)} %slice.17), channel_id=1, source_target_pairs={{0,3},{1,0},{2,1},{3,2},{4,7},{5,4},{6,5},{7,6},{8,11},{9,8},{10,9... | collective-permute-start | bytes 1572872 | tf_op jit(solution)/shard_map/ppermute | solution.py:31
  77.1 35.4 %collective-permute-start.11 = (bf16[2048,128]{1,0:T(8,128)(2,1)}, bf16[2048,128]{1,0:T(8,128)(2,1)}, u32[]{:S(2)}, u32[]{:S(2)}) collective-permute-start(bf16[2048,128]{1,0:T(8,128)(2,1)} %slice_bitcast_fusion.1), channel_id=1, source_target_pairs={{0,1},{1,2},{2,3},{3,0},{4,5},{5,6},{6,7},{7,4},{8,9},{9,10},{10,1... | collective-permute-start | bytes 1572872 | tf_op jit(solution)/shard_map/ppermute | solution.py:31
  83.1 31.4 %collective-permute-start.12 = (bf16[2048,128]{1,0:T(8,128)(2,1)}, bf16[2048,128]{1,0:T(8,128)(2,1)}, u32[]{:S(2)}, u32[]{:S(2)}) collective-permute-start(bf16[2048,128]{1,0:T(8,128)(2,1)} %slice_bitcast_fusion), channel_id=1, source_target_pairs={{0,3},{1,0},{2,1},{3,2},{4,7},{5,4},{6,5},{7,6},{8,11},{9,8},{10,9... | collective-permute-start | bytes 1572872 | tf_op jit(solution)/shard_map/ppermute | solution.py:31
  97.8 16.7 %copy-start.2 = (bf16[2,2048,128]{2,1,0:T(8,128)(2,1)S(1)}, bf16[2,2048,128]{2,1,0:T(8,128)(2,1)}, u32[]{:S(2)}) copy-start(bf16[2,2048,128]{2,1,0:T(8,128)(2,1)} %copy-done) | copy-start | bytes 3145732
  97.9 16.7 %copy-start.4 = (bf16[1,2048,128]{2,1,0:T(8,128)(2,1)S(1)}, bf16[1,2048,128]{2,1,0:T(8,128)(2,1)}, u32[]{:S(2)}) copy-start(bf16[1,2048,128]{2,1,0:T(8,128)(2,1)} %param.8) | copy-start | bytes 1572868
  97.9 16.7 %copy-start.6 = (bf16[1,2048,128]{2,1,0:T(8,128)(2,1)S(1)}, bf16[1,2048,128]{2,1,0:T(8,128)(2,1)}, u32[]{:S(2)}) copy-start(bf16[1,2048,128]{2,1,0:T(8,128)(2,1)} %param.9) | copy-start | bytes 1572868
  97.9 16.6 %collective-permute-start.13 = (bf16[2,512,128]{2,1,0:T(8,128)(2,1)S(1)}, bf16[2,512,128]{2,1,0:T(8,128)(2,1)S(1)}, u32[]{:S(2)}, u32[]{:S(2)}) collective-permute-start(bf16[2,512,128]{2,1,0:T(8,128)(2,1)S(1)} %get-tuple-element.25), channel_id=1, source_target_pairs={{0,32},{1,33},{2,34},{3,35},{4,36},{5,37},{6,38},{7,39},{8,40},{9,... | collective-permute-start | bytes 786440 | tf_op jit(solution)/shard_map/ppermute | solution.py:31
  101.8 12.7 %collective-permute-start.14 = (bf16[2,512,128]{2,1,0:T(8,128)(2,1)S(1)}, bf16[2,512,128]{2,1,0:T(8,128)(2,1)S(1)}, u32[]{:S(2)}, u32[]{:S(2)}) collective-permute-start(bf16[2,512,128]{2,1,0:T(8,128)(2,1)S(1)} %get-tuple-element.25), channel_id=1, source_target_pairs={{32,0},{33,1},{34,2},{35,3},{36,4},{37,5},{38,6},{39,7},{40,8},{41... | collective-permute-start | bytes 786440 | tf_op jit(solution)/shard_map/ppermute | solution.py:31
  107.6 14.9 %collective-permute-start.15 = (bf16[2,512,128]{2,1,0:T(8,128)(2,1)S(1)}, bf16[2,512,128]{2,1,0:T(8,128)(2,1)S(1)}, u32[]{:S(2)}, u32[]{:S(2)}) collective-permute-start(bf16[2,512,128]{2,1,0:T(8,128)(2,1)S(1)} %get-tuple-element.32), channel_id=1, source_target_pairs={{0,32},{1,33},{2,34},{3,35},{4,36},{5,37},{6,38},{7,39},{8,40},{9,... | collective-permute-start | bytes 786440 | tf_op jit(solution)/shard_map/ppermute | solution.py:31
  112.6 10.0 %collective-permute-start.16 = (bf16[2,512,128]{2,1,0:T(8,128)(2,1)S(1)}, bf16[2,512,128]{2,1,0:T(8,128)(2,1)S(1)}, u32[]{:S(2)}, u32[]{:S(2)}) collective-permute-start(bf16[2,512,128]{2,1,0:T(8,128)(2,1)S(1)} %get-tuple-element.32), channel_id=1, source_target_pairs={{32,0},{33,1},{34,2},{35,3},{36,4},{37,5},{38,6},{39,7},{40,8},{41... | collective-permute-start | bytes 786440 | tf_op jit(solution)/shard_map/ppermute | solution.py:31
  117.3 25.4 %collective-permute-start.17 = (bf16[2048,128]{1,0:T(8,128)(2,1)S(1)}, bf16[2048,128]{1,0:T(8,128)(2,1)S(1)}, u32[]{:S(2)}, u32[]{:S(2)}) collective-permute-start(bf16[2048,128]{1,0:T(8,128)(2,1)S(1)} %get-tuple-element.30), channel_id=1, source_target_pairs={{0,8},{1,9},{2,10},{3,11},{4,12},{5,13},{6,14},{7,15},{8,0},{9,1},... | collective-permute-start | bytes 1572872 | tf_op jit(solution)/shard_map/ppermute | solution.py:31
  122.6 21.2 %copy-start.8 = (f32[1,2048,128]{2,1,0:T(8,128)S(1)}, f32[1,2048,128]{2,1,0:T(8,128)}, u32[]{:S(2)}) copy-start(f32[1,2048,128]{2,1,0:T(8,128)} %param.5) | copy-start | bytes 3145732
  125.5 17.2 %collective-permute-start.19 = (bf16[2048,128]{1,0:T(8,128)(2,1)S(1)}, bf16[2048,128]{1,0:T(8,128)(2,1)S(1)}, u32[]{:S(2)}, u32[]{:S(2)}) collective-permute-start(bf16[2048,128]{1,0:T(8,128)(2,1)S(1)} %get-tuple-element.36), channel_id=1, source_target_pairs={{0,12},{1,13},{2,14},{3,15},{4,0},{5,1},{6,2},{7,3},{8,4},{9,5},{1... | collective-permute-start | bytes 1572872 | tf_op jit(solution)/shard_map/ppermute | solution.py:31
  128.6 15.1 %collective-permute-start.18 = (bf16[2048,128]{1,0:T(8,128)(2,1)S(1)}, bf16[2048,128]{1,0:T(8,128)(2,1)S(1)}, u32[]{:S(2)}, u32[]{:S(2)}) collective-permute-start(bf16[2048,128]{1,0:T(8,128)(2,1)S(1)} %get-tuple-element.35), channel_id=1, source_target_pairs={{0,4},{1,5},{2,6},{3,7},{4,8},{5,9},{6,10},{7,11},{8,12},{9,13},{1... | collective-permute-start | bytes 1572872 | tf_op jit(solution)/shard_map/ppermute | solution.py:31

commit v12 on v11

--- a/solution.py
+++ b/solution.py
@@ -160,7 +160,8 @@
 
     firsts = [v[0].reshape(Y, BLK, COL) for v in (lower_first, upper_first)]
     firsts = jnp.stack(firsts, axis=1)
-    sent_one = after(rhs, firsts).astype(jnp.bfloat16)
+    sent_one = rhs.astype(jnp.bfloat16)
+    firsts = after(firsts, sent_one)
     own = exchanged(firsts)
     near = jnp.stack([moved(sent_one, 1), moved(sent_one, -1)])
 

time: 146 us -> 146 us (level)
  transfers between devices with their start and end apart: 22 -> 22, of which waited for: 10 -> 8; matrix products, arithmetic and copies ran while one was open for 6% -> 7% of each run, Pallas kernels for 10% -> 10%
where the time goes in v12:
time: 146 us; the launch traced here: 145 us
  starting transfers between devices  77.9 us (53%)
  waiting for transfers between devices  40.3 us (28%)
  Pallas kernels  13.8 us (9%)
  local copies, waits for them, and re-layouts  6.5 us (4%)
  other arithmetic  6.07 us (4%)
    ppermute x20, starting transfers between devices, moved(): return lax.ppermute(value, AXES, pairs)  68.6 us
    ppermute x20, waiting for transfers between devices, moved(): return lax.ppermute(value, AXES, pairs)  36.4 us
    all_to_all x2, starting transfers between devices, exchanged(): return lax.all_to_all(value, 'y', 0, 0, tiled=True)  9.3 us
    pallas_call x2, Pallas kernels, first_level(): pl.pallas_call(functools.partial(first_kernel, groups), name='first_level...  8.14 us
    pallas_call x2, Pallas kernels, second_level(): pl.pallas_call(functools.partial(second_kernel, groups), name='second_lev...  5.65 us
    all_to_all x2, waiting for transfers between devices, exchanged(): return lax.all_to_all(value, 'y', 0, 0, tiled=True)  3.87 us
    slice x2, local copies, waits for them, and re-layouts, on_device(): far = (moved(left[:Y // 2], xs=1), moved(right[Y // 2:], xs=-1))  3.76 us
  transfers between devices with their start and end apart: 22, of which 8 were waited for; matrix products, arithmetic and copies ran while one was open for 7% of the time, Pallas kernels for 10%

profile of v12, /device:TPU:166, one launch (start us, length us, event | category | flops | bytes accessed | tf_op | source)
XLA Modules:
  0.0 145.0 jit_solution(797167772057845546)
XLA Ops:
  1.4 2.1 %collective-permute-start.4 = (bf16[2048,128]{1,0:T(8,128)(2,1)S(1)}, bf16[2048,128]{1,0:T(8,128)(2,1)}, u32[]{:S(2)}, u32[]{:S(2)}) collective-permute-start(bf16[2048,128]{1,0:T(8,128)(2,1)S(1)} %bitcast_convert_fusion), channel_id=1, source_target_pairs={{0,16},{1,17},{2,18},{3,19},{4,20},{5,21},{6,22},{7,23},{8,24},{9,... | collective-permute-start | bytes 1572872 | tf_op jit(solution)/shard_map/ppermute | solution.py:31
  3.5 3.6 %collective-permute-start.5 = (bf16[2048,128]{1,0:T(8,128)(2,1)S(1)}, bf16[2048,128]{1,0:T(8,128)(2,1)}, u32[]{:S(2)}, u32[]{:S(2)}) collective-permute-start(bf16[2048,128]{1,0:T(8,128)(2,1)S(1)} %bitcast_convert_fusion), channel_id=1, source_target_pairs={{16,0},{17,1},{18,2},{19,3},{20,4},{21,5},{22,6},{23,7},{24,8},{25... | collective-permute-start | bytes 1572872 | tf_op jit(solution)/shard_map/ppermute | solution.py:31
  8.2 2.7 %collective-permute-start.10 = (bf16[2,2048,128]{2,1,0:T(8,128)(2,1)}, bf16[2,2048,128]{2,1,0:T(8,128)(2,1)S(1)}, u32[]{:S(2)}, u32[]{:S(2)}) collective-permute-start(bf16[2,2048,128]{2,1,0:T(8,128)(2,1)} %pad_maximum_fusion.2), channel_id=1, source_target_pairs={{0,3},{1,0},{2,1},{3,2},{4,7},{5,4},{6,5},{7,6},{8,11},{9,8},{10,9... | collective-permute-start | bytes 3145736 | tf_op jit(solution)/shard_map/ppermute | solution.py:31
  12.0 4.5 %all-to-all-start = ((bf16[4,2,512,128]{3,2,1,0:T(8,128)(2,1)}), bf16[4,2,512,128]{3,2,1,0:T(8,128)(2,1)S(1)}, u32[]{:S(2)}, u32[]{:S(2)}) async-start(bf16[4,2,512,128]{3,2,1,0:T(8,128)(2,1)} %pad_maximum_fusion), calls=%async_computation | async-start | bytes 2097152 | tf_op jit(solution)/shard_map/all_to_all | solution.py:159
  16.5 4.3 %collective-permute-start.9 = (bf16[2,2048,128]{2,1,0:T(8,128)(2,1)}, bf16[2,2048,128]{2,1,0:T(8,128)(2,1)}, u32[]{:S(2)}, u32[]{:S(2)}) collective-permute-start(bf16[2,2048,128]{2,1,0:T(8,128)(2,1)} %pad_maximum_fusion.2), channel_id=1, source_target_pairs={{0,1},{1,2},{2,3},{3,0},{4,5},{5,6},{6,7},{7,4},{8,9},{9,10},{10,1... | collective-permute-start | bytes 3145736 | tf_op jit(solution)/shard_map/ppermute | solution.py:31
  22.1 3.9 %collective-permute-start.6 = (bf16[2,2048,128]{2,1,0:T(8,128)(2,1)S(1)}, bf16[2,2048,128]{2,1,0:T(8,128)(2,1)}, u32[]{:S(2)}, u32[]{:S(2)}) collective-permute-start(bf16[2,2048,128]{2,1,0:T(8,128)(2,1)S(1)} %pad_maximum_fusion.1.refs_7_.refs_8_), channel_id=1, source_target_pairs={{0,4},{1,5},{2,6},{3,7},{4,8},{5,9},{6,10},{7,11},{8,12},{9,13},{1... | collective-permute-start | bytes 3145736 | tf_op jit(solution)/shard_map/ppermute | solution.py:31
  26.0 3.1 %collective-permute-start.7 = (bf16[2,2048,128]{2,1,0:T(8,128)(2,1)S(1)}, bf16[2,2048,128]{2,1,0:T(8,128)(2,1)}, u32[]{:S(2)}, u32[]{:S(2)}) collective-permute-start(bf16[2,2048,128]{2,1,0:T(8,128)(2,1)S(1)} %pad_maximum_fusion.1.refs_7_.refs_8_), channel_id=1, source_target_pairs={{0,12},{1,13},{2,14},{3,15},{4,0},{5,1},{6,2},{7,3},{8,4},{9,5},{1... | collective-permute-start | bytes 3145736 | tf_op jit(solution)/shard_map/ppermute | solution.py:31
  29.2 3.9 %all-to-all-done.refs_0_ = bf16[4,2,512,128]{3,2,1,0:T(8,128)(2,1)S(1)} async-done(((bf16[4,2,512,128]{3,2,1,0:T(8,128)(2,1)}), bf16[4,2,512,128]{3,2,1,0:T(8,128)(2,1)S(1)}, u32[]{:S(2)}, u32[]{:S(2)}) %all-to-all-start) | async-done | bytes 1048608 | tf_op jit(solution)/shard_map/all_to_all | solution.py:159
  33.0 4.3 %collective-permute-start.1 = (bf16[4,2,512,128]{3,2,1,0:T(8,128)(2,1)S(1)}, bf16[4,2,512,128]{3,2,1,0:T(8,128)(2,1)}, u32[]{:S(2)}, u32[]{:S(2)}) collective-permute-start(bf16[4,2,512,128]{3,2,1,0:T(8,128)(2,1)S(1)} %all-to-all-done.refs_0_), channel_id=1, source_target_pairs={{0,1},{1,2},{2,3},{3,0},{4,5},{5,6},{6,7},{7,4},{8,9},{9,10},{10,1... | collective-permute-start | bytes 3145736 | tf_op jit(solution)/shard_map/ppermute | solution.py:31
  37.4 1.9 %collective-permute-start = (bf16[4,2,512,128]{3,2,1,0:T(8,128)(2,1)S(1)}, bf16[4,2,512,128]{3,2,1,0:T(8,128)(2,1)}, u32[]{:S(2)}, u32[]{:S(2)}) collective-permute-start(bf16[4,2,512,128]{3,2,1,0:T(8,128)(2,1)S(1)} %all-to-all-done.refs_0_), channel_id=1, source_target_pairs={{0,3},{1,0},{2,1},{3,2},{4,7},{5,4},{6,5},{7,6},{8,11},{9,8},{10,9... | collective-permute-start | bytes 3145736 | tf_op jit(solution)/shard_map/ppermute | solution.py:31
  39.3 5.4 %collective-permute-done.9.refs_2_ = bf16[2,2048,128]{2,1,0:T(8,128)(2,1)} collective-permute-done((bf16[2,2048,128]{2,1,0:T(8,128)(2,1)}, bf16[2,2048,128]{2,1,0:T(8,128)(2,1)}, u32[]{:S(2)}, u32[]{:S(2)}) %collective-permute-start.9) | collective-permute-done | bytes 1048608 | tf_op jit(solution)/shard_map/ppermute | solution.py:31
  44.7 4.8 %all-to-all-start.1 = ((f32[4,512,128]{2,1,0:T(8,128)}), f32[4,512,128]{2,1,0:T(8,128)S(1)}, u32[]{:S(2)}, u32[]{:S(2)}) async-start(f32[4,512,128]{2,1,0:T(8,128)} %bitcast.22), calls=%async_computation.1 | async-start | bytes 2097152 | tf_op jit(solution)/shard_map/all_to_all | solution.py:159
  49.6 4.9 %collective-permute-done.6.refs_5_.refs_6_ = bf16[2,2048,128]{2,1,0:T(8,128)(2,1)} collective-permute-done((bf16[2,2048,128]{2,1,0:T(8,128)(2,1)S(1)}, bf16[2,2048,128]{2,1,0:T(8,128)(2,1)}, u32[]{:S(2)}, u32[]{:S(2)}) %collective-permute-start.6) | collective-permute-done | bytes 1048608 | tf_op jit(solution)/shard_map/ppermute | solution.py:31
  54.4 4.3 %collective-permute-start.8 = (bf16[2,2048,128]{2,1,0:T(8,128)(2,1)S(1)}, bf16[2,2048,128]{2,1,0:T(8,128)(2,1)}, u32[]{:S(2)}, u32[]{:S(2)}) collective-permute-start(bf16[2,2048,128]{2,1,0:T(8,128)(2,1)S(1)} %pad_maximum_fusion.1.refs_7_.refs_8_), channel_id=1, source_target_pairs={{0,8},{1,9},{2,10},{3,11},{4,12},{5,13},{6,14},{7,15},{8,0},{9,1},... | collective-permute-start | bytes 3145736 | tf_op jit(solution)/shard_map/ppermute | solution.py:31
  60.6 5.3 %collective-permute-done.1.refs_4_ = bf16[4,2,512,128]{3,2,1,0:T(8,128)(2,1)} collective-permute-done((bf16[4,2,512,128]{3,2,1,0:T(8,128)(2,1)S(1)}, bf16[4,2,512,128]{3,2,1,0:T(8,128)(2,1)}, u32[]{:S(2)}, u32[]{:S(2)}) %collective-permute-start.1) | collective-permute-done | bytes 1048608 | tf_op jit(solution)/shard_map/ppermute | solution.py:31
  67.8 5.5 %collective-permute-start.2 = (bf16[2,2,512,128]{3,2,1,0:T(8,128)(2,1)}, bf16[2,2,512,128]{3,2,1,0:T(8,128)(2,1)}, u32[]{:S(2)}, u32[]{:S(2)}) collective-permute-start(bf16[2,2,512,128]{3,2,1,0:T(8,128)(2,1)} %slice.16), channel_id=1, source_target_pairs={{0,1},{1,2},{2,3},{3,0},{4,5},{5,6},{6,7},{7,4},{8,9},{9,10},{10,1... | collective-permute-start | bytes 1572872 | tf_op jit(solution)/shard_map/ppermute | solution.py:31
  75.2 1.9 %collective-permute-start.3 = (bf16[2,2,512,128]{3,2,1,0:T(8,128)(2,1)}, bf16[2,2,512,128]{3,2,1,0:T(8,128)(2,1)}, u32[]{:S(2)}, u32[]{:S(2)}) collective-permute-start(bf16[2,2,512,128]{3,2,1,0:T(8,128)(2,1)} %slice.17), channel_id=1, source_target_pairs={{0,3},{1,0},{2,1},{3,2},{4,7},{5,4},{6,5},{7,6},{8,11},{9,8},{10,9... | collective-permute-start | bytes 1572872 | tf_op jit(solution)/shard_map/ppermute | solution.py:31
  77.2 5.1 %collective-permute-start.11 = (bf16[2048,128]{1,0:T(8,128)(2,1)}, bf16[2048,128]{1,0:T(8,128)(2,1)}, u32[]{:S(2)}, u32[]{:S(2)}) collective-permute-start(bf16[2048,128]{1,0:T(8,128)(2,1)} %slice_bitcast_fusion.1), channel_id=1, source_target_pairs={{0,1},{1,2},{2,3},{3,0},{4,5},{5,6},{6,7},{7,4},{8,9},{9,10},{10,1... | collective-permute-start | bytes 1572872 | tf_op jit(solution)/shard_map/ppermute | solution.py:31
  83.1 1.9 %collective-permute-start.12 = (bf16[2048,128]{1,0:T(8,128)(2,1)}, bf16[2048,128]{1,0:T(8,128)(2,1)}, u32[]{:S(2)}, u32[]{:S(2)}) collective-permute-start(bf16[2048,128]{1,0:T(8,128)(2,1)} %slice_bitcast_fusion), channel_id=1, source_target_pairs={{0,3},{1,0},{2,1},{3,2},{4,7},{5,4},{6,5},{7,6},{8,11},{9,8},{10,9... | collective-permute-start | bytes 1572872 | tf_op jit(solution)/shard_map/ppermute | solution.py:31
  86.0 7.5 %collective-permute-done.3.refs_3_ = bf16[2,2,512,128]{3,2,1,0:T(8,128)(2,1)} collective-permute-done((bf16[2,2,512,128]{3,2,1,0:T(8,128)(2,1)}, bf16[2,2,512,128]{3,2,1,0:T(8,128)(2,1)}, u32[]{:S(2)}, u32[]{:S(2)}) %collective-permute-start.3) | collective-permute-done | bytes 524320 | tf_op jit(solution)/shard_map/ppermute | solution.py:31
  93.5 4.4 %first_level.2 = (f32[2,512,128]{2,1,0:T(8,128)S(1)}, bf16[2,512,128]{2,1,0:T(8,128)(2,1)S(1)}) custom-call(s32[2]{0:T(128)S(1)} %pad_add_fusion.at_ref, bf16[4,2,512,128]{3,2,1,0:T(8,128)(2,1)S(1)} %all-to-all-done.refs_0_, bf16[4,2,512,128]{3,2,1,0:T(8,128)(2,1)} %collective-permute-done.refs_1_, bf16[2,2,512,128]{3,2,1,0:T(8,128)(2,1)} %collective-permute-done.2.refs_2_, ...), custom_call_target="tpu_custom_call" | custom-call | flops 1073741824 | bytes 8388608 | tf_op jit(solution)/shard_map/first_level/pallas_call | solution.py:91
  97.9 4.0 %collective-permute-start.13 = (bf16[2,512,128]{2,1,0:T(8,128)(2,1)S(1)}, bf16[2,512,128]{2,1,0:T(8,128)(2,1)S(1)}, u32[]{:S(2)}, u32[]{:S(2)}) collective-permute-start(bf16[2,512,128]{2,1,0:T(8,128)(2,1)S(1)} %get-tuple-element.25), channel_id=1, source_target_pairs={{0,32},{1,33},{2,34},{3,35},{4,36},{5,37},{6,38},{7,39},{8,40},{9,... | collective-permute-start | bytes 786440 | tf_op jit(solution)/shard_map/ppermute | solution.py:31
  101.9 2.0 %collective-permute-start.14 = (bf16[2,512,128]{2,1,0:T(8,128)(2,1)S(1)}, bf16[2,512,128]{2,1,0:T(8,128)(2,1)S(1)}, u32[]{:S(2)}, u32[]{:S(2)}) collective-permute-start(bf16[2,512,128]{2,1,0:T(8,128)(2,1)S(1)} %get-tuple-element.25), channel_id=1, source_target_pairs={{32,0},{33,1},{34,2},{35,3},{36,4},{37,5},{38,6},{39,7},{40,8},{41... | collective-permute-start | bytes 786440 | tf_op jit(solution)/shard_map/ppermute | solution.py:31
  103.9 3.8 %first_level.3 = (f32[2,512,128]{2,1,0:T(8,128)S(1)}, bf16[2,512,128]{2,1,0:T(8,128)(2,1)S(1)}) custom-call(s32[2]{0:T(128)S(1)} %pad_add_fusion.at_ref, bf16[4,2,512,128]{3,2,1,0:T(8,128)(2,1)S(1)} %all-to-all-done.refs_0_, bf16[4,2,512,128]{3,2,1,0:T(8,128)(2,1)} %collective-permute-done.refs_1_, bf16[2,2,512,128]{3,2,1,0:T(8,128)(2,1)} %collective-permute-done.2.refs_2_, ...), custom_call_target="tpu_custom_call" | custom-call | flops 1073741824 | bytes 8388608 | tf_op jit(solution)/shard_map/first_level/pallas_call | solution.py:91
  107.7 4.9 %collective-permute-start.15 = (bf16[2,512,128]{2,1,0:T(8,128)(2,1)S(1)}, bf16[2,512,128]{2,1,0:T(8,128)(2,1)S(1)}, u32[]{:S(2)}, u32[]{:S(2)}) collective-permute-start(bf16[2,512,128]{2,1,0:T(8,128)(2,1)S(1)} %get-tuple-element.32), channel_id=1, source_target_pairs={{0,32},{1,33},{2,34},{3,35},{4,36},{5,37},{6,38},{7,39},{8,40},{9,... | collective-permute-start | bytes 786440 | tf_op jit(solution)/shard_map/ppermute | solution.py:31
  112.6 1.9 %collective-permute-start.16 = (bf16[2,512,128]{2,1,0:T(8,128)(2,1)S(1)}, bf16[2,512,128]{2,1,0:T(8,128)(2,1)S(1)}, u32[]{:S(2)}, u32[]{:S(2)}) collective-permute-start(bf16[2,512,128]{2,1,0:T(8,128)(2,1)S(1)} %get-tuple-element.32), channel_id=1, source_target_pairs={{32,0},{33,1},{34,2},{35,3},{36,4},{37,5},{38,6},{39,7},{40,8},{41... | collective-permute-start | bytes 786440 | tf_op jit(solution)/shard_map/ppermute | solution.py:31
  114.6 2.8 %second_level.2 = (bf16[2048,128]{1,0:T(8,128)(2,1)S(1)}, bf16[2048,128]{1,0:T(8,128)(2,1)S(1)}) custom-call(s32[2]{0:T(128)S(1)} %pad_add_fusion.at_ref, bf16[2048,128]{1,0:T(8,128)(2,1)S(1)} %bitcast.18, bf16[2048,128]{1,0:T(8,128)(2,1)S(1)} %bitcast.20, bf16[2,2048,128]{2,1,0:T(8,128)(2,1)} %collective-permute-done.9.refs_2_, ...), custom_call_target="tpu_custom_call" | custom-call | flops 1073741824 | bytes 6291456 | tf_op jit(solution)/shard_map/second_level/pallas_call | solution.py:136
  117.4 5.2 %collective-permute-start.17 = (bf16[2048,128]{1,0:T(8,128)(2,1)S(1)}, bf16[2048,128]{1,0:T(8,128)(2,1)S(1)}, u32[]{:S(2)}, u32[]{:S(2)}) collective-permute-start(bf16[2048,128]{1,0:T(8,128)(2,1)S(1)} %get-tuple-element.30), channel_id=1, source_target_pairs={{0,8},{1,9},{2,10},{3,11},{4,12},{5,13},{6,14},{7,15},{8,0},{9,1},... | collective-permute-start | bytes 1572872 | tf_op jit(solution)/shard_map/ppermute | solution.py:31
  122.6 2.9 %second_level.3 = (bf16[2048,128]{1,0:T(8,128)(2,1)S(1)}, f32[2048,128]{1,0:T(8,128)S(1)}) custom-call(s32[2]{0:T(128)S(1)} %pad_add_fusion.at_ref, bf16[2048,128]{1,0:T(8,128)(2,1)S(1)} %bitcast.19, bf16[2048,128]{1,0:T(8,128)(2,1)S(1)} %bitcast.21, bf16[2,2048,128]{2,1,0:T(8,128)(2,1)} %collective-permute-done.9.refs_2_, ...), custom_call_target="tpu_custom_call" | custom-call | flops 1073741824 | bytes 6291456 | tf_op jit(solution)/shard_map/second_level/pallas_call | solution.py:136
  125.5 3.1 %collective-permute-start.19 = (bf16[2048,128]{1,0:T(8,128)(2,1)S(1)}, bf16[2048,128]{1,0:T(8,128)(2,1)S(1)}, u32[]{:S(2)}, u32[]{:S(2)}) collective-permute-start(bf16[2048,128]{1,0:T(8,128)(2,1)S(1)} %get-tuple-element.36), channel_id=1, source_target_pairs={{0,12},{1,13},{2,14},{3,15},{4,0},{5,1},{6,2},{7,3},{8,4},{9,5},{1... | collective-permute-start | bytes 1572872 | tf_op jit(solution)/shard_map/ppermute | solution.py:31
  128.7 2.7 %collective-permute-start.18 = (bf16[2048,128]{1,0:T(8,128)(2,1)S(1)}, bf16[2048,128]{1,0:T(8,128)(2,1)S(1)}, u32[]{:S(2)}, u32[]{:S(2)}) collective-permute-start(bf16[2048,128]{1,0:T(8,128)(2,1)S(1)} %get-tuple-element.35), channel_id=1, source_target_pairs={{0,4},{1,5},{2,6},{3,7},{4,8},{5,9},{6,10},{7,11},{8,12},{9,13},{1... | collective-permute-start | bytes 1572872 | tf_op jit(solution)/shard_map/ppermute | solution.py:31
  131.4 11.4 %collective-permute-done.19 = bf16[2048,128]{1,0:T(8,128)(2,1)S(1)} collective-permute-done((bf16[2048,128]{1,0:T(8,128)(2,1)S(1)}, bf16[2048,128]{1,0:T(8,128)(2,1)S(1)}, u32[]{:S(2)}, u32[]{:S(2)}) %collective-permute-start.19) | collective-permute-done | bytes 524320 | tf_op jit(solution)/shard_map/ppermute | solution.py:31
  (46 shorter events, 14.5 us)
Async XLA Ops:
  0.0 7.1 %copy-start.3 = (bf16[1,2048,128]{2,1,0:T(8,128)(2,1)S(1)}, bf16[1,2048,128]{2,1,0:T(8,128)(2,1)}, u32[]{:S(2)}) copy-start(bf16[1,2048,128]{2,1,0:T(8,128)(2,1)} %param.8) | copy-start | bytes 1572868
  0.0 7.1 %copy-start.5 = (bf16[1,2048,128]{2,1,0:T(8,128)(2,1)S(1)}, bf16[1,2048,128]{2,1,0:T(8,128)(2,1)}, u32[]{:S(2)}) copy-start(bf16[1,2048,128]{2,1,0:T(8,128)(2,1)} %param.9) | copy-start | bytes 1572868
  1.4 9.6 %copy-start.8 = (bf16[1,2048,128]{2,1,0:T(8,128)(2,1)S(1)}, bf16[1,2048,128]{2,1,0:T(8,128)(2,1)}, u32[]{:S(2)}) copy-start(bf16[1,2048,128]{2,1,0:T(8,128)(2,1)} %param.7) | copy-start | bytes 1572868
  1.4 9.6 %copy-start.9 = (bf16[1,2048,128]{2,1,0:T(8,128)(2,1)S(1)}, bf16[1,2048,128]{2,1,0:T(8,128)(2,1)}, u32[]{:S(2)}) copy-start(bf16[1,2048,128]{2,1,0:T(8,128)(2,1)} %param.6) | copy-start | bytes 1572868
  1.4 19.4 %collective-permute-start.4 = (bf16[2048,128]{1,0:T(8,128)(2,1)S(1)}, bf16[2048,128]{1,0:T(8,128)(2,1)}, u32[]{:S(2)}, u32[]{:S(2)}) collective-permute-start(bf16[2048,128]{1,0:T(8,128)(2,1)S(1)} %bitcast_convert_fusion), channel_id=1, source_target_pairs={{0,16},{1,17},{2,18},{3,19},{4,20},{5,21},{6,22},{7,23},{8,24},{9,... | collective-permute-start | bytes 1572872 | tf_op jit(solution)/shard_map/ppermute | solution.py:31
  3.5 17.3 %collective-permute-start.5 = (bf16[2048,128]{1,0:T(8,128)(2,1)S(1)}, bf16[2048,128]{1,0:T(8,128)(2,1)}, u32[]{:S(2)}, u32[]{:S(2)}) collective-permute-start(bf16[2048,128]{1,0:T(8,128)(2,1)S(1)} %bitcast_convert_fusion), channel_id=1, source_target_pairs={{16,0},{17,1},{18,2},{19,3},{20,4},{21,5},{22,6},{23,7},{24,8},{25... | collective-permute-start | bytes 1572872 | tf_op jit(solution)/shard_map/ppermute | solution.py:31
  8.2 29.2 %collective-permute-start.10 = (bf16[2,2048,128]{2,1,0:T(8,128)(2,1)}, bf16[2,2048,128]{2,1,0:T(8,128)(2,1)S(1)}, u32[]{:S(2)}, u32[]{:S(2)}) collective-permute-start(bf16[2,2048,128]{2,1,0:T(8,128)(2,1)} %pad_maximum_fusion.2), channel_id=1, source_target_pairs={{0,3},{1,0},{2,1},{3,2},{4,7},{5,4},{6,5},{7,6},{8,11},{9,8},{10,9... | collective-permute-start | bytes 3145736 | tf_op jit(solution)/shard_map/ppermute | solution.py:31
  12.0 21.0 %all-to-all-start = ((bf16[4,2,512,128]{3,2,1,0:T(8,128)(2,1)}), bf16[4,2,512,128]{3,2,1,0:T(8,128)(2,1)S(1)}, u32[]{:S(2)}, u32[]{:S(2)}) async-start(bf16[4,2,512,128]{3,2,1,0:T(8,128)(2,1)} %pad_maximum_fusion), calls=%async_computation | async-start | bytes 2097152 | tf_op jit(solution)/shard_map/all_to_all | solution.py:159
  16.5 28.3 %collective-permute-start.9 = (bf16[2,2048,128]{2,1,0:T(8,128)(2,1)}, bf16[2,2048,128]{2,1,0:T(8,128)(2,1)}, u32[]{:S(2)}, u32[]{:S(2)}) collective-permute-start(bf16[2,2048,128]{2,1,0:T(8,128)(2,1)} %pad_maximum_fusion.2), channel_id=1, source_target_pairs={{0,1},{1,2},{2,3},{3,0},{4,5},{5,6},{6,7},{7,4},{8,9},{9,10},{10,1... | collective-permute-start | bytes 3145736 | tf_op jit(solution)/shard_map/ppermute | solution.py:31
  22.1 32.3 %collective-permute-start.6 = (bf16[2,2048,128]{2,1,0:T(8,128)(2,1)S(1)}, bf16[2,2048,128]{2,1,0:T(8,128)(2,1)}, u32[]{:S(2)}, u32[]{:S(2)}) collective-permute-start(bf16[2,2048,128]{2,1,0:T(8,128)(2,1)S(1)} %pad_maximum_fusion.1.refs_7_.refs_8_), channel_id=1, source_target_pairs={{0,4},{1,5},{2,6},{3,7},{4,8},{5,9},{6,10},{7,11},{8,12},{9,13},{1... | collective-permute-start | bytes 3145736 | tf_op jit(solution)/shard_map/ppermute | solution.py:31
  26.0 28.4 %collective-permute-start.7 = (bf16[2,2048,128]{2,1,0:T(8,128)(2,1)S(1)}, bf16[2,2048,128]{2,1,0:T(8,128)(2,1)}, u32[]{:S(2)}, u32[]{:S(2)}) collective-permute-start(bf16[2,2048,128]{2,1,0:T(8,128)(2,1)S(1)} %pad_maximum_fusion.1.refs_7_.refs_8_), channel_id=1, source_target_pairs={{0,12},{1,13},{2,14},{3,15},{4,0},{5,1},{6,2},{7,3},{8,4},{9,5},{1... | collective-permute-start | bytes 3145736 | tf_op jit(solution)/shard_map/ppermute | solution.py:31
  33.0 32.9 %collective-permute-start.1 = (bf16[4,2,512,128]{3,2,1,0:T(8,128)(2,1)S(1)}, bf16[4,2,512,128]{3,2,1,0:T(8,128)(2,1)}, u32[]{:S(2)}, u32[]{:S(2)}) collective-permute-start(bf16[4,2,512,128]{3,2,1,0:T(8,128)(2,1)S(1)} %all-to-all-done.refs_0_), channel_id=1, source_target_pairs={{0,1},{1,2},{2,3},{3,0},{4,5},{5,6},{6,7},{7,4},{8,9},{9,10},{10,1... | collective-permute-start | bytes 3145736 | tf_op jit(solution)/shard_map/ppermute | solution.py:31
  37.4 7.4 %copy-start = (bf16[2,2048,128]{2,1,0:T(8,128)(2,1)}, bf16[2,2048,128]{2,1,0:T(8,128)(2,1)S(1)}, u32[]{:S(2)}) copy-start(bf16[2,2048,128]{2,1,0:T(8,128)(2,1)S(1)} %collective-permute-done.10.refs_3_) | copy-start | bytes 3145732
  37.4 36.0 %collective-permute-start = (bf16[4,2,512,128]{3,2,1,0:T(8,128)(2,1)S(1)}, bf16[4,2,512,128]{3,2,1,0:T(8,128)(2,1)}, u32[]{:S(2)}, u32[]{:S(2)}) collective-permute-start(bf16[4,2,512,128]{3,2,1,0:T(8,128)(2,1)S(1)} %all-to-all-done.refs_0_), channel_id=1, source_target_pairs={{0,3},{1,0},{2,1},{3,2},{4,7},{5,4},{6,5},{7,6},{8,11},{9,8},{10,9... | collective-permute-start | bytes 3145736 | tf_op jit(solution)/shard_map/ppermute | solution.py:31
  44.7 40.4 %all-to-all-start.1 = ((f32[4,512,128]{2,1,0:T(8,128)}), f32[4,512,128]{2,1,0:T(8,128)S(1)}, u32[]{:S(2)}, u32[]{:S(2)}) async-start(f32[4,512,128]{2,1,0:T(8,128)} %bitcast.22), calls=%async_computation.1 | async-start | bytes 2097152 | tf_op jit(solution)/shard_map/all_to_all | solution.py:159
  54.4 39.1 %collective-permute-start.8 = (bf16[2,2048,128]{2,1,0:T(8,128)(2,1)S(1)}, bf16[2,2048,128]{2,1,0:T(8,128)(2,1)}, u32[]{:S(2)}, u32[]{:S(2)}) collective-permute-start(bf16[2,2048,128]{2,1,0:T(8,128)(2,1)S(1)} %pad_maximum_fusion.1.refs_7_.refs_8_), channel_id=1, source_target_pairs={{0,8},{1,9},{2,10},{3,11},{4,12},{5,13},{6,14},{7,15},{8,0},{9,1},... | collective-permute-start | bytes 3145736 | tf_op jit(solution)/shard_map/ppermute | solution.py:31
  60.6 21.7 %copy-start.1 = (bf16[2,2048,128]{2,1,0:T(8,128)(2,1)S(1)}, bf16[2,2048,128]{2,1,0:T(8,128)(2,1)}, u32[]{:S(2)}) copy-start(bf16[2,2048,128]{2,1,0:T(8,128)(2,1)} %copy-done) | copy-start | bytes 3145732
  67.8 18.2 %collective-permute-start.2 = (bf16[2,2,512,128]{3,2,1,0:T(8,128)(2,1)}, bf16[2,2,512,128]{3,2,1,0:T(8,128)(2,1)}, u32[]{:S(2)}, u32[]{:S(2)}) collective-permute-start(bf16[2,2,512,128]{3,2,1,0:T(8,128)(2,1)} %slice.16), channel_id=1, source_target_pairs={{0,1},{1,2},{2,3},{3,0},{4,5},{5,6},{6,7},{7,4},{8,9},{9,10},{10,1... | collective-permute-start | bytes 1572872 | tf_op jit(solution)/shard_map/ppermute | solution.py:31
  75.2 18.3 %collective-permute-start.3 = (bf16[2,2,512,128]{3,2,1,0:T(8,128)(2,1)}, bf16[2,2,512,128]{3,2,1,0:T(8,128)(2,1)}, u32[]{:S(2)}, u32[]{:S(2)}) collective-permute-start(bf16[2,2,512,128]{3,2,1,0:T(8,128)(2,1)} %slice.17), channel_id=1, source_target_pairs={{0,3},{1,0},{2,1},{3,2},{4,7},{5,4},{6,5},{7,6},{8,11},{9,8},{10,9... | collective-permute-start | bytes 1572872 | tf_op jit(solution)/shard_map/ppermute | solution.py:31
  77.2 35.4 %collective-permute-start.11 = (bf16[2048,128]{1,0:T(8,128)(2,1)}, bf16[2048,128]{1,0:T(8,128)(2,1)}, u32[]{:S(2)}, u32[]{:S(2)}) collective-permute-start(bf16[2048,128]{1,0:T(8,128)(2,1)} %slice_bitcast_fusion.1), channel_id=1, source_target_pairs={{0,1},{1,2},{2,3},{3,0},{4,5},{5,6},{6,7},{7,4},{8,9},{9,10},{10,1... | collective-permute-start | bytes 1572872 | tf_op jit(solution)/shard_map/ppermute | solution.py:31
  83.1 31.4 %collective-permute-start.12 = (bf16[2048,128]{1,0:T(8,128)(2,1)}, bf16[2048,128]{1,0:T(8,128)(2,1)}, u32[]{:S(2)}, u32[]{:S(2)}) collective-permute-start(bf16[2048,128]{1,0:T(8,128)(2,1)} %slice_bitcast_fusion), channel_id=1, source_target_pairs={{0,3},{1,0},{2,1},{3,2},{4,7},{5,4},{6,5},{7,6},{8,11},{9,8},{10,9... | collective-permute-start | bytes 1572872 | tf_op jit(solution)/shard_map/ppermute | solution.py:31
  97.9 16.7 %copy-start.2 = (bf16[2,2048,128]{2,1,0:T(8,128)(2,1)S(1)}, bf16[2,2048,128]{2,1,0:T(8,128)(2,1)}, u32[]{:S(2)}) copy-start(bf16[2,2048,128]{2,1,0:T(8,128)(2,1)} %copy-done) | copy-start | bytes 3145732
  97.9 16.7 %copy-start.4 = (bf16[1,2048,128]{2,1,0:T(8,128)(2,1)S(1)}, bf16[1,2048,128]{2,1,0:T(8,128)(2,1)}, u32[]{:S(2)}) copy-start(bf16[1,2048,128]{2,1,0:T(8,128)(2,1)} %param.8) | copy-start | bytes 1572868
  97.9 16.7 %copy-start.6 = (bf16[1,2048,128]{2,1,0:T(8,128)(2,1)S(1)}, bf16[1,2048,128]{2,1,0:T(8,128)(2,1)}, u32[]{:S(2)}) copy-start(bf16[1,2048,128]{2,1,0:T(8,128)(2,1)} %param.9) | copy-start | bytes 1572868
  97.9 16.6 %collective-permute-start.13 = (bf16[2,512,128]{2,1,0:T(8,128)(2,1)S(1)}, bf16[2,512,128]{2,1,0:T(8,128)(2,1)S(1)}, u32[]{:S(2)}, u32[]{:S(2)}) collective-permute-start(bf16[2,512,128]{2,1,0:T(8,128)(2,1)S(1)} %get-tuple-element.25), channel_id=1, source_target_pairs={{0,32},{1,33},{2,34},{3,35},{4,36},{5,37},{6,38},{7,39},{8,40},{9,... | collective-permute-start | bytes 786440 | tf_op jit(solution)/shard_map/ppermute | solution.py:31
  101.9 12.7 %collective-permute-start.14 = (bf16[2,512,128]{2,1,0:T(8,128)(2,1)S(1)}, bf16[2,512,128]{2,1,0:T(8,128)(2,1)S(1)}, u32[]{:S(2)}, u32[]{:S(2)}) collective-permute-start(bf16[2,512,128]{2,1,0:T(8,128)(2,1)S(1)} %get-tuple-element.25), channel_id=1, source_target_pairs={{32,0},{33,1},{34,2},{35,3},{36,4},{37,5},{38,6},{39,7},{40,8},{41... | collective-permute-start | bytes 786440 | tf_op jit(solution)/shard_map/ppermute | solution.py:31
  107.7 14.9 %collective-permute-start.15 = (bf16[2,512,128]{2,1,0:T(8,128)(2,1)S(1)}, bf16[2,512,128]{2,1,0:T(8,128)(2,1)S(1)}, u32[]{:S(2)}, u32[]{:S(2)}) collective-permute-start(bf16[2,512,128]{2,1,0:T(8,128)(2,1)S(1)} %get-tuple-element.32), channel_id=1, source_target_pairs={{0,32},{1,33},{2,34},{3,35},{4,36},{5,37},{6,38},{7,39},{8,40},{9,... | collective-permute-start | bytes 786440 | tf_op jit(solution)/shard_map/ppermute | solution.py:31
  112.6 10.0 %collective-permute-start.16 = (bf16[2,512,128]{2,1,0:T(8,128)(2,1)S(1)}, bf16[2,512,128]{2,1,0:T(8,128)(2,1)S(1)}, u32[]{:S(2)}, u32[]{:S(2)}) collective-permute-start(bf16[2,512,128]{2,1,0:T(8,128)(2,1)S(1)} %get-tuple-element.32), channel_id=1, source_target_pairs={{32,0},{33,1},{34,2},{35,3},{36,4},{37,5},{38,6},{39,7},{40,8},{41... | collective-permute-start | bytes 786440 | tf_op jit(solution)/shard_map/ppermute | solution.py:31
  117.4 25.3 %collective-permute-start.17 = (bf16[2048,128]{1,0:T(8,128)(2,1)S(1)}, bf16[2048,128]{1,0:T(8,128)(2,1)S(1)}, u32[]{:S(2)}, u32[]{:S(2)}) collective-permute-start(bf16[2048,128]{1,0:T(8,128)(2,1)S(1)} %get-tuple-element.30), channel_id=1, source_target_pairs={{0,8},{1,9},{2,10},{3,11},{4,12},{5,13},{6,14},{7,15},{8,0},{9,1},... | collective-permute-start | bytes 1572872 | tf_op jit(solution)/shard_map/ppermute | solution.py:31
  122.6 21.1 %copy-start.7 = (f32[1,2048,128]{2,1,0:T(8,128)S(1)}, f32[1,2048,128]{2,1,0:T(8,128)}, u32[]{:S(2)}) copy-start(f32[1,2048,128]{2,1,0:T(8,128)} %param.5) | copy-start | bytes 3145732
  125.5 17.2 %collective-permute-start.19 = (bf16[2048,128]{1,0:T(8,128)(2,1)S(1)}, bf16[2048,128]{1,0:T(8,128)(2,1)S(1)}, u32[]{:S(2)}, u32[]{:S(2)}) collective-permute-start(bf16[2048,128]{1,0:T(8,128)(2,1)S(1)} %get-tuple-element.36), channel_id=1, source_target_pairs={{0,12},{1,13},{2,14},{3,15},{4,0},{5,1},{6,2},{7,3},{8,4},{9,5},{1... | collective-permute-start | bytes 1572872 | tf_op jit(solution)/shard_map/ppermute | solution.py:31
  128.7 15.1 %collective-permute-start.18 = (bf16[2048,128]{1,0:T(8,128)(2,1)S(1)}, bf16[2048,128]{1,0:T(8,128)(2,1)S(1)}, u32[]{:S(2)}, u32[]{:S(2)}) collective-permute-start(bf16[2048,128]{1,0:T(8,128)(2,1)S(1)} %get-tuple-element.35), channel_id=1, source_target_pairs={{0,4},{1,5},{2,6},{3,7},{4,8},{5,9},{6,10},{7,11},{8,12},{9,13},{1... | collective-permute-start | bytes 1572872 | tf_op jit(solution)/shard_map/ppermute | solution.py:31
